TPU v7x, 32 devices: a whole 2x2x4 slice. The times are simulated.
32 devices in a mesh: row: 8 (over z, x), col: 4 (over y, core).
Axes of the slice: x: 2, y: 2, z: 4, core: 2. Of those that a mesh axis runs over, the one named last changes fastest.
Arguments:
- object_field: float32 [2, 3072, 1536], P(None, 'row', 'col'), may hold values from -6 to 6
- probe: float32 [2, 256, 256], replicated, may hold values from -5 to 5
- amplitudes: float32 [4096, 2048], P('row', 'col'), may hold values from 0.2 to 3
- offsets: int32 [16, 8, 2], P('row', 'col'), may hold values from 0 to 128, as said below
Outputs:
- updated_object: float32 [2, 3072, 1536], P(None, 'row', 'col')
Inputs may be any that keep to these rules, and one draw needn't show every extreme that they name: Both offsets of every scan position lie in 0 to 128, and each end of that range is taken in every draw.
All inputs are finite; a program needn't handle non-finite values.
Results may differ from a plain program's by a relative error of at most 0.0003.
Values sent between devices are 32-bit elements; how exact they have to be, the bound alone decides.
No kernel may reach another device: no remote copies, remote signals or barrier semaphores. Data moves between devices by JAX's collectives and lax.ppermute only.
A program may use at most 64 MiB of HBM per device.

v0:
```python
import functools
import math

import jax
import jax.numpy as jnp
import numpy as np
from jax import lax
from jax.experimental import pallas as pl
from jax.experimental.pallas import tpu as pltpu
from jax.sharding import PartitionSpec as P

WIN = 256
HALF = 128
MARGIN = 96
LANE = 128

step_size = 0.3
tv_weight = 0.2
tv_smooth = 0.1
amp_floor = 0.5

F32 = jnp.float32
BF16 = jnp.bfloat16


def tables():
    counter = np.arange(HALF)
    angle = (counter[:, None] * counter[None, :] % HALF) * (2.0 * math.pi / HALF)
    cosine = np.cos(angle) / math.sqrt(WIN)
    sine = np.sin(angle) / math.sqrt(WIN)
    first = np.block([[cosine, sine], [-sine, cosine]])
    second = np.block([[cosine, -sine], [sine, cosine]])
    parts = []
    for table in (first, second):
        table = table.astype(np.float32)
        high = table.astype(jnp.bfloat16)
        low = (table - high.astype(np.float32)).astype(jnp.bfloat16)
        parts += [high, low]
    turn = counter * (2.0 * math.pi / WIN)
    rows = np.stack([np.cos(turn), np.sin(turn)])
    by_row = np.broadcast_to(rows[:, :, None], (2, HALF, HALF))
    by_lane = np.broadcast_to(rows[:, None, :], (2, HALF, HALF))
    twiddle = np.concatenate([by_row, by_lane]).astype(np.float32)
    order = np.zeros((WIN, WIN), np.float32)
    for parity in range(2):
        order[2 * counter + parity, parity * HALF + counter] = 1.0
    return np.stack(parts), twiddle, order.astype(jnp.bfloat16)


def split(value):
    high = value.astype(BF16)
    return high, (value - high.astype(F32)).astype(BF16)


def mul(left, right):
    return jnp.dot(left, right, preferred_element_type=F32)


def vmem(count):
    return [pl.BlockSpec(memory_space=pltpu.VMEM)] * count


def prepare_kernel(off_ref, probe_ref, amp_ref, order_ref, probes_ref, amps_ref, parts_ref):
    order = order_ref[...]
    for i in range(2):
        for j in range(2):
            row = off_ref[i, j, 0]
            col = off_ref[i, j, 1] + (32 if j == 0 else 96)
            for channel in range(2):
                turned = pltpu.roll(probe_ref[channel], row, 0)
                probes_ref[2 * i + j, channel] = pltpu.roll(turned, col, 1)
            amp = amp_ref[i * WIN : (i + 1) * WIN, j * WIN : (j + 1) * WIN]
            high, rest = split(amp)
            middle, low = split(amp - high.astype(F32) - rest.astype(F32))
            sorted_lanes = mul(high, order) + mul(rest, order) + mul(middle, order)
            for q in range(2):
                parts_ref[...] = sorted_lanes[:, q * HALF : (q + 1) * HALF]
                for p in range(2):
                    at = q * WIN + p * HALF
                    amps_ref[2 * i + j, at : at + HALF, :] = parts_ref[pl.ds(p, HALF, stride=2), :]


def prepare(offsets, probe, amplitudes, order):
    return pl.pallas_call(
        prepare_kernel,
        out_shape=(
            jax.ShapeDtypeStruct((4, 2, WIN, WIN), F32),
            jax.ShapeDtypeStruct((4, 2 * WIN, HALF), F32),
        ),
        in_specs=[pl.BlockSpec(memory_space=pltpu.SMEM)] + vmem(3),
        out_specs=tuple(vmem(2)),
        scratch_shapes=[pltpu.VMEM((WIN, HALF), F32)],
        cost_estimate=pl.CostEstimate(flops=400_000_000, bytes_accessed=6_000_000, transcendentals=0),
        name="prepare",
    )(offsets, probe, amplitudes, order)


def windows_kernel(i, plan, acc_at, outs, off_ref, tab_ref, tw_ref, probes_ref, amps_ref, *refs):
    operands = sum(len(part) for part in plan)
    ins, refs = refs[:operands], refs[operands:]
    carried = ()
    if acc_at is not None:
        carried, refs = refs[:3], refs[3:]
    out_refs, refs = refs[: 3 * len(outs)], refs[3 * len(outs) :]
    reg, can, gh, gl, hh, hl, wide, tall = refs
    spans = ((0, LANE), (LANE, 4 * LANE), (4 * LANE, 5 * LANE))

    which = 0
    for part, (lo, hi) in zip(plan, spans):
        row = 0
        for first, rows in part:
            for channel in range(2):
                reg[channel, row : row + rows, lo:hi] = ins[which][channel, first : first + rows, :]
            row += rows
            which += 1

    can[...] = jnp.zeros_like(can)
    if acc_at is not None:
        for ref, (lo, hi) in zip(carried, spans):
            for channel in range(2):
                can[channel, acc_at : acc_at + 192, lo:hi] = ref[channel]

    def variation(step, _):
        base = pl.multiple_of(MARGIN - 8 + step * 32, 8)
        flows = []
        power = tv_smooth
        for channel in range(2):
            block = reg[channel, pl.ds(base, 48), :]
            down = pltpu.roll(block, 47, 0) - block
            right = pltpu.roll(block, 5 * LANE - 1, 1) - block
            power = power + down * down + right * right
            flows.append((down, right))
        inverse = lax.rsqrt(power)
        for channel in range(2):
            down, right = flows[channel]
            down = down * inverse
            right = right * inverse
            change = pltpu.roll(down, 1, 0) - down + pltpu.roll(right, 1, 1) - right
            at = pl.multiple_of(base + 8, 8)
            here = (channel, pl.ds(at, 32), slice(LANE, 4 * LANE))
            can[here] = can[here] + tv_weight * change[8:40, LANE : 4 * LANE]
        return 0

    lax.fori_loop(0, 6, variation, 0)

    row_iota = lax.broadcasted_iota(jnp.int32, (HALF, HALF), 0)
    lane_iota = lax.broadcasted_iota(jnp.int32, (HALF, HALF), 1)
    first_h, first_l, second_h, second_l = (tab_ref[n] for n in range(4))

    def store_split(high_ref, low_ref, at, value):
        high, low = split(value)
        high_ref[at] = high
        low_ref[at] = low

    def window(j, _):
        row_start = off_ref[i, j, 0]
        col_start = off_ref[i, j, 1] + 32 + 64 * j
        in_row = row_iota >= row_start

        def lanes(cb):
            return pl.ds(pl.multiple_of((j + cb) * LANE, LANE), LANE)

        number = 2 * i + j
        for cb in range(2):
            in_col = lane_iota + cb * LANE >= col_start
            field = []
            for rb in range(2):
                value = []
                for channel in range(2):
                    near = reg[channel, rb * HALF : (rb + 1) * HALF, lanes(cb)]
                    far = reg[channel, rb * HALF : (rb + 1) * HALF, lanes(cb + 2)]
                    picked = jnp.where(in_col, near, far)
                    if rb == 0:
                        near = reg[channel, WIN : WIN + HALF, lanes(cb)]
                        far = reg[channel, WIN : WIN + HALF, lanes(cb + 2)]
                        picked = jnp.where(in_row, picked, jnp.where(in_col, near, far))
                    value.append(picked)
                box = (slice(rb * HALF, (rb + 1) * HALF), slice(cb * LANE, (cb + 1) * LANE))
                p_re = probes_ref[(number, 0) + box]
                p_im = probes_ref[(number, 1) + box]
                field.append((p_re * value[0] - p_im * value[1], p_re * value[1] + p_im * value[0]))
            (re0, im0), (re1, im1) = field
            even = slice(cb * LANE, (cb + 1) * LANE)
            odd = slice(WIN + cb * LANE, WIN + (cb + 1) * LANE)
            store_split(gh, gl, (slice(0, HALF), even), re0 + re1)
            store_split(gh, gl, (slice(HALF, WIN), even), im0 + im1)
            d_re = re0 - re1
            d_im = im0 - im1
            tw_c, tw_s = tw_ref[0], tw_ref[1]
            store_split(gh, gl, (slice(0, HALF), odd), d_re * tw_c + d_im * tw_s)
            store_split(gh, gl, (slice(HALF, WIN), odd), d_im * tw_c - d_re * tw_s)
        g_h = gh[...]
        wide[...] = mul(first_h, g_h) + mul(first_h, gl[...]) + mul(first_l, g_h)

        tl_c, tl_s = tw_ref[2], tw_ref[3]
        re_l, im_l = slice(0, HALF), slice(HALF, WIN)
        for p in range(2):
            c0 = slice(p * WIN, p * WIN + LANE)
            c1 = slice(p * WIN + LANE, (p + 1) * WIN)
            re0, re1 = wide[:HALF, c0], wide[:HALF, c1]
            im0, im1 = wide[HALF:, c0], wide[HALF:, c1]
            rows = slice(p * HALF, (p + 1) * HALF)
            store_split(hh, hl, (rows, re_l), re0 + re1)
            store_split(hh, hl, (rows, im_l), im0 + im1)
            d_re = re0 - re1
            d_im = im0 - im1
            rows = slice(WIN + p * HALF, WIN + (p + 1) * HALF)
            store_split(hh, hl, (rows, re_l), d_re * tl_c + d_im * tl_s)
            store_split(hh, hl, (rows, im_l), d_im * tl_c - d_re * tl_s)
        h_h = hh[...]
        tall[...] = mul(h_h, second_h) + mul(hl[...], second_h) + mul(h_h, second_l)

        for n in range(4):
            rows = slice(n * HALF, (n + 1) * HALF)
            re, im = tall[rows, re_l], tall[rows, im_l]
            power = jnp.maximum(re * re + im * im, amp_floor * amp_floor)
            keeping = 1.0 - amps_ref[number, rows, :] * lax.rsqrt(power)
            store_split(hh, hl, (rows, re_l), re * keeping)
            store_split(hh, hl, (rows, im_l), im * keeping)
        h_h = hh[...]
        tall[...] = mul(h_h, first_h) + mul(hl[...], first_h) + mul(h_h, first_l)

        for p in range(2):
            rows = slice(p * HALF, (p + 1) * HALF)
            u_re, u_im = tall[rows, re_l], tall[rows, im_l]
            rows = slice(WIN + p * HALF, WIN + (p + 1) * HALF)
            v_re, v_im = tall[rows, re_l], tall[rows, im_l]
            w_re = v_re * tl_c - v_im * tl_s
            w_im = v_im * tl_c + v_re * tl_s
            c0 = slice(p * WIN, p * WIN + LANE)
            c1 = slice(p * WIN + LANE, (p + 1) * WIN)
            store_split(gh, gl, (re_l, c0), u_re + w_re)
            store_split(gh, gl, (re_l, c1), u_re - w_re)
            store_split(gh, gl, (im_l, c0), u_im + w_im)
            store_split(gh, gl, (im_l, c1), u_im - w_im)
        g_h = gh[...]
        wide[...] = mul(second_h, g_h) + mul(second_h, gl[...]) + mul(second_l, g_h)

        tw_c, tw_s = tw_ref[0], tw_ref[1]
        for cb in range(2):
            in_col = lane_iota + cb * LANE >= col_start
            c0 = slice(cb * LANE, (cb + 1) * LANE)
            c1 = slice(WIN + cb * LANE, WIN + (cb + 1) * LANE)
            u_re, u_im = wide[:HALF, c0], wide[HALF:, c0]
            v_re, v_im = wide[:HALF, c1], wide[HALF:, c1]
            w_re = v_re * tw_c - v_im * tw_s
            w_im = v_im * tw_c + v_re * tw_s
            for rb in range(2):
                b_re = u_re + w_re if rb == 0 else u_re - w_re
                b_im = u_im + w_im if rb == 0 else u_im - w_im
                box = (slice(rb * HALF, (rb + 1) * HALF), c0)
                p_re = probes_ref[(number, 0) + box]
                p_im = probes_ref[(number, 1) + box]
                grads = (p_re * b_re + p_im * b_im, p_re * b_im - p_im * b_re)
                for channel in range(2):
                    grad = grads[channel]
                    targets = [(rb * HALF, grad)]
                    if rb == 0:
                        targets = [
                            (0, jnp.where(in_row, grad, 0.0)),
                            (WIN, jnp.where(in_row, 0.0, grad)),
                        ]
                    for at, piece in targets:
                        here = (channel, slice(at, at + HALF), lanes(cb))
                        can[here] = can[here] + jnp.where(in_col, piece, 0.0)
                        here = (channel, slice(at, at + HALF), lanes(cb + 2))
                        can[here] = can[here] + jnp.where(in_col, 0.0, piece)
        return 0

    lax.fori_loop(0, 2, window, 0)

    which = 0
    for first, rows in outs:
        for lo, hi in spans:
            for channel in range(2):
                out_refs[which][channel] = can[channel, first : first + rows, lo:hi]
            which += 1


def windows(i, consts, parts, carried, acc_at, outs):
    offsets, table, twiddle, probes, amps = consts
    plan = tuple(tuple((first, rows) for _, first, rows in part) for part in parts)
    operands = [array for part in parts for array, _, _ in part]
    extra = list(carried) if carried is not None else []
    own = parts[1][0][0].shape[-1]
    assert own == 3 * LANE
    shapes = []
    for _, rows in outs:
        for width in (LANE, own, LANE):
            shapes.append(jax.ShapeDtypeStruct((2, rows, width), F32))
    return pl.pallas_call(
        functools.partial(windows_kernel, i, plan, acc_at, outs),
        out_shape=tuple(shapes),
        in_specs=[pl.BlockSpec(memory_space=pltpu.SMEM)] + vmem(4 + len(operands) + len(extra)),
        out_specs=tuple(vmem(len(shapes))),
        scratch_shapes=[
            pltpu.VMEM((2, own, 5 * LANE), F32),
            pltpu.VMEM((2, own, 5 * LANE), F32),
            pltpu.VMEM((WIN, 2 * WIN), BF16),
            pltpu.VMEM((WIN, 2 * WIN), BF16),
            pltpu.VMEM((2 * WIN, WIN), BF16),
            pltpu.VMEM((2 * WIN, WIN), BF16),
            pltpu.VMEM((WIN, 2 * WIN), F32),
            pltpu.VMEM((2 * WIN, WIN), F32),
        ],
        cost_estimate=pl.CostEstimate(flops=1_600_000_000, bytes_accessed=10_000_000, transcendentals=0),
        name=f"windows_{i}",
    )(offsets, table, twiddle, probes, amps, *operands, *extra)


def totals_kernel(outs, own_ref, left_ref, right_ref, *out_refs):
    for (first, rows), out in zip(outs, out_refs):
        span = slice(first, first + rows)
        for channel in range(2):
            out[channel, :, :LANE] = own_ref[channel, span, :LANE] + left_ref[channel, span, :]
            out[channel, :, LANE : 2 * LANE] = own_ref[channel, span, LANE : 2 * LANE]
            out[channel, :, 2 * LANE :] = own_ref[channel, span, 2 * LANE :] + right_ref[channel, span, :]


def totals(own, from_left, from_right, outs):
    return pl.pallas_call(
        functools.partial(totals_kernel, outs),
        out_shape=tuple(jax.ShapeDtypeStruct((2, rows, own.shape[2]), F32) for _, rows in outs),
        in_specs=vmem(3),
        out_specs=tuple(vmem(len(outs))),
        cost_estimate=pl.CostEstimate(flops=500_000, bytes_accessed=3_000_000, transcendentals=0),
        name="totals",
    )(own, from_left, from_right)


def update_kernel(pieces, guard, *refs):
    new, left, right = refs[-3:]
    ins = refs[:-3]
    row = 0
    for which, first, rows, grads, masked in pieces:
        for channel in range(2):
            total = None
            for grad, at in grads:
                term = ins[grad][channel, at : at + rows, :]
                total = term if total is None else total + term
            value = ins[which][channel, first : first + rows, :] - step_size * total
            if masked:
                value = jnp.where(guard(), value, 0.0)
            new[channel, row : row + rows, :] = value
            left[channel, row : row + rows, :] = value[:, :LANE]
            right[channel, row : row + rows, :] = value[:, 2 * LANE :]
        row += rows


def update(operands, pieces, guard):
    rows = sum(piece[2] for piece in pieces)
    shape = [jax.ShapeDtypeStruct((2, rows, width), F32) for width in (3 * LANE, LANE, LANE)]
    return pl.pallas_call(
        functools.partial(update_kernel, pieces, guard),
        out_shape=tuple(shape),
        in_specs=vmem(len(operands)),
        out_specs=tuple(vmem(3)),
        cost_estimate=pl.CostEstimate(flops=1_000_000, bytes_accessed=4_000_000, transcendentals=0),
        name="update",
    )(*operands)


def finish_kernel(top_ref, bottom_ref, mid_ref, low_ref, above_ref, below_ref, out_ref):
    for channel in range(2):
        above = mid_ref[channel, :MARGIN, :] + above_ref[channel]
        out_ref[channel, :MARGIN, :] = top_ref[channel, MARGIN:, :] - step_size * above
        out_ref[channel, MARGIN:288, :] = bottom_ref[channel, :192, :] - step_size * mid_ref[channel, MARGIN:, :]
        below = low_ref[channel] + below_ref[channel]
        out_ref[channel, 288:, :] = bottom_ref[channel, 192:288, :] - step_size * below


def finish(*operands):
    return pl.pallas_call(
        finish_kernel,
        out_shape=jax.ShapeDtypeStruct((2, 3 * LANE, 3 * LANE), F32),
        in_specs=vmem(len(operands)),
        out_specs=pl.BlockSpec(memory_space=pltpu.VMEM),
        cost_estimate=pl.CostEstimate(flops=1_000_000, bytes_accessed=4_000_000, transcendentals=0),
        name="finish",
    )(*operands)


def moved(block, axis, distance):
    devices = range(lax.axis_size(axis))
    route = [(n, n + distance) for n in devices if n + distance in devices]
    return lax.ppermute(block, axis, route)


def sideways(to_right, to_left):
    return moved(to_right, "col", 1), moved(to_left, "col", -1)


def on_device(table, twiddle, order, object_field, probe, amplitudes, offsets):
    tile = object_field.shape[1]
    last = tile - MARGIN
    band = 2 * MARGIN
    edge = tile - LANE
    obj = object_field

    top = moved(obj[:, last:, :], "row", 1)
    bottom = moved(obj[:, :MARGIN, :], "row", -1)
    left, right = sideways(obj[:, :, edge:], obj[:, :, :LANE])
    probes, amps = prepare(offsets, probe, amplitudes, order)
    consts = (offsets, table, twiddle, probes, amps)

    top_l, top_r = sideways(top[:, :, edge:], top[:, :, :LANE])
    parts = (
        [(top_l, 0, MARGIN), (left, 0, last)],
        [(top, 0, MARGIN), (obj, 0, last)],
        [(top_r, 0, MARGIN), (right, 0, last)],
    )
    lo_l, lo_o, lo_r, mid_l, mid_o, mid_r = windows(0, consts, parts, None, None, ((0, band), (band, band)))
    in_l, in_r = sideways(lo_r, lo_l)
    (top_sum,) = totals(lo_o, in_l, in_r, ((0, band),))
    from_below = moved(top_sum, "row", -1)

    bot_l, bot_r = sideways(bottom[:, :, edge:], bottom[:, :, :LANE])
    parts = (
        [(left, MARGIN, last), (bot_l, 0, MARGIN)],
        [(obj, MARGIN, last), (bottom, 0, MARGIN)],
        [(right, MARGIN, last), (bot_r, 0, MARGIN)],
    )
    hi_l, hi_o, hi_r = windows(1, consts, parts, (mid_l, mid_o, mid_r), 0, ((0, tile),))
    in_l, in_r = sideways(hi_r, hi_l)
    mid_sum, bot_sum = totals(hi_o, in_l, in_r, ((0, band), (band, band)))
    from_above = moved(bot_sum, "row", 1)

    def not_last():
        return lax.axis_index("row") < lax.axis_size("row") - 1

    def not_first():
        return lax.axis_index("row") > 0

    low, low_to_left, low_to_right = update(
        (obj, bottom, mid_sum, bot_sum, from_below),
        (
            (0, MARGIN, band, ((2, 0),), False),
            (0, last, MARGIN, ((3, 0), (4, 0)), False),
            (1, 0, MARGIN, ((3, MARGIN), (4, MARGIN)), True),
        ),
        not_last,
    )
    low_l, low_r = sideways(low_to_right, low_to_left)
    parts = ([(low_l, 0, tile)], [(low, 0, tile)], [(low_r, 0, tile)])
    mid_l, mid_o, mid_r, hi_l, hi_o, hi_r = windows(1, consts, parts, None, None, ((0, band), (band, band)))
    in_l, in_r = sideways(hi_r, hi_l)
    low_sum, over = totals(hi_o, in_l, in_r, ((0, MARGIN), (MARGIN, MARGIN)))
    last_above = moved(over, "row", 1)

    up, up_to_left, up_to_right = update(
        (top, obj, top_sum, from_above),
        (
            (0, 0, MARGIN, ((2, 0), (3, 0)), True),
            (1, 0, MARGIN, ((2, MARGIN), (3, MARGIN)), False),
        ),
        not_first,
    )
    up_l, up_r = sideways(up_to_right, up_to_left)
    parts = (
        [(up_l, 0, band), (low_l, 0, band)],
        [(up, 0, band), (low, 0, band)],
        [(up_r, 0, band), (low_r, 0, band)],
    )
    lo_l, lo_o, lo_r = windows(0, consts, parts, (mid_l, mid_o, mid_r), band, ((0, tile),))
    in_l, in_r = sideways(lo_r, lo_l)
    over, mid_sum = totals(lo_o, in_l, in_r, ((0, MARGIN), (MARGIN, last)))
    last_below = moved(over, "row", -1)
    return finish(up, low, mid_sum, low_sum, last_above, last_below)


def solution(mesh):
    table, twiddle, order = tables()
    body = jax.shard_map(
        on_device,
        mesh=mesh,
        in_specs=(P(), P(), P(), P(None, "row", "col"), P(), P("row", "col"), P("row", "col", None)),
        out_specs=P(None, "row", "col"),
        check_vma=False,
    )

    def step(object_field, probe, amplitudes, offsets):
        return body(table, twiddle, order, object_field, probe, amplitudes, offsets)

    return step
```

profile of v0, /device:TPU:3, one launch (start us, length us, event | category | flops | bytes accessed | tf_op | source)
XLA Modules:
  0.0 174.4 jit_solution(13194491842166887149)
XLA Ops:
  0.0 1.2 fusion
  1.2 3.2 %collective-permute-start = (f32[2,96,384]{2,1,0:T(8,128)S(1)}, f32[2,96,384]{2,1,0:T(8,128)S(1)}, u32[]{:S(2)}, u32[]{:S(2)}) collective-permute-start(f32[2,96,384]{2,1,0:T(8,128)S(1)} %get-tuple-element.70), channel_id=1, source_target_pairs={{0,4},{4,8},{8,12},{12,16},{16,20},{20,24},{24,28},{1,5},{5,9},{9,... | collective-permute-start | bytes 884744 | tf_op jit(solution)/shard_map/ppermute | solution.py:386
  4.4 2.1 %collective-permute-start.7 = (f32[2,96,384]{2,1,0:T(8,128)S(1)}, f32[2,96,384]{2,1,0:T(8,128)S(1)}, u32[]{:S(2)}, u32[]{:S(2)}) collective-permute-start(f32[2,96,384]{2,1,0:T(8,128)S(1)} %get-tuple-element.69), channel_id=1, source_target_pairs={{4,0},{8,4},{12,8},{16,12},{20,16},{24,20},{28,24},{5,1},{9,5},{13... | collective-permute-start | bytes 884744 | tf_op jit(solution)/shard_map/ppermute | solution.py:386
  6.6 4.3 %collective-permute-start.2 = (f32[2,384,128]{2,1,0:T(8,128)S(1)}, f32[2,384,128]{2,1,0:T(8,128)S(1)}, u32[]{:S(2)}, u32[]{:S(2)}) collective-permute-start(f32[2,384,128]{2,1,0:T(8,128)S(1)} %get-tuple-element.72), channel_id=1, source_target_pairs={{0,1},{1,2},{2,3},{4,5},{5,6},{6,7},{8,9},{9,10},{10,11},{12,13},{... | collective-permute-start | bytes 1179656 | tf_op jit(solution)/shard_map/ppermute | solution.py:386
  10.9 1.9 %collective-permute-start.4 = (f32[2,384,128]{2,1,0:T(8,128)S(1)}, f32[2,384,128]{2,1,0:T(8,128)S(1)}, u32[]{:S(2)}, u32[]{:S(2)}) collective-permute-start(f32[2,384,128]{2,1,0:T(8,128)S(1)} %get-tuple-element.71), channel_id=1, source_target_pairs={{1,0},{2,1},{3,2},{5,4},{6,5},{7,6},{9,8},{10,9},{11,10},{13,12},{... | collective-permute-start | bytes 1179656 | tf_op jit(solution)/shard_map/ppermute | solution.py:386
  12.8 4.3 %prepare.1 = (f32[4,2,256,256]{3,2,1,0:T(8,128)}, f32[4,512,128]{2,1,0:T(8,128)}) custom-call(s32[2,2,2]{2,1,0:T(2,128)} %off_ref.9, f32[2,256,256]{2,1,0:T(8,128)} %probe_ref.1, f32[512,512]{1,0:T(8,128)} %amp_ref.1, bf16[256,256]{1,0:T(8,128)(2,1)} %constant.8.clone.order_ref), custom_call_target="tpu_custom_call" | custom-call | flops 400000000 | bytes 6000000 | tf_op jit(solution)/shard_map/prepare/pallas_call | solution.py:84
  17.3 4.6 %collective-permute-start.1 = (f32[2,96,128]{2,1,0:T(8,128)S(1)}, f32[2,96,128]{2,1,0:T(8,128)S(1)}, u32[]{:S(2)}, u32[]{:S(2)}) collective-permute-start(f32[2,96,128]{2,1,0:T(8,128)S(1)} %get-tuple-element.76), channel_id=1, source_target_pairs={{0,1},{1,2},{2,3},{4,5},{5,6},{6,7},{8,9},{9,10},{10,11},{12,13},{... | collective-permute-start | bytes 294920 | tf_op jit(solution)/shard_map/ppermute | solution.py:386
  21.9 1.9 %collective-permute-start.3 = (f32[2,96,128]{2,1,0:T(8,128)S(1)}, f32[2,96,128]{2,1,0:T(8,128)S(1)}, u32[]{:S(2)}, u32[]{:S(2)}) collective-permute-start(f32[2,96,128]{2,1,0:T(8,128)S(1)} %get-tuple-element.75), channel_id=1, source_target_pairs={{1,0},{2,1},{3,2},{5,4},{6,5},{7,6},{9,8},{10,9},{11,10},{13,12},{... | collective-permute-start | bytes 294920 | tf_op jit(solution)/shard_map/ppermute | solution.py:386
  23.9 3.6 %collective-permute-start.8 = (f32[2,96,128]{2,1,0:T(8,128)S(1)}, f32[2,96,128]{2,1,0:T(8,128)S(1)}, u32[]{:S(2)}, u32[]{:S(2)}) collective-permute-start(f32[2,96,128]{2,1,0:T(8,128)S(1)} %get-tuple-element.74), channel_id=1, source_target_pairs={{0,1},{1,2},{2,3},{4,5},{5,6},{6,7},{8,9},{9,10},{10,11},{12,13},{... | collective-permute-start | bytes 294920 | tf_op jit(solution)/shard_map/ppermute | solution.py:386
  27.5 1.9 %collective-permute-start.9 = (f32[2,96,128]{2,1,0:T(8,128)S(1)}, f32[2,96,128]{2,1,0:T(8,128)S(1)}, u32[]{:S(2)}, u32[]{:S(2)}) collective-permute-start(f32[2,96,128]{2,1,0:T(8,128)S(1)} %get-tuple-element.73), channel_id=1, source_target_pairs={{1,0},{2,1},{3,2},{5,4},{6,5},{7,6},{9,8},{10,9},{11,10},{13,12},{... | collective-permute-start | bytes 294920 | tf_op jit(solution)/shard_map/ppermute | solution.py:386
  30.4 10.3 %windows_0.2 = (f32[2,192,128]{2,1,0:T(8,128)}, f32[2,192,384]{2,1,0:T(8,128)}, f32[2,192,128]{2,1,0:T(8,128)}, f32[2,192,128]{2,1,0:T(8,128)}, f32[2,192,384]{2,1,0:T(8,128)}, /*index=5*/f32[2,192,128]{2,1,0:T(8,128)}) custom-call(s32[2,2,2]{2,1,0:T(2,128)} %off_ref.9, bf16[4,256,256]{2,1,0:T(8,128)(2,1)} %constant.6.clone.tab_ref, ...), custom_call_target="tpu_custom_call" | custom-call | flops 1600000000 | bytes 10000000 | tf_op jit(solution)/shard_map/windows_0/pallas_call | solution.py:291
  40.7 3.6 %collective-permute-start.5 = (f32[2,192,128]{2,1,0:T(8,128)}, f32[2,192,128]{2,1,0:T(8,128)S(1)}, u32[]{:S(2)}, u32[]{:S(2)}) collective-permute-start(f32[2,192,128]{2,1,0:T(8,128)} %get-tuple-element.40), channel_id=1, source_target_pairs={{0,1},{1,2},{2,3},{4,5},{5,6},{6,7},{8,9},{9,10},{10,11},{12,13},{... | collective-permute-start | bytes 589832 | tf_op jit(solution)/shard_map/ppermute | solution.py:386
  44.4 1.9 %collective-permute-start.6 = (f32[2,192,128]{2,1,0:T(8,128)}, f32[2,192,128]{2,1,0:T(8,128)S(1)}, u32[]{:S(2)}, u32[]{:S(2)}) collective-permute-start(f32[2,192,128]{2,1,0:T(8,128)} %get-tuple-element.41), channel_id=1, source_target_pairs={{1,0},{2,1},{3,2},{5,4},{6,5},{7,6},{9,8},{10,9},{11,10},{13,12},{... | collective-permute-start | bytes 589832 | tf_op jit(solution)/shard_map/ppermute | solution.py:386
  47.0 10.6 %windows_1.2 = (f32[2,384,128]{2,1,0:T(8,128)}, f32[2,384,384]{2,1,0:T(8,128)}, f32[2,384,128]{2,1,0:T(8,128)}) custom-call(s32[2,2,2]{2,1,0:T(2,128)} %off_ref.9, bf16[4,256,256]{2,1,0:T(8,128)(2,1)} %constant.6.clone.tab_ref, f32[4,128,128]{2,1,0:T(8,128)} %constant.7.clone.tw_ref, f32[4,2,256,256]{3,2,1,0:T(8,128)} %get-tuple-element.37.probes_ref, ...), custom_call_target="tpu_custom_call" | custom-call | flops 1600000000 | bytes 10000000 | tf_op jit(solution)/shard_map/windows_1/pallas_call | solution.py:291
  57.6 3.6 %collective-permute-start.10 = (f32[2,384,128]{2,1,0:T(8,128)}, f32[2,384,128]{2,1,0:T(8,128)S(1)}, u32[]{:S(2)}, u32[]{:S(2)}) collective-permute-start(f32[2,384,128]{2,1,0:T(8,128)} %get-tuple-element.46), channel_id=1, source_target_pairs={{0,1},{1,2},{2,3},{4,5},{5,6},{6,7},{8,9},{9,10},{10,11},{12,13},{... | collective-permute-start | bytes 1179656 | tf_op jit(solution)/shard_map/ppermute | solution.py:386
  61.2 1.9 %collective-permute-start.11 = (f32[2,384,128]{2,1,0:T(8,128)}, f32[2,384,128]{2,1,0:T(8,128)S(1)}, u32[]{:S(2)}, u32[]{:S(2)}) collective-permute-start(f32[2,384,128]{2,1,0:T(8,128)} %get-tuple-element.47), channel_id=1, source_target_pairs={{1,0},{2,1},{3,2},{5,4},{6,5},{7,6},{9,8},{10,9},{11,10},{13,12},{... | collective-permute-start | bytes 1179656 | tf_op jit(solution)/shard_map/ppermute | solution.py:386
  63.9 2.1 %totals.4.refs_2_ = f32[2,192,384]{2,1,0:T(8,128)} custom-call(f32[2,192,384]{2,1,0:T(8,128)} %get-tuple-element.39.own_ref, f32[2,192,128]{2,1,0:T(8,128)} %copy-done.15, f32[2,192,128]{2,1,0:T(8,128)} %copy-done.16), custom_call_target="tpu_custom_call" | custom-call | flops 500000 | bytes 3000000 | tf_op jit(solution)/shard_map/totals/pallas_call | solution.py:321
  66.0 1.9 %collective-permute-start.13 = (f32[2,192,384]{2,1,0:T(8,128)}, f32[2,192,384]{2,1,0:T(8,128)S(1)}, u32[]{:S(2)}, u32[]{:S(2)}) collective-permute-start(f32[2,192,384]{2,1,0:T(8,128)} %totals.4.refs_2_), channel_id=1, source_target_pairs={{4,0},{8,4},{12,8},{16,12},{20,16},{24,20},{28,24},{5,1},{9,5},{13... | collective-permute-start | bytes 1769480 | tf_op jit(solution)/shard_map/ppermute | solution.py:386
  67.9 2.9 %collective-permute-done.11.right_ref = f32[2,384,128]{2,1,0:T(8,128)S(1)} collective-permute-done((f32[2,384,128]{2,1,0:T(8,128)}, f32[2,384,128]{2,1,0:T(8,128)S(1)}, u32[]{:S(2)}, u32[]{:S(2)}) %collective-permute-start.11) | collective-permute-done | bytes 393248 | tf_op jit(solution)/shard_map/ppermute | solution.py:386
  70.8 0.7 copy-done.12
  71.5 2.5 %totals.5 = (f32[2,192,384]{2,1,0:T(8,128)}, f32[2,192,384]{2,1,0:T(8,128)}) custom-call(f32[2,384,384]{2,1,0:T(8,128)} %get-tuple-element.45.own_ref, f32[2,384,128]{2,1,0:T(8,128)} %copy-done.11, f32[2,384,128]{2,1,0:T(8,128)} %copy-done.12), custom_call_target="tpu_custom_call" | custom-call | flops 500000 | bytes 3000000 | tf_op jit(solution)/shard_map/totals/pallas_call | solution.py:321
  74.1 2.9 %collective-permute-start.12 = (f32[2,192,384]{2,1,0:T(8,128)}, f32[2,192,384]{2,1,0:T(8,128)S(1)}, u32[]{:S(2)}, u32[]{:S(2)}) collective-permute-start(f32[2,192,384]{2,1,0:T(8,128)} %get-tuple-element.48.refs_3_), channel_id=1, source_target_pairs={{0,4},{4,8},{8,12},{12,16},{16,20},{20,24},{24,28},{1,5},{5,9},{9,... | collective-permute-start | bytes 1769480 | tf_op jit(solution)/shard_map/ppermute | solution.py:386
  77.0 5.8 %collective-permute-done.13.refs_4_ = f32[2,192,384]{2,1,0:T(8,128)S(1)} collective-permute-done((f32[2,192,384]{2,1,0:T(8,128)}, f32[2,192,384]{2,1,0:T(8,128)S(1)}, u32[]{:S(2)}, u32[]{:S(2)}) %collective-permute-start.13) | collective-permute-done | bytes 589856 | tf_op jit(solution)/shard_map/ppermute | solution.py:386
  82.8 0.8 copy-done.5
  83.6 3.2 %update.3 = (f32[2,384,384]{2,1,0:T(8,128)}, f32[2,384,128]{2,1,0:T(8,128)}, f32[2,384,128]{2,1,0:T(8,128)}) custom-call(f32[2,384,384]{2,1,0:T(8,128)} %refs_0_.1, f32[2,96,384]{2,1,0:T(8,128)} %copy-done.1, f32[2,192,384]{2,1,0:T(8,128)} %get-tuple-element.50.refs_2_, f32[2,192,384]{2,1,0:T(8,128)} %get-tuple-element.48.refs_3_, f32[2,192,384]{2,1,0:T(8,128)} %copy-done.5), custom_call_target="tpu_custom_call" | custom-call | flops 1000000 | bytes 4000000 | tf_op jit(solution)/shard_map/update/pallas_call | solution.py:353
  86.8 4.0 %collective-permute-start.15 = (f32[2,384,128]{2,1,0:T(8,128)}, f32[2,384,128]{2,1,0:T(8,128)S(1)}, u32[]{:S(2)}, u32[]{:S(2)}) collective-permute-start(f32[2,384,128]{2,1,0:T(8,128)} %get-tuple-element.53), channel_id=1, source_target_pairs={{0,1},{1,2},{2,3},{4,5},{5,6},{6,7},{8,9},{9,10},{10,11},{12,13},{... | collective-permute-start | bytes 1179656 | tf_op jit(solution)/shard_map/ppermute | solution.py:386
  90.8 1.9 %collective-permute-start.17 = (f32[2,384,128]{2,1,0:T(8,128)}, f32[2,384,128]{2,1,0:T(8,128)S(1)}, u32[]{:S(2)}, u32[]{:S(2)}) collective-permute-start(f32[2,384,128]{2,1,0:T(8,128)} %get-tuple-element.55), channel_id=1, source_target_pairs={{1,0},{2,1},{3,2},{5,4},{6,5},{7,6},{9,8},{10,9},{11,10},{13,12},{... | collective-permute-start | bytes 1179656 | tf_op jit(solution)/shard_map/ppermute | solution.py:386
  92.7 2.8 %collective-permute-done.12.refs_3_ = f32[2,192,384]{2,1,0:T(8,128)S(1)} collective-permute-done((f32[2,192,384]{2,1,0:T(8,128)}, f32[2,192,384]{2,1,0:T(8,128)S(1)}, u32[]{:S(2)}, u32[]{:S(2)}) %collective-permute-start.12) | collective-permute-done | bytes 589856 | tf_op jit(solution)/shard_map/ppermute | solution.py:386
  95.5 0.8 copy-done.6
  96.3 2.8 %update.2 = (f32[2,192,384]{2,1,0:T(8,128)}, f32[2,192,128]{2,1,0:T(8,128)}, f32[2,192,128]{2,1,0:T(8,128)}) custom-call(f32[2,96,384]{2,1,0:T(8,128)} %copy-done.2, f32[2,384,384]{2,1,0:T(8,128)} %refs_0_.1, f32[2,192,384]{2,1,0:T(8,128)} %totals.4.refs_2_, f32[2,192,384]{2,1,0:T(8,128)} %copy-done.6), custom_call_target="tpu_custom_call" | custom-call | flops 1000000 | bytes 4000000 | tf_op jit(solution)/shard_map/update/pallas_call | solution.py:353
  99.1 3.8 %collective-permute-start.14 = (f32[2,192,128]{2,1,0:T(8,128)}, f32[2,192,128]{2,1,0:T(8,128)S(1)}, u32[]{:S(2)}, u32[]{:S(2)}) collective-permute-start(f32[2,192,128]{2,1,0:T(8,128)} %get-tuple-element.52), channel_id=1, source_target_pairs={{0,1},{1,2},{2,3},{4,5},{5,6},{6,7},{8,9},{9,10},{10,11},{12,13},{... | collective-permute-start | bytes 589832 | tf_op jit(solution)/shard_map/ppermute | solution.py:386
  102.9 2.1 %collective-permute-start.16 = (f32[2,192,128]{2,1,0:T(8,128)}, f32[2,192,128]{2,1,0:T(8,128)S(1)}, u32[]{:S(2)}, u32[]{:S(2)}) collective-permute-start(f32[2,192,128]{2,1,0:T(8,128)} %get-tuple-element.54), channel_id=1, source_target_pairs={{1,0},{2,1},{3,2},{5,4},{6,5},{7,6},{9,8},{10,9},{11,10},{13,12},{... | collective-permute-start | bytes 589832 | tf_op jit(solution)/shard_map/ppermute | solution.py:386
  105.0 0.7 copy-done.7
  106.0 10.2 %windows_1.3 = (f32[2,192,128]{2,1,0:T(8,128)}, f32[2,192,384]{2,1,0:T(8,128)}, f32[2,192,128]{2,1,0:T(8,128)}, f32[2,192,128]{2,1,0:T(8,128)}, f32[2,192,384]{2,1,0:T(8,128)}, /*index=5*/f32[2,192,128]{2,1,0:T(8,128)}) custom-call(s32[2,2,2]{2,1,0:T(2,128)} %off_ref.9, bf16[4,256,256]{2,1,0:T(8,128)(2,1)} %constant.6.clone.tab_ref, ...), custom_call_target="tpu_custom_call" | custom-call | flops 1600000000 | bytes 10000000 | tf_op jit(solution)/shard_map/windows_1/pallas_call | solution.py:291
  117.0 10.7 %windows_0.3 = (f32[2,384,128]{2,1,0:T(8,128)}, f32[2,384,384]{2,1,0:T(8,128)}, f32[2,384,128]{2,1,0:T(8,128)}) custom-call(s32[2,2,2]{2,1,0:T(2,128)} %off_ref.9, bf16[4,256,256]{2,1,0:T(8,128)(2,1)} %constant.6.clone.tab_ref, f32[4,128,128]{2,1,0:T(8,128)} %constant.7.clone.tw_ref, f32[4,2,256,256]{3,2,1,0:T(8,128)} %get-tuple-element.37.probes_ref, ...), custom_call_target="tpu_custom_call" | custom-call | flops 1600000000 | bytes 10000000 | tf_op jit(solution)/shard_map/windows_0/pallas_call | solution.py:291
  127.7 3.6 %collective-permute-start.18 = (f32[2,384,128]{2,1,0:T(8,128)}, f32[2,384,128]{2,1,0:T(8,128)S(1)}, u32[]{:S(2)}, u32[]{:S(2)}) collective-permute-start(f32[2,384,128]{2,1,0:T(8,128)} %get-tuple-element.60), channel_id=1, source_target_pairs={{0,1},{1,2},{2,3},{4,5},{5,6},{6,7},{8,9},{9,10},{10,11},{12,13},{... | collective-permute-start | bytes 1179656 | tf_op jit(solution)/shard_map/ppermute | solution.py:386
  131.4 1.9 %collective-permute-start.19 = (f32[2,384,128]{2,1,0:T(8,128)}, f32[2,384,128]{2,1,0:T(8,128)S(1)}, u32[]{:S(2)}, u32[]{:S(2)}) collective-permute-start(f32[2,384,128]{2,1,0:T(8,128)} %get-tuple-element.61), channel_id=1, source_target_pairs={{1,0},{2,1},{3,2},{5,4},{6,5},{7,6},{9,8},{10,9},{11,10},{13,12},{... | collective-permute-start | bytes 1179656 | tf_op jit(solution)/shard_map/ppermute | solution.py:386
  133.3 3.6 %collective-permute-start.20 = (f32[2,192,128]{2,1,0:T(8,128)S(1)}, f32[2,192,128]{2,1,0:T(8,128)S(1)}, u32[]{:S(2)}, u32[]{:S(2)}) collective-permute-start(f32[2,192,128]{2,1,0:T(8,128)S(1)} %copy-done.26), channel_id=1, source_target_pairs={{0,1},{1,2},{2,3},{4,5},{5,6},{6,7},{8,9},{9,10},{10,11},{12,13},{... | collective-permute-start | bytes 589832 | tf_op jit(solution)/shard_map/ppermute | solution.py:386
  137.0 1.9 %collective-permute-start.21 = (f32[2,192,128]{2,1,0:T(8,128)S(1)}, f32[2,192,128]{2,1,0:T(8,128)S(1)}, u32[]{:S(2)}, u32[]{:S(2)}) collective-permute-start(f32[2,192,128]{2,1,0:T(8,128)S(1)} %copy-done.25), channel_id=1, source_target_pairs={{1,0},{2,1},{3,2},{5,4},{6,5},{7,6},{9,8},{10,9},{11,10},{13,12},{... | collective-permute-start | bytes 589832 | tf_op jit(solution)/shard_map/ppermute | solution.py:386
  139.5 4.4 %collective-permute-done.21.right_ref = f32[2,192,128]{2,1,0:T(8,128)S(1)} collective-permute-done((f32[2,192,128]{2,1,0:T(8,128)S(1)}, f32[2,192,128]{2,1,0:T(8,128)S(1)}, u32[]{:S(2)}, u32[]{:S(2)}) %collective-permute-start.21) | collective-permute-done | bytes 196640 | tf_op jit(solution)/shard_map/ppermute | solution.py:386
  144.6 2.1 %totals.7 = (f32[2,96,384]{2,1,0:T(8,128)}, f32[2,96,384]{2,1,0:T(8,128)}) custom-call(f32[2,192,384]{2,1,0:T(8,128)} %get-tuple-element.63.own_ref, f32[2,192,128]{2,1,0:T(8,128)} %copy-done.17, f32[2,192,128]{2,1,0:T(8,128)} %copy-done.18), custom_call_target="tpu_custom_call" | custom-call | flops 500000 | bytes 3000000 | tf_op jit(solution)/shard_map/totals/pallas_call | solution.py:321
  146.7 11.6 %collective-permute-start.22 = (f32[2,96,384]{2,1,0:T(8,128)}, f32[2,96,384]{2,1,0:T(8,128)S(1)}, u32[]{:S(2)}, u32[]{:S(2)}) collective-permute-start(f32[2,96,384]{2,1,0:T(8,128)} %get-tuple-element.67), channel_id=1, source_target_pairs={{0,4},{4,8},{8,12},{12,16},{16,20},{20,24},{24,28},{1,5},{5,9},{9,... | collective-permute-start | bytes 884744 | tf_op jit(solution)/shard_map/ppermute | solution.py:386
  158.3 0.7 copy-done.9
  159.2 2.5 %totals.6 = (f32[2,96,384]{2,1,0:T(8,128)}, f32[2,288,384]{2,1,0:T(8,128)}) custom-call(f32[2,384,384]{2,1,0:T(8,128)} %get-tuple-element.59.own_ref, f32[2,384,128]{2,1,0:T(8,128)} %copy-done.9, f32[2,384,128]{2,1,0:T(8,128)} %copy-done.10), custom_call_target="tpu_custom_call" | custom-call | flops 500000 | bytes 3000000 | tf_op jit(solution)/shard_map/totals/pallas_call | solution.py:321
  161.7 1.9 %collective-permute-start.23 = (f32[2,96,384]{2,1,0:T(8,128)}, f32[2,96,384]{2,1,0:T(8,128)S(1)}, u32[]{:S(2)}, u32[]{:S(2)}) collective-permute-start(f32[2,96,384]{2,1,0:T(8,128)} %get-tuple-element.68), channel_id=1, source_target_pairs={{4,0},{8,4},{12,8},{16,12},{20,16},{24,20},{28,24},{5,1},{9,5},{13... | collective-permute-start | bytes 884744 | tf_op jit(solution)/shard_map/ppermute | solution.py:386
  163.6 6.9 %collective-permute-done.23.below_ref = f32[2,96,384]{2,1,0:T(8,128)S(1)} collective-permute-done((f32[2,96,384]{2,1,0:T(8,128)}, f32[2,96,384]{2,1,0:T(8,128)S(1)}, u32[]{:S(2)}, u32[]{:S(2)}) %collective-permute-start.23) | collective-permute-done | bytes 294944 | tf_op jit(solution)/shard_map/ppermute | solution.py:386
  170.5 0.7 copy-done.14
  171.3 3.1 %finish.1 = f32[2,384,384]{2,1,0:T(8,128)} custom-call(f32[2,192,384]{2,1,0:T(8,128)} %get-tuple-element.49.refs_2_.top_ref, f32[2,384,384]{2,1,0:T(8,128)} %get-tuple-element.51.refs_1_.refs_3_.bottom_ref, f32[2,288,384]{2,1,0:T(8,128)} %get-tuple-element.62.mid_ref, f32[2,96,384]{2,1,0:T(8,128)} %get-tuple-element.66.low_ref, f32[2,96,384]{2,1,0:T(8,128)} %copy-done.13, ...), custom_call_target="tpu_custom_call" | custom-call | flops 1000000 | bytes 4000000 | tf_op jit(solution)/shard_map/finish/pallas_call | solution.py:373
  (70 shorter events, 5.1 us)
Async XLA Ops:
  0.0 6.5 %copy-start = (f32[2,384,384]{2,1,0:T(8,128)S(1)}, f32[2,384,384]{2,1,0:T(8,128)}, u32[]{:S(2)}) copy-start(f32[2,384,384]{2,1,0:T(8,128)} %refs_0_.1) | copy-start | bytes 3538948
  1.2 16.1 %collective-permute-start = (f32[2,96,384]{2,1,0:T(8,128)S(1)}, f32[2,96,384]{2,1,0:T(8,128)S(1)}, u32[]{:S(2)}, u32[]{:S(2)}) collective-permute-start(f32[2,96,384]{2,1,0:T(8,128)S(1)} %get-tuple-element.70), channel_id=1, source_target_pairs={{0,4},{4,8},{8,12},{12,16},{16,20},{20,24},{24,28},{1,5},{5,9},{9,... | collective-permute-start | bytes 884744 | tf_op jit(solution)/shard_map/ppermute | solution.py:386
  4.4 19.4 %collective-permute-start.7 = (f32[2,96,384]{2,1,0:T(8,128)S(1)}, f32[2,96,384]{2,1,0:T(8,128)S(1)}, u32[]{:S(2)}, u32[]{:S(2)}) collective-permute-start(f32[2,96,384]{2,1,0:T(8,128)S(1)} %get-tuple-element.69), channel_id=1, source_target_pairs={{4,0},{8,4},{12,8},{16,12},{20,16},{24,20},{28,24},{5,1},{9,5},{13... | collective-permute-start | bytes 884744 | tf_op jit(solution)/shard_map/ppermute | solution.py:386
  6.6 22.9 %collective-permute-start.2 = (f32[2,384,128]{2,1,0:T(8,128)S(1)}, f32[2,384,128]{2,1,0:T(8,128)S(1)}, u32[]{:S(2)}, u32[]{:S(2)}) collective-permute-start(f32[2,384,128]{2,1,0:T(8,128)S(1)} %get-tuple-element.72), channel_id=1, source_target_pairs={{0,1},{1,2},{2,3},{4,5},{5,6},{6,7},{8,9},{9,10},{10,11},{12,13},{... | collective-permute-start | bytes 1179656 | tf_op jit(solution)/shard_map/ppermute | solution.py:386
  10.9 18.7 %collective-permute-start.4 = (f32[2,384,128]{2,1,0:T(8,128)S(1)}, f32[2,384,128]{2,1,0:T(8,128)S(1)}, u32[]{:S(2)}, u32[]{:S(2)}) collective-permute-start(f32[2,384,128]{2,1,0:T(8,128)S(1)} %get-tuple-element.71), channel_id=1, source_target_pairs={{1,0},{2,1},{3,2},{5,4},{6,5},{7,6},{9,8},{10,9},{11,10},{13,12},{... | collective-permute-start | bytes 1179656 | tf_op jit(solution)/shard_map/ppermute | solution.py:386
  17.3 12.2 %copy-start.2 = (f32[2,96,384]{2,1,0:T(8,128)}, f32[2,96,384]{2,1,0:T(8,128)S(1)}, u32[]{:S(2)}) copy-start(f32[2,96,384]{2,1,0:T(8,128)S(1)} %collective-permute-done.refs_2_.refs_0_) | copy-start | bytes 884740
  17.3 10.2 %collective-permute-start.1 = (f32[2,96,128]{2,1,0:T(8,128)S(1)}, f32[2,96,128]{2,1,0:T(8,128)S(1)}, u32[]{:S(2)}, u32[]{:S(2)}) collective-permute-start(f32[2,96,128]{2,1,0:T(8,128)S(1)} %get-tuple-element.76), channel_id=1, source_target_pairs={{0,1},{1,2},{2,3},{4,5},{5,6},{6,7},{8,9},{9,10},{10,11},{12,13},{... | collective-permute-start | bytes 294920 | tf_op jit(solution)/shard_map/ppermute | solution.py:386
  21.9 7.6 %collective-permute-start.3 = (f32[2,96,128]{2,1,0:T(8,128)S(1)}, f32[2,96,128]{2,1,0:T(8,128)S(1)}, u32[]{:S(2)}, u32[]{:S(2)}) collective-permute-start(f32[2,96,128]{2,1,0:T(8,128)S(1)} %get-tuple-element.75), channel_id=1, source_target_pairs={{1,0},{2,1},{3,2},{5,4},{6,5},{7,6},{9,8},{10,9},{11,10},{13,12},{... | collective-permute-start | bytes 294920 | tf_op jit(solution)/shard_map/ppermute | solution.py:386
  23.8 16.9 %copy-start.1 = (f32[2,96,384]{2,1,0:T(8,128)}, f32[2,96,384]{2,1,0:T(8,128)S(1)}, u32[]{:S(2)}) copy-start(f32[2,96,384]{2,1,0:T(8,128)S(1)} %collective-permute-done.7.refs_3_.refs_1_) | copy-start | bytes 884740
  23.9 22.4 %collective-permute-start.8 = (f32[2,96,128]{2,1,0:T(8,128)S(1)}, f32[2,96,128]{2,1,0:T(8,128)S(1)}, u32[]{:S(2)}, u32[]{:S(2)}) collective-permute-start(f32[2,96,128]{2,1,0:T(8,128)S(1)} %get-tuple-element.74), channel_id=1, source_target_pairs={{0,1},{1,2},{2,3},{4,5},{5,6},{6,7},{8,9},{9,10},{10,11},{12,13},{... | collective-permute-start | bytes 294920 | tf_op jit(solution)/shard_map/ppermute | solution.py:386
  27.5 2.0 %copy-start.23 = (f32[2,96,128]{2,1,0:T(8,128)}, f32[2,96,128]{2,1,0:T(8,128)S(1)}, u32[]{:S(2)}) copy-start(f32[2,96,128]{2,1,0:T(8,128)S(1)} %collective-permute-done.1.refs_0_) | copy-start | bytes 294916
  27.5 18.8 %collective-permute-start.9 = (f32[2,96,128]{2,1,0:T(8,128)S(1)}, f32[2,96,128]{2,1,0:T(8,128)S(1)}, u32[]{:S(2)}, u32[]{:S(2)}) collective-permute-start(f32[2,96,128]{2,1,0:T(8,128)S(1)} %get-tuple-element.73), channel_id=1, source_target_pairs={{1,0},{2,1},{3,2},{5,4},{6,5},{7,6},{9,8},{10,9},{11,10},{13,12},{... | collective-permute-start | bytes 294920 | tf_op jit(solution)/shard_map/ppermute | solution.py:386
  29.5 0.8 copy-start.3
  29.5 0.9 copy-start.4
  40.7 22.4 %collective-permute-start.5 = (f32[2,192,128]{2,1,0:T(8,128)}, f32[2,192,128]{2,1,0:T(8,128)S(1)}, u32[]{:S(2)}, u32[]{:S(2)}) collective-permute-start(f32[2,192,128]{2,1,0:T(8,128)} %get-tuple-element.40), channel_id=1, source_target_pairs={{0,1},{1,2},{2,3},{4,5},{5,6},{6,7},{8,9},{9,10},{10,11},{12,13},{... | collective-permute-start | bytes 589832 | tf_op jit(solution)/shard_map/ppermute | solution.py:386
  44.4 18.8 %collective-permute-start.6 = (f32[2,192,128]{2,1,0:T(8,128)}, f32[2,192,128]{2,1,0:T(8,128)S(1)}, u32[]{:S(2)}, u32[]{:S(2)}) collective-permute-start(f32[2,192,128]{2,1,0:T(8,128)} %get-tuple-element.41), channel_id=1, source_target_pairs={{1,0},{2,1},{3,2},{5,4},{6,5},{7,6},{9,8},{10,9},{11,10},{13,12},{... | collective-permute-start | bytes 589832 | tf_op jit(solution)/shard_map/ppermute | solution.py:386
  57.6 10.4 %collective-permute-start.10 = (f32[2,384,128]{2,1,0:T(8,128)}, f32[2,384,128]{2,1,0:T(8,128)S(1)}, u32[]{:S(2)}, u32[]{:S(2)}) collective-permute-start(f32[2,384,128]{2,1,0:T(8,128)} %get-tuple-element.46), channel_id=1, source_target_pairs={{0,1},{1,2},{2,3},{4,5},{5,6},{6,7},{8,9},{9,10},{10,11},{12,13},{... | collective-permute-start | bytes 1179656 | tf_op jit(solution)/shard_map/ppermute | solution.py:386
  61.2 9.6 %collective-permute-start.11 = (f32[2,384,128]{2,1,0:T(8,128)}, f32[2,384,128]{2,1,0:T(8,128)S(1)}, u32[]{:S(2)}, u32[]{:S(2)}) collective-permute-start(f32[2,384,128]{2,1,0:T(8,128)} %get-tuple-element.47), channel_id=1, source_target_pairs={{1,0},{2,1},{3,2},{5,4},{6,5},{7,6},{9,8},{10,9},{11,10},{13,12},{... | collective-permute-start | bytes 1179656 | tf_op jit(solution)/shard_map/ppermute | solution.py:386
  63.1 0.7 copy-start.15
  63.2 0.8 copy-start.16
  66.0 16.8 %collective-permute-start.13 = (f32[2,192,384]{2,1,0:T(8,128)}, f32[2,192,384]{2,1,0:T(8,128)S(1)}, u32[]{:S(2)}, u32[]{:S(2)}) collective-permute-start(f32[2,192,384]{2,1,0:T(8,128)} %totals.4.refs_2_), channel_id=1, source_target_pairs={{4,0},{8,4},{12,8},{16,12},{20,16},{24,20},{28,24},{5,1},{9,5},{13... | collective-permute-start | bytes 1769480 | tf_op jit(solution)/shard_map/ppermute | solution.py:386
  67.9 2.9 %copy-start.11 = (f32[2,384,128]{2,1,0:T(8,128)}, f32[2,384,128]{2,1,0:T(8,128)S(1)}, u32[]{:S(2)}) copy-start(f32[2,384,128]{2,1,0:T(8,128)S(1)} %collective-permute-done.10.left_ref) | copy-start | bytes 1179652
  70.8 0.7 copy-start.12
  74.1 21.4 %collective-permute-start.12 = (f32[2,192,384]{2,1,0:T(8,128)}, f32[2,192,384]{2,1,0:T(8,128)S(1)}, u32[]{:S(2)}, u32[]{:S(2)}) collective-permute-start(f32[2,192,384]{2,1,0:T(8,128)} %get-tuple-element.48.refs_3_), channel_id=1, source_target_pairs={{0,4},{4,8},{8,12},{12,16},{16,20},{20,24},{24,28},{1,5},{5,9},{9,... | collective-permute-start | bytes 1769480 | tf_op jit(solution)/shard_map/ppermute | solution.py:386
  82.8 0.8 copy-start.5
  86.8 18.2 %collective-permute-start.15 = (f32[2,384,128]{2,1,0:T(8,128)}, f32[2,384,128]{2,1,0:T(8,128)S(1)}, u32[]{:S(2)}, u32[]{:S(2)}) collective-permute-start(f32[2,384,128]{2,1,0:T(8,128)} %get-tuple-element.53), channel_id=1, source_target_pairs={{0,1},{1,2},{2,3},{4,5},{5,6},{6,7},{8,9},{9,10},{10,11},{12,13},{... | collective-permute-start | bytes 1179656 | tf_op jit(solution)/shard_map/ppermute | solution.py:386
  90.8 14.3 %collective-permute-start.17 = (f32[2,384,128]{2,1,0:T(8,128)}, f32[2,384,128]{2,1,0:T(8,128)S(1)}, u32[]{:S(2)}, u32[]{:S(2)}) collective-permute-start(f32[2,384,128]{2,1,0:T(8,128)} %get-tuple-element.55), channel_id=1, source_target_pairs={{1,0},{2,1},{3,2},{5,4},{6,5},{7,6},{9,8},{10,9},{11,10},{13,12},{... | collective-permute-start | bytes 1179656 | tf_op jit(solution)/shard_map/ppermute | solution.py:386
  95.5 0.8 copy-start.6
  99.1 17.1 %collective-permute-start.14 = (f32[2,192,128]{2,1,0:T(8,128)}, f32[2,192,128]{2,1,0:T(8,128)S(1)}, u32[]{:S(2)}, u32[]{:S(2)}) collective-permute-start(f32[2,192,128]{2,1,0:T(8,128)} %get-tuple-element.52), channel_id=1, source_target_pairs={{0,1},{1,2},{2,3},{4,5},{5,6},{6,7},{8,9},{9,10},{10,11},{12,13},{... | collective-permute-start | bytes 589832 | tf_op jit(solution)/shard_map/ppermute | solution.py:386
  102.9 13.3 %collective-permute-start.16 = (f32[2,192,128]{2,1,0:T(8,128)}, f32[2,192,128]{2,1,0:T(8,128)S(1)}, u32[]{:S(2)}, u32[]{:S(2)}) collective-permute-start(f32[2,192,128]{2,1,0:T(8,128)} %get-tuple-element.54), channel_id=1, source_target_pairs={{1,0},{2,1},{3,2},{5,4},{6,5},{7,6},{9,8},{10,9},{11,10},{13,12},{... | collective-permute-start | bytes 589832 | tf_op jit(solution)/shard_map/ppermute | solution.py:386
  105.0 0.8 copy-start.7
  105.0 0.9 copy-start.8
  116.2 0.7 copy-start.19
  116.2 0.8 copy-start.20
  117.0 16.3 %copy-start.26 = (f32[2,192,128]{2,1,0:T(8,128)S(1)}, f32[2,192,128]{2,1,0:T(8,128)}, u32[]{:S(2)}) copy-start(f32[2,192,128]{2,1,0:T(8,128)} %get-tuple-element.64) | copy-start | bytes 589828
  117.0 20.0 %copy-start.25 = (f32[2,192,128]{2,1,0:T(8,128)S(1)}, f32[2,192,128]{2,1,0:T(8,128)}, u32[]{:S(2)}) copy-start(f32[2,192,128]{2,1,0:T(8,128)} %get-tuple-element.65) | copy-start | bytes 589828
  127.7 30.6 %collective-permute-start.18 = (f32[2,384,128]{2,1,0:T(8,128)}, f32[2,384,128]{2,1,0:T(8,128)S(1)}, u32[]{:S(2)}, u32[]{:S(2)}) collective-permute-start(f32[2,384,128]{2,1,0:T(8,128)} %get-tuple-element.60), channel_id=1, source_target_pairs={{0,1},{1,2},{2,3},{4,5},{5,6},{6,7},{8,9},{9,10},{10,11},{12,13},{... | collective-permute-start | bytes 1179656 | tf_op jit(solution)/shard_map/ppermute | solution.py:386
  131.4 27.0 %collective-permute-start.19 = (f32[2,384,128]{2,1,0:T(8,128)}, f32[2,384,128]{2,1,0:T(8,128)S(1)}, u32[]{:S(2)}, u32[]{:S(2)}) collective-permute-start(f32[2,384,128]{2,1,0:T(8,128)} %get-tuple-element.61), channel_id=1, source_target_pairs={{1,0},{2,1},{3,2},{5,4},{6,5},{7,6},{9,8},{10,9},{11,10},{13,12},{... | collective-permute-start | bytes 1179656 | tf_op jit(solution)/shard_map/ppermute | solution.py:386
  133.3 6.2 %collective-permute-start.20 = (f32[2,192,128]{2,1,0:T(8,128)S(1)}, f32[2,192,128]{2,1,0:T(8,128)S(1)}, u32[]{:S(2)}, u32[]{:S(2)}) collective-permute-start(f32[2,192,128]{2,1,0:T(8,128)S(1)} %copy-done.26), channel_id=1, source_target_pairs={{0,1},{1,2},{2,3},{4,5},{5,6},{6,7},{8,9},{9,10},{10,11},{12,13},{... | collective-permute-start | bytes 589832 | tf_op jit(solution)/shard_map/ppermute | solution.py:386
  137.0 7.0 %collective-permute-start.21 = (f32[2,192,128]{2,1,0:T(8,128)S(1)}, f32[2,192,128]{2,1,0:T(8,128)S(1)}, u32[]{:S(2)}, u32[]{:S(2)}) collective-permute-start(f32[2,192,128]{2,1,0:T(8,128)S(1)} %copy-done.25), channel_id=1, source_target_pairs={{1,0},{2,1},{3,2},{5,4},{6,5},{7,6},{9,8},{10,9},{11,10},{13,12},{... | collective-permute-start | bytes 589832 | tf_op jit(solution)/shard_map/ppermute | solution.py:386
  139.5 4.4 %copy-start.17 = (f32[2,192,128]{2,1,0:T(8,128)}, f32[2,192,128]{2,1,0:T(8,128)S(1)}, u32[]{:S(2)}) copy-start(f32[2,192,128]{2,1,0:T(8,128)S(1)} %collective-permute-done.20.left_ref) | copy-start | bytes 589828
  143.9 0.7 copy-start.18
  146.7 17.0 %collective-permute-start.22 = (f32[2,96,384]{2,1,0:T(8,128)}, f32[2,96,384]{2,1,0:T(8,128)S(1)}, u32[]{:S(2)}, u32[]{:S(2)}) collective-permute-start(f32[2,96,384]{2,1,0:T(8,128)} %get-tuple-element.67), channel_id=1, source_target_pairs={{0,4},{4,8},{8,12},{12,16},{16,20},{20,24},{24,28},{1,5},{5,9},{9,... | collective-permute-start | bytes 884744 | tf_op jit(solution)/shard_map/ppermute | solution.py:386
  158.3 0.7 copy-start.9
  158.3 0.9 copy-start.10
  161.7 8.8 %collective-permute-start.23 = (f32[2,96,384]{2,1,0:T(8,128)}, f32[2,96,384]{2,1,0:T(8,128)S(1)}, u32[]{:S(2)}, u32[]{:S(2)}) collective-permute-start(f32[2,96,384]{2,1,0:T(8,128)} %get-tuple-element.68), channel_id=1, source_target_pairs={{4,0},{8,4},{12,8},{16,12},{20,16},{24,20},{28,24},{5,1},{9,5},{13... | collective-permute-start | bytes 884744 | tf_op jit(solution)/shard_map/ppermute | solution.py:386
  163.6 6.9 %copy-start.13 = (f32[2,96,384]{2,1,0:T(8,128)}, f32[2,96,384]{2,1,0:T(8,128)S(1)}, u32[]{:S(2)}) copy-start(f32[2,96,384]{2,1,0:T(8,128)S(1)} %collective-permute-done.22.above_ref) | copy-start | bytes 884740
  170.5 0.7 copy-start.14
  (3 other events, 1.9 us)
where the time goes:
time: 175 us; the launch traced here: 174 us
  starting transfers between devices  75.8 us (43%)
  Pallas kernels  64.4 us (37%)
  waiting for transfers between devices  23.7 us (14%)
  local copies, waits for them, and re-layouts  9.86 us (6%)
    ppermute x24, starting transfers between devices, moved(): return lax.ppermute(block, axis, route)  75.8 us
    pallas_call x4, Pallas kernels, windows(): pl.pallas_call(functools.partial(windows_kernel, i, plan, acc_at, outs),...  41.9 us
    ppermute x24, waiting for transfers between devices, moved(): return lax.ppermute(block, axis, route)  23.7 us
    pallas_call x4, Pallas kernels, totals(): pl.pallas_call(functools.partial(totals_kernel, outs), out_shape=tuple((j...  9.21 us
    unnamed x54, local copies, waits for them, and re-layouts  8.59 us
    pallas_call x2, Pallas kernels, update(): pl.pallas_call(functools.partial(update_kernel, pieces, guard), out_shape...  5.94 us
    pallas_call x1, Pallas kernels, prepare(): pl.pallas_call(prepare_kernel, out_shape=(jax.ShapeDtypeStruct((4, 2, WIN...  4.27 us
  transfers between devices with their start and end apart: 24, of which 7 were waited for; matrix products, arithmetic and copies ran while one was open for 0% of the time, Pallas kernels for 29%

commit v1 on v0

--- a/solution.py
+++ b/solution.py
@@ -13,6 +13,7 @@
 HALF = 128
 MARGIN = 96
 LANE = 128
+VMEM_LIMIT = 24 * 1024 * 1024
 
 step_size = 0.3
 tv_weight = 0.2
@@ -91,6 +92,7 @@
         out_specs=tuple(vmem(2)),
         scratch_shapes=[pltpu.VMEM((WIN, HALF), F32)],
         cost_estimate=pl.CostEstimate(flops=400_000_000, bytes_accessed=6_000_000, transcendentals=0),
+        compiler_params=pltpu.CompilerParams(vmem_limit_bytes=VMEM_LIMIT),
         name="prepare",
     )(offsets, probe, amplitudes, order)
 
@@ -304,6 +306,7 @@
             pltpu.VMEM((2 * WIN, WIN), F32),
         ],
         cost_estimate=pl.CostEstimate(flops=1_600_000_000, bytes_accessed=10_000_000, transcendentals=0),
+        compiler_params=pltpu.CompilerParams(vmem_limit_bytes=VMEM_LIMIT),
         name=f"windows_{i}",
     )(offsets, table, twiddle, probes, amps, *operands, *extra)
 
@@ -324,6 +327,7 @@
         in_specs=vmem(3),
         out_specs=tuple(vmem(len(outs))),
         cost_estimate=pl.CostEstimate(flops=500_000, bytes_accessed=3_000_000, transcendentals=0),
+        compiler_params=pltpu.CompilerParams(vmem_limit_bytes=VMEM_LIMIT),
         name="totals",
     )(own, from_left, from_right)
 
@@ -356,6 +360,7 @@
         in_specs=vmem(len(operands)),
         out_specs=tuple(vmem(3)),
         cost_estimate=pl.CostEstimate(flops=1_000_000, bytes_accessed=4_000_000, transcendentals=0),
+        compiler_params=pltpu.CompilerParams(vmem_limit_bytes=VMEM_LIMIT),
         name="update",
     )(*operands)
 
@@ -376,6 +381,7 @@
         in_specs=vmem(len(operands)),
         out_specs=pl.BlockSpec(memory_space=pltpu.VMEM),
         cost_estimate=pl.CostEstimate(flops=1_000_000, bytes_accessed=4_000_000, transcendentals=0),
+        compiler_params=pltpu.CompilerParams(vmem_limit_bytes=VMEM_LIMIT),
         name="finish",
     )(*operands)
 

time: 175 us -> 142 us (0.81)
  the two profiles are of different devices: /device:TPU:3 before, /device:TPU:17 now
where the time goes in v1:
time: 142 us; the launch traced here: 141 us
  starting transfers between devices  71.5 us (50%)
  waiting for transfers between devices  35.3 us (25%)
  Pallas kernels  31.4 us (22%)
  local copies, waits for them, and re-layouts  2.26 us (2%)
    ppermute x24, starting transfers between devices, moved(): return lax.ppermute(block, axis, route)  71.5 us
    ppermute x24, waiting for transfers between devices, moved(): return lax.ppermute(block, axis, route)  35.3 us
    pallas_call x4, Pallas kernels, windows(): pl.pallas_call(functools.partial(windows_kernel, i, plan, acc_at, outs),...  27.6 us
  transfers between devices with their start and end apart: 24, of which 7 were waited for; matrix products, arithmetic and copies ran while one was open for 0% of the time, Pallas kernels for 17%

profile of v1, /device:TPU:17, one launch (start us, length us, event | category | flops | bytes accessed | tf_op | source)
XLA Modules:
  0.0 140.9 jit_solution(12290779825444581704)
XLA Ops:
  0.0 1.2 fusion
  1.3 3.1 %collective-permute-start = (f32[2,96,384]{2,1,0:T(8,128)S(1)}, f32[2,96,384]{2,1,0:T(8,128)S(1)}, u32[]{:S(2)}, u32[]{:S(2)}) collective-permute-start(f32[2,96,384]{2,1,0:T(8,128)S(1)} %get-tuple-element.70), channel_id=1, source_target_pairs={{0,4},{4,8},{8,12},{12,16},{16,20},{20,24},{24,28},{1,5},{5,9},{9,... | collective-permute-start | bytes 884744 | tf_op jit(solution)/shard_map/ppermute | solution.py:392
  4.4 3.1 %collective-permute-start.7 = (f32[2,96,384]{2,1,0:T(8,128)S(1)}, f32[2,96,384]{2,1,0:T(8,128)S(1)}, u32[]{:S(2)}, u32[]{:S(2)}) collective-permute-start(f32[2,96,384]{2,1,0:T(8,128)S(1)} %get-tuple-element.69), channel_id=1, source_target_pairs={{4,0},{8,4},{12,8},{16,12},{20,16},{24,20},{28,24},{5,1},{9,5},{13... | collective-permute-start | bytes 884744 | tf_op jit(solution)/shard_map/ppermute | solution.py:392
  7.5 0.1 fusion.1
  7.5 4.3 %collective-permute-start.2 = (f32[2,384,128]{2,1,0:T(8,128)S(1)}, f32[2,384,128]{2,1,0:T(8,128)S(1)}, u32[]{:S(2)}, u32[]{:S(2)}) collective-permute-start(f32[2,384,128]{2,1,0:T(8,128)S(1)} %get-tuple-element.72), channel_id=1, source_target_pairs={{0,1},{1,2},{2,3},{4,5},{5,6},{6,7},{8,9},{9,10},{10,11},{12,13},{... | collective-permute-start | bytes 1179656 | tf_op jit(solution)/shard_map/ppermute | solution.py:392
  11.8 0.0 copy-start.1
  11.8 0.0 copy-start.2
  11.8 2.1 %collective-permute-start.4 = (f32[2,384,128]{2,1,0:T(8,128)S(1)}, f32[2,384,128]{2,1,0:T(8,128)S(1)}, u32[]{:S(2)}, u32[]{:S(2)}) collective-permute-start(f32[2,384,128]{2,1,0:T(8,128)S(1)} %get-tuple-element.71), channel_id=1, source_target_pairs={{1,0},{2,1},{3,2},{5,4},{6,5},{7,6},{9,8},{10,9},{11,10},{13,12},{... | collective-permute-start | bytes 1179656 | tf_op jit(solution)/shard_map/ppermute | solution.py:392
  13.9 0.9 copy-done.5
  14.8 1.8 %prepare.1 = (f32[4,2,256,256]{3,2,1,0:T(8,128)S(1)}, f32[4,512,128]{2,1,0:T(8,128)S(1)}) custom-call(s32[2,2,2]{2,1,0:T(2,128)S(1)} %copy-done.6, f32[2,256,256]{2,1,0:T(8,128)S(1)} %copy-done.4, f32[512,512]{1,0:T(8,128)S(1)} %copy-done.3, bf16[256,256]{1,0:T(8,128)(2,1)S(1)} %copy-done.5), custom_call_target="tpu_custom_call" | custom-call | flops 400000000 | bytes 6000000 | tf_op jit(solution)/shard_map/prepare/pallas_call | solution.py:85
  16.7 4.2 %collective-permute-start.1 = (f32[2,96,128]{2,1,0:T(8,128)S(1)}, f32[2,96,128]{2,1,0:T(8,128)S(1)}, u32[]{:S(2)}, u32[]{:S(2)}) collective-permute-start(f32[2,96,128]{2,1,0:T(8,128)S(1)} %get-tuple-element.76), channel_id=1, source_target_pairs={{0,1},{1,2},{2,3},{4,5},{5,6},{6,7},{8,9},{9,10},{10,11},{12,13},{... | collective-permute-start | bytes 294920 | tf_op jit(solution)/shard_map/ppermute | solution.py:392
  21.0 1.9 %collective-permute-start.3 = (f32[2,96,128]{2,1,0:T(8,128)S(1)}, f32[2,96,128]{2,1,0:T(8,128)S(1)}, u32[]{:S(2)}, u32[]{:S(2)}) collective-permute-start(f32[2,96,128]{2,1,0:T(8,128)S(1)} %get-tuple-element.75), channel_id=1, source_target_pairs={{1,0},{2,1},{3,2},{5,4},{6,5},{7,6},{9,8},{10,9},{11,10},{13,12},{... | collective-permute-start | bytes 294920 | tf_op jit(solution)/shard_map/ppermute | solution.py:392
  22.9 3.6 %collective-permute-start.8 = (f32[2,96,128]{2,1,0:T(8,128)S(1)}, f32[2,96,128]{2,1,0:T(8,128)S(1)}, u32[]{:S(2)}, u32[]{:S(2)}) collective-permute-start(f32[2,96,128]{2,1,0:T(8,128)S(1)} %get-tuple-element.74), channel_id=1, source_target_pairs={{0,1},{1,2},{2,3},{4,5},{5,6},{6,7},{8,9},{9,10},{10,11},{12,13},{... | collective-permute-start | bytes 294920 | tf_op jit(solution)/shard_map/ppermute | solution.py:392
  26.6 1.9 %collective-permute-start.9 = (f32[2,96,128]{2,1,0:T(8,128)S(1)}, f32[2,96,128]{2,1,0:T(8,128)S(1)}, u32[]{:S(2)}, u32[]{:S(2)}) collective-permute-start(f32[2,96,128]{2,1,0:T(8,128)S(1)} %get-tuple-element.73), channel_id=1, source_target_pairs={{1,0},{2,1},{3,2},{5,4},{6,5},{7,6},{9,8},{10,9},{11,10},{13,12},{... | collective-permute-start | bytes 294920 | tf_op jit(solution)/shard_map/ppermute | solution.py:392
  28.6 6.9 %windows_0.2 = (f32[2,192,128]{2,1,0:T(8,128)S(1)}, f32[2,192,384]{2,1,0:T(8,128)S(1)}, f32[2,192,128]{2,1,0:T(8,128)S(1)}, f32[2,192,128]{2,1,0:T(8,128)S(1)}, ...) custom-call(s32[2,2,2]{2,1,0:T(2,128)S(1)} %copy-done.6, bf16[4,256,256]{2,1,0:T(8,128)(2,1)S(1)} %copy-done.1, ...), custom_call_target="tpu_custom_call" | custom-call | flops 1600000000 | bytes 10000000 | tf_op jit(solution)/shard_map/windows_0/pallas_call | solution.py:293
  35.5 3.6 %collective-permute-start.5 = (f32[2,192,128]{2,1,0:T(8,128)S(1)}, f32[2,192,128]{2,1,0:T(8,128)S(1)}, u32[]{:S(2)}, u32[]{:S(2)}) collective-permute-start(f32[2,192,128]{2,1,0:T(8,128)S(1)} %get-tuple-element.40), channel_id=1, source_target_pairs={{0,1},{1,2},{2,3},{4,5},{5,6},{6,7},{8,9},{9,10},{10,11},{12,13},{... | collective-permute-start | bytes 589832 | tf_op jit(solution)/shard_map/ppermute | solution.py:392
  39.1 1.9 %collective-permute-start.6 = (f32[2,192,128]{2,1,0:T(8,128)S(1)}, f32[2,192,128]{2,1,0:T(8,128)S(1)}, u32[]{:S(2)}, u32[]{:S(2)}) collective-permute-start(f32[2,192,128]{2,1,0:T(8,128)S(1)} %get-tuple-element.41), channel_id=1, source_target_pairs={{1,0},{2,1},{3,2},{5,4},{6,5},{7,6},{9,8},{10,9},{11,10},{13,12},{... | collective-permute-start | bytes 589832 | tf_op jit(solution)/shard_map/ppermute | solution.py:392
  41.1 6.9 %windows_1.2 = (f32[2,384,128]{2,1,0:T(8,128)S(1)}, f32[2,384,384]{2,1,0:T(8,128)S(1)}, f32[2,384,128]{2,1,0:T(8,128)S(1)}) custom-call(s32[2,2,2]{2,1,0:T(2,128)S(1)} %copy-done.6, bf16[4,256,256]{2,1,0:T(8,128)(2,1)S(1)} %copy-done.1, f32[4,128,128]{2,1,0:T(8,128)S(1)} %copy-done.2, f32[4,2,256,256]{3,2,1,0:T(8,128)S(1)} %get-tuple-element.37.probes_ref, ...), custom_call_target="tpu_custom_call" | custom-call | flops 1600000000 | bytes 10000000 | tf_op jit(solution)/shard_map/windows_1/pallas_call | solution.py:293
  48.0 3.6 %collective-permute-start.10 = (f32[2,384,128]{2,1,0:T(8,128)S(1)}, f32[2,384,128]{2,1,0:T(8,128)S(1)}, u32[]{:S(2)}, u32[]{:S(2)}) collective-permute-start(f32[2,384,128]{2,1,0:T(8,128)S(1)} %get-tuple-element.46), channel_id=1, source_target_pairs={{0,1},{1,2},{2,3},{4,5},{5,6},{6,7},{8,9},{9,10},{10,11},{12,13},{... | collective-permute-start | bytes 1179656 | tf_op jit(solution)/shard_map/ppermute | solution.py:392
  51.6 1.9 %collective-permute-start.11 = (f32[2,384,128]{2,1,0:T(8,128)S(1)}, f32[2,384,128]{2,1,0:T(8,128)S(1)}, u32[]{:S(2)}, u32[]{:S(2)}) collective-permute-start(f32[2,384,128]{2,1,0:T(8,128)S(1)} %get-tuple-element.47), channel_id=1, source_target_pairs={{1,0},{2,1},{3,2},{5,4},{6,5},{7,6},{9,8},{10,9},{11,10},{13,12},{... | collective-permute-start | bytes 1179656 | tf_op jit(solution)/shard_map/ppermute | solution.py:392
  53.6 0.1 totals.4.refs_2_
  53.6 4.0 %collective-permute-start.13 = (f32[2,192,384]{2,1,0:T(8,128)S(1)}, f32[2,192,384]{2,1,0:T(8,128)S(1)}, u32[]{:S(2)}, u32[]{:S(2)}) collective-permute-start(f32[2,192,384]{2,1,0:T(8,128)S(1)} %totals.4.refs_2_), channel_id=1, source_target_pairs={{4,0},{8,4},{12,8},{16,12},{20,16},{24,20},{28,24},{5,1},{9,5},{13... | collective-permute-start | bytes 1769480 | tf_op jit(solution)/shard_map/ppermute | solution.py:392
  57.7 3.4 %collective-permute-done.11.right_ref = f32[2,384,128]{2,1,0:T(8,128)S(1)} collective-permute-done((f32[2,384,128]{2,1,0:T(8,128)S(1)}, f32[2,384,128]{2,1,0:T(8,128)S(1)}, u32[]{:S(2)}, u32[]{:S(2)}) %collective-permute-start.11) | collective-permute-done | bytes 393248 | tf_op jit(solution)/shard_map/ppermute | solution.py:392
  61.0 0.1 totals.5
  61.1 4.1 %collective-permute-start.12 = (f32[2,192,384]{2,1,0:T(8,128)S(1)}, f32[2,192,384]{2,1,0:T(8,128)S(1)}, u32[]{:S(2)}, u32[]{:S(2)}) collective-permute-start(f32[2,192,384]{2,1,0:T(8,128)S(1)} %get-tuple-element.48.refs_3_), channel_id=1, source_target_pairs={{0,4},{4,8},{8,12},{12,16},{16,20},{20,24},{24,28},{1,5},{5,9},{9,... | collective-permute-start | bytes 1769480 | tf_op jit(solution)/shard_map/ppermute | solution.py:392
  65.3 17.1 %collective-permute-done.13.refs_4_ = f32[2,192,384]{2,1,0:T(8,128)S(1)} collective-permute-done((f32[2,192,384]{2,1,0:T(8,128)S(1)}, f32[2,192,384]{2,1,0:T(8,128)S(1)}, u32[]{:S(2)}, u32[]{:S(2)}) %collective-permute-start.13) | collective-permute-done | bytes 589856 | tf_op jit(solution)/shard_map/ppermute | solution.py:392
  82.3 0.2 update.3
  82.6 4.3 %collective-permute-start.15 = (f32[2,384,128]{2,1,0:T(8,128)S(1)}, f32[2,384,128]{2,1,0:T(8,128)S(1)}, u32[]{:S(2)}, u32[]{:S(2)}) collective-permute-start(f32[2,384,128]{2,1,0:T(8,128)S(1)} %get-tuple-element.53), channel_id=1, source_target_pairs={{0,1},{1,2},{2,3},{4,5},{5,6},{6,7},{8,9},{9,10},{10,11},{12,13},{... | collective-permute-start | bytes 1179656 | tf_op jit(solution)/shard_map/ppermute | solution.py:392
  86.8 1.9 %collective-permute-start.17 = (f32[2,384,128]{2,1,0:T(8,128)S(1)}, f32[2,384,128]{2,1,0:T(8,128)S(1)}, u32[]{:S(2)}, u32[]{:S(2)}) collective-permute-start(f32[2,384,128]{2,1,0:T(8,128)S(1)} %get-tuple-element.55), channel_id=1, source_target_pairs={{1,0},{2,1},{3,2},{5,4},{6,5},{7,6},{9,8},{10,9},{11,10},{13,12},{... | collective-permute-start | bytes 1179656 | tf_op jit(solution)/shard_map/ppermute | solution.py:392
  88.8 0.1 update.2
  88.9 3.6 %collective-permute-start.14 = (f32[2,192,128]{2,1,0:T(8,128)S(1)}, f32[2,192,128]{2,1,0:T(8,128)S(1)}, u32[]{:S(2)}, u32[]{:S(2)}) collective-permute-start(f32[2,192,128]{2,1,0:T(8,128)S(1)} %get-tuple-element.52), channel_id=1, source_target_pairs={{0,1},{1,2},{2,3},{4,5},{5,6},{6,7},{8,9},{9,10},{10,11},{12,13},{... | collective-permute-start | bytes 589832 | tf_op jit(solution)/shard_map/ppermute | solution.py:392
  92.6 2.1 %collective-permute-start.16 = (f32[2,192,128]{2,1,0:T(8,128)S(1)}, f32[2,192,128]{2,1,0:T(8,128)S(1)}, u32[]{:S(2)}, u32[]{:S(2)}) collective-permute-start(f32[2,192,128]{2,1,0:T(8,128)S(1)} %get-tuple-element.54), channel_id=1, source_target_pairs={{1,0},{2,1},{3,2},{5,4},{6,5},{7,6},{9,8},{10,9},{11,10},{13,12},{... | collective-permute-start | bytes 589832 | tf_op jit(solution)/shard_map/ppermute | solution.py:392
  94.7 1.3 collective-permute-done.17.refs_2_.refs_5_
  95.9 6.9 %windows_1.3 = (f32[2,192,128]{2,1,0:T(8,128)S(1)}, f32[2,192,384]{2,1,0:T(8,128)S(1)}, f32[2,192,128]{2,1,0:T(8,128)S(1)}, f32[2,192,128]{2,1,0:T(8,128)S(1)}, ...) custom-call(s32[2,2,2]{2,1,0:T(2,128)S(1)} %copy-done.6, bf16[4,256,256]{2,1,0:T(8,128)(2,1)S(1)} %copy-done.1, ...), custom_call_target="tpu_custom_call" | custom-call | flops 1600000000 | bytes 10000000 | tf_op jit(solution)/shard_map/windows_1/pallas_call | solution.py:293
  102.8 6.9 %windows_0.3 = (f32[2,384,128]{2,1,0:T(8,128)S(1)}, f32[2,384,384]{2,1,0:T(8,128)S(1)}, f32[2,384,128]{2,1,0:T(8,128)S(1)}) custom-call(s32[2,2,2]{2,1,0:T(2,128)S(1)} %copy-done.6, bf16[4,256,256]{2,1,0:T(8,128)(2,1)S(1)} %copy-done.1, f32[4,128,128]{2,1,0:T(8,128)S(1)} %copy-done.2, f32[4,2,256,256]{3,2,1,0:T(8,128)S(1)} %get-tuple-element.37.probes_ref, ...), custom_call_target="tpu_custom_call" | custom-call | flops 1600000000 | bytes 10000000 | tf_op jit(solution)/shard_map/windows_0/pallas_call | solution.py:293
  109.7 2.4 %collective-permute-start.18 = (f32[2,384,128]{2,1,0:T(8,128)S(1)}, f32[2,384,128]{2,1,0:T(8,128)S(1)}, u32[]{:S(2)}, u32[]{:S(2)}) collective-permute-start(f32[2,384,128]{2,1,0:T(8,128)S(1)} %get-tuple-element.60), channel_id=1, source_target_pairs={{0,1},{1,2},{2,3},{4,5},{5,6},{6,7},{8,9},{9,10},{10,11},{12,13},{... | collective-permute-start | bytes 1179656 | tf_op jit(solution)/shard_map/ppermute | solution.py:392
  112.2 1.9 %collective-permute-start.19 = (f32[2,384,128]{2,1,0:T(8,128)S(1)}, f32[2,384,128]{2,1,0:T(8,128)S(1)}, u32[]{:S(2)}, u32[]{:S(2)}) collective-permute-start(f32[2,384,128]{2,1,0:T(8,128)S(1)} %get-tuple-element.61), channel_id=1, source_target_pairs={{1,0},{2,1},{3,2},{5,4},{6,5},{7,6},{9,8},{10,9},{11,10},{13,12},{... | collective-permute-start | bytes 1179656 | tf_op jit(solution)/shard_map/ppermute | solution.py:392
  114.1 3.6 %collective-permute-start.20 = (f32[2,192,128]{2,1,0:T(8,128)S(1)}, f32[2,192,128]{2,1,0:T(8,128)S(1)}, u32[]{:S(2)}, u32[]{:S(2)}) collective-permute-start(f32[2,192,128]{2,1,0:T(8,128)S(1)} %get-tuple-element.64), channel_id=1, source_target_pairs={{0,1},{1,2},{2,3},{4,5},{5,6},{6,7},{8,9},{9,10},{10,11},{12,13},{... | collective-permute-start | bytes 589832 | tf_op jit(solution)/shard_map/ppermute | solution.py:392
  117.8 1.9 %collective-permute-start.21 = (f32[2,192,128]{2,1,0:T(8,128)S(1)}, f32[2,192,128]{2,1,0:T(8,128)S(1)}, u32[]{:S(2)}, u32[]{:S(2)}) collective-permute-start(f32[2,192,128]{2,1,0:T(8,128)S(1)} %get-tuple-element.65), channel_id=1, source_target_pairs={{1,0},{2,1},{3,2},{5,4},{6,5},{7,6},{9,8},{10,9},{11,10},{13,12},{... | collective-permute-start | bytes 589832 | tf_op jit(solution)/shard_map/ppermute | solution.py:392
  119.7 0.7 collective-permute-done.20.left_ref
  120.3 4.4 %collective-permute-done.21.right_ref = f32[2,192,128]{2,1,0:T(8,128)S(1)} collective-permute-done((f32[2,192,128]{2,1,0:T(8,128)S(1)}, f32[2,192,128]{2,1,0:T(8,128)S(1)}, u32[]{:S(2)}, u32[]{:S(2)}) %collective-permute-start.21) | collective-permute-done | bytes 196640 | tf_op jit(solution)/shard_map/ppermute | solution.py:392
  124.7 0.1 totals.7
  124.8 1.9 %collective-permute-start.22 = (f32[2,96,384]{2,1,0:T(8,128)S(1)}, f32[2,96,384]{2,1,0:T(8,128)S(1)}, u32[]{:S(2)}, u32[]{:S(2)}) collective-permute-start(f32[2,96,384]{2,1,0:T(8,128)S(1)} %get-tuple-element.67), channel_id=1, source_target_pairs={{0,4},{4,8},{8,12},{12,16},{16,20},{20,24},{24,28},{1,5},{5,9},{9,... | collective-permute-start | bytes 884744 | tf_op jit(solution)/shard_map/ppermute | solution.py:392
  126.8 0.1 totals.6
  126.9 4.3 %collective-permute-start.23 = (f32[2,96,384]{2,1,0:T(8,128)S(1)}, f32[2,96,384]{2,1,0:T(8,128)S(1)}, u32[]{:S(2)}, u32[]{:S(2)}) collective-permute-start(f32[2,96,384]{2,1,0:T(8,128)S(1)} %get-tuple-element.68), channel_id=1, source_target_pairs={{4,0},{8,4},{12,8},{16,12},{20,16},{24,20},{28,24},{5,1},{9,5},{13... | collective-permute-start | bytes 884744 | tf_op jit(solution)/shard_map/ppermute | solution.py:392
  131.2 5.5 %collective-permute-done.22.above_ref = f32[2,96,384]{2,1,0:T(8,128)S(1)} collective-permute-done((f32[2,96,384]{2,1,0:T(8,128)S(1)}, f32[2,96,384]{2,1,0:T(8,128)S(1)}, u32[]{:S(2)}, u32[]{:S(2)}) %collective-permute-start.22) | collective-permute-done | bytes 294944 | tf_op jit(solution)/shard_map/ppermute | solution.py:392
  136.7 3.0 %collective-permute-done.23.below_ref = f32[2,96,384]{2,1,0:T(8,128)S(1)} collective-permute-done((f32[2,96,384]{2,1,0:T(8,128)S(1)}, f32[2,96,384]{2,1,0:T(8,128)S(1)}, u32[]{:S(2)}, u32[]{:S(2)}) %collective-permute-start.23) | collective-permute-done | bytes 294944 | tf_op jit(solution)/shard_map/ppermute | solution.py:392
  139.7 1.2 finish.1
  (30 shorter events, 0.1 us)
Async XLA Ops:
  0.0 7.5 %copy-start = (f32[2,384,384]{2,1,0:T(8,128)S(1)}, f32[2,384,384]{2,1,0:T(8,128)}, u32[]{:S(2)}) copy-start(f32[2,384,384]{2,1,0:T(8,128)} %refs_0_.1) | copy-start | bytes 3538948
  0.0 13.9 %copy-start.6 = (s32[2,2,2]{2,1,0:T(2,128)S(1)}, s32[2,2,2]{2,1,0:T(2,128)}, u32[]{:S(2)}) copy-start(s32[2,2,2]{2,1,0:T(2,128)} %off_ref.9) | copy-start | bytes 100
  0.0 13.9 %copy-start.4 = (f32[2,256,256]{2,1,0:T(8,128)S(1)}, f32[2,256,256]{2,1,0:T(8,128)}, u32[]{:S(2)}) copy-start(f32[2,256,256]{2,1,0:T(8,128)} %probe_ref.1) | copy-start | bytes 1572868
  0.0 13.9 %copy-start.3 = (f32[512,512]{1,0:T(8,128)S(1)}, f32[512,512]{1,0:T(8,128)}, u32[]{:S(2)}) copy-start(f32[512,512]{1,0:T(8,128)} %amp_ref.1) | copy-start | bytes 3145732
  1.3 15.4 %collective-permute-start = (f32[2,96,384]{2,1,0:T(8,128)S(1)}, f32[2,96,384]{2,1,0:T(8,128)S(1)}, u32[]{:S(2)}, u32[]{:S(2)}) collective-permute-start(f32[2,96,384]{2,1,0:T(8,128)S(1)} %get-tuple-element.70), channel_id=1, source_target_pairs={{0,4},{4,8},{8,12},{12,16},{16,20},{20,24},{24,28},{1,5},{5,9},{9,... | collective-permute-start | bytes 884744 | tf_op jit(solution)/shard_map/ppermute | solution.py:392
  4.4 18.5 %collective-permute-start.7 = (f32[2,96,384]{2,1,0:T(8,128)S(1)}, f32[2,96,384]{2,1,0:T(8,128)S(1)}, u32[]{:S(2)}, u32[]{:S(2)}) collective-permute-start(f32[2,96,384]{2,1,0:T(8,128)S(1)} %get-tuple-element.69), channel_id=1, source_target_pairs={{4,0},{8,4},{12,8},{16,12},{20,16},{24,20},{28,24},{5,1},{9,5},{13... | collective-permute-start | bytes 884744 | tf_op jit(solution)/shard_map/ppermute | solution.py:392
  7.5 21.0 %collective-permute-start.2 = (f32[2,384,128]{2,1,0:T(8,128)S(1)}, f32[2,384,128]{2,1,0:T(8,128)S(1)}, u32[]{:S(2)}, u32[]{:S(2)}) collective-permute-start(f32[2,384,128]{2,1,0:T(8,128)S(1)} %get-tuple-element.72), channel_id=1, source_target_pairs={{0,1},{1,2},{2,3},{4,5},{5,6},{6,7},{8,9},{9,10},{10,11},{12,13},{... | collective-permute-start | bytes 1179656 | tf_op jit(solution)/shard_map/ppermute | solution.py:392
  11.8 16.7 %copy-start.1 = (bf16[4,256,256]{2,1,0:T(8,128)(2,1)S(1)}, bf16[4,256,256]{2,1,0:T(8,128)(2,1)}, u32[]{:S(2)}) copy-start(bf16[4,256,256]{2,1,0:T(8,128)(2,1)} %constant.6.clone.tab_ref) | copy-start | bytes 1572868
  11.8 16.7 %copy-start.2 = (f32[4,128,128]{2,1,0:T(8,128)S(1)}, f32[4,128,128]{2,1,0:T(8,128)}, u32[]{:S(2)}) copy-start(f32[4,128,128]{2,1,0:T(8,128)} %constant.7.clone.tw_ref) | copy-start | bytes 786436
  11.8 16.7 %collective-permute-start.4 = (f32[2,384,128]{2,1,0:T(8,128)S(1)}, f32[2,384,128]{2,1,0:T(8,128)S(1)}, u32[]{:S(2)}, u32[]{:S(2)}) collective-permute-start(f32[2,384,128]{2,1,0:T(8,128)S(1)} %get-tuple-element.71), channel_id=1, source_target_pairs={{1,0},{2,1},{3,2},{5,4},{6,5},{7,6},{9,8},{10,9},{11,10},{13,12},{... | collective-permute-start | bytes 1179656 | tf_op jit(solution)/shard_map/ppermute | solution.py:392
  13.9 0.9 copy-start.5
  16.7 9.9 %collective-permute-start.1 = (f32[2,96,128]{2,1,0:T(8,128)S(1)}, f32[2,96,128]{2,1,0:T(8,128)S(1)}, u32[]{:S(2)}, u32[]{:S(2)}) collective-permute-start(f32[2,96,128]{2,1,0:T(8,128)S(1)} %get-tuple-element.76), channel_id=1, source_target_pairs={{0,1},{1,2},{2,3},{4,5},{5,6},{6,7},{8,9},{9,10},{10,11},{12,13},{... | collective-permute-start | bytes 294920 | tf_op jit(solution)/shard_map/ppermute | solution.py:392
  21.0 7.6 %collective-permute-start.3 = (f32[2,96,128]{2,1,0:T(8,128)S(1)}, f32[2,96,128]{2,1,0:T(8,128)S(1)}, u32[]{:S(2)}, u32[]{:S(2)}) collective-permute-start(f32[2,96,128]{2,1,0:T(8,128)S(1)} %get-tuple-element.75), channel_id=1, source_target_pairs={{1,0},{2,1},{3,2},{5,4},{6,5},{7,6},{9,8},{10,9},{11,10},{13,12},{... | collective-permute-start | bytes 294920 | tf_op jit(solution)/shard_map/ppermute | solution.py:392
  22.9 18.1 %collective-permute-start.8 = (f32[2,96,128]{2,1,0:T(8,128)S(1)}, f32[2,96,128]{2,1,0:T(8,128)S(1)}, u32[]{:S(2)}, u32[]{:S(2)}) collective-permute-start(f32[2,96,128]{2,1,0:T(8,128)S(1)} %get-tuple-element.74), channel_id=1, source_target_pairs={{0,1},{1,2},{2,3},{4,5},{5,6},{6,7},{8,9},{9,10},{10,11},{12,13},{... | collective-permute-start | bytes 294920 | tf_op jit(solution)/shard_map/ppermute | solution.py:392
  26.6 14.5 %collective-permute-start.9 = (f32[2,96,128]{2,1,0:T(8,128)S(1)}, f32[2,96,128]{2,1,0:T(8,128)S(1)}, u32[]{:S(2)}, u32[]{:S(2)}) collective-permute-start(f32[2,96,128]{2,1,0:T(8,128)S(1)} %get-tuple-element.73), channel_id=1, source_target_pairs={{1,0},{2,1},{3,2},{5,4},{6,5},{7,6},{9,8},{10,9},{11,10},{13,12},{... | collective-permute-start | bytes 294920 | tf_op jit(solution)/shard_map/ppermute | solution.py:392
  35.5 18.1 %collective-permute-start.5 = (f32[2,192,128]{2,1,0:T(8,128)S(1)}, f32[2,192,128]{2,1,0:T(8,128)S(1)}, u32[]{:S(2)}, u32[]{:S(2)}) collective-permute-start(f32[2,192,128]{2,1,0:T(8,128)S(1)} %get-tuple-element.40), channel_id=1, source_target_pairs={{0,1},{1,2},{2,3},{4,5},{5,6},{6,7},{8,9},{9,10},{10,11},{12,13},{... | collective-permute-start | bytes 589832 | tf_op jit(solution)/shard_map/ppermute | solution.py:392
  39.1 14.4 %collective-permute-start.6 = (f32[2,192,128]{2,1,0:T(8,128)S(1)}, f32[2,192,128]{2,1,0:T(8,128)S(1)}, u32[]{:S(2)}, u32[]{:S(2)}) collective-permute-start(f32[2,192,128]{2,1,0:T(8,128)S(1)} %get-tuple-element.41), channel_id=1, source_target_pairs={{1,0},{2,1},{3,2},{5,4},{6,5},{7,6},{9,8},{10,9},{11,10},{13,12},{... | collective-permute-start | bytes 589832 | tf_op jit(solution)/shard_map/ppermute | solution.py:392
  48.0 9.7 %collective-permute-start.10 = (f32[2,384,128]{2,1,0:T(8,128)S(1)}, f32[2,384,128]{2,1,0:T(8,128)S(1)}, u32[]{:S(2)}, u32[]{:S(2)}) collective-permute-start(f32[2,384,128]{2,1,0:T(8,128)S(1)} %get-tuple-element.46), channel_id=1, source_target_pairs={{0,1},{1,2},{2,3},{4,5},{5,6},{6,7},{8,9},{9,10},{10,11},{12,13},{... | collective-permute-start | bytes 1179656 | tf_op jit(solution)/shard_map/ppermute | solution.py:392
  51.6 9.4 %collective-permute-start.11 = (f32[2,384,128]{2,1,0:T(8,128)S(1)}, f32[2,384,128]{2,1,0:T(8,128)S(1)}, u32[]{:S(2)}, u32[]{:S(2)}) collective-permute-start(f32[2,384,128]{2,1,0:T(8,128)S(1)} %get-tuple-element.47), channel_id=1, source_target_pairs={{1,0},{2,1},{3,2},{5,4},{6,5},{7,6},{9,8},{10,9},{11,10},{13,12},{... | collective-permute-start | bytes 1179656 | tf_op jit(solution)/shard_map/ppermute | solution.py:392
  53.6 28.7 %collective-permute-start.13 = (f32[2,192,384]{2,1,0:T(8,128)S(1)}, f32[2,192,384]{2,1,0:T(8,128)S(1)}, u32[]{:S(2)}, u32[]{:S(2)}) collective-permute-start(f32[2,192,384]{2,1,0:T(8,128)S(1)} %totals.4.refs_2_), channel_id=1, source_target_pairs={{4,0},{8,4},{12,8},{16,12},{20,16},{24,20},{28,24},{5,1},{9,5},{13... | collective-permute-start | bytes 1769480 | tf_op jit(solution)/shard_map/ppermute | solution.py:392
  61.1 27.6 %collective-permute-start.12 = (f32[2,192,384]{2,1,0:T(8,128)S(1)}, f32[2,192,384]{2,1,0:T(8,128)S(1)}, u32[]{:S(2)}, u32[]{:S(2)}) collective-permute-start(f32[2,192,384]{2,1,0:T(8,128)S(1)} %get-tuple-element.48.refs_3_), channel_id=1, source_target_pairs={{0,4},{4,8},{8,12},{12,16},{16,20},{20,24},{24,28},{1,5},{5,9},{9,... | collective-permute-start | bytes 1769480 | tf_op jit(solution)/shard_map/ppermute | solution.py:392
  82.6 12.1 %collective-permute-start.15 = (f32[2,384,128]{2,1,0:T(8,128)S(1)}, f32[2,384,128]{2,1,0:T(8,128)S(1)}, u32[]{:S(2)}, u32[]{:S(2)}) collective-permute-start(f32[2,384,128]{2,1,0:T(8,128)S(1)} %get-tuple-element.53), channel_id=1, source_target_pairs={{0,1},{1,2},{2,3},{4,5},{5,6},{6,7},{8,9},{9,10},{10,11},{12,13},{... | collective-permute-start | bytes 1179656 | tf_op jit(solution)/shard_map/ppermute | solution.py:392
  86.8 9.1 %collective-permute-start.17 = (f32[2,384,128]{2,1,0:T(8,128)S(1)}, f32[2,384,128]{2,1,0:T(8,128)S(1)}, u32[]{:S(2)}, u32[]{:S(2)}) collective-permute-start(f32[2,384,128]{2,1,0:T(8,128)S(1)} %get-tuple-element.55), channel_id=1, source_target_pairs={{1,0},{2,1},{3,2},{5,4},{6,5},{7,6},{9,8},{10,9},{11,10},{13,12},{... | collective-permute-start | bytes 1179656 | tf_op jit(solution)/shard_map/ppermute | solution.py:392
  88.9 13.9 %collective-permute-start.14 = (f32[2,192,128]{2,1,0:T(8,128)S(1)}, f32[2,192,128]{2,1,0:T(8,128)S(1)}, u32[]{:S(2)}, u32[]{:S(2)}) collective-permute-start(f32[2,192,128]{2,1,0:T(8,128)S(1)} %get-tuple-element.52), channel_id=1, source_target_pairs={{0,1},{1,2},{2,3},{4,5},{5,6},{6,7},{8,9},{9,10},{10,11},{12,13},{... | collective-permute-start | bytes 589832 | tf_op jit(solution)/shard_map/ppermute | solution.py:392
  92.6 10.3 %collective-permute-start.16 = (f32[2,192,128]{2,1,0:T(8,128)S(1)}, f32[2,192,128]{2,1,0:T(8,128)S(1)}, u32[]{:S(2)}, u32[]{:S(2)}) collective-permute-start(f32[2,192,128]{2,1,0:T(8,128)S(1)} %get-tuple-element.54), channel_id=1, source_target_pairs={{1,0},{2,1},{3,2},{5,4},{6,5},{7,6},{9,8},{10,9},{11,10},{13,12},{... | collective-permute-start | bytes 589832 | tf_op jit(solution)/shard_map/ppermute | solution.py:392
  109.7 17.0 %collective-permute-start.18 = (f32[2,384,128]{2,1,0:T(8,128)S(1)}, f32[2,384,128]{2,1,0:T(8,128)S(1)}, u32[]{:S(2)}, u32[]{:S(2)}) collective-permute-start(f32[2,384,128]{2,1,0:T(8,128)S(1)} %get-tuple-element.60), channel_id=1, source_target_pairs={{0,1},{1,2},{2,3},{4,5},{5,6},{6,7},{8,9},{9,10},{10,11},{12,13},{... | collective-permute-start | bytes 1179656 | tf_op jit(solution)/shard_map/ppermute | solution.py:392
  112.2 14.6 %collective-permute-start.19 = (f32[2,384,128]{2,1,0:T(8,128)S(1)}, f32[2,384,128]{2,1,0:T(8,128)S(1)}, u32[]{:S(2)}, u32[]{:S(2)}) collective-permute-start(f32[2,384,128]{2,1,0:T(8,128)S(1)} %get-tuple-element.61), channel_id=1, source_target_pairs={{1,0},{2,1},{3,2},{5,4},{6,5},{7,6},{9,8},{10,9},{11,10},{13,12},{... | collective-permute-start | bytes 1179656 | tf_op jit(solution)/shard_map/ppermute | solution.py:392
  114.1 6.2 %collective-permute-start.20 = (f32[2,192,128]{2,1,0:T(8,128)S(1)}, f32[2,192,128]{2,1,0:T(8,128)S(1)}, u32[]{:S(2)}, u32[]{:S(2)}) collective-permute-start(f32[2,192,128]{2,1,0:T(8,128)S(1)} %get-tuple-element.64), channel_id=1, source_target_pairs={{0,1},{1,2},{2,3},{4,5},{5,6},{6,7},{8,9},{9,10},{10,11},{12,13},{... | collective-permute-start | bytes 589832 | tf_op jit(solution)/shard_map/ppermute | solution.py:392
  117.8 7.0 %collective-permute-start.21 = (f32[2,192,128]{2,1,0:T(8,128)S(1)}, f32[2,192,128]{2,1,0:T(8,128)S(1)}, u32[]{:S(2)}, u32[]{:S(2)}) collective-permute-start(f32[2,192,128]{2,1,0:T(8,128)S(1)} %get-tuple-element.65), channel_id=1, source_target_pairs={{1,0},{2,1},{3,2},{5,4},{6,5},{7,6},{9,8},{10,9},{11,10},{13,12},{... | collective-permute-start | bytes 589832 | tf_op jit(solution)/shard_map/ppermute | solution.py:392
  124.8 11.9 %collective-permute-start.22 = (f32[2,96,384]{2,1,0:T(8,128)S(1)}, f32[2,96,384]{2,1,0:T(8,128)S(1)}, u32[]{:S(2)}, u32[]{:S(2)}) collective-permute-start(f32[2,96,384]{2,1,0:T(8,128)S(1)} %get-tuple-element.67), channel_id=1, source_target_pairs={{0,4},{4,8},{8,12},{12,16},{16,20},{20,24},{24,28},{1,5},{5,9},{9,... | collective-permute-start | bytes 884744 | tf_op jit(solution)/shard_map/ppermute | solution.py:392
  126.9 12.8 %collective-permute-start.23 = (f32[2,96,384]{2,1,0:T(8,128)S(1)}, f32[2,96,384]{2,1,0:T(8,128)S(1)}, u32[]{:S(2)}, u32[]{:S(2)}) collective-permute-start(f32[2,96,384]{2,1,0:T(8,128)S(1)} %get-tuple-element.68), channel_id=1, source_target_pairs={{4,0},{8,4},{12,8},{16,12},{20,16},{24,20},{28,24},{5,1},{9,5},{13... | collective-permute-start | bytes 884744 | tf_op jit(solution)/shard_map/ppermute | solution.py:392

commit v2 on v1

--- a/solution.py
+++ b/solution.py
@@ -53,6 +53,22 @@
     return high, (value - high.astype(F32)).astype(BF16)
 
 
+def has(side):
+    if side == "above":
+        return lax.axis_index("row") > 0
+    if side == "below":
+        return lax.axis_index("row") < lax.axis_size("row") - 1
+    if side == "left":
+        return lax.axis_index("col") > 0
+    return lax.axis_index("col") < lax.axis_size("col") - 1
+
+
+def kept(value, *sides):
+    for side in sides:
+        value = jnp.where(has(side), value, 0.0)
+    return value
+
+
 def mul(left, right):
     return jnp.dot(left, right, preferred_element_type=F32)
 
@@ -110,9 +126,9 @@
     which = 0
     for part, (lo, hi) in zip(plan, spans):
         row = 0
-        for first, rows in part:
+        for first, rows, sides in part:
             for channel in range(2):
-                reg[channel, row : row + rows, lo:hi] = ins[which][channel, first : first + rows, :]
+                reg[channel, row : row + rows, lo:hi] = kept(ins[which][channel, first : first + rows, :], *sides)
             row += rows
             which += 1
 
@@ -281,8 +297,11 @@
 
 def windows(i, consts, parts, carried, acc_at, outs):
     offsets, table, twiddle, probes, amps = consts
-    plan = tuple(tuple((first, rows) for _, first, rows in part) for part in parts)
-    operands = [array for part in parts for array, _, _ in part]
+    plan = tuple(
+        tuple((piece[1], piece[2], piece[3:] + side) for piece in part)
+        for part, side in zip(parts, (("left",), (), ("right",)))
+    )
+    operands = [piece[0] for part in parts for piece in part]
     extra = list(carried) if carried is not None else []
     own = parts[1][0][0].shape[-1]
     assert own == 3 * LANE
@@ -315,9 +334,9 @@
     for (first, rows), out in zip(outs, out_refs):
         span = slice(first, first + rows)
         for channel in range(2):
-            out[channel, :, :LANE] = own_ref[channel, span, :LANE] + left_ref[channel, span, :]
+            out[channel, :, :LANE] = own_ref[channel, span, :LANE] + kept(left_ref[channel, span, :], "left")
             out[channel, :, LANE : 2 * LANE] = own_ref[channel, span, LANE : 2 * LANE]
-            out[channel, :, 2 * LANE :] = own_ref[channel, span, 2 * LANE :] + right_ref[channel, span, :]
+            out[channel, :, 2 * LANE :] = own_ref[channel, span, 2 * LANE :] + kept(right_ref[channel, span, :], "right")
 
 
 def totals(own, from_left, from_right, outs):
@@ -332,7 +351,7 @@
     )(own, from_left, from_right)
 
 
-def update_kernel(pieces, guard, *refs):
+def update_kernel(pieces, side, *refs):
     new, left, right = refs[-3:]
     ins = refs[:-3]
     row = 0
@@ -341,21 +360,23 @@
             total = None
             for grad, at in grads:
                 term = ins[grad][channel, at : at + rows, :]
+                if grad == len(ins) - 1:
+                    term = kept(term, side)
                 total = term if total is None else total + term
             value = ins[which][channel, first : first + rows, :] - step_size * total
             if masked:
-                value = jnp.where(guard(), value, 0.0)
+                value = kept(value, side)
             new[channel, row : row + rows, :] = value
             left[channel, row : row + rows, :] = value[:, :LANE]
             right[channel, row : row + rows, :] = value[:, 2 * LANE :]
         row += rows
 
 
-def update(operands, pieces, guard):
+def update(operands, pieces, side):
     rows = sum(piece[2] for piece in pieces)
     shape = [jax.ShapeDtypeStruct((2, rows, width), F32) for width in (3 * LANE, LANE, LANE)]
     return pl.pallas_call(
-        functools.partial(update_kernel, pieces, guard),
+        functools.partial(update_kernel, pieces, side),
         out_shape=tuple(shape),
         in_specs=vmem(len(operands)),
         out_specs=tuple(vmem(3)),
@@ -367,10 +388,10 @@
 
 def finish_kernel(top_ref, bottom_ref, mid_ref, low_ref, above_ref, below_ref, out_ref):
     for channel in range(2):
-        above = mid_ref[channel, :MARGIN, :] + above_ref[channel]
+        above = mid_ref[channel, :MARGIN, :] + kept(above_ref[channel], "above")
         out_ref[channel, :MARGIN, :] = top_ref[channel, MARGIN:, :] - step_size * above
         out_ref[channel, MARGIN:288, :] = bottom_ref[channel, :192, :] - step_size * mid_ref[channel, MARGIN:, :]
-        below = low_ref[channel] + below_ref[channel]
+        below = low_ref[channel] + kept(below_ref[channel], "below")
         out_ref[channel, 288:, :] = bottom_ref[channel, 192:288, :] - step_size * below
 
 
@@ -387,9 +408,8 @@
 
 
 def moved(block, axis, distance):
-    devices = range(lax.axis_size(axis))
-    route = [(n, n + distance) for n in devices if n + distance in devices]
-    return lax.ppermute(block, axis, route)
+    count = lax.axis_size(axis)
+    return lax.ppermute(block, axis, [(n, (n + distance) % count) for n in range(count)])
 
 
 def sideways(to_right, to_left):
@@ -411,31 +431,27 @@
 
     top_l, top_r = sideways(top[:, :, edge:], top[:, :, :LANE])
     parts = (
-        [(top_l, 0, MARGIN), (left, 0, last)],
-        [(top, 0, MARGIN), (obj, 0, last)],
-        [(top_r, 0, MARGIN), (right, 0, last)],
+        [(top_l, 0, MARGIN, "above"), (left, 0, last)],
+        [(top, 0, MARGIN, "above"), (obj, 0, last)],
+        [(top_r, 0, MARGIN, "above"), (right, 0, last)],
     )
     lo_l, lo_o, lo_r, mid_l, mid_o, mid_r = windows(0, consts, parts, None, None, ((0, band), (band, band)))
+    bottom, lo_l = lax.optimization_barrier((bottom, lo_l))
     in_l, in_r = sideways(lo_r, lo_l)
     (top_sum,) = totals(lo_o, in_l, in_r, ((0, band),))
     from_below = moved(top_sum, "row", -1)
 
+    mid_o, top_sum = lax.optimization_barrier((mid_o, top_sum))
     bot_l, bot_r = sideways(bottom[:, :, edge:], bottom[:, :, :LANE])
     parts = (
-        [(left, MARGIN, last), (bot_l, 0, MARGIN)],
-        [(obj, MARGIN, last), (bottom, 0, MARGIN)],
-        [(right, MARGIN, last), (bot_r, 0, MARGIN)],
+        [(left, MARGIN, last), (bot_l, 0, MARGIN, "below")],
+        [(obj, MARGIN, last), (bottom, 0, MARGIN, "below")],
+        [(right, MARGIN, last), (bot_r, 0, MARGIN, "below")],
     )
     hi_l, hi_o, hi_r = windows(1, consts, parts, (mid_l, mid_o, mid_r), 0, ((0, tile),))
     in_l, in_r = sideways(hi_r, hi_l)
     mid_sum, bot_sum = totals(hi_o, in_l, in_r, ((0, band), (band, band)))
     from_above = moved(bot_sum, "row", 1)
-
-    def not_last():
-        return lax.axis_index("row") < lax.axis_size("row") - 1
-
-    def not_first():
-        return lax.axis_index("row") > 0
 
     low, low_to_left, low_to_right = update(
         (obj, bottom, mid_sum, bot_sum, from_below),
@@ -444,7 +460,7 @@
             (0, last, MARGIN, ((3, 0), (4, 0)), False),
             (1, 0, MARGIN, ((3, MARGIN), (4, MARGIN)), True),
         ),
-        not_last,
+        "below",
     )
     low_l, low_r = sideways(low_to_right, low_to_left)
     parts = ([(low_l, 0, tile)], [(low, 0, tile)], [(low_r, 0, tile)])
@@ -459,7 +475,7 @@
             (0, 0, MARGIN, ((2, 0), (3, 0)), True),
             (1, 0, MARGIN, ((2, MARGIN), (3, MARGIN)), False),
         ),
-        not_first,
+        "above",
     )
     up_l, up_r = sideways(up_to_right, up_to_left)
     parts = (
@@ -467,6 +483,7 @@
         [(up, 0, band), (low, 0, band)],
         [(up_r, 0, band), (low_r, 0, band)],
     )
+    mid_o, over = lax.optimization_barrier((mid_o, over))
     lo_l, lo_o, lo_r = windows(0, consts, parts, (mid_l, mid_o, mid_r), band, ((0, tile),))
     in_l, in_r = sideways(lo_r, lo_l)
     over, mid_sum = totals(lo_o, in_l, in_r, ((0, MARGIN), (MARGIN, last)))

time: 142 us -> 120 us (0.85)
  the two profiles are of different devices: /device:TPU:17 before, /device:TPU:0 now
where the time goes in v2:
time: 120 us
  waiting for transfers between devices  56.2 us (47%)
  Pallas kernels  31.4 us (26%)
  starting transfers between devices  30.7 us (26%)
  local copies, waits for them, and re-layouts  1.31 us (1%)
    ppermute x24, waiting for transfers between devices, moved(): lax.ppermute(block, axis, [(n, (n + distance) % count) for n in range(cou...  56.2 us
    ppermute x24, starting transfers between devices, moved(): lax.ppermute(block, axis, [(n, (n + distance) % count) for n in range(cou...  30.7 us
    pallas_call x4, Pallas kernels, windows(): pl.pallas_call(functools.partial(windows_kernel, i, plan, acc_at, outs),...  27.6 us
  transfers between devices with their start and end apart: 24, of which 15 were waited for; matrix products, arithmetic and copies ran while one was open for 0% of the time, Pallas kernels for 19%

profile of v2, /device:TPU:0, one launch (start us, length us, event | category | flops | bytes accessed | tf_op | source)
XLA Modules:
  0.0 119.7 jit_solution(5884450632169985940)
XLA Ops:
  0.0 1.2 fusion
  1.2 3.0 %collective-permute-start = (f32[2,96,384]{2,1,0:T(8,128)S(1)}, f32[2,96,384]{2,1,0:T(8,128)S(1)}, u32[]{:S(2)}, u32[]{:S(2)}) collective-permute-start(f32[2,96,384]{2,1,0:T(8,128)S(1)} %get-tuple-element.80), channel_id=1, source_target_pairs={{0,4},{4,8},{8,12},{12,16},{16,20},{20,24},{24,28},{28,0},{1,5},{5... | collective-permute-start | bytes 884744 | tf_op jit(solution)/shard_map/ppermute | solution.py:412
  4.3 0.7 collective-permute-start.4
  5.1 3.5 %collective-permute-start.6 = (f32[2,96,384]{2,1,0:T(8,128)S(1)}, f32[2,96,384]{2,1,0:T(8,128)S(1)}, u32[]{:S(2)}, u32[]{:S(2)}) collective-permute-start(f32[2,96,384]{2,1,0:T(8,128)S(1)} %get-tuple-element.79), channel_id=1, source_target_pairs={{0,28},{4,0},{8,4},{12,8},{16,12},{20,16},{24,20},{28,24},{1,29},{... | collective-permute-start | bytes 884744 | tf_op jit(solution)/shard_map/ppermute | solution.py:412
  8.6 8.3 %collective-permute-done.refs_2_.refs_0_ = f32[2,96,384]{2,1,0:T(8,128)S(1)} collective-permute-done((f32[2,96,384]{2,1,0:T(8,128)S(1)}, f32[2,96,384]{2,1,0:T(8,128)S(1)}, u32[]{:S(2)}, u32[]{:S(2)}) %collective-permute-start) | collective-permute-done | bytes 294944 | tf_op jit(solution)/shard_map/ppermute | solution.py:412
  16.9 0.2 collective-permute-start.3
  17.0 0.4 collective-permute-start.1
  17.4 1.8 %prepare.1 = (f32[4,2,256,256]{3,2,1,0:T(8,128)S(1)}, f32[4,512,128]{2,1,0:T(8,128)S(1)}) custom-call(s32[2,2,2]{2,1,0:T(2,128)S(1)} %copy-done.6, f32[2,256,256]{2,1,0:T(8,128)S(1)} %copy-done.4, f32[512,512]{1,0:T(8,128)S(1)} %copy-done.3, bf16[256,256]{1,0:T(8,128)(2,1)S(1)} %copy-done.5), custom_call_target="tpu_custom_call" | custom-call | flops 400000000 | bytes 6000000 | tf_op jit(solution)/shard_map/prepare/pallas_call | solution.py:101
  19.3 2.8 %collective-permute-done.1.refs_0_ = f32[2,96,128]{2,1,0:T(8,128)S(1)} collective-permute-done((f32[2,96,128]{2,1,0:T(8,128)S(1)}, f32[2,96,128]{2,1,0:T(8,128)S(1)}, u32[]{:S(2)}, u32[]{:S(2)}) %collective-permute-start.1) | collective-permute-done | bytes 98336 | tf_op jit(solution)/shard_map/ppermute | solution.py:412
  22.1 6.9 %windows_0.2 = (f32[2,192,128]{2,1,0:T(8,128)S(1)}, f32[2,192,384]{2,1,0:T(8,128)S(1)}, f32[2,192,128]{2,1,0:T(8,128)S(1)}, f32[2,192,128]{2,1,0:T(8,128)S(1)}, ...) custom-call(s32[2,2,2]{2,1,0:T(2,128)S(1)} %copy-done.6, bf16[4,256,256]{2,1,0:T(8,128)(2,1)S(1)} %copy-done.1, ...), custom_call_target="tpu_custom_call" | custom-call | flops 1600000000 | bytes 10000000 | tf_op jit(solution)/shard_map/windows_0/pallas_call | solution.py:312
  29.1 0.5 collective-permute-start.5
  29.6 1.4 %collective-permute-start.9 = (f32[2,96,128]{2,1,0:T(8,128)S(1)}, f32[2,96,128]{2,1,0:T(8,128)S(1)}, u32[]{:S(2)}, u32[]{:S(2)}) collective-permute-start(f32[2,96,128]{2,1,0:T(8,128)S(1)} %get-tuple-element.83), channel_id=1, source_target_pairs={{0,3},{1,0},{2,1},{3,2},{4,7},{5,4},{6,5},{7,6},{8,11},{9,8},{10,9... | collective-permute-start | bytes 294920 | tf_op jit(solution)/shard_map/ppermute | solution.py:412
  31.0 0.1 collective-permute-start.8
  31.1 2.2 %collective-permute-done.7.right_ref = f32[2,192,128]{2,1,0:T(8,128)S(1)} collective-permute-done((f32[2,192,128]{2,1,0:T(8,128)S(1)}, f32[2,192,128]{2,1,0:T(8,128)S(1)}, u32[]{:S(2)}, u32[]{:S(2)}) %collective-permute-start.7) | collective-permute-done | bytes 196640 | tf_op jit(solution)/shard_map/ppermute | solution.py:412
  33.2 2.9 %collective-permute-done.5.left_ref = f32[2,192,128]{2,1,0:T(8,128)S(1)} collective-permute-done((f32[2,192,128]{2,1,0:T(8,128)S(1)}, f32[2,192,128]{2,1,0:T(8,128)S(1)}, u32[]{:S(2)}, u32[]{:S(2)}) %collective-permute-start.5) | collective-permute-done | bytes 196640 | tf_op jit(solution)/shard_map/ppermute | solution.py:412
  36.1 0.1 totals.4.refs_2_
  36.2 5.6 %collective-permute-start.13 = (f32[2,192,384]{2,1,0:T(8,128)S(1)}, f32[2,192,384]{2,1,0:T(8,128)S(1)}, u32[]{:S(2)}, u32[]{:S(2)}) collective-permute-start(f32[2,192,384]{2,1,0:T(8,128)S(1)} %totals.4.refs_2_), channel_id=1, source_target_pairs={{0,28},{4,0},{8,4},{12,8},{16,12},{20,16},{24,20},{28,24},{1,29},{... | collective-permute-start | bytes 1769480 | tf_op jit(solution)/shard_map/ppermute | solution.py:412
  41.8 6.9 %windows_1.2 = (f32[2,384,128]{2,1,0:T(8,128)S(1)}, f32[2,384,384]{2,1,0:T(8,128)S(1)}, f32[2,384,128]{2,1,0:T(8,128)S(1)}) custom-call(s32[2,2,2]{2,1,0:T(2,128)S(1)} %copy-done.6, bf16[4,256,256]{2,1,0:T(8,128)(2,1)S(1)} %copy-done.1, f32[4,128,128]{2,1,0:T(8,128)S(1)} %copy-done.2, f32[4,2,256,256]{3,2,1,0:T(8,128)S(1)} %get-tuple-element.42.probes_ref, ...), custom_call_target="tpu_custom_call" | custom-call | flops 1600000000 | bytes 10000000 | tf_op jit(solution)/shard_map/windows_1/pallas_call | solution.py:312
  48.7 0.3 collective-permute-start.10
  49.0 1.5 %collective-permute-start.11 = (f32[2,384,128]{2,1,0:T(8,128)S(1)}, f32[2,384,128]{2,1,0:T(8,128)S(1)}, u32[]{:S(2)}, u32[]{:S(2)}) collective-permute-start(f32[2,384,128]{2,1,0:T(8,128)S(1)} %get-tuple-element.56), channel_id=1, source_target_pairs={{0,3},{1,0},{2,1},{3,2},{4,7},{5,4},{6,5},{7,6},{8,11},{9,8},{10,9... | collective-permute-start | bytes 1179656 | tf_op jit(solution)/shard_map/ppermute | solution.py:412
  50.5 7.6 %collective-permute-done.10.left_ref = f32[2,384,128]{2,1,0:T(8,128)S(1)} collective-permute-done((f32[2,384,128]{2,1,0:T(8,128)S(1)}, f32[2,384,128]{2,1,0:T(8,128)S(1)}, u32[]{:S(2)}, u32[]{:S(2)}) %collective-permute-start.10) | collective-permute-done | bytes 393248 | tf_op jit(solution)/shard_map/ppermute | solution.py:412
  58.1 1.4 %collective-permute-done.11.right_ref = f32[2,384,128]{2,1,0:T(8,128)S(1)} collective-permute-done((f32[2,384,128]{2,1,0:T(8,128)S(1)}, f32[2,384,128]{2,1,0:T(8,128)S(1)}, u32[]{:S(2)}, u32[]{:S(2)}) %collective-permute-start.11) | collective-permute-done | bytes 393248 | tf_op jit(solution)/shard_map/ppermute | solution.py:412
  59.5 0.1 totals.5
  59.7 0.2 update.3
  59.9 0.6 collective-permute-start.15
  60.5 1.5 %collective-permute-start.17 = (f32[2,384,128]{2,1,0:T(8,128)S(1)}, f32[2,384,128]{2,1,0:T(8,128)S(1)}, u32[]{:S(2)}, u32[]{:S(2)}) collective-permute-start(f32[2,384,128]{2,1,0:T(8,128)S(1)} %get-tuple-element.64), channel_id=1, source_target_pairs={{0,3},{1,0},{2,1},{3,2},{4,7},{5,4},{6,5},{7,6},{8,11},{9,8},{10,9... | collective-permute-start | bytes 1179656 | tf_op jit(solution)/shard_map/ppermute | solution.py:412
  61.9 7.5 %collective-permute-done.15.refs_0_.refs_1_ = f32[2,384,128]{2,1,0:T(8,128)S(1)} collective-permute-done((f32[2,384,128]{2,1,0:T(8,128)S(1)}, f32[2,384,128]{2,1,0:T(8,128)S(1)}, u32[]{:S(2)}, u32[]{:S(2)}) %collective-permute-start.15) | collective-permute-done | bytes 393248 | tf_op jit(solution)/shard_map/ppermute | solution.py:412
  69.5 1.4 %collective-permute-done.17.refs_2_.refs_5_ = f32[2,384,128]{2,1,0:T(8,128)S(1)} collective-permute-done((f32[2,384,128]{2,1,0:T(8,128)S(1)}, f32[2,384,128]{2,1,0:T(8,128)S(1)}, u32[]{:S(2)}, u32[]{:S(2)}) %collective-permute-start.17) | collective-permute-done | bytes 393248 | tf_op jit(solution)/shard_map/ppermute | solution.py:412
  70.9 6.9 %windows_1.3 = (f32[2,192,128]{2,1,0:T(8,128)S(1)}, f32[2,192,384]{2,1,0:T(8,128)S(1)}, f32[2,192,128]{2,1,0:T(8,128)S(1)}, f32[2,192,128]{2,1,0:T(8,128)S(1)}, ...) custom-call(s32[2,2,2]{2,1,0:T(2,128)S(1)} %copy-done.6, bf16[4,256,256]{2,1,0:T(8,128)(2,1)S(1)} %copy-done.1, ...), custom_call_target="tpu_custom_call" | custom-call | flops 1600000000 | bytes 10000000 | tf_op jit(solution)/shard_map/windows_1/pallas_call | solution.py:312
  77.8 0.9 collective-permute-start.18
  78.6 1.5 %collective-permute-start.19 = (f32[2,192,128]{2,1,0:T(8,128)S(1)}, f32[2,192,128]{2,1,0:T(8,128)S(1)}, u32[]{:S(2)}, u32[]{:S(2)}) collective-permute-start(f32[2,192,128]{2,1,0:T(8,128)S(1)} %get-tuple-element.69), channel_id=1, source_target_pairs={{0,3},{1,0},{2,1},{3,2},{4,7},{5,4},{6,5},{7,6},{8,11},{9,8},{10,9... | collective-permute-start | bytes 589832 | tf_op jit(solution)/shard_map/ppermute | solution.py:412
  80.1 0.1 update.2
  80.3 1.7 %collective-permute-start.16 = (f32[2,192,128]{2,1,0:T(8,128)S(1)}, f32[2,192,128]{2,1,0:T(8,128)S(1)}, u32[]{:S(2)}, u32[]{:S(2)}) collective-permute-start(f32[2,192,128]{2,1,0:T(8,128)S(1)} %get-tuple-element.63), channel_id=1, source_target_pairs={{0,3},{1,0},{2,1},{3,2},{4,7},{5,4},{6,5},{7,6},{8,11},{9,8},{10,9... | collective-permute-start | bytes 589832 | tf_op jit(solution)/shard_map/ppermute | solution.py:412
  82.0 1.7 %collective-permute-done.18.left_ref = f32[2,192,128]{2,1,0:T(8,128)S(1)} collective-permute-done((f32[2,192,128]{2,1,0:T(8,128)S(1)}, f32[2,192,128]{2,1,0:T(8,128)S(1)}, u32[]{:S(2)}, u32[]{:S(2)}) %collective-permute-start.18) | collective-permute-done | bytes 196640 | tf_op jit(solution)/shard_map/ppermute | solution.py:412
  83.7 1.6 %collective-permute-done.19.right_ref = f32[2,192,128]{2,1,0:T(8,128)S(1)} collective-permute-done((f32[2,192,128]{2,1,0:T(8,128)S(1)}, f32[2,192,128]{2,1,0:T(8,128)S(1)}, u32[]{:S(2)}, u32[]{:S(2)}) %collective-permute-start.19) | collective-permute-done | bytes 196640 | tf_op jit(solution)/shard_map/ppermute | solution.py:412
  85.4 0.1 totals.6
  85.4 2.5 %collective-permute-done.14.refs_0_ = f32[2,192,128]{2,1,0:T(8,128)S(1)} collective-permute-done((f32[2,192,128]{2,1,0:T(8,128)S(1)}, f32[2,192,128]{2,1,0:T(8,128)S(1)}, u32[]{:S(2)}, u32[]{:S(2)}) %collective-permute-start.14) | collective-permute-done | bytes 196640 | tf_op jit(solution)/shard_map/ppermute | solution.py:412
  87.9 0.7 collective-permute-done.16.refs_4_
  88.6 6.9 %windows_0.3 = (f32[2,384,128]{2,1,0:T(8,128)S(1)}, f32[2,384,384]{2,1,0:T(8,128)S(1)}, f32[2,384,128]{2,1,0:T(8,128)S(1)}) custom-call(s32[2,2,2]{2,1,0:T(2,128)S(1)} %copy-done.6, bf16[4,256,256]{2,1,0:T(8,128)(2,1)S(1)} %copy-done.1, f32[4,128,128]{2,1,0:T(8,128)S(1)} %copy-done.2, f32[4,2,256,256]{3,2,1,0:T(8,128)S(1)} %get-tuple-element.42.probes_ref, ...), custom_call_target="tpu_custom_call" | custom-call | flops 1600000000 | bytes 10000000 | tf_op jit(solution)/shard_map/windows_0/pallas_call | solution.py:312
  95.5 0.9 collective-permute-start.20
  96.4 1.1 collective-permute-start.21
  97.5 0.1 collective-permute-start.22
  97.7 7.8 %collective-permute-done.20.left_ref = f32[2,384,128]{2,1,0:T(8,128)S(1)} collective-permute-done((f32[2,384,128]{2,1,0:T(8,128)S(1)}, f32[2,384,128]{2,1,0:T(8,128)S(1)}, u32[]{:S(2)}, u32[]{:S(2)}) %collective-permute-start.20) | collective-permute-done | bytes 393248 | tf_op jit(solution)/shard_map/ppermute | solution.py:412
  105.5 0.6 collective-permute-done.21.right_ref
  106.1 0.1 totals.7
  106.2 5.2 %collective-permute-start.23 = (f32[2,96,384]{2,1,0:T(8,128)S(1)}, f32[2,96,384]{2,1,0:T(8,128)S(1)}, u32[]{:S(2)}, u32[]{:S(2)}) collective-permute-start(f32[2,96,384]{2,1,0:T(8,128)S(1)} %get-tuple-element.78), channel_id=1, source_target_pairs={{0,28},{4,0},{8,4},{12,8},{16,12},{20,16},{24,20},{28,24},{1,29},{... | collective-permute-start | bytes 884744 | tf_op jit(solution)/shard_map/ppermute | solution.py:412
  111.4 7.1 %collective-permute-done.23.below_ref = f32[2,96,384]{2,1,0:T(8,128)S(1)} collective-permute-done((f32[2,96,384]{2,1,0:T(8,128)S(1)}, f32[2,96,384]{2,1,0:T(8,128)S(1)}, u32[]{:S(2)}, u32[]{:S(2)}) %collective-permute-start.23) | collective-permute-done | bytes 294944 | tf_op jit(solution)/shard_map/ppermute | solution.py:412
  118.5 1.2 %finish.1 = f32[2,384,384]{2,1,0:T(8,128)} custom-call(f32[2,192,384]{2,1,0:T(8,128)S(1)} %get-tuple-element.58.refs_2_.top_ref, f32[2,384,384]{2,1,0:T(8,128)S(1)} %get-tuple-element.60.refs_1_.refs_3_.bottom_ref, f32[2,288,384]{2,1,0:T(8,128)S(1)} %get-tuple-element.76.mid_ref, f32[2,96,384]{2,1,0:T(8,128)S(1)} %get-tuple-element.77.low_ref, ...), custom_call_target="tpu_custom_call" | custom-call | flops 1000000 | bytes 4000000 | tf_op jit(solution)/shard_map/finish/pallas_call | solution.py:399
  (30 shorter events, 0.3 us)
Async XLA Ops:
  0.0 4.3 %copy-start = (f32[2,384,384]{2,1,0:T(8,128)S(1)}, f32[2,384,384]{2,1,0:T(8,128)}, u32[]{:S(2)}) copy-start(f32[2,384,384]{2,1,0:T(8,128)} %refs_0_.1) | copy-start | bytes 3538948
  1.2 16.2 %copy-start.3 = (f32[512,512]{1,0:T(8,128)S(1)}, f32[512,512]{1,0:T(8,128)}, u32[]{:S(2)}) copy-start(f32[512,512]{1,0:T(8,128)} %amp_ref.1) | copy-start | bytes 3145732
  1.2 16.2 %copy-start.4 = (f32[2,256,256]{2,1,0:T(8,128)S(1)}, f32[2,256,256]{2,1,0:T(8,128)}, u32[]{:S(2)}) copy-start(f32[2,256,256]{2,1,0:T(8,128)} %probe_ref.1) | copy-start | bytes 1572868
  1.2 16.2 %copy-start.5 = (bf16[256,256]{1,0:T(8,128)(2,1)S(1)}, bf16[256,256]{1,0:T(8,128)(2,1)}, u32[]{:S(2)}) copy-start(bf16[256,256]{1,0:T(8,128)(2,1)} %constant.8.clone.order_ref) | copy-start | bytes 393220
  1.2 16.2 %copy-start.6 = (s32[2,2,2]{2,1,0:T(2,128)S(1)}, s32[2,2,2]{2,1,0:T(2,128)}, u32[]{:S(2)}) copy-start(s32[2,2,2]{2,1,0:T(2,128)} %off_ref.9) | copy-start | bytes 100
  1.2 15.6 %collective-permute-start = (f32[2,96,384]{2,1,0:T(8,128)S(1)}, f32[2,96,384]{2,1,0:T(8,128)S(1)}, u32[]{:S(2)}, u32[]{:S(2)}) collective-permute-start(f32[2,96,384]{2,1,0:T(8,128)S(1)} %get-tuple-element.80), channel_id=1, source_target_pairs={{0,4},{4,8},{8,12},{12,16},{16,20},{20,24},{24,28},{28,0},{1,5},{5... | collective-permute-start | bytes 884744 | tf_op jit(solution)/shard_map/ppermute | solution.py:412
  4.3 17.8 %copy-start.1 = (bf16[4,256,256]{2,1,0:T(8,128)(2,1)S(1)}, bf16[4,256,256]{2,1,0:T(8,128)(2,1)}, u32[]{:S(2)}) copy-start(bf16[4,256,256]{2,1,0:T(8,128)(2,1)} %constant.6.clone.tab_ref) | copy-start | bytes 1572868
  4.3 17.8 %copy-start.2 = (f32[4,128,128]{2,1,0:T(8,128)S(1)}, f32[4,128,128]{2,1,0:T(8,128)}, u32[]{:S(2)}) copy-start(f32[4,128,128]{2,1,0:T(8,128)} %constant.7.clone.tw_ref) | copy-start | bytes 786436
  4.3 17.7 %collective-permute-start.4 = (f32[2,384,128]{2,1,0:T(8,128)S(1)}, f32[2,384,128]{2,1,0:T(8,128)S(1)}, u32[]{:S(2)}, u32[]{:S(2)}) collective-permute-start(f32[2,384,128]{2,1,0:T(8,128)S(1)} %get-tuple-element.81), channel_id=1, source_target_pairs={{0,3},{1,0},{2,1},{3,2},{4,7},{5,4},{6,5},{7,6},{8,11},{9,8},{10,9... | collective-permute-start | bytes 1179656 | tf_op jit(solution)/shard_map/ppermute | solution.py:412
  5.1 17.0 %collective-permute-start.2 = (f32[2,384,128]{2,1,0:T(8,128)S(1)}, f32[2,384,128]{2,1,0:T(8,128)S(1)}, u32[]{:S(2)}, u32[]{:S(2)}) collective-permute-start(f32[2,384,128]{2,1,0:T(8,128)S(1)} %get-tuple-element.82), channel_id=1, source_target_pairs={{0,1},{1,2},{2,3},{3,0},{4,5},{5,6},{6,7},{7,4},{8,9},{9,10},{10,1... | collective-permute-start | bytes 1179656 | tf_op jit(solution)/shard_map/ppermute | solution.py:412
  5.1 23.9 %collective-permute-start.6 = (f32[2,96,384]{2,1,0:T(8,128)S(1)}, f32[2,96,384]{2,1,0:T(8,128)S(1)}, u32[]{:S(2)}, u32[]{:S(2)}) collective-permute-start(f32[2,96,384]{2,1,0:T(8,128)S(1)} %get-tuple-element.79), channel_id=1, source_target_pairs={{0,28},{4,0},{8,4},{12,8},{16,12},{20,16},{24,20},{28,24},{1,29},{... | collective-permute-start | bytes 884744 | tf_op jit(solution)/shard_map/ppermute | solution.py:412
  16.9 2.4 %collective-permute-start.3 = (f32[2,96,128]{2,1,0:T(8,128)S(1)}, f32[2,96,128]{2,1,0:T(8,128)S(1)}, u32[]{:S(2)}, u32[]{:S(2)}) collective-permute-start(f32[2,96,128]{2,1,0:T(8,128)S(1)} %get-tuple-element.85), channel_id=1, source_target_pairs={{0,3},{1,0},{2,1},{3,2},{4,7},{5,4},{6,5},{7,6},{8,11},{9,8},{10,9... | collective-permute-start | bytes 294920 | tf_op jit(solution)/shard_map/ppermute | solution.py:412
  17.0 5.1 %collective-permute-start.1 = (f32[2,96,128]{2,1,0:T(8,128)S(1)}, f32[2,96,128]{2,1,0:T(8,128)S(1)}, u32[]{:S(2)}, u32[]{:S(2)}) collective-permute-start(f32[2,96,128]{2,1,0:T(8,128)S(1)} %get-tuple-element.86), channel_id=1, source_target_pairs={{0,1},{1,2},{2,3},{3,0},{4,5},{5,6},{6,7},{7,4},{8,9},{9,10},{10,1... | collective-permute-start | bytes 294920 | tf_op jit(solution)/shard_map/ppermute | solution.py:412
  29.0 4.2 %collective-permute-start.7 = (f32[2,192,128]{2,1,0:T(8,128)S(1)}, f32[2,192,128]{2,1,0:T(8,128)S(1)}, u32[]{:S(2)}, u32[]{:S(2)}) collective-permute-start(f32[2,192,128]{2,1,0:T(8,128)S(1)} %get-tuple-element.48), channel_id=1, source_target_pairs={{0,3},{1,0},{2,1},{3,2},{4,7},{5,4},{6,5},{7,6},{8,11},{9,8},{10,9... | collective-permute-start | bytes 589832 | tf_op jit(solution)/shard_map/ppermute | solution.py:412
  29.1 7.0 %collective-permute-start.5 = (f32[2,192,128]{2,1,0:T(8,128)S(1)}, f32[2,192,128]{2,1,0:T(8,128)S(1)}, u32[]{:S(2)}, u32[]{:S(2)}) collective-permute-start(f32[2,192,128]{2,1,0:T(8,128)S(1)} %get-tuple-element.46), channel_id=1, source_target_pairs={{0,1},{1,2},{2,3},{3,0},{4,5},{5,6},{6,7},{7,4},{8,9},{9,10},{10,1... | collective-permute-start | bytes 589832 | tf_op jit(solution)/shard_map/ppermute | solution.py:412
  29.6 12.2 %collective-permute-start.9 = (f32[2,96,128]{2,1,0:T(8,128)S(1)}, f32[2,96,128]{2,1,0:T(8,128)S(1)}, u32[]{:S(2)}, u32[]{:S(2)}) collective-permute-start(f32[2,96,128]{2,1,0:T(8,128)S(1)} %get-tuple-element.83), channel_id=1, source_target_pairs={{0,3},{1,0},{2,1},{3,2},{4,7},{5,4},{6,5},{7,6},{8,11},{9,8},{10,9... | collective-permute-start | bytes 294920 | tf_op jit(solution)/shard_map/ppermute | solution.py:412
  31.0 10.8 %collective-permute-start.8 = (f32[2,96,128]{2,1,0:T(8,128)S(1)}, f32[2,96,128]{2,1,0:T(8,128)S(1)}, u32[]{:S(2)}, u32[]{:S(2)}) collective-permute-start(f32[2,96,128]{2,1,0:T(8,128)S(1)} %get-tuple-element.84), channel_id=1, source_target_pairs={{0,1},{1,2},{2,3},{3,0},{4,5},{5,6},{6,7},{7,4},{8,9},{9,10},{10,1... | collective-permute-start | bytes 294920 | tf_op jit(solution)/shard_map/ppermute | solution.py:412
  36.2 23.5 %collective-permute-start.13 = (f32[2,192,384]{2,1,0:T(8,128)S(1)}, f32[2,192,384]{2,1,0:T(8,128)S(1)}, u32[]{:S(2)}, u32[]{:S(2)}) collective-permute-start(f32[2,192,384]{2,1,0:T(8,128)S(1)} %totals.4.refs_2_), channel_id=1, source_target_pairs={{0,28},{4,0},{8,4},{12,8},{16,12},{20,16},{24,20},{28,24},{1,29},{... | collective-permute-start | bytes 1769480 | tf_op jit(solution)/shard_map/ppermute | solution.py:412
  48.7 9.4 %collective-permute-start.10 = (f32[2,384,128]{2,1,0:T(8,128)S(1)}, f32[2,384,128]{2,1,0:T(8,128)S(1)}, u32[]{:S(2)}, u32[]{:S(2)}) collective-permute-start(f32[2,384,128]{2,1,0:T(8,128)S(1)} %get-tuple-element.55), channel_id=1, source_target_pairs={{0,1},{1,2},{2,3},{3,0},{4,5},{5,6},{6,7},{7,4},{8,9},{9,10},{10,1... | collective-permute-start | bytes 1179656 | tf_op jit(solution)/shard_map/ppermute | solution.py:412
  49.0 10.4 %collective-permute-start.11 = (f32[2,384,128]{2,1,0:T(8,128)S(1)}, f32[2,384,128]{2,1,0:T(8,128)S(1)}, u32[]{:S(2)}, u32[]{:S(2)}) collective-permute-start(f32[2,384,128]{2,1,0:T(8,128)S(1)} %get-tuple-element.56), channel_id=1, source_target_pairs={{0,3},{1,0},{2,1},{3,2},{4,7},{5,4},{6,5},{7,6},{8,11},{9,8},{10,9... | collective-permute-start | bytes 1179656 | tf_op jit(solution)/shard_map/ppermute | solution.py:412
  59.6 20.5 %collective-permute-start.12 = (f32[2,192,384]{2,1,0:T(8,128)S(1)}, f32[2,192,384]{2,1,0:T(8,128)S(1)}, u32[]{:S(2)}, u32[]{:S(2)}) collective-permute-start(f32[2,192,384]{2,1,0:T(8,128)S(1)} %get-tuple-element.57.refs_3_), channel_id=1, source_target_pairs={{0,4},{4,8},{8,12},{12,16},{16,20},{20,24},{24,28},{28,0},{1,5},{5... | collective-permute-start | bytes 1769480 | tf_op jit(solution)/shard_map/ppermute | solution.py:412
  59.9 9.5 %collective-permute-start.15 = (f32[2,384,128]{2,1,0:T(8,128)S(1)}, f32[2,384,128]{2,1,0:T(8,128)S(1)}, u32[]{:S(2)}, u32[]{:S(2)}) collective-permute-start(f32[2,384,128]{2,1,0:T(8,128)S(1)} %get-tuple-element.62), channel_id=1, source_target_pairs={{0,1},{1,2},{2,3},{3,0},{4,5},{5,6},{6,7},{7,4},{8,9},{9,10},{10,1... | collective-permute-start | bytes 1179656 | tf_op jit(solution)/shard_map/ppermute | solution.py:412
  60.5 10.4 %collective-permute-start.17 = (f32[2,384,128]{2,1,0:T(8,128)S(1)}, f32[2,384,128]{2,1,0:T(8,128)S(1)}, u32[]{:S(2)}, u32[]{:S(2)}) collective-permute-start(f32[2,384,128]{2,1,0:T(8,128)S(1)} %get-tuple-element.64), channel_id=1, source_target_pairs={{0,3},{1,0},{2,1},{3,2},{4,7},{5,4},{6,5},{7,6},{8,11},{9,8},{10,9... | collective-permute-start | bytes 1179656 | tf_op jit(solution)/shard_map/ppermute | solution.py:412
  77.8 6.0 %collective-permute-start.18 = (f32[2,192,128]{2,1,0:T(8,128)S(1)}, f32[2,192,128]{2,1,0:T(8,128)S(1)}, u32[]{:S(2)}, u32[]{:S(2)}) collective-permute-start(f32[2,192,128]{2,1,0:T(8,128)S(1)} %get-tuple-element.68), channel_id=1, source_target_pairs={{0,1},{1,2},{2,3},{3,0},{4,5},{5,6},{6,7},{7,4},{8,9},{9,10},{10,1... | collective-permute-start | bytes 589832 | tf_op jit(solution)/shard_map/ppermute | solution.py:412
  78.6 6.7 %collective-permute-start.19 = (f32[2,192,128]{2,1,0:T(8,128)S(1)}, f32[2,192,128]{2,1,0:T(8,128)S(1)}, u32[]{:S(2)}, u32[]{:S(2)}) collective-permute-start(f32[2,192,128]{2,1,0:T(8,128)S(1)} %get-tuple-element.69), channel_id=1, source_target_pairs={{0,3},{1,0},{2,1},{3,2},{4,7},{5,4},{6,5},{7,6},{8,11},{9,8},{10,9... | collective-permute-start | bytes 589832 | tf_op jit(solution)/shard_map/ppermute | solution.py:412
  80.2 7.8 %collective-permute-start.14 = (f32[2,192,128]{2,1,0:T(8,128)S(1)}, f32[2,192,128]{2,1,0:T(8,128)S(1)}, u32[]{:S(2)}, u32[]{:S(2)}) collective-permute-start(f32[2,192,128]{2,1,0:T(8,128)S(1)} %get-tuple-element.61), channel_id=1, source_target_pairs={{0,1},{1,2},{2,3},{3,0},{4,5},{5,6},{6,7},{7,4},{8,9},{9,10},{10,1... | collective-permute-start | bytes 589832 | tf_op jit(solution)/shard_map/ppermute | solution.py:412
  80.3 8.4 %collective-permute-start.16 = (f32[2,192,128]{2,1,0:T(8,128)S(1)}, f32[2,192,128]{2,1,0:T(8,128)S(1)}, u32[]{:S(2)}, u32[]{:S(2)}) collective-permute-start(f32[2,192,128]{2,1,0:T(8,128)S(1)} %get-tuple-element.63), channel_id=1, source_target_pairs={{0,3},{1,0},{2,1},{3,2},{4,7},{5,4},{6,5},{7,6},{8,11},{9,8},{10,9... | collective-permute-start | bytes 589832 | tf_op jit(solution)/shard_map/ppermute | solution.py:412
  95.5 9.9 %collective-permute-start.20 = (f32[2,384,128]{2,1,0:T(8,128)S(1)}, f32[2,384,128]{2,1,0:T(8,128)S(1)}, u32[]{:S(2)}, u32[]{:S(2)}) collective-permute-start(f32[2,384,128]{2,1,0:T(8,128)S(1)} %get-tuple-element.74), channel_id=1, source_target_pairs={{0,1},{1,2},{2,3},{3,0},{4,5},{5,6},{6,7},{7,4},{8,9},{9,10},{10,1... | collective-permute-start | bytes 1179656 | tf_op jit(solution)/shard_map/ppermute | solution.py:412
  96.4 9.6 %collective-permute-start.21 = (f32[2,384,128]{2,1,0:T(8,128)S(1)}, f32[2,384,128]{2,1,0:T(8,128)S(1)}, u32[]{:S(2)}, u32[]{:S(2)}) collective-permute-start(f32[2,384,128]{2,1,0:T(8,128)S(1)} %get-tuple-element.75), channel_id=1, source_target_pairs={{0,3},{1,0},{2,1},{3,2},{4,7},{5,4},{6,5},{7,6},{8,11},{9,8},{10,9... | collective-permute-start | bytes 1179656 | tf_op jit(solution)/shard_map/ppermute | solution.py:412
  97.5 13.9 %collective-permute-start.22 = (f32[2,96,384]{2,1,0:T(8,128)S(1)}, f32[2,96,384]{2,1,0:T(8,128)S(1)}, u32[]{:S(2)}, u32[]{:S(2)}) collective-permute-start(f32[2,96,384]{2,1,0:T(8,128)S(1)} %get-tuple-element.70), channel_id=1, source_target_pairs={{0,4},{4,8},{8,12},{12,16},{16,20},{20,24},{24,28},{28,0},{1,5},{5... | collective-permute-start | bytes 884744 | tf_op jit(solution)/shard_map/ppermute | solution.py:412
  106.2 12.3 %collective-permute-start.23 = (f32[2,96,384]{2,1,0:T(8,128)S(1)}, f32[2,96,384]{2,1,0:T(8,128)S(1)}, u32[]{:S(2)}, u32[]{:S(2)}) collective-permute-start(f32[2,96,384]{2,1,0:T(8,128)S(1)} %get-tuple-element.78), channel_id=1, source_target_pairs={{0,28},{4,0},{8,4},{12,8},{16,12},{20,16},{24,20},{28,24},{1,29},{... | collective-permute-start | bytes 884744 | tf_op jit(solution)/shard_map/ppermute | solution.py:412

commit v3 on v2

v3 whole, which is shorter than its diff:
```python
import functools
import math

import jax
import jax.numpy as jnp
import numpy as np
from jax import lax
from jax.experimental import pallas as pl
from jax.experimental.pallas import tpu as pltpu
from jax.sharding import PartitionSpec as P

WIN = 256
HALF = 128
MARGIN = 96
LANE = 128
VMEM_LIMIT = 24 * 1024 * 1024

step_size = 0.3
tv_weight = 0.2
tv_smooth = 0.1
amp_floor = 0.5

F32 = jnp.float32
BF16 = jnp.bfloat16


def tables():
    counter = np.arange(HALF)
    angle = (counter[:, None] * counter[None, :] % HALF) * (2.0 * math.pi / HALF)
    cosine = np.cos(angle) / math.sqrt(WIN)
    sine = np.sin(angle) / math.sqrt(WIN)
    first = np.block([[cosine, sine], [-sine, cosine]])
    second = np.block([[cosine, -sine], [sine, cosine]])
    parts = []
    for table in (first, second):
        table = table.astype(np.float32)
        high = table.astype(jnp.bfloat16)
        low = (table - high.astype(np.float32)).astype(jnp.bfloat16)
        parts += [high, low]
    turn = counter * (2.0 * math.pi / WIN)
    rows = np.stack([np.cos(turn), np.sin(turn)])
    by_row = np.broadcast_to(rows[:, :, None], (2, HALF, HALF))
    by_lane = np.broadcast_to(rows[:, None, :], (2, HALF, HALF))
    twiddle = np.concatenate([by_row, by_lane]).astype(np.float32)
    order = np.zeros((WIN, WIN), np.float32)
    for parity in range(2):
        order[2 * counter + parity, parity * HALF + counter] = 1.0
    return np.stack(parts), twiddle, order.astype(jnp.bfloat16)


def split(value):
    high = value.astype(BF16)
    return high, (value - high.astype(F32)).astype(BF16)


def has(side):
    if side == "above":
        return lax.axis_index("row") > 0
    if side == "below":
        return lax.axis_index("row") < lax.axis_size("row") - 1
    if side == "left":
        return lax.axis_index("col") > 0
    return lax.axis_index("col") < lax.axis_size("col") - 1


def kept(value, *sides):
    for side in sides:
        value = jnp.where(has(side), value, 0.0)
    return value


def mul(left, right):
    return jnp.dot(left, right, preferred_element_type=F32)


def vmem(count):
    return [pl.BlockSpec(memory_space=pltpu.VMEM)] * count


def prepare_kernel(off_ref, probe_ref, amp_ref, order_ref, probes_ref, amps_ref, parts_ref):
    order = order_ref[...]
    for i in range(2):
        for j in range(2):
            row = off_ref[i, j, 0]
            col = off_ref[i, j, 1] + (32 if j == 0 else 96)
            for channel in range(2):
                turned = pltpu.roll(probe_ref[channel], row, 0)
                probes_ref[2 * i + j, channel] = pltpu.roll(turned, col, 1)
            amp = amp_ref[i * WIN : (i + 1) * WIN, j * WIN : (j + 1) * WIN]
            high, rest = split(amp)
            middle, low = split(amp - high.astype(F32) - rest.astype(F32))
            sorted_lanes = mul(high, order) + mul(rest, order) + mul(middle, order)
            for q in range(2):
                parts_ref[...] = sorted_lanes[:, q * HALF : (q + 1) * HALF]
                for p in range(2):
                    at = q * WIN + p * HALF
                    amps_ref[2 * i + j, at : at + HALF, :] = parts_ref[pl.ds(p, HALF, stride=2), :]


def prepare(offsets, probe, amplitudes, order):
    return pl.pallas_call(
        prepare_kernel,
        out_shape=(
            jax.ShapeDtypeStruct((4, 2, WIN, WIN), F32),
            jax.ShapeDtypeStruct((4, 2 * WIN, HALF), F32),
        ),
        in_specs=[pl.BlockSpec(memory_space=pltpu.SMEM)] + vmem(3),
        out_specs=tuple(vmem(2)),
        scratch_shapes=[pltpu.VMEM((WIN, HALF), F32)],
        cost_estimate=pl.CostEstimate(flops=400_000_000, bytes_accessed=6_000_000, transcendentals=0),
        compiler_params=pltpu.CompilerParams(vmem_limit_bytes=VMEM_LIMIT),
        name="prepare",
    )(offsets, probe, amplitudes, order)


def rows_of(pieces, refs, first, rows):
    found, at = [], 0
    for ref, (start, count, sides) in zip(refs, pieces):
        lo, hi = max(first, at), min(first + rows, at + count)
        if lo < hi:
            found.append((ref, start + lo - at, hi - lo, sides))
        at += count
    return found


def window_kernel(i, j, side, own, carried_own, carried_side, outs, *refs):
    off_ref, tab_ref, tw_ref, probes_ref, amps_ref = refs[:5]
    refs = refs[5:]
    side_refs, refs = refs[: len(side)], refs[len(side) :]
    own_refs, refs = refs[: len(own)], refs[len(own) :]
    sum_refs, refs = refs[: len(carried_own)], refs[len(carried_own) :]
    strip_refs, refs = refs[: len(carried_side)], refs[len(carried_side) :]
    out_refs, refs = refs[: 2 * len(outs)], refs[2 * len(outs) :]
    halves = [refs[n : n + 2] for n in range(0, 16, 2)]
    g_in, h_in, m_in, g_out = halves[0:2], halves[2:4], halves[4:6], halves[6:8]
    wide, tall, tall_back, wide_back = refs[16:18], refs[18:20], refs[20:22], refs[22:24]

    number = 2 * i + j
    row_start = off_ref[i, j, 0]
    col_start = off_ref[i, j, 1] + 32 + 64 * j
    row_iota = lax.broadcasted_iota(jnp.int32, (HALF, HALF), 0)
    lane_iota = lax.broadcasted_iota(jnp.int32, (HALF, HALF), 1)
    in_row = row_iota >= row_start
    first_h, first_l, second_h, second_l = (tab_ref.at[n] for n in range(4))
    strip_at = 0 if j == 0 else 3

    def place(group):
        if group == strip_at:
            return True, slice(0, LANE)
        at = (group - (1 if j == 0 else 0)) * LANE
        return False, slice(at, at + LANE)

    def load(channel, first, group):
        is_strip, lanes = place(group)
        pieces, sources = (side, side_refs) if is_strip else (own, own_refs)
        blocks = [
            kept(ref[channel, at : at + rows, lanes], *sides)
            for ref, at, rows, sides in rows_of(pieces, sources, first, HALF)
        ]
        return blocks[0] if len(blocks) == 1 else jnp.concatenate(blocks, axis=0)

    def emit(channel, first, group, value):
        is_strip, lanes = place(group)
        extra = (carried_side, strip_refs) if is_strip else (carried_own, sum_refs)
        which = 1 if is_strip else 0
        for n, (start, count) in enumerate(outs):
            lo, hi = max(first, start), min(first + HALF, start + count)
            if lo >= hi:
                continue
            cuts = sorted({lo, hi} | {c for at, rows in extra[0] for c in (at, at + rows) if lo < c < hi})
            for a, b in zip(cuts, cuts[1:]):
                part = value[a - first : b - first]
                for (at, rows), ref in zip(*extra):
                    if at <= a and b <= at + rows:
                        part = part + ref[channel, a - at : b - at, lanes]
                out_refs[2 * n + which][channel, a - start : b - start, lanes] = part

    def store_split(pair, rows, lanes, value):
        high, low = split(value)
        pair[0][rows, lanes] = high
        pair[1][rows, lanes] = low

    lo, hi = slice(0, HALF), slice(HALF, WIN)
    tw_c, tw_s = tw_ref[0], tw_ref[1]
    for cb in range(2):
        in_col = lane_iota + cb * LANE >= col_start
        field = []
        for rb in range(2):
            value = []
            for channel in range(2):
                picked = jnp.where(in_col, load(channel, rb * HALF, cb), load(channel, rb * HALF, cb + 2))
                if rb == 0:
                    other = jnp.where(in_col, load(channel, WIN, cb), load(channel, WIN, cb + 2))
                    picked = jnp.where(in_row, picked, other)
                value.append(picked)
            box = (slice(rb * HALF, (rb + 1) * HALF), slice(cb * LANE, (cb + 1) * LANE))
            p_re = probes_ref[(number, 0) + box]
            p_im = probes_ref[(number, 1) + box]
            field.append((p_re * value[0] - p_im * value[1], p_re * value[1] + p_im * value[0]))
        (re0, im0), (re1, im1) = field
        store_split(g_in[cb], lo, lo, re0 + re1)
        store_split(g_in[cb], hi, lo, im0 + im1)
        d_re = re0 - re1
        d_im = im0 - im1
        store_split(g_in[cb], lo, hi, d_re * tw_c + d_im * tw_s)
        store_split(g_in[cb], hi, hi, d_im * tw_c - d_re * tw_s)
        high, low = g_in[cb][0][...], g_in[cb][1][...]
        wide[cb][...] = mul(first_h[...], high) + mul(first_h[...], low) + mul(first_l[...], high)

    for p in range(2):
        tl_c, tl_s = tw_ref[2], tw_ref[3]
        cols = slice(p * HALF, (p + 1) * HALF)
        re0, re1 = wide[0][lo, cols], wide[1][lo, cols]
        im0, im1 = wide[0][hi, cols], wide[1][hi, cols]
        store_split(h_in[p], lo, lo, re0 + re1)
        store_split(h_in[p], lo, hi, im0 + im1)
        d_re = re0 - re1
        d_im = im0 - im1
        store_split(h_in[p], hi, lo, d_re * tl_c + d_im * tl_s)
        store_split(h_in[p], hi, hi, d_im * tl_c - d_re * tl_s)
        high, low = h_in[p][0][...], h_in[p][1][...]
        tall[p][...] = mul(high, second_h[...]) + mul(low, second_h[...]) + mul(high, second_l[...])

    for p in range(2):
        for q, rows in enumerate((lo, hi)):
            re, im = tall[p][rows, lo], tall[p][rows, hi]
            power = jnp.maximum(re * re + im * im, amp_floor * amp_floor)
            at = q * WIN + p * HALF
            keeping = 1.0 - amps_ref[number, at : at + HALF, :] * lax.rsqrt(power)
            store_split(m_in[p], rows, lo, re * keeping)
            store_split(m_in[p], rows, hi, im * keeping)
        high, low = m_in[p][0][...], m_in[p][1][...]
        tall_back[p][...] = mul(high, first_h[...]) + mul(low, first_h[...]) + mul(high, first_l[...])

    for p in range(2):
        tl_c, tl_s = tw_ref[2], tw_ref[3]
        u_re, u_im = tall_back[p][lo, lo], tall_back[p][lo, hi]
        v_re, v_im = tall_back[p][hi, lo], tall_back[p][hi, hi]
        w_re = v_re * tl_c - v_im * tl_s
        w_im = v_im * tl_c + v_re * tl_s
        store_split(g_out[p], lo, lo, u_re + w_re)
        store_split(g_out[p], lo, hi, u_re - w_re)
        store_split(g_out[p], hi, lo, u_im + w_im)
        store_split(g_out[p], hi, hi, u_im - w_im)
        high, low = g_out[p][0][...], g_out[p][1][...]
        wide_back[p][...] = mul(second_h[...], high) + mul(second_h[...], low) + mul(second_l[...], high)

    for cb in range(2):
        in_col = lane_iota + cb * LANE >= col_start
        cols = slice(cb * LANE, (cb + 1) * LANE)
        u_re, u_im = wide_back[0][lo, cols], wide_back[0][hi, cols]
        v_re, v_im = wide_back[1][lo, cols], wide_back[1][hi, cols]
        w_re = v_re * tw_c - v_im * tw_s
        w_im = v_im * tw_c + v_re * tw_s
        for rb in range(2):
            b_re = u_re + w_re if rb == 0 else u_re - w_re
            b_im = u_im + w_im if rb == 0 else u_im - w_im
            box = (slice(rb * HALF, (rb + 1) * HALF), cols)
            p_re = probes_ref[(number, 0) + box]
            p_im = probes_ref[(number, 1) + box]
            grads = (p_re * b_re + p_im * b_im, p_re * b_im - p_im * b_re)
            for channel in range(2):
                grad = grads[channel]
                targets = [(rb * HALF, grad)]
                if rb == 0:
                    targets = [(0, jnp.where(in_row, grad, 0.0)), (WIN, jnp.where(in_row, 0.0, grad))]
                for at, piece in targets:
                    emit(channel, at, cb, jnp.where(in_col, piece, 0.0))
                    emit(channel, at, cb + 2, jnp.where(in_col, 0.0, piece))


def window(i, j, consts, side, own, carried_own, carried_side, outs):
    border = ("left",) if j == 0 else ("right",)
    own_width = 3 * LANE
    shapes = []
    for _, rows in outs:
        shapes += [jax.ShapeDtypeStruct((2, rows, width), F32) for width in (own_width, LANE)]
    operands = [piece[0] for piece in list(side) + list(own) + list(carried_own) + list(carried_side)]
    kernel = functools.partial(
        window_kernel,
        i,
        j,
        tuple((p[1], p[2], p[3:] + border) for p in side),
        tuple((p[1], p[2], p[3:]) for p in own),
        tuple((at, array.shape[1]) for array, at in carried_own),
        tuple((at, array.shape[1]) for array, at in carried_side),
        outs,
    )
    return pl.pallas_call(
        kernel,
        out_shape=tuple(shapes),
        in_specs=[pl.BlockSpec(memory_space=pltpu.SMEM)] + vmem(4 + len(operands)),
        out_specs=tuple(vmem(len(shapes))),
        scratch_shapes=[pltpu.VMEM((WIN, WIN), BF16)] * 16 + [pltpu.VMEM((WIN, WIN), F32)] * 8,
        cost_estimate=pl.CostEstimate(flops=1_600_000_000, bytes_accessed=5_000_000, transcendentals=0),
        compiler_params=pltpu.CompilerParams(vmem_limit_bytes=VMEM_LIMIT),
        name=f"window_{i}{j}",
    )(*consts, *operands)


def variation_kernel(plan, *refs):
    reg = refs[-1]
    out_ref = refs[-2]
    which = 0
    for part, (lo, hi) in zip(plan, ((0, LANE), (LANE, 4 * LANE), (4 * LANE, 5 * LANE))):
        row = 0
        for first, rows, sides in part:
            for channel in range(2):
                reg[channel, row : row + rows, lo:hi] = kept(refs[which][channel, first : first + rows, :], *sides)
            row += rows
            which += 1

    def chunk(step, _):
        base = pl.multiple_of(step * 32, 8)
        flows = []
        power = tv_smooth
        for channel in range(2):
            block = reg[channel, pl.ds(base, 48), :]
            down = pltpu.roll(block, 47, 0) - block
            right = pltpu.roll(block, 5 * LANE - 1, 1) - block
            power = power + down * down + right * right
            flows.append((down, right))
        inverse = lax.rsqrt(power)
        for channel in range(2):
            down, right = flows[channel]
            down = down * inverse
            right = right * inverse
            change = pltpu.roll(down, 1, 0) - down + pltpu.roll(right, 1, 1) - right
            out_ref[channel, pl.ds(base, 32), :] = tv_weight * change[8:40, LANE : 4 * LANE]
        return 0

    lax.fori_loop(0, 6, chunk, 0)


def variation(left, own, right):
    parts = (left, own, right)
    plan = tuple(
        tuple((p[1], p[2], p[3:] + border) for p in part) for part, border in zip(parts, (("left",), (), ("right",)))
    )
    operands = [piece[0] for part in parts for piece in part]
    return pl.pallas_call(
        functools.partial(variation_kernel, plan),
        out_shape=jax.ShapeDtypeStruct((2, 192, 3 * LANE), F32),
        in_specs=vmem(len(operands)),
        out_specs=pl.BlockSpec(memory_space=pltpu.VMEM),
        scratch_shapes=[pltpu.VMEM((2, 208, 5 * LANE), F32)],
        cost_estimate=pl.CostEstimate(flops=200_000_000, bytes_accessed=5_000_000, transcendentals=0),
        compiler_params=pltpu.CompilerParams(vmem_limit_bytes=VMEM_LIMIT),
        name="variation",
    )(*operands)


def totals_kernel(outs, extras, own_ref, left_ref, right_ref, *refs):
    added, out_refs = refs[: len(extras)], refs[len(extras) :]
    for (first, rows), out in zip(outs, out_refs):
        cuts = {first, first + rows}
        for at, count, _ in extras:
            cuts |= {c for c in (at, at + count) if first < c < first + rows}
        cuts = sorted(cuts)
        for a, b in zip(cuts, cuts[1:]):
            for channel in range(2):
                value = own_ref[channel, a:b, :]
                for (at, count, source), ref in zip(extras, added):
                    if at <= a and b <= at + count:
                        value = value + ref[channel, source + a - at : source + b - at, :]
                to = slice(a - first, b - first)
                out[channel, to, :LANE] = value[:, :LANE] + kept(left_ref[channel, a:b, :], "left")
                out[channel, to, LANE : 2 * LANE] = value[:, LANE : 2 * LANE]
                out[channel, to, 2 * LANE :] = value[:, 2 * LANE :] + kept(right_ref[channel, a:b, :], "right")


def totals(own, from_left, from_right, outs, extras):
    plan = tuple((at, rows, source) for _, source, at, rows in extras)
    return pl.pallas_call(
        functools.partial(totals_kernel, outs, plan),
        out_shape=tuple(jax.ShapeDtypeStruct((2, rows, own.shape[2]), F32) for _, rows in outs),
        in_specs=vmem(3 + len(extras)),
        out_specs=tuple(vmem(len(outs))),
        cost_estimate=pl.CostEstimate(flops=500_000, bytes_accessed=3_000_000, transcendentals=0),
        compiler_params=pltpu.CompilerParams(vmem_limit_bytes=VMEM_LIMIT),
        name="totals",
    )(own, from_left, from_right, *[extra[0] for extra in extras])


def update_kernel(pieces, side, *refs):
    new, left, right = refs[-3:]
    ins = refs[:-3]
    row = 0
    for which, first, rows, grads, masked in pieces:
        for channel in range(2):
            total = None
            for grad, at in grads:
                term = ins[grad][channel, at : at + rows, :]
                if grad == len(ins) - 1:
                    term = kept(term, side)
                total = term if total is None else total + term
            value = ins[which][channel, first : first + rows, :] - step_size * total
            if masked:
                value = kept(value, side)
            new[channel, row : row + rows, :] = value
            left[channel, row : row + rows, :] = value[:, :LANE]
            right[channel, row : row + rows, :] = value[:, 2 * LANE :]
        row += rows


def update(operands, pieces, side):
    rows = sum(piece[2] for piece in pieces)
    shape = [jax.ShapeDtypeStruct((2, rows, width), F32) for width in (3 * LANE, LANE, LANE)]
    return pl.pallas_call(
        functools.partial(update_kernel, pieces, side),
        out_shape=tuple(shape),
        in_specs=vmem(len(operands)),
        out_specs=tuple(vmem(3)),
        cost_estimate=pl.CostEstimate(flops=1_000_000, bytes_accessed=4_000_000, transcendentals=0),
        compiler_params=pltpu.CompilerParams(vmem_limit_bytes=VMEM_LIMIT),
        name="update",
    )(*operands)


def finish_kernel(top_ref, bottom_ref, mid_ref, low_ref, above_ref, below_ref, out_ref):
    for channel in range(2):
        above = mid_ref[channel, :MARGIN, :] + kept(above_ref[channel], "above")
        out_ref[channel, :MARGIN, :] = top_ref[channel, MARGIN:, :] - step_size * above
        out_ref[channel, MARGIN:288, :] = bottom_ref[channel, :192, :] - step_size * mid_ref[channel, MARGIN:, :]
        below = low_ref[channel] + kept(below_ref[channel], "below")
        out_ref[channel, 288:, :] = bottom_ref[channel, 192:288, :] - step_size * below


def finish(*operands):
    return pl.pallas_call(
        finish_kernel,
        out_shape=jax.ShapeDtypeStruct((2, 3 * LANE, 3 * LANE), F32),
        in_specs=vmem(len(operands)),
        out_specs=pl.BlockSpec(memory_space=pltpu.VMEM),
        cost_estimate=pl.CostEstimate(flops=1_000_000, bytes_accessed=4_000_000, transcendentals=0),
        compiler_params=pltpu.CompilerParams(vmem_limit_bytes=VMEM_LIMIT),
        name="finish",
    )(*operands)


def moved(block, axis, distance):
    count = lax.axis_size(axis)
    return lax.ppermute(block, axis, [(n, (n + distance) % count) for n in range(count)])


def rightward(block):
    return moved(block, "col", 1)


def leftward(block):
    return moved(block, "col", -1)


def on_device(table, twiddle, order, object_field, probe, amplitudes, offsets):
    tile = object_field.shape[1]
    last = tile - MARGIN
    band = 2 * MARGIN
    edge = tile - LANE
    obj = object_field
    after = lax.optimization_barrier

    top = moved(obj[:, last:, :], "row", 1)
    left, right = rightward(obj[:, :, edge:]), leftward(obj[:, :, :LANE])
    up_rows, top = after((obj[:, :MARGIN, :], top))
    bottom = moved(up_rows, "row", -1)
    probes, amps = prepare(offsets, probe, amplitudes, order)
    consts = (offsets, table, twiddle, probes, amps)

    top_l, top_r = rightward(top[:, :, edge:]), leftward(top[:, :, :LANE])
    own = [(top, 0, MARGIN, "above"), (obj, 0, last)]
    halves = ((0, band), (band, band))
    lo_o, lo_l, mid_o, mid_l = window(
        0, 0, consts, [(top_l, 0, MARGIN, "above"), (left, 0, last)], own, [], [], halves
    )
    in_r = leftward(lo_l)
    lo_o, lo_r, mid_o, mid_r = window(
        0, 1, consts, [(top_r, 0, MARGIN, "above"), (right, 0, last)], own, [(lo_o, 0), (mid_o, band)], [], halves
    )
    in_l = rightward(lo_r)
    bottom, lo_r = after((bottom, lo_r))
    bot_l, bot_r = rightward(bottom[:, :, edge:]), leftward(bottom[:, :, :LANE])
    tv_top = variation(
        [(top_l, 88, 8, "above"), (left, 0, 200)],
        [(top, 88, 8, "above"), (obj, 0, 200)],
        [(top_r, 88, 8, "above"), (right, 0, 200)],
    )
    (top_sum,) = totals(lo_o, in_l, in_r, ((0, band),), [(tv_top, 0, MARGIN, MARGIN)])
    from_below = moved(top_sum, "row", -1)

    mid_o, top_sum = after((mid_o, top_sum))
    own = [(obj, MARGIN, last), (bottom, 0, MARGIN, "below")]
    whole = ((0, tile),)
    hi_o, hi_l = window(
        1, 0, consts, [(left, MARGIN, last), (bot_l, 0, MARGIN, "below")], own, [(mid_o, 0)], [(mid_l, 0)], whole
    )
    in_r = leftward(hi_l)
    hi_o, hi_r = window(
        1, 1, consts, [(right, MARGIN, last), (bot_r, 0, MARGIN, "below")], own, [(hi_o, 0)], [(mid_r, 0)], whole
    )
    in_l = rightward(hi_r)
    tv_bottom = variation(
        [(left, 184, 200), (bot_l, 0, 8, "below")],
        [(obj, 184, 200), (bottom, 0, 8, "below")],
        [(right, 184, 200), (bot_r, 0, 8, "below")],
    )
    mid_sum, bot_sum = totals(
        hi_o, in_l, in_r, halves, [(tv_top, MARGIN, 0, MARGIN), (tv_bottom, 0, MARGIN, band)]
    )
    from_above = moved(bot_sum, "row", 1)

    low, low_to_left, low_to_right = update(
        (obj, bottom, mid_sum, bot_sum, from_below),
        (
            (0, MARGIN, band, ((2, 0),), False),
            (0, last, MARGIN, ((3, 0), (4, 0)), False),
            (1, 0, MARGIN, ((3, MARGIN), (4, MARGIN)), True),
        ),
        "below",
    )
    low_l, low_r = rightward(low_to_right), leftward(low_to_left)
    own = [(low, 0, tile)]
    mid_o, mid_l, hi_o, hi_l = window(1, 0, consts, [(low_l, 0, tile)], own, [], [], halves)
    in_r = leftward(hi_l)
    mid_o, mid_r, hi_o, hi_r = window(
        1, 1, consts, [(low_r, 0, tile)], own, [(mid_o, 0), (hi_o, band)], [], halves
    )
    in_l = rightward(hi_r)
    tv_bottom = variation([(low_l, 88, 208)], [(low, 88, 208)], [(low_r, 88, 208)])
    low_sum, over = totals(hi_o, in_l, in_r, ((0, MARGIN), (MARGIN, MARGIN)), [(tv_bottom, MARGIN, 0, MARGIN)])
    last_above = moved(over, "row", 1)

    up, up_to_left, up_to_right = update(
        (top, obj, top_sum, from_above),
        (
            (0, 0, MARGIN, ((2, 0), (3, 0)), True),
            (1, 0, MARGIN, ((2, MARGIN), (3, MARGIN)), False),
        ),
        "above",
    )
    up_l, up_r = rightward(up_to_right), leftward(up_to_left)
    mid_o, over = after((mid_o, over))
    own = [(up, 0, band), (low, 0, band)]
    cut = ((0, MARGIN), (MARGIN, last))
    over_o, over_l, lo_o, lo_l = window(
        0, 0, consts, [(up_l, 0, band), (low_l, 0, band)], own, [(mid_o, band)], [(mid_l, band)], cut
    )
    over_r, in_r = leftward(over_l), leftward(lo_l)
    over_o, over_rr, lo_o, lo_r = window(
        0, 1, consts, [(up_r, 0, band), (low_r, 0, band)], own, [(over_o, 0), (lo_o, MARGIN)], [(mid_r, band)], cut
    )
    over_l = rightward(over_rr)
    (over,) = totals(over_o, over_l, over_r, ((0, MARGIN),), [])
    last_below = moved(over, "row", -1)
    in_l = rightward(lo_r)
    tv_top = variation(
        [(up_l, 88, 104), (low_l, 0, 104)], [(up, 88, 104), (low, 0, 104)], [(up_r, 88, 104), (low_r, 0, 104)]
    )
    (mid_sum,) = totals(lo_o, in_l, in_r, ((0, last),), [(tv_top, 0, 0, band), (tv_bottom, 0, band, MARGIN)])
    return finish(up, low, mid_sum, low_sum, last_above, last_below)


def solution(mesh):
    table, twiddle, order = tables()
    body = jax.shard_map(
        on_device,
        mesh=mesh,
        in_specs=(P(), P(), P(), P(None, "row", "col"), P(), P("row", "col"), P("row", "col", None)),
        out_specs=P(None, "row", "col"),
        check_vma=False,
    )

    def step(object_field, probe, amplitudes, offsets):
        return body(table, twiddle, order, object_field, probe, amplitudes, offsets)

    return step
```

time: 120 us -> 102 us (0.85)
  waiting for transfers between devices: 56.2 us -> 42 us
  starting transfers between devices: 30.7 us -> 28.1 us
    ppermute x24 -> x26, waiting for transfers between devices: 56.2 us -> 42 us  [moved(): lax.ppermute(block, axis, [(n, (n + distance) % count) for n in range(cou...]
    ppermute x24 -> x26, starting transfers between devices: 30.7 us -> 28.1 us  [moved(): lax.ppermute(block, axis, [(n, (n + distance) % count) for n in range(cou...]
    pallas_call x8 -> x17, Pallas kernels: 28 us -> 26.9 us  [the longest x8 21 us: window(): pl.pallas_call(kernel, out_shape=tuple(shapes), in_specs=[pl.BlockSpec(me...]
  transfers between devices with their start and end apart: 24 -> 26, of which waited for: 15 -> 13; matrix products, arithmetic and copies ran while one was open for 0% -> 0% of each run, Pallas kernels for 19% -> 26%
where the time goes in v3:
time: 102 us
  waiting for transfers between devices  42 us (41%)
  Pallas kernels  30.2 us (30%)
  starting transfers between devices  28.1 us (28%)
  local copies, waits for them, and re-layouts  1.31 us (1%)
    ppermute x26, waiting for transfers between devices, moved(): lax.ppermute(block, axis, [(n, (n + distance) % count) for n in range(cou...  42 us
    ppermute x26, starting transfers between devices, moved(): lax.ppermute(block, axis, [(n, (n + distance) % count) for n in range(cou...  28.1 us
    pallas_call x8, Pallas kernels, window(): pl.pallas_call(kernel, out_shape=tuple(shapes), in_specs=[pl.BlockSpec(me...  21 us
    pallas_call x4, Pallas kernels, variation(): pl.pallas_call(functools.partial(variation_kernel, plan), out_shape=jax.S...  5.32 us
  transfers between devices with their start and end apart: 26, of which 13 were waited for; matrix products, arithmetic and copies ran while one was open for 0% of the time, Pallas kernels for 26%

profile of v3, /device:TPU:0, one launch (start us, length us, event | category | flops | bytes accessed | tf_op | source)
XLA Modules:
  0.0 102.0 jit_solution(814280991457423345)
XLA Ops:
  0.0 1.2 %fusion.1 = (f32[2,96,384]{2,1,0:T(8,128)S(1)}, f32[2,96,384]{2,1,0:T(8,128)S(1)}) fusion(f32[2,384,384]{2,1,0:T(8,128)} %refs_0_.13), kind=kLoop, calls=%fused_computation.1 | loop fusion | bytes 1179648 | tf_op jit(solution)/shard_map/slice | solution.py:462
  1.2 3.0 %collective-permute-start = (f32[2,96,384]{2,1,0:T(8,128)S(1)}, f32[2,96,384]{2,1,0:T(8,128)S(1)}, u32[]{:S(2)}, u32[]{:S(2)}) collective-permute-start(f32[2,96,384]{2,1,0:T(8,128)S(1)} %get-tuple-element.99), channel_id=1, source_target_pairs={{0,4},{4,8},{8,12},{12,16},{16,20},{20,24},{24,28},{28,0},{1,5},{5... | collective-permute-start | bytes 884744 | tf_op jit(solution)/shard_map/ppermute | solution.py:443
  4.4 1.7 %collective-permute-start.2 = (f32[2,384,128]{2,1,0:T(8,128)S(1)}, f32[2,384,128]{2,1,0:T(8,128)S(1)}, u32[]{:S(2)}, u32[]{:S(2)}) collective-permute-start(f32[2,384,128]{2,1,0:T(8,128)S(1)} %get-tuple-element.98), channel_id=1, source_target_pairs={{0,3},{1,0},{2,1},{3,2},{4,7},{5,4},{6,5},{7,6},{8,11},{9,8},{10,9... | collective-permute-start | bytes 1179656 | tf_op jit(solution)/shard_map/ppermute | solution.py:443
  6.1 8.2 %collective-permute-done.refs_7_.refs_2_.refs_0_ = f32[2,96,384]{2,1,0:T(8,128)S(1)} collective-permute-done((f32[2,96,384]{2,1,0:T(8,128)S(1)}, f32[2,96,384]{2,1,0:T(8,128)S(1)}, u32[]{:S(2)}, u32[]{:S(2)}) %collective-permute-start) | collective-permute-done | bytes 294944 | tf_op jit(solution)/shard_map/ppermute | solution.py:443
  14.4 1.8 %prepare.1 = (f32[4,2,256,256]{3,2,1,0:T(8,128)S(1)}, f32[4,512,128]{2,1,0:T(8,128)S(1)}) custom-call(s32[2,2,2]{2,1,0:T(2,128)S(1)} %copy-done.6, f32[2,256,256]{2,1,0:T(8,128)S(1)} %copy-done.4, f32[512,512]{1,0:T(8,128)S(1)} %copy-done.3, bf16[256,256]{1,0:T(8,128)(2,1)S(1)} %copy-done.5), custom_call_target="tpu_custom_call" | custom-call | flops 400000000 | bytes 6000000 | tf_op jit(solution)/shard_map/prepare/pallas_call | solution.py:101
  16.3 1.8 %collective-permute-start.1 = (f32[2,96,128]{2,1,0:T(8,128)S(1)}, f32[2,96,128]{2,1,0:T(8,128)S(1)}, u32[]{:S(2)}, u32[]{:S(2)}) collective-permute-start(f32[2,96,128]{2,1,0:T(8,128)S(1)} %get-tuple-element.104), channel_id=1, source_target_pairs={{0,3},{1,0},{2,1},{3,2},{4,7},{5,4},{6,5},{7,6},{8,11},{9,8},{10,9... | collective-permute-start | bytes 294920 | tf_op jit(solution)/shard_map/ppermute | solution.py:443
  18.0 1.7 %collective-permute-start.7 = (f32[2,96,384]{2,1,0:T(8,128)S(1)}, f32[2,96,384]{2,1,0:T(8,128)S(1)}, u32[]{:S(2)}, u32[]{:S(2)}) collective-permute-start(f32[2,96,384]{2,1,0:T(8,128)S(1)} %get-tuple-element.61), channel_id=1, source_target_pairs={{0,28},{4,0},{8,4},{12,8},{16,12},{20,16},{24,20},{28,24},{1,29},{... | collective-permute-start | bytes 884744 | tf_op jit(solution)/shard_map/ppermute | solution.py:443
  19.8 2.6 %window_00.2 = (f32[2,192,384]{2,1,0:T(8,128)S(1)}, f32[2,192,128]{2,1,0:T(8,128)S(1)}, f32[2,192,384]{2,1,0:T(8,128)S(1)}, f32[2,192,128]{2,1,0:T(8,128)S(1)}) custom-call(s32[2,2,2]{2,1,0:T(2,128)S(1)} %copy-done.6, bf16[4,256,256]{2,1,0:T(8,128)(2,1)S(1)} %copy-done.1, f32[4,128,128]{2,1,0:T(8,128)S(1)} %copy-done.2, ...), custom_call_target="tpu_custom_call" | custom-call | flops 1600000000 | bytes 5000000 | tf_op jit(solution)/shard_map/window_00/pallas_call | solution.py:289
  22.5 2.7 %window_01.2 = (f32[2,192,384]{2,1,0:T(8,128)S(1)}, f32[2,192,128]{2,1,0:T(8,128)S(1)}, f32[2,192,384]{2,1,0:T(8,128)S(1)}, f32[2,192,128]{2,1,0:T(8,128)S(1)}) custom-call(s32[2,2,2]{2,1,0:T(2,128)S(1)} %copy-done.6, bf16[4,256,256]{2,1,0:T(8,128)(2,1)S(1)} %copy-done.1, f32[4,128,128]{2,1,0:T(8,128)S(1)} %copy-done.2, ...), custom_call_target="tpu_custom_call" | custom-call | flops 1600000000 | bytes 5000000 | tf_op jit(solution)/shard_map/window_01/pallas_call | solution.py:289
  25.2 0.5 collective-permute-start.5
  25.7 1.2 %collective-permute-done.7.refs_8_.refs_3_.refs_1_ = f32[2,96,384]{2,1,0:T(8,128)S(1)} collective-permute-done((f32[2,96,384]{2,1,0:T(8,128)S(1)}, f32[2,96,384]{2,1,0:T(8,128)S(1)}, u32[]{:S(2)}, u32[]{:S(2)}) %collective-permute-start.7) | collective-permute-done | bytes 294944 | tf_op jit(solution)/shard_map/ppermute | solution.py:443
  27.0 1.3 %variation.4.refs_0_ = f32[2,192,384]{2,1,0:T(8,128)S(1)} custom-call(f32[2,96,128]{2,1,0:T(8,128)S(1)} %collective-permute-done.3.refs_5_.refs_0_, f32[2,384,128]{2,1,0:T(8,128)S(1)} %collective-permute-done.4.refs_6_.refs_1_.refs_5_.refs_0_, f32[2,96,384]{2,1,0:T(8,128)S(1)} %collective-permute-done.refs_7_.refs_2_.refs_0_, f32[2,384,384]{2,1,0:T(8,128)S(1)} %copy-done, ...), custom_call_target="tpu_custom_call" | custom-call | flops 200000000 | bytes 5000000 | tf_op jit(solution)/shard_map/variation/pallas_call | solution.py:341
  28.3 1.8 %collective-permute-start.8 = (f32[2,96,128]{2,1,0:T(8,128)S(1)}, f32[2,96,128]{2,1,0:T(8,128)S(1)}, u32[]{:S(2)}, u32[]{:S(2)}) collective-permute-start(f32[2,96,128]{2,1,0:T(8,128)S(1)} %get-tuple-element.102), channel_id=1, source_target_pairs={{0,3},{1,0},{2,1},{3,2},{4,7},{5,4},{6,5},{7,6},{8,11},{9,8},{10,9... | collective-permute-start | bytes 294920 | tf_op jit(solution)/shard_map/ppermute | solution.py:443
  30.1 0.2 collective-permute-done.5.left_ref
  30.4 4.3 %collective-permute-start.13 = (f32[2,192,384]{2,1,0:T(8,128)S(1)}, f32[2,192,384]{2,1,0:T(8,128)S(1)}, u32[]{:S(2)}, u32[]{:S(2)}) collective-permute-start(f32[2,192,384]{2,1,0:T(8,128)S(1)} %totals.5.refs_2_), channel_id=1, source_target_pairs={{0,28},{4,0},{8,4},{12,8},{16,12},{20,16},{24,20},{28,24},{1,29},{... | collective-permute-start | bytes 1769480 | tf_op jit(solution)/shard_map/ppermute | solution.py:443
  34.7 2.6 %window_10.2 = (f32[2,384,384]{2,1,0:T(8,128)S(1)}, f32[2,384,128]{2,1,0:T(8,128)S(1)}) custom-call(s32[2,2,2]{2,1,0:T(2,128)S(1)} %copy-done.6, bf16[4,256,256]{2,1,0:T(8,128)(2,1)S(1)} %copy-done.1, f32[4,128,128]{2,1,0:T(8,128)S(1)} %copy-done.2, f32[4,2,256,256]{3,2,1,0:T(8,128)S(1)} %get-tuple-element.52.refs_3_, ...), custom_call_target="tpu_custom_call" | custom-call | flops 1600000000 | bytes 5000000 | tf_op jit(solution)/shard_map/window_10/pallas_call | solution.py:289
  37.3 2.7 %window_11.2 = (f32[2,384,384]{2,1,0:T(8,128)S(1)}, f32[2,384,128]{2,1,0:T(8,128)S(1)}) custom-call(s32[2,2,2]{2,1,0:T(2,128)S(1)} %copy-done.6, bf16[4,256,256]{2,1,0:T(8,128)(2,1)S(1)} %copy-done.1, f32[4,128,128]{2,1,0:T(8,128)S(1)} %copy-done.2, f32[4,2,256,256]{3,2,1,0:T(8,128)S(1)} %get-tuple-element.52.refs_3_, ...), custom_call_target="tpu_custom_call" | custom-call | flops 1600000000 | bytes 5000000 | tf_op jit(solution)/shard_map/window_11/pallas_call | solution.py:289
  40.1 1.7 %collective-permute-start.11 = (f32[2,384,128]{2,1,0:T(8,128)S(1)}, f32[2,384,128]{2,1,0:T(8,128)S(1)}, u32[]{:S(2)}, u32[]{:S(2)}) collective-permute-start(f32[2,384,128]{2,1,0:T(8,128)S(1)} %get-tuple-element.69), channel_id=1, source_target_pairs={{0,3},{1,0},{2,1},{3,2},{4,7},{5,4},{6,5},{7,6},{8,11},{9,8},{10,9... | collective-permute-start | bytes 1179656 | tf_op jit(solution)/shard_map/ppermute | solution.py:443
  41.8 1.3 %variation.5.refs_1_ = f32[2,192,384]{2,1,0:T(8,128)S(1)} custom-call(f32[2,384,128]{2,1,0:T(8,128)S(1)} %collective-permute-done.4.refs_6_.refs_1_.refs_5_.refs_0_, f32[2,96,128]{2,1,0:T(8,128)S(1)} %collective-permute-done.9.refs_6_.refs_1_, f32[2,384,384]{2,1,0:T(8,128)S(1)} %copy-done, f32[2,96,384]{2,1,0:T(8,128)S(1)} %collective-permute-done.7.refs_8_.refs_3_.refs_1_, ...), custom_call_target="tpu_custom_call" | custom-call | flops 200000000 | bytes 5000000 | tf_op jit(solution)/shard_map/variation/pallas_call | solution.py:341
  43.2 7.5 %collective-permute-done.10.left_ref = f32[2,384,128]{2,1,0:T(8,128)S(1)} collective-permute-done((f32[2,384,128]{2,1,0:T(8,128)S(1)}, f32[2,384,128]{2,1,0:T(8,128)S(1)}, u32[]{:S(2)}, u32[]{:S(2)}) %collective-permute-start.10) | collective-permute-done | bytes 393248 | tf_op jit(solution)/shard_map/ppermute | solution.py:443
  50.7 0.2 totals.6
  50.9 0.2 update.3
  51.1 0.7 collective-permute-start.17
  51.8 1.1 %collective-permute-start.15 = (f32[2,384,128]{2,1,0:T(8,128)S(1)}, f32[2,384,128]{2,1,0:T(8,128)S(1)}, u32[]{:S(2)}, u32[]{:S(2)}) collective-permute-start(f32[2,384,128]{2,1,0:T(8,128)S(1)} %get-tuple-element.75), channel_id=1, source_target_pairs={{0,3},{1,0},{2,1},{3,2},{4,7},{5,4},{6,5},{7,6},{8,11},{9,8},{10,9... | collective-permute-start | bytes 1179656 | tf_op jit(solution)/shard_map/ppermute | solution.py:443
  52.9 8.7 %collective-permute-done.17.refs_5_.refs_0_.refs_6_.refs_1_ = f32[2,384,128]{2,1,0:T(8,128)S(1)} collective-permute-done((f32[2,384,128]{2,1,0:T(8,128)S(1)}, f32[2,384,128]{2,1,0:T(8,128)S(1)}, u32[]{:S(2)}, u32[]{:S(2)}) %collective-permute-start.17) | collective-permute-done | bytes 393248 | tf_op jit(solution)/shard_map/ppermute | solution.py:443
  61.6 2.6 %window_10.3 = (f32[2,192,384]{2,1,0:T(8,128)S(1)}, f32[2,192,128]{2,1,0:T(8,128)S(1)}, f32[2,192,384]{2,1,0:T(8,128)S(1)}, f32[2,192,128]{2,1,0:T(8,128)S(1)}) custom-call(s32[2,2,2]{2,1,0:T(2,128)S(1)} %copy-done.6, bf16[4,256,256]{2,1,0:T(8,128)(2,1)S(1)} %copy-done.1, f32[4,128,128]{2,1,0:T(8,128)S(1)} %copy-done.2, ...), custom_call_target="tpu_custom_call" | custom-call | flops 1600000000 | bytes 5000000 | tf_op jit(solution)/shard_map/window_10/pallas_call | solution.py:289
  64.2 0.2 collective-permute-start.19
  64.5 2.6 %window_11.3 = (f32[2,192,384]{2,1,0:T(8,128)S(1)}, f32[2,192,128]{2,1,0:T(8,128)S(1)}, f32[2,192,384]{2,1,0:T(8,128)S(1)}, f32[2,192,128]{2,1,0:T(8,128)S(1)}) custom-call(s32[2,2,2]{2,1,0:T(2,128)S(1)} %copy-done.6, bf16[4,256,256]{2,1,0:T(8,128)(2,1)S(1)} %copy-done.1, f32[4,128,128]{2,1,0:T(8,128)S(1)} %copy-done.2, ...), custom_call_target="tpu_custom_call" | custom-call | flops 1600000000 | bytes 5000000 | tf_op jit(solution)/shard_map/window_11/pallas_call | solution.py:289
  67.1 0.5 collective-permute-start.18
  67.6 2.1 %collective-permute-done.12.refs_3_ = f32[2,192,384]{2,1,0:T(8,128)S(1)} collective-permute-done((f32[2,192,384]{2,1,0:T(8,128)S(1)}, f32[2,192,384]{2,1,0:T(8,128)S(1)}, u32[]{:S(2)}, u32[]{:S(2)}) %collective-permute-start.12) | collective-permute-done | bytes 589856 | tf_op jit(solution)/shard_map/ppermute | solution.py:443
  69.9 1.7 %collective-permute-start.14 = (f32[2,192,128]{2,1,0:T(8,128)S(1)}, f32[2,192,128]{2,1,0:T(8,128)S(1)}, u32[]{:S(2)}, u32[]{:S(2)}) collective-permute-start(f32[2,192,128]{2,1,0:T(8,128)S(1)} %get-tuple-element.74), channel_id=1, source_target_pairs={{0,3},{1,0},{2,1},{3,2},{4,7},{5,4},{6,5},{7,6},{8,11},{9,8},{10,9... | collective-permute-start | bytes 589832 | tf_op jit(solution)/shard_map/ppermute | solution.py:443
  71.7 1.3 %variation.6.refs_0_.refs_1_ = f32[2,192,384]{2,1,0:T(8,128)S(1)} custom-call(f32[2,384,128]{2,1,0:T(8,128)S(1)} %collective-permute-done.17.refs_5_.refs_0_.refs_6_.refs_1_, f32[2,384,384]{2,1,0:T(8,128)S(1)} %get-tuple-element.73.refs_6_.refs_1_.refs_8_.refs_3_.bottom_ref, f32[2,384,128]{2,1,0:T(8,128)S(1)} %collective-permute-done.15.refs_5_.refs_2_.refs_6_), custom_call_target="tpu_custom_call" | custom-call | flops 200000000 | bytes 5000000 | tf_op jit(solution)/shard_map/variation/pallas_call | solution.py:341
  73.1 2.3 %collective-permute-done.16.refs_5_.refs_0_ = f32[2,192,128]{2,1,0:T(8,128)S(1)} collective-permute-done((f32[2,192,128]{2,1,0:T(8,128)S(1)}, f32[2,192,128]{2,1,0:T(8,128)S(1)}, u32[]{:S(2)}, u32[]{:S(2)}) %collective-permute-start.16) | collective-permute-done | bytes 196640 | tf_op jit(solution)/shard_map/ppermute | solution.py:443
  75.5 2.6 %window_00.3 = (f32[2,96,384]{2,1,0:T(8,128)S(1)}, f32[2,96,128]{2,1,0:T(8,128)S(1)}, f32[2,288,384]{2,1,0:T(8,128)S(1)}, f32[2,288,128]{2,1,0:T(8,128)S(1)}) custom-call(s32[2,2,2]{2,1,0:T(2,128)S(1)} %copy-done.6, bf16[4,256,256]{2,1,0:T(8,128)(2,1)S(1)} %copy-done.1, f32[4,128,128]{2,1,0:T(8,128)S(1)} %copy-done.2, ...), custom_call_target="tpu_custom_call" | custom-call | flops 1600000000 | bytes 5000000 | tf_op jit(solution)/shard_map/window_00/pallas_call | solution.py:289
  78.1 2.6 %window_01.3 = (f32[2,96,384]{2,1,0:T(8,128)S(1)}, f32[2,96,128]{2,1,0:T(8,128)S(1)}, f32[2,288,384]{2,1,0:T(8,128)S(1)}, f32[2,288,128]{2,1,0:T(8,128)S(1)}) custom-call(s32[2,2,2]{2,1,0:T(2,128)S(1)} %copy-done.6, bf16[4,256,256]{2,1,0:T(8,128)(2,1)S(1)} %copy-done.1, f32[4,128,128]{2,1,0:T(8,128)S(1)} %copy-done.2, ...), custom_call_target="tpu_custom_call" | custom-call | flops 1600000000 | bytes 5000000 | tf_op jit(solution)/shard_map/window_01/pallas_call | solution.py:289
  80.8 1.7 %collective-permute-start.24 = (f32[2,96,128]{2,1,0:T(8,128)S(1)}, f32[2,96,128]{2,1,0:T(8,128)S(1)}, u32[]{:S(2)}, u32[]{:S(2)}) collective-permute-start(f32[2,96,128]{2,1,0:T(8,128)S(1)} %get-tuple-element.96), channel_id=1, source_target_pairs={{0,3},{1,0},{2,1},{3,2},{4,7},{5,4},{6,5},{7,6},{8,11},{9,8},{10,9... | collective-permute-start | bytes 294920 | tf_op jit(solution)/shard_map/ppermute | solution.py:443
  82.6 0.5 collective-permute-start.20
  83.0 1.3 %collective-permute-start.21 = (f32[2,288,128]{2,1,0:T(8,128)S(1)}, f32[2,288,128]{2,1,0:T(8,128)S(1)}, u32[]{:S(2)}, u32[]{:S(2)}) collective-permute-start(f32[2,288,128]{2,1,0:T(8,128)S(1)} %get-tuple-element.92), channel_id=1, source_target_pairs={{0,3},{1,0},{2,1},{3,2},{4,7},{5,4},{6,5},{7,6},{8,11},{9,8},{10,9... | collective-permute-start | bytes 884744 | tf_op jit(solution)/shard_map/ppermute | solution.py:443
  84.3 0.5 collective-permute-done.23.left_ref
  84.9 0.9 collective-permute-done.24.right_ref
  85.8 3.3 %collective-permute-start.25 = (f32[2,96,384]{2,1,0:T(8,128)S(1)}, f32[2,96,384]{2,1,0:T(8,128)S(1)}, u32[]{:S(2)}, u32[]{:S(2)}) collective-permute-start(f32[2,96,384]{2,1,0:T(8,128)S(1)} %totals.9), channel_id=1, source_target_pairs={{0,28},{4,0},{8,4},{12,8},{16,12},{20,16},{24,20},{28,24},{1,29},{... | collective-permute-start | bytes 884744 | tf_op jit(solution)/shard_map/ppermute | solution.py:443
  89.1 1.3 %variation.7.refs_0_ = f32[2,192,384]{2,1,0:T(8,128)S(1)} custom-call(f32[2,192,128]{2,1,0:T(8,128)S(1)} %collective-permute-done.16.refs_5_.refs_0_, f32[2,384,128]{2,1,0:T(8,128)S(1)} %collective-permute-done.17.refs_5_.refs_0_.refs_6_.refs_1_, f32[2,192,384]{2,1,0:T(8,128)S(1)} %get-tuple-element.71.refs_7_.refs_2_.top_ref, ...), custom_call_target="tpu_custom_call" | custom-call | flops 200000000 | bytes 5000000 | tf_op jit(solution)/shard_map/variation/pallas_call | solution.py:341
  90.5 0.8 collective-permute-done.20.left_ref
  91.2 0.6 collective-permute-done.21.right_ref
  91.8 0.1 totals.8.mid_ref
  92.0 4.1 %collective-permute-done.22.above_ref = f32[2,96,384]{2,1,0:T(8,128)S(1)} collective-permute-done((f32[2,96,384]{2,1,0:T(8,128)S(1)}, f32[2,96,384]{2,1,0:T(8,128)S(1)}, u32[]{:S(2)}, u32[]{:S(2)}) %collective-permute-start.22) | collective-permute-done | bytes 294944 | tf_op jit(solution)/shard_map/ppermute | solution.py:443
  96.0 4.8 %collective-permute-done.25.below_ref = f32[2,96,384]{2,1,0:T(8,128)S(1)} collective-permute-done((f32[2,96,384]{2,1,0:T(8,128)S(1)}, f32[2,96,384]{2,1,0:T(8,128)S(1)}, u32[]{:S(2)}, u32[]{:S(2)}) %collective-permute-start.25) | collective-permute-done | bytes 294944 | tf_op jit(solution)/shard_map/ppermute | solution.py:443
  100.8 1.2 %finish.1 = f32[2,384,384]{2,1,0:T(8,128)} custom-call(f32[2,192,384]{2,1,0:T(8,128)S(1)} %get-tuple-element.71.refs_7_.refs_2_.top_ref, f32[2,384,384]{2,1,0:T(8,128)S(1)} %get-tuple-element.73.refs_6_.refs_1_.refs_8_.refs_3_.bottom_ref, f32[2,288,384]{2,1,0:T(8,128)S(1)} %totals.8.mid_ref, f32[2,96,384]{2,1,0:T(8,128)S(1)} %get-tuple-element.93.low_ref, ...), custom_call_target="tpu_custom_call" | custom-call | flops 1000000 | bytes 4000000 | tf_op jit(solution)/shard_map/finish/pallas_call | solution.py:430
  (43 shorter events, 0.9 us)
Async XLA Ops:
  0.0 4.3 %copy-start = (f32[2,384,384]{2,1,0:T(8,128)S(1)}, f32[2,384,384]{2,1,0:T(8,128)}, u32[]{:S(2)}) copy-start(f32[2,384,384]{2,1,0:T(8,128)} %refs_0_.13) | copy-start | bytes 3538948
  1.2 13.2 %copy-start.3 = (f32[512,512]{1,0:T(8,128)S(1)}, f32[512,512]{1,0:T(8,128)}, u32[]{:S(2)}) copy-start(f32[512,512]{1,0:T(8,128)} %amp_ref.1) | copy-start | bytes 3145732
  1.2 13.2 %copy-start.4 = (f32[2,256,256]{2,1,0:T(8,128)S(1)}, f32[2,256,256]{2,1,0:T(8,128)}, u32[]{:S(2)}) copy-start(f32[2,256,256]{2,1,0:T(8,128)} %probe_ref.1) | copy-start | bytes 1572868
  1.2 13.2 %copy-start.5 = (bf16[256,256]{1,0:T(8,128)(2,1)S(1)}, bf16[256,256]{1,0:T(8,128)(2,1)}, u32[]{:S(2)}) copy-start(bf16[256,256]{1,0:T(8,128)(2,1)} %constant.8.clone.order_ref) | copy-start | bytes 393220
  1.2 13.2 %copy-start.6 = (s32[2,2,2]{2,1,0:T(2,128)S(1)}, s32[2,2,2]{2,1,0:T(2,128)}, u32[]{:S(2)}) copy-start(s32[2,2,2]{2,1,0:T(2,128)} %refs_0_.17) | copy-start | bytes 100
  1.2 13.1 %collective-permute-start = (f32[2,96,384]{2,1,0:T(8,128)S(1)}, f32[2,96,384]{2,1,0:T(8,128)S(1)}, u32[]{:S(2)}, u32[]{:S(2)}) collective-permute-start(f32[2,96,384]{2,1,0:T(8,128)S(1)} %get-tuple-element.99), channel_id=1, source_target_pairs={{0,4},{4,8},{8,12},{12,16},{16,20},{20,24},{24,28},{28,0},{1,5},{5... | collective-permute-start | bytes 884744 | tf_op jit(solution)/shard_map/ppermute | solution.py:443
  4.3 15.5 %copy-start.1 = (bf16[4,256,256]{2,1,0:T(8,128)(2,1)S(1)}, bf16[4,256,256]{2,1,0:T(8,128)(2,1)}, u32[]{:S(2)}) copy-start(bf16[4,256,256]{2,1,0:T(8,128)(2,1)} %constant.6.clone.refs_1_) | copy-start | bytes 1572868
  4.3 15.5 %copy-start.2 = (f32[4,128,128]{2,1,0:T(8,128)S(1)}, f32[4,128,128]{2,1,0:T(8,128)}, u32[]{:S(2)}) copy-start(f32[4,128,128]{2,1,0:T(8,128)} %constant.7.clone.refs_2_) | copy-start | bytes 786436
  4.3 15.4 %collective-permute-start.4 = (f32[2,384,128]{2,1,0:T(8,128)S(1)}, f32[2,384,128]{2,1,0:T(8,128)S(1)}, u32[]{:S(2)}, u32[]{:S(2)}) collective-permute-start(f32[2,384,128]{2,1,0:T(8,128)S(1)} %get-tuple-element.97), channel_id=1, source_target_pairs={{0,1},{1,2},{2,3},{3,0},{4,5},{5,6},{6,7},{7,4},{8,9},{9,10},{10,1... | collective-permute-start | bytes 1179656 | tf_op jit(solution)/shard_map/ppermute | solution.py:443
  4.4 18.1 %collective-permute-start.2 = (f32[2,384,128]{2,1,0:T(8,128)S(1)}, f32[2,384,128]{2,1,0:T(8,128)S(1)}, u32[]{:S(2)}, u32[]{:S(2)}) collective-permute-start(f32[2,384,128]{2,1,0:T(8,128)S(1)} %get-tuple-element.98), channel_id=1, source_target_pairs={{0,3},{1,0},{2,1},{3,2},{4,7},{5,4},{6,5},{7,6},{8,11},{9,8},{10,9... | collective-permute-start | bytes 1179656 | tf_op jit(solution)/shard_map/ppermute | solution.py:443
  14.3 5.5 %collective-permute-start.3 = (f32[2,96,128]{2,1,0:T(8,128)S(1)}, f32[2,96,128]{2,1,0:T(8,128)S(1)}, u32[]{:S(2)}, u32[]{:S(2)}) collective-permute-start(f32[2,96,128]{2,1,0:T(8,128)S(1)} %get-tuple-element.103), channel_id=1, source_target_pairs={{0,1},{1,2},{2,3},{3,0},{4,5},{5,6},{6,7},{7,4},{8,9},{9,10},{10,1... | collective-permute-start | bytes 294920 | tf_op jit(solution)/shard_map/ppermute | solution.py:443
  16.3 6.2 %collective-permute-start.1 = (f32[2,96,128]{2,1,0:T(8,128)S(1)}, f32[2,96,128]{2,1,0:T(8,128)S(1)}, u32[]{:S(2)}, u32[]{:S(2)}) collective-permute-start(f32[2,96,128]{2,1,0:T(8,128)S(1)} %get-tuple-element.104), channel_id=1, source_target_pairs={{0,3},{1,0},{2,1},{3,2},{4,7},{5,4},{6,5},{7,6},{8,11},{9,8},{10,9... | collective-permute-start | bytes 294920 | tf_op jit(solution)/shard_map/ppermute | solution.py:443
  18.0 8.9 %collective-permute-start.7 = (f32[2,96,384]{2,1,0:T(8,128)S(1)}, f32[2,96,384]{2,1,0:T(8,128)S(1)}, u32[]{:S(2)}, u32[]{:S(2)}) collective-permute-start(f32[2,96,384]{2,1,0:T(8,128)S(1)} %get-tuple-element.61), channel_id=1, source_target_pairs={{0,28},{4,0},{8,4},{12,8},{16,12},{20,16},{24,20},{28,24},{1,29},{... | collective-permute-start | bytes 884744 | tf_op jit(solution)/shard_map/ppermute | solution.py:443
  22.4 7.7 %collective-permute-start.6 = (f32[2,192,128]{2,1,0:T(8,128)S(1)}, f32[2,192,128]{2,1,0:T(8,128)S(1)}, u32[]{:S(2)}, u32[]{:S(2)}) collective-permute-start(f32[2,192,128]{2,1,0:T(8,128)S(1)} %get-tuple-element.59), channel_id=1, source_target_pairs={{0,3},{1,0},{2,1},{3,2},{4,7},{5,4},{6,5},{7,6},{8,11},{9,8},{10,9... | collective-permute-start | bytes 589832 | tf_op jit(solution)/shard_map/ppermute | solution.py:443
  25.2 5.1 %collective-permute-start.5 = (f32[2,192,128]{2,1,0:T(8,128)S(1)}, f32[2,192,128]{2,1,0:T(8,128)S(1)}, u32[]{:S(2)}, u32[]{:S(2)}) collective-permute-start(f32[2,192,128]{2,1,0:T(8,128)S(1)} %get-tuple-element.58), channel_id=1, source_target_pairs={{0,1},{1,2},{2,3},{3,0},{4,5},{5,6},{6,7},{7,4},{8,9},{9,10},{10,1... | collective-permute-start | bytes 589832 | tf_op jit(solution)/shard_map/ppermute | solution.py:443
  26.9 7.8 %collective-permute-start.9 = (f32[2,96,128]{2,1,0:T(8,128)S(1)}, f32[2,96,128]{2,1,0:T(8,128)S(1)}, u32[]{:S(2)}, u32[]{:S(2)}) collective-permute-start(f32[2,96,128]{2,1,0:T(8,128)S(1)} %get-tuple-element.101), channel_id=1, source_target_pairs={{0,1},{1,2},{2,3},{3,0},{4,5},{5,6},{6,7},{7,4},{8,9},{9,10},{10,1... | collective-permute-start | bytes 294920 | tf_op jit(solution)/shard_map/ppermute | solution.py:443
  28.3 9.0 %collective-permute-start.8 = (f32[2,96,128]{2,1,0:T(8,128)S(1)}, f32[2,96,128]{2,1,0:T(8,128)S(1)}, u32[]{:S(2)}, u32[]{:S(2)}) collective-permute-start(f32[2,96,128]{2,1,0:T(8,128)S(1)} %get-tuple-element.102), channel_id=1, source_target_pairs={{0,3},{1,0},{2,1},{3,2},{4,7},{5,4},{6,5},{7,6},{8,11},{9,8},{10,9... | collective-permute-start | bytes 294920 | tf_op jit(solution)/shard_map/ppermute | solution.py:443
  30.4 20.5 %collective-permute-start.13 = (f32[2,192,384]{2,1,0:T(8,128)S(1)}, f32[2,192,384]{2,1,0:T(8,128)S(1)}, u32[]{:S(2)}, u32[]{:S(2)}) collective-permute-start(f32[2,192,384]{2,1,0:T(8,128)S(1)} %totals.5.refs_2_), channel_id=1, source_target_pairs={{0,28},{4,0},{8,4},{12,8},{16,12},{20,16},{24,20},{28,24},{1,29},{... | collective-permute-start | bytes 1769480 | tf_op jit(solution)/shard_map/ppermute | solution.py:443
  40.0 10.7 %collective-permute-start.10 = (f32[2,384,128]{2,1,0:T(8,128)S(1)}, f32[2,384,128]{2,1,0:T(8,128)S(1)}, u32[]{:S(2)}, u32[]{:S(2)}) collective-permute-start(f32[2,384,128]{2,1,0:T(8,128)S(1)} %get-tuple-element.68), channel_id=1, source_target_pairs={{0,1},{1,2},{2,3},{3,0},{4,5},{5,6},{6,7},{7,4},{8,9},{9,10},{10,1... | collective-permute-start | bytes 1179656 | tf_op jit(solution)/shard_map/ppermute | solution.py:443
  40.1 10.6 %collective-permute-start.11 = (f32[2,384,128]{2,1,0:T(8,128)S(1)}, f32[2,384,128]{2,1,0:T(8,128)S(1)}, u32[]{:S(2)}, u32[]{:S(2)}) collective-permute-start(f32[2,384,128]{2,1,0:T(8,128)S(1)} %get-tuple-element.69), channel_id=1, source_target_pairs={{0,3},{1,0},{2,1},{3,2},{4,7},{5,4},{6,5},{7,6},{8,11},{9,8},{10,9... | collective-permute-start | bytes 1179656 | tf_op jit(solution)/shard_map/ppermute | solution.py:443
  51.1 10.5 %collective-permute-start.17 = (f32[2,384,128]{2,1,0:T(8,128)S(1)}, f32[2,384,128]{2,1,0:T(8,128)S(1)}, u32[]{:S(2)}, u32[]{:S(2)}) collective-permute-start(f32[2,384,128]{2,1,0:T(8,128)S(1)} %get-tuple-element.77), channel_id=1, source_target_pairs={{0,1},{1,2},{2,3},{3,0},{4,5},{5,6},{6,7},{7,4},{8,9},{9,10},{10,1... | collective-permute-start | bytes 1179656 | tf_op jit(solution)/shard_map/ppermute | solution.py:443
  51.8 18.0 %collective-permute-start.12 = (f32[2,192,384]{2,1,0:T(8,128)S(1)}, f32[2,192,384]{2,1,0:T(8,128)S(1)}, u32[]{:S(2)}, u32[]{:S(2)}) collective-permute-start(f32[2,192,384]{2,1,0:T(8,128)S(1)} %get-tuple-element.70.refs_3_), channel_id=1, source_target_pairs={{0,4},{4,8},{8,12},{12,16},{16,20},{20,24},{24,28},{28,0},{1,5},{5... | collective-permute-start | bytes 1769480 | tf_op jit(solution)/shard_map/ppermute | solution.py:443
  51.8 12.7 %collective-permute-start.15 = (f32[2,384,128]{2,1,0:T(8,128)S(1)}, f32[2,384,128]{2,1,0:T(8,128)S(1)}, u32[]{:S(2)}, u32[]{:S(2)}) collective-permute-start(f32[2,384,128]{2,1,0:T(8,128)S(1)} %get-tuple-element.75), channel_id=1, source_target_pairs={{0,3},{1,0},{2,1},{3,2},{4,7},{5,4},{6,5},{7,6},{8,11},{9,8},{10,9... | collective-permute-start | bytes 1179656 | tf_op jit(solution)/shard_map/ppermute | solution.py:443
  64.2 8.8 %collective-permute-start.19 = (f32[2,192,128]{2,1,0:T(8,128)S(1)}, f32[2,192,128]{2,1,0:T(8,128)S(1)}, u32[]{:S(2)}, u32[]{:S(2)}) collective-permute-start(f32[2,192,128]{2,1,0:T(8,128)S(1)} %get-tuple-element.83), channel_id=1, source_target_pairs={{0,3},{1,0},{2,1},{3,2},{4,7},{5,4},{6,5},{7,6},{8,11},{9,8},{10,9... | collective-permute-start | bytes 589832 | tf_op jit(solution)/shard_map/ppermute | solution.py:443
  67.1 5.9 %collective-permute-start.18 = (f32[2,192,128]{2,1,0:T(8,128)S(1)}, f32[2,192,128]{2,1,0:T(8,128)S(1)}, u32[]{:S(2)}, u32[]{:S(2)}) collective-permute-start(f32[2,192,128]{2,1,0:T(8,128)S(1)} %get-tuple-element.82), channel_id=1, source_target_pairs={{0,1},{1,2},{2,3},{3,0},{4,5},{5,6},{6,7},{7,4},{8,9},{9,10},{10,1... | collective-permute-start | bytes 589832 | tf_op jit(solution)/shard_map/ppermute | solution.py:443
  69.9 5.6 %collective-permute-start.16 = (f32[2,192,128]{2,1,0:T(8,128)S(1)}, f32[2,192,128]{2,1,0:T(8,128)S(1)}, u32[]{:S(2)}, u32[]{:S(2)}) collective-permute-start(f32[2,192,128]{2,1,0:T(8,128)S(1)} %get-tuple-element.76), channel_id=1, source_target_pairs={{0,1},{1,2},{2,3},{3,0},{4,5},{5,6},{6,7},{7,4},{8,9},{9,10},{10,1... | collective-permute-start | bytes 589832 | tf_op jit(solution)/shard_map/ppermute | solution.py:443
  69.9 8.1 %collective-permute-start.14 = (f32[2,192,128]{2,1,0:T(8,128)S(1)}, f32[2,192,128]{2,1,0:T(8,128)S(1)}, u32[]{:S(2)}, u32[]{:S(2)}) collective-permute-start(f32[2,192,128]{2,1,0:T(8,128)S(1)} %get-tuple-element.74), channel_id=1, source_target_pairs={{0,3},{1,0},{2,1},{3,2},{4,7},{5,4},{6,5},{7,6},{8,11},{9,8},{10,9... | collective-permute-start | bytes 589832 | tf_op jit(solution)/shard_map/ppermute | solution.py:443
  80.8 4.1 %collective-permute-start.23 = (f32[2,96,128]{2,1,0:T(8,128)S(1)}, f32[2,96,128]{2,1,0:T(8,128)S(1)}, u32[]{:S(2)}, u32[]{:S(2)}) collective-permute-start(f32[2,96,128]{2,1,0:T(8,128)S(1)} %get-tuple-element.95), channel_id=1, source_target_pairs={{0,1},{1,2},{2,3},{3,0},{4,5},{5,6},{6,7},{7,4},{8,9},{9,10},{10,1... | collective-permute-start | bytes 294920 | tf_op jit(solution)/shard_map/ppermute | solution.py:443
  80.8 4.9 %collective-permute-start.24 = (f32[2,96,128]{2,1,0:T(8,128)S(1)}, f32[2,96,128]{2,1,0:T(8,128)S(1)}, u32[]{:S(2)}, u32[]{:S(2)}) collective-permute-start(f32[2,96,128]{2,1,0:T(8,128)S(1)} %get-tuple-element.96), channel_id=1, source_target_pairs={{0,3},{1,0},{2,1},{3,2},{4,7},{5,4},{6,5},{7,6},{8,11},{9,8},{10,9... | collective-permute-start | bytes 294920 | tf_op jit(solution)/shard_map/ppermute | solution.py:443
  82.6 13.5 %collective-permute-start.22 = (f32[2,96,384]{2,1,0:T(8,128)S(1)}, f32[2,96,384]{2,1,0:T(8,128)S(1)}, u32[]{:S(2)}, u32[]{:S(2)}) collective-permute-start(f32[2,96,384]{2,1,0:T(8,128)S(1)} %get-tuple-element.84), channel_id=1, source_target_pairs={{0,4},{4,8},{8,12},{12,16},{16,20},{20,24},{24,28},{28,0},{1,5},{5... | collective-permute-start | bytes 884744 | tf_op jit(solution)/shard_map/ppermute | solution.py:443
  82.6 8.7 %collective-permute-start.20 = (f32[2,288,128]{2,1,0:T(8,128)S(1)}, f32[2,288,128]{2,1,0:T(8,128)S(1)}, u32[]{:S(2)}, u32[]{:S(2)}) collective-permute-start(f32[2,288,128]{2,1,0:T(8,128)S(1)} %get-tuple-element.91), channel_id=1, source_target_pairs={{0,1},{1,2},{2,3},{3,0},{4,5},{5,6},{6,7},{7,4},{8,9},{9,10},{10,1... | collective-permute-start | bytes 884744 | tf_op jit(solution)/shard_map/ppermute | solution.py:443
  83.0 8.8 %collective-permute-start.21 = (f32[2,288,128]{2,1,0:T(8,128)S(1)}, f32[2,288,128]{2,1,0:T(8,128)S(1)}, u32[]{:S(2)}, u32[]{:S(2)}) collective-permute-start(f32[2,288,128]{2,1,0:T(8,128)S(1)} %get-tuple-element.92), channel_id=1, source_target_pairs={{0,3},{1,0},{2,1},{3,2},{4,7},{5,4},{6,5},{7,6},{8,11},{9,8},{10,9... | collective-permute-start | bytes 884744 | tf_op jit(solution)/shard_map/ppermute | solution.py:443
  85.8 15.1 %collective-permute-start.25 = (f32[2,96,384]{2,1,0:T(8,128)S(1)}, f32[2,96,384]{2,1,0:T(8,128)S(1)}, u32[]{:S(2)}, u32[]{:S(2)}) collective-permute-start(f32[2,96,384]{2,1,0:T(8,128)S(1)} %totals.9), channel_id=1, source_target_pairs={{0,28},{4,0},{8,4},{12,8},{16,12},{20,16},{24,20},{28,24},{1,29},{... | collective-permute-start | bytes 884744 | tf_op jit(solution)/shard_map/ppermute | solution.py:443

commit v4 on v3

--- a/solution.py
+++ b/solution.py
@@ -58,9 +58,11 @@
         return lax.axis_index("row") > 0
     if side == "below":
         return lax.axis_index("row") < lax.axis_size("row") - 1
-    if side == "left":
-        return lax.axis_index("col") > 0
-    return lax.axis_index("col") < lax.axis_size("col") - 1
+    return (lax.axis_index("col") > 0) & (lax.axis_index("col") < lax.axis_size("col") - 1)
+
+
+def even_column():
+    return lax.axis_index("col") % 2 == 0
 
 
 def kept(value, *sides):
@@ -82,7 +84,7 @@
     for i in range(2):
         for j in range(2):
             row = off_ref[i, j, 0]
-            col = off_ref[i, j, 1] + (32 if j == 0 else 96)
+            col = (off_ref[i, j, 1] + (32 if j == 0 else 224)) % WIN
             for channel in range(2):
                 turned = pltpu.roll(probe_ref[channel], row, 0)
                 probes_ref[2 * i + j, channel] = pltpu.roll(turned, col, 1)
@@ -123,7 +125,7 @@
     return found
 
 
-def window_kernel(i, j, side, own, carried_own, carried_side, outs, *refs):
+def window_kernel(i, near, side, own, carried_own, carried_side, outs, *refs):
     off_ref, tab_ref, tw_ref, probes_ref, amps_ref = refs[:5]
     refs = refs[5:]
     side_refs, refs = refs[: len(side)], refs[len(side) :]
@@ -135,20 +137,26 @@
     g_in, h_in, m_in, g_out = halves[0:2], halves[2:4], halves[4:6], halves[6:8]
     wide, tall, tall_back, wide_back = refs[16:18], refs[18:20], refs[20:22], refs[22:24]
 
+    to_right = even_column() if near else jnp.logical_not(even_column())
+    j = jnp.where(to_right, 1, 0)
     number = 2 * i + j
     row_start = off_ref[i, j, 0]
-    col_start = off_ref[i, j, 1] + 32 + 64 * j
+    col_start = off_ref[i, j, 1]
     row_iota = lax.broadcasted_iota(jnp.int32, (HALF, HALF), 0)
     lane_iota = lax.broadcasted_iota(jnp.int32, (HALF, HALF), 1)
     in_row = row_iota >= row_start
+    sign = jnp.where(to_right, -1, 1)
+    in_first = (
+        sign * lane_iota >= jnp.where(to_right, 33 - col_start, 32 + col_start),
+        lane_iota >= jnp.where(to_right, 96 + col_start, col_start - 96),
+    )
     first_h, first_l, second_h, second_l = (tab_ref.at[n] for n in range(4))
-    strip_at = 0 if j == 0 else 3
+    groups = (("strip", 1), (0, 2))
 
     def place(group):
-        if group == strip_at:
+        if group == "strip":
             return True, slice(0, LANE)
-        at = (group - (1 if j == 0 else 0)) * LANE
-        return False, slice(at, at + LANE)
+        return False, slice(group * LANE, (group + 1) * LANE)
 
     def load(channel, first, group):
         is_strip, lanes = place(group)
@@ -183,14 +191,16 @@
     lo, hi = slice(0, HALF), slice(HALF, WIN)
     tw_c, tw_s = tw_ref[0], tw_ref[1]
     for cb in range(2):
-        in_col = lane_iota + cb * LANE >= col_start
+        in_col = in_first[cb]
+        first_group, second_group = groups[cb]
         field = []
         for rb in range(2):
             value = []
             for channel in range(2):
-                picked = jnp.where(in_col, load(channel, rb * HALF, cb), load(channel, rb * HALF, cb + 2))
+                at = rb * HALF
+                picked = jnp.where(in_col, load(channel, at, first_group), load(channel, at, second_group))
                 if rb == 0:
-                    other = jnp.where(in_col, load(channel, WIN, cb), load(channel, WIN, cb + 2))
+                    other = jnp.where(in_col, load(channel, WIN, first_group), load(channel, WIN, second_group))
                     picked = jnp.where(in_row, picked, other)
                 value.append(picked)
             box = (slice(rb * HALF, (rb + 1) * HALF), slice(cb * LANE, (cb + 1) * LANE))
@@ -246,7 +256,8 @@
         wide_back[p][...] = mul(second_h[...], high) + mul(second_h[...], low) + mul(second_l[...], high)
 
     for cb in range(2):
-        in_col = lane_iota + cb * LANE >= col_start
+        in_col = in_first[cb]
+        first_group, second_group = groups[cb]
         cols = slice(cb * LANE, (cb + 1) * LANE)
         u_re, u_im = wide_back[0][lo, cols], wide_back[0][hi, cols]
         v_re, v_im = wide_back[1][lo, cols], wide_back[1][hi, cols]
@@ -265,12 +276,12 @@
                 if rb == 0:
                     targets = [(0, jnp.where(in_row, grad, 0.0)), (WIN, jnp.where(in_row, 0.0, grad))]
                 for at, piece in targets:
-                    emit(channel, at, cb, jnp.where(in_col, piece, 0.0))
-                    emit(channel, at, cb + 2, jnp.where(in_col, 0.0, piece))
-
-
-def window(i, j, consts, side, own, carried_own, carried_side, outs):
-    border = ("left",) if j == 0 else ("right",)
+                    emit(channel, at, first_group, jnp.where(in_col, piece, 0.0))
+                    emit(channel, at, second_group, jnp.where(in_col, 0.0, piece))
+
+
+def window(i, near, consts, side, own, carried_own, carried_side, outs):
+    border = () if near else ("beside",)
     own_width = 3 * LANE
     shapes = []
     for _, rows in outs:
@@ -279,7 +290,7 @@
     kernel = functools.partial(
         window_kernel,
         i,
-        j,
+        near,
         tuple((p[1], p[2], p[3:] + border) for p in side),
         tuple((p[1], p[2], p[3:]) for p in own),
         tuple((at, array.shape[1]) for array, at in carried_own),
@@ -294,21 +305,31 @@
         scratch_shapes=[pltpu.VMEM((WIN, WIN), BF16)] * 16 + [pltpu.VMEM((WIN, WIN), F32)] * 8,
         cost_estimate=pl.CostEstimate(flops=1_600_000_000, bytes_accessed=5_000_000, transcendentals=0),
         compiler_params=pltpu.CompilerParams(vmem_limit_bytes=VMEM_LIMIT),
-        name=f"window_{i}{j}",
+        name=f"window_{i}" + ("a" if near else "b"),
     )(*consts, *operands)
 
 
-def variation_kernel(plan, *refs):
+def variation_kernel(near, own, far, *refs):
     reg = refs[-1]
     out_ref = refs[-2]
-    which = 0
-    for part, (lo, hi) in zip(plan, ((0, LANE), (LANE, 4 * LANE), (4 * LANE, 5 * LANE))):
-        row = 0
-        for first, rows, sides in part:
-            for channel in range(2):
-                reg[channel, row : row + rows, lo:hi] = kept(refs[which][channel, first : first + rows, :], *sides)
-            row += rows
-            which += 1
+    near_refs, refs = refs[: len(near)], refs[len(near) :]
+    own_refs, far_refs = refs[: len(own)], refs[len(own) : len(own) + len(far)]
+    even = even_column()
+
+    def block(pieces, sources, at, channel):
+        first, rows, sides = pieces[at]
+        return kept(sources[at][channel, first : first + rows, :], *sides)
+
+    row = 0
+    for n, (_, rows, _) in enumerate(own):
+        for channel in range(2):
+            span = slice(row, row + rows)
+            one = block(near, near_refs, n, channel)
+            other = block(far, far_refs, n, channel)
+            reg[channel, span, LANE : 4 * LANE] = block(own, own_refs, n, channel)
+            reg[channel, span, :LANE] = jnp.where(even, other, one)
+            reg[channel, span, 4 * LANE :] = jnp.where(even, one, other)
+        row += rows
 
     def chunk(step, _):
         base = pl.multiple_of(step * 32, 8)
@@ -332,14 +353,14 @@
     lax.fori_loop(0, 6, chunk, 0)
 
 
-def variation(left, own, right):
-    parts = (left, own, right)
-    plan = tuple(
-        tuple((p[1], p[2], p[3:] + border) for p in part) for part, border in zip(parts, (("left",), (), ("right",)))
-    )
+def variation(near, own, far):
+    parts = (near, own, far)
+    plan = [
+        tuple((p[1], p[2], p[3:] + border) for p in part) for part, border in zip(parts, ((), (), ("beside",)))
+    ]
     operands = [piece[0] for part in parts for piece in part]
     return pl.pallas_call(
-        functools.partial(variation_kernel, plan),
+        functools.partial(variation_kernel, *plan),
         out_shape=jax.ShapeDtypeStruct((2, 192, 3 * LANE), F32),
         in_specs=vmem(len(operands)),
         out_specs=pl.BlockSpec(memory_space=pltpu.VMEM),
@@ -350,8 +371,9 @@
     )(*operands)
 
 
-def totals_kernel(outs, extras, own_ref, left_ref, right_ref, *refs):
+def totals_kernel(outs, extras, own_ref, near_ref, far_ref, *refs):
     added, out_refs = refs[: len(extras)], refs[len(extras) :]
+    even = even_column()
     for (first, rows), out in zip(outs, out_refs):
         cuts = {first, first + rows}
         for at, count, _ in extras:
@@ -364,12 +386,14 @@
                     if at <= a and b <= at + count:
                         value = value + ref[channel, source + a - at : source + b - at, :]
                 to = slice(a - first, b - first)
-                out[channel, to, :LANE] = value[:, :LANE] + kept(left_ref[channel, a:b, :], "left")
+                one = near_ref[channel, a:b, :]
+                other = kept(far_ref[channel, a:b, :], "beside")
+                out[channel, to, :LANE] = value[:, :LANE] + jnp.where(even, other, one)
                 out[channel, to, LANE : 2 * LANE] = value[:, LANE : 2 * LANE]
-                out[channel, to, 2 * LANE :] = value[:, 2 * LANE :] + kept(right_ref[channel, a:b, :], "right")
-
-
-def totals(own, from_left, from_right, outs, extras):
+                out[channel, to, 2 * LANE :] = value[:, 2 * LANE :] + jnp.where(even, one, other)
+
+
+def totals(own, near, far, outs, extras):
     plan = tuple((at, rows, source) for _, source, at, rows in extras)
     return pl.pallas_call(
         functools.partial(totals_kernel, outs, plan),
@@ -379,11 +403,12 @@
         cost_estimate=pl.CostEstimate(flops=500_000, bytes_accessed=3_000_000, transcendentals=0),
         compiler_params=pltpu.CompilerParams(vmem_limit_bytes=VMEM_LIMIT),
         name="totals",
-    )(own, from_left, from_right, *[extra[0] for extra in extras])
+    )(own, near, far, *[extra[0] for extra in extras])
 
 
 def update_kernel(pieces, side, *refs):
-    new, left, right = refs[-3:]
+    new, near, far = refs[-3:]
+    even = even_column()
     ins = refs[:-3]
     row = 0
     for which, first, rows, grads, masked in pieces:
@@ -398,8 +423,8 @@
             if masked:
                 value = kept(value, side)
             new[channel, row : row + rows, :] = value
-            left[channel, row : row + rows, :] = value[:, :LANE]
-            right[channel, row : row + rows, :] = value[:, 2 * LANE :]
+            near[channel, row : row + rows, :] = jnp.where(even, value[:, 2 * LANE :], value[:, :LANE])
+            far[channel, row : row + rows, :] = jnp.where(even, value[:, :LANE], value[:, 2 * LANE :])
         row += rows
 
 
@@ -443,72 +468,90 @@
     return lax.ppermute(block, axis, [(n, (n + distance) % count) for n in range(count)])
 
 
-def rightward(block):
-    return moved(block, "col", 1)
-
-
-def leftward(block):
-    return moved(block, "col", -1)
+def to_near(block):
+    rows, cols = lax.axis_size("row"), lax.axis_size("col")
+    return lax.ppermute(block, ("row", "col"), [(r * cols + c, r * cols + (c ^ 1)) for r in range(rows) for c in range(cols)])
+
+
+def to_far(block):
+    rows, cols = lax.axis_size("row"), lax.axis_size("col")
+    step = 2 if rows % 4 == 0 else 1 if rows % 2 == 0 else 0
+    route = []
+    for r in range(rows):
+        for c in range(cols):
+            other = c - 1 if c % 2 == 0 else c + 1
+            inside = 0 <= other < cols
+            route.append((r * cols + c, r * cols + other if inside else (r ^ step) * cols + c))
+    return lax.ppermute(block, ("row", "col"), route)
+
+
+def edges(block):
+    width = block.shape[2]
+    low, high = block[:, :, :LANE], block[:, :, width - LANE :]
+    even = even_column()
+    return jnp.where(even, high, low), jnp.where(even, low, high)
 
 
 def on_device(table, twiddle, order, object_field, probe, amplitudes, offsets):
     tile = object_field.shape[1]
     last = tile - MARGIN
     band = 2 * MARGIN
-    edge = tile - LANE
     obj = object_field
     after = lax.optimization_barrier
 
     top = moved(obj[:, last:, :], "row", 1)
-    left, right = rightward(obj[:, :, edge:]), leftward(obj[:, :, :LANE])
+    near_strip, far_strip = edges(obj)
+    far, near = to_far(far_strip), to_near(near_strip)
     up_rows, top = after((obj[:, :MARGIN, :], top))
     bottom = moved(up_rows, "row", -1)
     probes, amps = prepare(offsets, probe, amplitudes, order)
     consts = (offsets, table, twiddle, probes, amps)
 
-    top_l, top_r = rightward(top[:, :, edge:]), leftward(top[:, :, :LANE])
+    near_strip, far_strip = edges(top)
+    top_b, top_a = to_far(far_strip), to_near(near_strip)
     own = [(top, 0, MARGIN, "above"), (obj, 0, last)]
     halves = ((0, band), (band, band))
-    lo_o, lo_l, mid_o, mid_l = window(
-        0, 0, consts, [(top_l, 0, MARGIN, "above"), (left, 0, last)], own, [], [], halves
-    )
-    in_r = leftward(lo_l)
-    lo_o, lo_r, mid_o, mid_r = window(
-        0, 1, consts, [(top_r, 0, MARGIN, "above"), (right, 0, last)], own, [(lo_o, 0), (mid_o, band)], [], halves
-    )
-    in_l = rightward(lo_r)
-    bottom, lo_r = after((bottom, lo_r))
-    bot_l, bot_r = rightward(bottom[:, :, edge:]), leftward(bottom[:, :, :LANE])
+    lo_o, lo_b, mid_o, mid_b = window(
+        0, False, consts, [(top_b, 0, MARGIN, "above"), (far, 0, last)], own, [], [], halves
+    )
+    in_b = to_far(lo_b)
+    lo_o, lo_a, mid_o, mid_a = window(
+        0, True, consts, [(top_a, 0, MARGIN, "above"), (near, 0, last)], own, [(lo_o, 0), (mid_o, band)], [], halves
+    )
+    in_a = to_near(lo_a)
+    bottom, lo_a = after((bottom, lo_a))
+    near_strip, far_strip = edges(bottom)
+    bot_b, bot_a = to_far(far_strip), to_near(near_strip)
     tv_top = variation(
-        [(top_l, 88, 8, "above"), (left, 0, 200)],
+        [(top_a, 88, 8, "above"), (near, 0, 200)],
         [(top, 88, 8, "above"), (obj, 0, 200)],
-        [(top_r, 88, 8, "above"), (right, 0, 200)],
-    )
-    (top_sum,) = totals(lo_o, in_l, in_r, ((0, band),), [(tv_top, 0, MARGIN, MARGIN)])
+        [(top_b, 88, 8, "above"), (far, 0, 200)],
+    )
+    (top_sum,) = totals(lo_o, in_a, in_b, ((0, band),), [(tv_top, 0, MARGIN, MARGIN)])
     from_below = moved(top_sum, "row", -1)
 
     mid_o, top_sum = after((mid_o, top_sum))
     own = [(obj, MARGIN, last), (bottom, 0, MARGIN, "below")]
     whole = ((0, tile),)
-    hi_o, hi_l = window(
-        1, 0, consts, [(left, MARGIN, last), (bot_l, 0, MARGIN, "below")], own, [(mid_o, 0)], [(mid_l, 0)], whole
-    )
-    in_r = leftward(hi_l)
-    hi_o, hi_r = window(
-        1, 1, consts, [(right, MARGIN, last), (bot_r, 0, MARGIN, "below")], own, [(hi_o, 0)], [(mid_r, 0)], whole
-    )
-    in_l = rightward(hi_r)
+    hi_o, hi_b = window(
+        1, False, consts, [(far, MARGIN, last), (bot_b, 0, MARGIN, "below")], own, [(mid_o, 0)], [(mid_b, 0)], whole
+    )
+    in_b = to_far(hi_b)
+    hi_o, hi_a = window(
+        1, True, consts, [(near, MARGIN, last), (bot_a, 0, MARGIN, "below")], own, [(hi_o, 0)], [(mid_a, 0)], whole
+    )
+    in_a = to_near(hi_a)
     tv_bottom = variation(
-        [(left, 184, 200), (bot_l, 0, 8, "below")],
+        [(near, 184, 200), (bot_a, 0, 8, "below")],
         [(obj, 184, 200), (bottom, 0, 8, "below")],
-        [(right, 184, 200), (bot_r, 0, 8, "below")],
+        [(far, 184, 200), (bot_b, 0, 8, "below")],
     )
     mid_sum, bot_sum = totals(
-        hi_o, in_l, in_r, halves, [(tv_top, MARGIN, 0, MARGIN), (tv_bottom, 0, MARGIN, band)]
+        hi_o, in_a, in_b, halves, [(tv_top, MARGIN, 0, MARGIN), (tv_bottom, 0, MARGIN, band)]
     )
     from_above = moved(bot_sum, "row", 1)
 
-    low, low_to_left, low_to_right = update(
+    low, near_strip, far_strip = update(
         (obj, bottom, mid_sum, bot_sum, from_below),
         (
             (0, MARGIN, band, ((2, 0),), False),
@@ -517,19 +560,19 @@
         ),
         "below",
     )
-    low_l, low_r = rightward(low_to_right), leftward(low_to_left)
+    low_b, low_a = to_far(far_strip), to_near(near_strip)
     own = [(low, 0, tile)]
-    mid_o, mid_l, hi_o, hi_l = window(1, 0, consts, [(low_l, 0, tile)], own, [], [], halves)
-    in_r = leftward(hi_l)
-    mid_o, mid_r, hi_o, hi_r = window(
-        1, 1, consts, [(low_r, 0, tile)], own, [(mid_o, 0), (hi_o, band)], [], halves
-    )
-    in_l = rightward(hi_r)
-    tv_bottom = variation([(low_l, 88, 208)], [(low, 88, 208)], [(low_r, 88, 208)])
-    low_sum, over = totals(hi_o, in_l, in_r, ((0, MARGIN), (MARGIN, MARGIN)), [(tv_bottom, MARGIN, 0, MARGIN)])
+    mid_o, mid_a, hi_o, hi_a = window(1, True, consts, [(low_a, 0, tile)], own, [], [], halves)
+    in_a = to_near(hi_a)
+    mid_o, mid_b, hi_o, hi_b = window(
+        1, False, consts, [(low_b, 0, tile)], own, [(mid_o, 0), (hi_o, band)], [], halves
+    )
+    in_b = to_far(hi_b)
+    tv_bottom = variation([(low_a, 88, 208)], [(low, 88, 208)], [(low_b, 88, 208)])
+    low_sum, over = totals(hi_o, in_a, in_b, ((0, MARGIN), (MARGIN, MARGIN)), [(tv_bottom, MARGIN, 0, MARGIN)])
     last_above = moved(over, "row", 1)
 
-    up, up_to_left, up_to_right = update(
+    up, near_strip, far_strip = update(
         (top, obj, top_sum, from_above),
         (
             (0, 0, MARGIN, ((2, 0), (3, 0)), True),
@@ -537,25 +580,25 @@
         ),
         "above",
     )
-    up_l, up_r = rightward(up_to_right), leftward(up_to_left)
+    up_b, up_a = to_far(far_strip), to_near(near_strip)
     mid_o, over = after((mid_o, over))
     own = [(up, 0, band), (low, 0, band)]
     cut = ((0, MARGIN), (MARGIN, last))
-    over_o, over_l, lo_o, lo_l = window(
-        0, 0, consts, [(up_l, 0, band), (low_l, 0, band)], own, [(mid_o, band)], [(mid_l, band)], cut
-    )
-    over_r, in_r = leftward(over_l), leftward(lo_l)
-    over_o, over_rr, lo_o, lo_r = window(
-        0, 1, consts, [(up_r, 0, band), (low_r, 0, band)], own, [(over_o, 0), (lo_o, MARGIN)], [(mid_r, band)], cut
-    )
-    over_l = rightward(over_rr)
-    (over,) = totals(over_o, over_l, over_r, ((0, MARGIN),), [])
+    over_o, over_a, lo_o, lo_a = window(
+        0, True, consts, [(up_a, 0, band), (low_a, 0, band)], own, [(mid_o, band)], [(mid_a, band)], cut
+    )
+    over_a, in_a = to_near(over_a), to_near(lo_a)
+    over_o, over_b, lo_o, lo_b = window(
+        0, False, consts, [(up_b, 0, band), (low_b, 0, band)], own, [(over_o, 0), (lo_o, MARGIN)], [(mid_b, band)], cut
+    )
+    over_b = to_far(over_b)
+    (over,) = totals(over_o, over_a, over_b, ((0, MARGIN),), [])
     last_below = moved(over, "row", -1)
-    in_l = rightward(lo_r)
+    in_b = to_far(lo_b)
     tv_top = variation(
-        [(up_l, 88, 104), (low_l, 0, 104)], [(up, 88, 104), (low, 0, 104)], [(up_r, 88, 104), (low_r, 0, 104)]
-    )
-    (mid_sum,) = totals(lo_o, in_l, in_r, ((0, last),), [(tv_top, 0, 0, band), (tv_bottom, 0, band, MARGIN)])
+        [(up_a, 88, 104), (low_a, 0, 104)], [(up, 88, 104), (low, 0, 104)], [(up_b, 88, 104), (low_b, 0, 104)]
+    )
+    (mid_sum,) = totals(lo_o, in_a, in_b, ((0, last),), [(tv_top, 0, 0, band), (tv_bottom, 0, band, MARGIN)])
     return finish(up, low, mid_sum, low_sum, last_above, last_below)
 
 

time: 102 us -> 108 us (1.059)
  starting transfers between devices: 28.1 us -> 37.7 us
  waiting for transfers between devices: 42 us -> 37.1 us
    ppermute x26 -> x6, waiting for transfers between devices: 42 us -> 21.8 us  [moved(): lax.ppermute(block, axis, [(n, (n + distance) % count) for n in range(cou...]
    ppermute x0 -> x20, waiting for transfers between devices: none -> 15.3 us  [the longest x10 15 us: to_far(): return lax.ppermute(block, ('row', 'col'), route)]
    ppermute x0 -> x20, starting transfers between devices: none -> 14.3 us  [the longest x10 9.19 us: to_far(): return lax.ppermute(block, ('row', 'col'), route)]
    ppermute x26 -> x6, starting transfers between devices: 28.1 us -> 23.4 us  [moved(): lax.ppermute(block, axis, [(n, (n + distance) % count) for n in range(cou...]
  transfers between devices with their start and end apart: 26 -> 26, of which waited for: 13 -> 10; matrix products, arithmetic and copies ran while one was open for 0% -> 0% of each run, Pallas kernels for 26% -> 24%
where the time goes in v4:
time: 108 us; the launch traced here: 107 us
  starting transfers between devices  37.7 us (35%)
  waiting for transfers between devices  37.1 us (34%)
  Pallas kernels  30.3 us (28%)
  local copies, waits for them, and re-layouts  1.93 us (2%)
    ppermute x6, starting transfers between devices, moved(): lax.ppermute(block, axis, [(n, (n + distance) % count) for n in range(cou...  23.4 us
    ppermute x6, waiting for transfers between devices, moved(): lax.ppermute(block, axis, [(n, (n + distance) % count) for n in range(cou...  21.8 us
    pallas_call x8, Pallas kernels, window(): pl.pallas_call(kernel, out_shape=tuple(shapes), in_specs=[pl.BlockSpec(me...  21.1 us
    ppermute x10, waiting for transfers between devices, to_far(): return lax.ppermute(block, ('row', 'col'), route)  15 us
    ppermute x10, starting transfers between devices, to_far(): return lax.ppermute(block, ('row', 'col'), route)  9.19 us
    pallas_call x4, Pallas kernels, variation(): pl.pallas_call(functools.partial(variation_kernel, *plan), out_shape=jax....  5.33 us
    ppermute x10, starting transfers between devices, to_near(): lax.ppermute(block, ('row', 'col'), [(r * cols + c, r * cols + (c ^ 1)) f...  5.07 us
  transfers between devices with their start and end apart: 26, of which 10 were waited for; matrix products, arithmetic and copies ran while one was open for 0% of the time, Pallas kernels for 24%

profile of v4, /device:TPU:0, one launch (start us, length us, event | category | flops | bytes accessed | tf_op | source)
XLA Modules:
  0.0 107.5 jit_solution(13414709160478996146)
XLA Ops:
  0.0 1.9 %fusion = (f32[2,96,384]{2,1,0:T(8,128)}, f32[2,96,384]{2,1,0:T(8,128)S(1)}) fusion(f32[2,384,384]{2,1,0:T(8,128)} %refs_0_.13), kind=kLoop, calls=%fused_computation.6 | loop fusion | bytes 1179648 | tf_op jit(solution)/shard_map/slice | solution.py:502
  1.9 3.0 %collective-permute-start = (f32[2,96,384]{2,1,0:T(8,128)}, f32[2,96,384]{2,1,0:T(8,128)S(1)}, u32[]{:S(2)}, u32[]{:S(2)}) collective-permute-start(f32[2,96,384]{2,1,0:T(8,128)} %get-tuple-element.99), channel_id=1, source_target_pairs={{0,4},{4,8},{8,12},{12,16},{16,20},{20,24},{24,28},{28,0},{1,5},{5... | collective-permute-start | bytes 884744 | tf_op jit(solution)/shard_map/ppermute | solution.py:468
  5.0 1.6 %collective-permute-start.4 = (f32[2,384,128]{2,1,0:T(8,128)S(1)}, f32[2,384,128]{2,1,0:T(8,128)S(1)}, u32[]{:S(2)}, u32[]{:S(2)}) collective-permute-start(f32[2,384,128]{2,1,0:T(8,128)S(1)} %get-tuple-element.97), channel_id=1, source_target_pairs={{0,8},{1,2},{2,1},{3,11},{4,12},{5,6},{6,5},{7,15},{8,0},{9,10},{1... | collective-permute-start | bytes 1179656 | tf_op jit(solution)/shard_map/ppermute | solution.py:485
  6.7 8.6 %collective-permute-done.refs_7_.refs_2_.refs_0_ = f32[2,96,384]{2,1,0:T(8,128)S(1)} collective-permute-done((f32[2,96,384]{2,1,0:T(8,128)}, f32[2,96,384]{2,1,0:T(8,128)S(1)}, u32[]{:S(2)}, u32[]{:S(2)}) %collective-permute-start) | collective-permute-done | bytes 294944 | tf_op jit(solution)/shard_map/ppermute | solution.py:468
  15.4 1.8 %prepare.1 = (f32[4,2,256,256]{3,2,1,0:T(8,128)S(1)}, f32[4,512,128]{2,1,0:T(8,128)S(1)}) custom-call(s32[2,2,2]{2,1,0:T(2,128)S(1)} %copy-done.6, f32[2,256,256]{2,1,0:T(8,128)S(1)} %copy-done.4, f32[512,512]{1,0:T(8,128)S(1)} %copy-done.3, bf16[256,256]{1,0:T(8,128)(2,1)S(1)} %copy-done.5), custom_call_target="tpu_custom_call" | custom-call | flops 400000000 | bytes 6000000 | tf_op jit(solution)/shard_map/prepare/pallas_call | solution.py:103
  17.2 2.6 %collective-permute-start.1 = (f32[2,96,128]{2,1,0:T(8,128)S(1)}, f32[2,96,128]{2,1,0:T(8,128)S(1)}, u32[]{:S(2)}, u32[]{:S(2)}) collective-permute-start(f32[2,96,128]{2,1,0:T(8,128)S(1)} %get-tuple-element.104), channel_id=1, source_target_pairs={{0,1},{1,0},{2,3},{3,2},{4,5},{5,4},{6,7},{7,6},{8,9},{9,8},{10,11... | collective-permute-start | bytes 294920 | tf_op jit(solution)/shard_map/ppermute | solution.py:473
  19.8 0.7 collective-permute-start.7
  20.5 2.6 %window_0b.2 = (f32[2,192,384]{2,1,0:T(8,128)S(1)}, f32[2,192,128]{2,1,0:T(8,128)S(1)}, f32[2,192,384]{2,1,0:T(8,128)S(1)}, f32[2,192,128]{2,1,0:T(8,128)S(1)}) custom-call(s32[2,2,2]{2,1,0:T(2,128)S(1)} %copy-done.6, bf16[4,256,256]{2,1,0:T(8,128)(2,1)S(1)} %copy-done.1, f32[4,128,128]{2,1,0:T(8,128)S(1)} %copy-done.2, ...), custom_call_target="tpu_custom_call" | custom-call | flops 1600000000 | bytes 5000000 | tf_op jit(solution)/shard_map/window_0b/pallas_call | solution.py:300
  23.3 2.7 %window_0a.2 = (f32[2,192,384]{2,1,0:T(8,128)S(1)}, f32[2,192,128]{2,1,0:T(8,128)S(1)}, f32[2,192,384]{2,1,0:T(8,128)S(1)}, f32[2,192,128]{2,1,0:T(8,128)S(1)}) custom-call(s32[2,2,2]{2,1,0:T(2,128)S(1)} %copy-done.6, bf16[4,256,256]{2,1,0:T(8,128)(2,1)S(1)} %copy-done.1, f32[4,128,128]{2,1,0:T(8,128)S(1)} %copy-done.2, ...), custom_call_target="tpu_custom_call" | custom-call | flops 1600000000 | bytes 5000000 | tf_op jit(solution)/shard_map/window_0a/pallas_call | solution.py:300
  25.9 1.5 %collective-permute-start.5 = (f32[2,192,128]{2,1,0:T(8,128)S(1)}, f32[2,192,128]{2,1,0:T(8,128)S(1)}, u32[]{:S(2)}, u32[]{:S(2)}) collective-permute-start(f32[2,192,128]{2,1,0:T(8,128)S(1)} %get-tuple-element.58), channel_id=1, source_target_pairs={{0,1},{1,0},{2,3},{3,2},{4,5},{5,4},{6,7},{7,6},{8,9},{9,8},{10,11... | collective-permute-start | bytes 589832 | tf_op jit(solution)/shard_map/ppermute | solution.py:473
  27.5 1.3 %collective-permute-done.7.refs_8_.refs_3_.refs_1_ = f32[2,96,384]{2,1,0:T(8,128)S(1)} collective-permute-done((f32[2,96,384]{2,1,0:T(8,128)S(1)}, f32[2,96,384]{2,1,0:T(8,128)S(1)}, u32[]{:S(2)}, u32[]{:S(2)}) %collective-permute-start.7) | collective-permute-done | bytes 294944 | tf_op jit(solution)/shard_map/ppermute | solution.py:468
  28.9 1.3 %variation.4.refs_0_ = f32[2,192,384]{2,1,0:T(8,128)S(1)} custom-call(f32[2,96,128]{2,1,0:T(8,128)S(1)} %collective-permute-done.1.refs_5_.refs_0_, f32[2,384,128]{2,1,0:T(8,128)S(1)} %collective-permute-done.2.refs_6_.refs_1_.refs_5_.refs_0_, f32[2,96,384]{2,1,0:T(8,128)S(1)} %collective-permute-done.refs_7_.refs_2_.refs_0_, f32[2,384,384]{2,1,0:T(8,128)S(1)} %copy-done, ...), custom_call_target="tpu_custom_call" | custom-call | flops 200000000 | bytes 5000000 | tf_op jit(solution)/shard_map/variation/pallas_call | solution.py:362
  30.2 0.5 collective-permute-start.8
  30.9 4.0 %collective-permute-start.13 = (f32[2,192,384]{2,1,0:T(8,128)S(1)}, f32[2,192,384]{2,1,0:T(8,128)S(1)}, u32[]{:S(2)}, u32[]{:S(2)}) collective-permute-start(f32[2,192,384]{2,1,0:T(8,128)S(1)} %totals.5.refs_2_), channel_id=1, source_target_pairs={{0,28},{4,0},{8,4},{12,8},{16,12},{20,16},{24,20},{28,24},{1,29},{... | collective-permute-start | bytes 1769480 | tf_op jit(solution)/shard_map/ppermute | solution.py:468
  34.8 2.6 %window_1b.2 = (f32[2,384,384]{2,1,0:T(8,128)S(1)}, f32[2,384,128]{2,1,0:T(8,128)S(1)}) custom-call(s32[2,2,2]{2,1,0:T(2,128)S(1)} %copy-done.6, bf16[4,256,256]{2,1,0:T(8,128)(2,1)S(1)} %copy-done.1, f32[4,128,128]{2,1,0:T(8,128)S(1)} %copy-done.2, f32[4,2,256,256]{3,2,1,0:T(8,128)S(1)} %get-tuple-element.52.refs_3_, ...), custom_call_target="tpu_custom_call" | custom-call | flops 1600000000 | bytes 5000000 | tf_op jit(solution)/shard_map/window_1b/pallas_call | solution.py:300
  37.5 2.7 %window_1a.2 = (f32[2,384,384]{2,1,0:T(8,128)S(1)}, f32[2,384,128]{2,1,0:T(8,128)S(1)}) custom-call(s32[2,2,2]{2,1,0:T(2,128)S(1)} %copy-done.6, bf16[4,256,256]{2,1,0:T(8,128)(2,1)S(1)} %copy-done.1, f32[4,128,128]{2,1,0:T(8,128)S(1)} %copy-done.2, f32[4,2,256,256]{3,2,1,0:T(8,128)S(1)} %get-tuple-element.52.refs_3_, ...), custom_call_target="tpu_custom_call" | custom-call | flops 1600000000 | bytes 5000000 | tf_op jit(solution)/shard_map/window_1a/pallas_call | solution.py:300
  40.2 0.1 collective-permute-start.10
  40.3 1.3 %variation.5.refs_1_ = f32[2,192,384]{2,1,0:T(8,128)S(1)} custom-call(f32[2,384,128]{2,1,0:T(8,128)S(1)} %collective-permute-done.2.refs_6_.refs_1_.refs_5_.refs_0_, f32[2,96,128]{2,1,0:T(8,128)S(1)} %collective-permute-done.8.refs_6_.refs_1_, f32[2,384,384]{2,1,0:T(8,128)S(1)} %copy-done, f32[2,96,384]{2,1,0:T(8,128)S(1)} %collective-permute-done.7.refs_8_.refs_3_.refs_1_, ...), custom_call_target="tpu_custom_call" | custom-call | flops 200000000 | bytes 5000000 | tf_op jit(solution)/shard_map/variation/pallas_call | solution.py:362
  41.7 0.3 collective-permute-done.10.near_ref
  42.0 9.9 %collective-permute-done.11.far_ref = f32[2,384,128]{2,1,0:T(8,128)S(1)} collective-permute-done((f32[2,384,128]{2,1,0:T(8,128)S(1)}, f32[2,384,128]{2,1,0:T(8,128)S(1)}, u32[]{:S(2)}, u32[]{:S(2)}) %collective-permute-start.11) | collective-permute-done | bytes 393248 | tf_op jit(solution)/shard_map/ppermute | solution.py:485
  51.8 0.2 totals.6
  52.0 0.2 update.3
  52.2 0.1 collective-permute-start.17
  52.3 0.2 collective-permute-start.12
  52.6 2.5 %collective-permute-start.15 = (f32[2,384,128]{2,1,0:T(8,128)S(1)}, f32[2,384,128]{2,1,0:T(8,128)S(1)}, u32[]{:S(2)}, u32[]{:S(2)}) collective-permute-start(f32[2,384,128]{2,1,0:T(8,128)S(1)} %get-tuple-element.75), channel_id=1, source_target_pairs={{0,8},{1,2},{2,1},{3,11},{4,12},{5,6},{6,5},{7,15},{8,0},{9,10},{1... | collective-permute-start | bytes 1179656 | tf_op jit(solution)/shard_map/ppermute | solution.py:485
  55.1 2.6 %window_1a.3 = (f32[2,192,384]{2,1,0:T(8,128)S(1)}, f32[2,192,128]{2,1,0:T(8,128)S(1)}, f32[2,192,384]{2,1,0:T(8,128)S(1)}, f32[2,192,128]{2,1,0:T(8,128)S(1)}) custom-call(s32[2,2,2]{2,1,0:T(2,128)S(1)} %copy-done.6, bf16[4,256,256]{2,1,0:T(8,128)(2,1)S(1)} %copy-done.1, f32[4,128,128]{2,1,0:T(8,128)S(1)} %copy-done.2, ...), custom_call_target="tpu_custom_call" | custom-call | flops 1600000000 | bytes 5000000 | tf_op jit(solution)/shard_map/window_1a/pallas_call | solution.py:300
  57.8 3.1 %collective-permute-done.15.refs_5_.refs_2_.refs_6_ = f32[2,384,128]{2,1,0:T(8,128)S(1)} collective-permute-done((f32[2,384,128]{2,1,0:T(8,128)S(1)}, f32[2,384,128]{2,1,0:T(8,128)S(1)}, u32[]{:S(2)}, u32[]{:S(2)}) %collective-permute-start.15) | collective-permute-done | bytes 393248 | tf_op jit(solution)/shard_map/ppermute | solution.py:485
  60.9 2.6 %window_1b.3 = (f32[2,192,384]{2,1,0:T(8,128)S(1)}, f32[2,192,128]{2,1,0:T(8,128)S(1)}, f32[2,192,384]{2,1,0:T(8,128)S(1)}, f32[2,192,128]{2,1,0:T(8,128)S(1)}) custom-call(s32[2,2,2]{2,1,0:T(2,128)S(1)} %copy-done.6, bf16[4,256,256]{2,1,0:T(8,128)(2,1)S(1)} %copy-done.1, f32[4,128,128]{2,1,0:T(8,128)S(1)} %copy-done.2, ...), custom_call_target="tpu_custom_call" | custom-call | flops 1600000000 | bytes 5000000 | tf_op jit(solution)/shard_map/window_1b/pallas_call | solution.py:300
  63.5 2.1 %collective-permute-start.19 = (f32[2,192,128]{2,1,0:T(8,128)S(1)}, f32[2,192,128]{2,1,0:T(8,128)S(1)}, u32[]{:S(2)}, u32[]{:S(2)}) collective-permute-start(f32[2,192,128]{2,1,0:T(8,128)S(1)} %get-tuple-element.83), channel_id=1, source_target_pairs={{0,8},{1,2},{2,1},{3,11},{4,12},{5,6},{6,5},{7,15},{8,0},{9,10},{1... | collective-permute-start | bytes 589832 | tf_op jit(solution)/shard_map/ppermute | solution.py:485
  65.6 5.2 %collective-permute-done.12.refs_3_ = f32[2,192,384]{2,1,0:T(8,128)S(1)} collective-permute-done((f32[2,192,384]{2,1,0:T(8,128)S(1)}, f32[2,192,384]{2,1,0:T(8,128)S(1)}, u32[]{:S(2)}, u32[]{:S(2)}) %collective-permute-start.12) | collective-permute-done | bytes 589856 | tf_op jit(solution)/shard_map/ppermute | solution.py:468
  70.8 0.1 update.2
  71.0 0.1 collective-permute-start.16
  71.0 0.7 collective-permute-start.14
  71.7 1.3 %variation.6.refs_0_.refs_1_ = f32[2,192,384]{2,1,0:T(8,128)S(1)} custom-call(f32[2,384,128]{2,1,0:T(8,128)S(1)} %collective-permute-done.17.refs_5_.refs_0_.refs_6_.refs_1_, f32[2,384,384]{2,1,0:T(8,128)S(1)} %get-tuple-element.73.refs_6_.refs_1_.refs_8_.refs_3_.bottom_ref, f32[2,384,128]{2,1,0:T(8,128)S(1)} %collective-permute-done.15.refs_5_.refs_2_.refs_6_), custom_call_target="tpu_custom_call" | custom-call | flops 200000000 | bytes 5000000 | tf_op jit(solution)/shard_map/variation/pallas_call | solution.py:362
  73.1 0.1 totals.7
  73.1 2.6 %window_0a.3 = (f32[2,96,384]{2,1,0:T(8,128)S(1)}, f32[2,96,128]{2,1,0:T(8,128)S(1)}, f32[2,288,384]{2,1,0:T(8,128)S(1)}, f32[2,288,128]{2,1,0:T(8,128)S(1)}) custom-call(s32[2,2,2]{2,1,0:T(2,128)S(1)} %copy-done.6, bf16[4,256,256]{2,1,0:T(8,128)(2,1)S(1)} %copy-done.1, f32[4,128,128]{2,1,0:T(8,128)S(1)} %copy-done.2, ...), custom_call_target="tpu_custom_call" | custom-call | flops 1600000000 | bytes 5000000 | tf_op jit(solution)/shard_map/window_0a/pallas_call | solution.py:300
  75.8 1.0 collective-permute-done.14.refs_5_.refs_4_
  76.8 2.6 %window_0b.3 = (f32[2,96,384]{2,1,0:T(8,128)S(1)}, f32[2,96,128]{2,1,0:T(8,128)S(1)}, f32[2,288,384]{2,1,0:T(8,128)S(1)}, f32[2,288,128]{2,1,0:T(8,128)S(1)}) custom-call(s32[2,2,2]{2,1,0:T(2,128)S(1)} %copy-done.6, bf16[4,256,256]{2,1,0:T(8,128)(2,1)S(1)} %copy-done.1, f32[4,128,128]{2,1,0:T(8,128)S(1)} %copy-done.2, ...), custom_call_target="tpu_custom_call" | custom-call | flops 1600000000 | bytes 5000000 | tf_op jit(solution)/shard_map/window_0b/pallas_call | solution.py:300
  79.4 0.7 collective-permute-start.24
  80.1 9.9 %collective-permute-start.22 = (f32[2,96,384]{2,1,0:T(8,128)S(1)}, f32[2,96,384]{2,1,0:T(8,128)S(1)}, u32[]{:S(2)}, u32[]{:S(2)}) collective-permute-start(f32[2,96,384]{2,1,0:T(8,128)S(1)} %get-tuple-element.84), channel_id=1, source_target_pairs={{0,4},{4,8},{8,12},{12,16},{16,20},{20,24},{24,28},{28,0},{1,5},{5... | collective-permute-start | bytes 884744 | tf_op jit(solution)/shard_map/ppermute | solution.py:468
  90.1 1.3 %collective-permute-start.21 = (f32[2,288,128]{2,1,0:T(8,128)S(1)}, f32[2,288,128]{2,1,0:T(8,128)S(1)}, u32[]{:S(2)}, u32[]{:S(2)}) collective-permute-start(f32[2,288,128]{2,1,0:T(8,128)S(1)} %get-tuple-element.92), channel_id=1, source_target_pairs={{0,8},{1,2},{2,1},{3,11},{4,12},{5,6},{6,5},{7,15},{8,0},{9,10},{1... | collective-permute-start | bytes 884744 | tf_op jit(solution)/shard_map/ppermute | solution.py:485
  91.5 5.6 %collective-permute-start.25 = (f32[2,96,384]{2,1,0:T(8,128)S(1)}, f32[2,96,384]{2,1,0:T(8,128)S(1)}, u32[]{:S(2)}, u32[]{:S(2)}) collective-permute-start(f32[2,96,384]{2,1,0:T(8,128)S(1)} %totals.9), channel_id=1, source_target_pairs={{0,28},{4,0},{8,4},{12,8},{16,12},{20,16},{24,20},{28,24},{1,29},{... | collective-permute-start | bytes 884744 | tf_op jit(solution)/shard_map/ppermute | solution.py:468
  97.1 1.3 %variation.7.refs_0_ = f32[2,192,384]{2,1,0:T(8,128)S(1)} custom-call(f32[2,192,128]{2,1,0:T(8,128)S(1)} %collective-permute-done.16.refs_5_.refs_0_, f32[2,384,128]{2,1,0:T(8,128)S(1)} %collective-permute-done.17.refs_5_.refs_0_.refs_6_.refs_1_, f32[2,192,384]{2,1,0:T(8,128)S(1)} %get-tuple-element.71.refs_7_.refs_2_.top_ref, ...), custom_call_target="tpu_custom_call" | custom-call | flops 200000000 | bytes 5000000 | tf_op jit(solution)/shard_map/variation/pallas_call | solution.py:362
  98.4 1.1 %collective-permute-done.21.far_ref = f32[2,288,128]{2,1,0:T(8,128)S(1)} collective-permute-done((f32[2,288,128]{2,1,0:T(8,128)S(1)}, f32[2,288,128]{2,1,0:T(8,128)S(1)}, u32[]{:S(2)}, u32[]{:S(2)}) %collective-permute-start.21) | collective-permute-done | bytes 294944 | tf_op jit(solution)/shard_map/ppermute | solution.py:485
  99.5 0.1 totals.8.mid_ref
  99.7 3.7 %collective-permute-done.22.above_ref = f32[2,96,384]{2,1,0:T(8,128)S(1)} collective-permute-done((f32[2,96,384]{2,1,0:T(8,128)S(1)}, f32[2,96,384]{2,1,0:T(8,128)S(1)}, u32[]{:S(2)}, u32[]{:S(2)}) %collective-permute-start.22) | collective-permute-done | bytes 294944 | tf_op jit(solution)/shard_map/ppermute | solution.py:468
  103.3 2.9 %collective-permute-done.25.below_ref = f32[2,96,384]{2,1,0:T(8,128)S(1)} collective-permute-done((f32[2,96,384]{2,1,0:T(8,128)S(1)}, f32[2,96,384]{2,1,0:T(8,128)S(1)}, u32[]{:S(2)}, u32[]{:S(2)}) %collective-permute-start.25) | collective-permute-done | bytes 294944 | tf_op jit(solution)/shard_map/ppermute | solution.py:468
  106.3 1.2 %finish.1 = f32[2,384,384]{2,1,0:T(8,128)} custom-call(f32[2,192,384]{2,1,0:T(8,128)S(1)} %get-tuple-element.71.refs_7_.refs_2_.top_ref, f32[2,384,384]{2,1,0:T(8,128)S(1)} %get-tuple-element.73.refs_6_.refs_1_.refs_8_.refs_3_.bottom_ref, f32[2,288,384]{2,1,0:T(8,128)S(1)} %totals.8.mid_ref, f32[2,96,384]{2,1,0:T(8,128)S(1)} %get-tuple-element.93.low_ref, ...), custom_call_target="tpu_custom_call" | custom-call | flops 1000000 | bytes 4000000 | tf_op jit(solution)/shard_map/finish/pallas_call | solution.py:455
  (43 shorter events, 0.7 us)
Async XLA Ops:
  0.0 4.9 %copy-start = (f32[2,384,384]{2,1,0:T(8,128)S(1)}, f32[2,384,384]{2,1,0:T(8,128)}, u32[]{:S(2)}) copy-start(f32[2,384,384]{2,1,0:T(8,128)} %refs_0_.13) | copy-start | bytes 3538948
  1.9 13.5 %copy-start.3 = (f32[512,512]{1,0:T(8,128)S(1)}, f32[512,512]{1,0:T(8,128)}, u32[]{:S(2)}) copy-start(f32[512,512]{1,0:T(8,128)} %amp_ref.1) | copy-start | bytes 3145732
  1.9 13.5 %copy-start.4 = (f32[2,256,256]{2,1,0:T(8,128)S(1)}, f32[2,256,256]{2,1,0:T(8,128)}, u32[]{:S(2)}) copy-start(f32[2,256,256]{2,1,0:T(8,128)} %probe_ref.1) | copy-start | bytes 1572868
  1.9 13.5 %copy-start.5 = (bf16[256,256]{1,0:T(8,128)(2,1)S(1)}, bf16[256,256]{1,0:T(8,128)(2,1)}, u32[]{:S(2)}) copy-start(bf16[256,256]{1,0:T(8,128)(2,1)} %constant.30.clone.order_ref) | copy-start | bytes 393220
  1.9 13.5 %copy-start.6 = (s32[2,2,2]{2,1,0:T(2,128)S(1)}, s32[2,2,2]{2,1,0:T(2,128)}, u32[]{:S(2)}) copy-start(s32[2,2,2]{2,1,0:T(2,128)} %refs_0_.17) | copy-start | bytes 100
  1.9 13.4 %collective-permute-start = (f32[2,96,384]{2,1,0:T(8,128)}, f32[2,96,384]{2,1,0:T(8,128)S(1)}, u32[]{:S(2)}, u32[]{:S(2)}) collective-permute-start(f32[2,96,384]{2,1,0:T(8,128)} %get-tuple-element.99), channel_id=1, source_target_pairs={{0,4},{4,8},{8,12},{12,16},{16,20},{20,24},{24,28},{28,0},{1,5},{5... | collective-permute-start | bytes 884744 | tf_op jit(solution)/shard_map/ppermute | solution.py:468
  5.0 15.5 %copy-start.1 = (bf16[4,256,256]{2,1,0:T(8,128)(2,1)S(1)}, bf16[4,256,256]{2,1,0:T(8,128)(2,1)}, u32[]{:S(2)}) copy-start(bf16[4,256,256]{2,1,0:T(8,128)(2,1)} %constant.28.clone.refs_1_) | copy-start | bytes 1572868
  5.0 15.5 %copy-start.2 = (f32[4,128,128]{2,1,0:T(8,128)S(1)}, f32[4,128,128]{2,1,0:T(8,128)}, u32[]{:S(2)}) copy-start(f32[4,128,128]{2,1,0:T(8,128)} %constant.29.clone.refs_2_) | copy-start | bytes 786436
  5.0 15.5 %collective-permute-start.4 = (f32[2,384,128]{2,1,0:T(8,128)S(1)}, f32[2,384,128]{2,1,0:T(8,128)S(1)}, u32[]{:S(2)}, u32[]{:S(2)}) collective-permute-start(f32[2,384,128]{2,1,0:T(8,128)S(1)} %get-tuple-element.97), channel_id=1, source_target_pairs={{0,8},{1,2},{2,1},{3,11},{4,12},{5,6},{6,5},{7,15},{8,0},{9,10},{1... | collective-permute-start | bytes 1179656 | tf_op jit(solution)/shard_map/ppermute | solution.py:485
  6.7 16.6 %collective-permute-start.2 = (f32[2,384,128]{2,1,0:T(8,128)S(1)}, f32[2,384,128]{2,1,0:T(8,128)S(1)}, u32[]{:S(2)}, u32[]{:S(2)}) collective-permute-start(f32[2,384,128]{2,1,0:T(8,128)S(1)} %get-tuple-element.98), channel_id=1, source_target_pairs={{0,1},{1,0},{2,3},{3,2},{4,5},{5,4},{6,7},{7,6},{8,9},{9,8},{10,11... | collective-permute-start | bytes 1179656 | tf_op jit(solution)/shard_map/ppermute | solution.py:473
  15.3 5.2 %collective-permute-start.3 = (f32[2,96,128]{2,1,0:T(8,128)S(1)}, f32[2,96,128]{2,1,0:T(8,128)S(1)}, u32[]{:S(2)}, u32[]{:S(2)}) collective-permute-start(f32[2,96,128]{2,1,0:T(8,128)S(1)} %get-tuple-element.103), channel_id=1, source_target_pairs={{0,8},{1,2},{2,1},{3,11},{4,12},{5,6},{6,5},{7,15},{8,0},{9,10},{1... | collective-permute-start | bytes 294920 | tf_op jit(solution)/shard_map/ppermute | solution.py:485
  17.2 6.0 %collective-permute-start.1 = (f32[2,96,128]{2,1,0:T(8,128)S(1)}, f32[2,96,128]{2,1,0:T(8,128)S(1)}, u32[]{:S(2)}, u32[]{:S(2)}) collective-permute-start(f32[2,96,128]{2,1,0:T(8,128)S(1)} %get-tuple-element.104), channel_id=1, source_target_pairs={{0,1},{1,0},{2,3},{3,2},{4,5},{5,4},{6,7},{7,6},{8,9},{9,8},{10,11... | collective-permute-start | bytes 294920 | tf_op jit(solution)/shard_map/ppermute | solution.py:473
  19.8 9.0 %collective-permute-start.7 = (f32[2,96,384]{2,1,0:T(8,128)S(1)}, f32[2,96,384]{2,1,0:T(8,128)S(1)}, u32[]{:S(2)}, u32[]{:S(2)}) collective-permute-start(f32[2,96,384]{2,1,0:T(8,128)S(1)} %get-tuple-element.61), channel_id=1, source_target_pairs={{0,28},{4,0},{8,4},{12,8},{16,12},{20,16},{24,20},{28,24},{1,29},{... | collective-permute-start | bytes 884744 | tf_op jit(solution)/shard_map/ppermute | solution.py:468
  23.2 7.6 %collective-permute-start.6 = (f32[2,192,128]{2,1,0:T(8,128)S(1)}, f32[2,192,128]{2,1,0:T(8,128)S(1)}, u32[]{:S(2)}, u32[]{:S(2)}) collective-permute-start(f32[2,192,128]{2,1,0:T(8,128)S(1)} %get-tuple-element.59), channel_id=1, source_target_pairs={{0,8},{1,2},{2,1},{3,11},{4,12},{5,6},{6,5},{7,15},{8,0},{9,10},{1... | collective-permute-start | bytes 589832 | tf_op jit(solution)/shard_map/ppermute | solution.py:485
  25.9 4.8 %collective-permute-start.5 = (f32[2,192,128]{2,1,0:T(8,128)S(1)}, f32[2,192,128]{2,1,0:T(8,128)S(1)}, u32[]{:S(2)}, u32[]{:S(2)}) collective-permute-start(f32[2,192,128]{2,1,0:T(8,128)S(1)} %get-tuple-element.58), channel_id=1, source_target_pairs={{0,1},{1,0},{2,3},{3,2},{4,5},{5,4},{6,7},{7,6},{8,9},{9,8},{10,11... | collective-permute-start | bytes 589832 | tf_op jit(solution)/shard_map/ppermute | solution.py:473
  28.8 6.0 %collective-permute-start.9 = (f32[2,96,128]{2,1,0:T(8,128)S(1)}, f32[2,96,128]{2,1,0:T(8,128)S(1)}, u32[]{:S(2)}, u32[]{:S(2)}) collective-permute-start(f32[2,96,128]{2,1,0:T(8,128)S(1)} %get-tuple-element.101), channel_id=1, source_target_pairs={{0,8},{1,2},{2,1},{3,11},{4,12},{5,6},{6,5},{7,15},{8,0},{9,10},{1... | collective-permute-start | bytes 294920 | tf_op jit(solution)/shard_map/ppermute | solution.py:485
  30.2 7.2 %collective-permute-start.8 = (f32[2,96,128]{2,1,0:T(8,128)S(1)}, f32[2,96,128]{2,1,0:T(8,128)S(1)}, u32[]{:S(2)}, u32[]{:S(2)}) collective-permute-start(f32[2,96,128]{2,1,0:T(8,128)S(1)} %get-tuple-element.102), channel_id=1, source_target_pairs={{0,1},{1,0},{2,3},{3,2},{4,5},{5,4},{6,7},{7,6},{8,9},{9,8},{10,11... | collective-permute-start | bytes 294920 | tf_op jit(solution)/shard_map/ppermute | solution.py:473
  30.9 21.2 %collective-permute-start.13 = (f32[2,192,384]{2,1,0:T(8,128)S(1)}, f32[2,192,384]{2,1,0:T(8,128)S(1)}, u32[]{:S(2)}, u32[]{:S(2)}) collective-permute-start(f32[2,192,384]{2,1,0:T(8,128)S(1)} %totals.5.refs_2_), channel_id=1, source_target_pairs={{0,28},{4,0},{8,4},{12,8},{16,12},{20,16},{24,20},{28,24},{1,29},{... | collective-permute-start | bytes 1769480 | tf_op jit(solution)/shard_map/ppermute | solution.py:468
  40.2 1.8 %collective-permute-start.10 = (f32[2,384,128]{2,1,0:T(8,128)S(1)}, f32[2,384,128]{2,1,0:T(8,128)S(1)}, u32[]{:S(2)}, u32[]{:S(2)}) collective-permute-start(f32[2,384,128]{2,1,0:T(8,128)S(1)} %get-tuple-element.68), channel_id=1, source_target_pairs={{0,1},{1,0},{2,3},{3,2},{4,5},{5,4},{6,7},{7,6},{8,9},{9,8},{10,11... | collective-permute-start | bytes 1179656 | tf_op jit(solution)/shard_map/ppermute | solution.py:473
  40.2 11.6 %collective-permute-start.11 = (f32[2,384,128]{2,1,0:T(8,128)S(1)}, f32[2,384,128]{2,1,0:T(8,128)S(1)}, u32[]{:S(2)}, u32[]{:S(2)}) collective-permute-start(f32[2,384,128]{2,1,0:T(8,128)S(1)} %get-tuple-element.69), channel_id=1, source_target_pairs={{0,8},{1,2},{2,1},{3,11},{4,12},{5,6},{6,5},{7,15},{8,0},{9,10},{1... | collective-permute-start | bytes 1179656 | tf_op jit(solution)/shard_map/ppermute | solution.py:485
  52.2 2.9 %collective-permute-start.17 = (f32[2,384,128]{2,1,0:T(8,128)S(1)}, f32[2,384,128]{2,1,0:T(8,128)S(1)}, u32[]{:S(2)}, u32[]{:S(2)}) collective-permute-start(f32[2,384,128]{2,1,0:T(8,128)S(1)} %get-tuple-element.77), channel_id=1, source_target_pairs={{0,1},{1,0},{2,3},{3,2},{4,5},{5,4},{6,7},{7,6},{8,9},{9,8},{10,11... | collective-permute-start | bytes 1179656 | tf_op jit(solution)/shard_map/ppermute | solution.py:473
  52.3 18.5 %collective-permute-start.12 = (f32[2,192,384]{2,1,0:T(8,128)S(1)}, f32[2,192,384]{2,1,0:T(8,128)S(1)}, u32[]{:S(2)}, u32[]{:S(2)}) collective-permute-start(f32[2,192,384]{2,1,0:T(8,128)S(1)} %get-tuple-element.70.refs_3_), channel_id=1, source_target_pairs={{0,4},{4,8},{8,12},{12,16},{16,20},{20,24},{24,28},{28,0},{1,5},{5... | collective-permute-start | bytes 1769480 | tf_op jit(solution)/shard_map/ppermute | solution.py:468
  52.6 8.3 %collective-permute-start.15 = (f32[2,384,128]{2,1,0:T(8,128)S(1)}, f32[2,384,128]{2,1,0:T(8,128)S(1)}, u32[]{:S(2)}, u32[]{:S(2)}) collective-permute-start(f32[2,384,128]{2,1,0:T(8,128)S(1)} %get-tuple-element.75), channel_id=1, source_target_pairs={{0,8},{1,2},{2,1},{3,11},{4,12},{5,6},{6,5},{7,15},{8,0},{9,10},{1... | collective-permute-start | bytes 1179656 | tf_op jit(solution)/shard_map/ppermute | solution.py:485
  57.7 15.3 %collective-permute-start.18 = (f32[2,192,128]{2,1,0:T(8,128)S(1)}, f32[2,192,128]{2,1,0:T(8,128)S(1)}, u32[]{:S(2)}, u32[]{:S(2)}) collective-permute-start(f32[2,192,128]{2,1,0:T(8,128)S(1)} %get-tuple-element.82), channel_id=1, source_target_pairs={{0,1},{1,0},{2,3},{3,2},{4,5},{5,4},{6,7},{7,6},{8,9},{9,8},{10,11... | collective-permute-start | bytes 589832 | tf_op jit(solution)/shard_map/ppermute | solution.py:473
  63.5 9.5 %collective-permute-start.19 = (f32[2,192,128]{2,1,0:T(8,128)S(1)}, f32[2,192,128]{2,1,0:T(8,128)S(1)}, u32[]{:S(2)}, u32[]{:S(2)}) collective-permute-start(f32[2,192,128]{2,1,0:T(8,128)S(1)} %get-tuple-element.83), channel_id=1, source_target_pairs={{0,8},{1,2},{2,1},{3,11},{4,12},{5,6},{6,5},{7,15},{8,0},{9,10},{1... | collective-permute-start | bytes 589832 | tf_op jit(solution)/shard_map/ppermute | solution.py:485
  71.0 2.2 %collective-permute-start.16 = (f32[2,192,128]{2,1,0:T(8,128)S(1)}, f32[2,192,128]{2,1,0:T(8,128)S(1)}, u32[]{:S(2)}, u32[]{:S(2)}) collective-permute-start(f32[2,192,128]{2,1,0:T(8,128)S(1)} %get-tuple-element.76), channel_id=1, source_target_pairs={{0,1},{1,0},{2,3},{3,2},{4,5},{5,4},{6,7},{7,6},{8,9},{9,8},{10,11... | collective-permute-start | bytes 589832 | tf_op jit(solution)/shard_map/ppermute | solution.py:473
  71.0 5.7 %collective-permute-start.14 = (f32[2,192,128]{2,1,0:T(8,128)S(1)}, f32[2,192,128]{2,1,0:T(8,128)S(1)}, u32[]{:S(2)}, u32[]{:S(2)}) collective-permute-start(f32[2,192,128]{2,1,0:T(8,128)S(1)} %get-tuple-element.74), channel_id=1, source_target_pairs={{0,8},{1,2},{2,1},{3,11},{4,12},{5,6},{6,5},{7,15},{8,0},{9,10},{1... | collective-permute-start | bytes 589832 | tf_op jit(solution)/shard_map/ppermute | solution.py:485
  79.4 12.0 %collective-permute-start.24 = (f32[2,96,128]{2,1,0:T(8,128)S(1)}, f32[2,96,128]{2,1,0:T(8,128)S(1)}, u32[]{:S(2)}, u32[]{:S(2)}) collective-permute-start(f32[2,96,128]{2,1,0:T(8,128)S(1)} %get-tuple-element.96), channel_id=1, source_target_pairs={{0,8},{1,2},{2,1},{3,11},{4,12},{5,6},{6,5},{7,15},{8,0},{9,10},{1... | collective-permute-start | bytes 294920 | tf_op jit(solution)/shard_map/ppermute | solution.py:485
  80.1 11.3 %collective-permute-start.23 = (f32[2,96,128]{2,1,0:T(8,128)S(1)}, f32[2,96,128]{2,1,0:T(8,128)S(1)}, u32[]{:S(2)}, u32[]{:S(2)}) collective-permute-start(f32[2,96,128]{2,1,0:T(8,128)S(1)} %get-tuple-element.95), channel_id=1, source_target_pairs={{0,1},{1,0},{2,3},{3,2},{4,5},{5,4},{6,7},{7,6},{8,9},{9,8},{10,11... | collective-permute-start | bytes 294920 | tf_op jit(solution)/shard_map/ppermute | solution.py:473
  80.1 23.2 %collective-permute-start.22 = (f32[2,96,384]{2,1,0:T(8,128)S(1)}, f32[2,96,384]{2,1,0:T(8,128)S(1)}, u32[]{:S(2)}, u32[]{:S(2)}) collective-permute-start(f32[2,96,384]{2,1,0:T(8,128)S(1)} %get-tuple-element.84), channel_id=1, source_target_pairs={{0,4},{4,8},{8,12},{12,16},{16,20},{20,24},{24,28},{28,0},{1,5},{5... | collective-permute-start | bytes 884744 | tf_op jit(solution)/shard_map/ppermute | solution.py:468
  90.1 9.5 %collective-permute-start.21 = (f32[2,288,128]{2,1,0:T(8,128)S(1)}, f32[2,288,128]{2,1,0:T(8,128)S(1)}, u32[]{:S(2)}, u32[]{:S(2)}) collective-permute-start(f32[2,288,128]{2,1,0:T(8,128)S(1)} %get-tuple-element.92), channel_id=1, source_target_pairs={{0,8},{1,2},{2,1},{3,11},{4,12},{5,6},{6,5},{7,15},{8,0},{9,10},{1... | collective-permute-start | bytes 884744 | tf_op jit(solution)/shard_map/ppermute | solution.py:485
  91.4 8.1 %collective-permute-start.20 = (f32[2,288,128]{2,1,0:T(8,128)S(1)}, f32[2,288,128]{2,1,0:T(8,128)S(1)}, u32[]{:S(2)}, u32[]{:S(2)}) collective-permute-start(f32[2,288,128]{2,1,0:T(8,128)S(1)} %get-tuple-element.91), channel_id=1, source_target_pairs={{0,1},{1,0},{2,3},{3,2},{4,5},{5,4},{6,7},{7,6},{8,9},{9,8},{10,11... | collective-permute-start | bytes 884744 | tf_op jit(solution)/shard_map/ppermute | solution.py:473
  91.5 14.8 %collective-permute-start.25 = (f32[2,96,384]{2,1,0:T(8,128)S(1)}, f32[2,96,384]{2,1,0:T(8,128)S(1)}, u32[]{:S(2)}, u32[]{:S(2)}) collective-permute-start(f32[2,96,384]{2,1,0:T(8,128)S(1)} %totals.9), channel_id=1, source_target_pairs={{0,28},{4,0},{8,4},{12,8},{16,12},{20,16},{24,20},{28,24},{1,29},{... | collective-permute-start | bytes 884744 | tf_op jit(solution)/shard_map/ppermute | solution.py:468

commit v5 on v4

--- a/solution.py
+++ b/solution.py
@@ -9,10 +9,12 @@
 from jax.experimental.pallas import tpu as pltpu
 from jax.sharding import PartitionSpec as P
 
+
 WIN = 256
 HALF = 128
 MARGIN = 96
 LANE = 128
+COST = pl.CostEstimate(flops=100_000, bytes_accessed=100_000, transcendentals=0)
 VMEM_LIMIT = 24 * 1024 * 1024
 
 step_size = 0.3
@@ -90,7 +92,7 @@
                 probes_ref[2 * i + j, channel] = pltpu.roll(turned, col, 1)
             amp = amp_ref[i * WIN : (i + 1) * WIN, j * WIN : (j + 1) * WIN]
             high, rest = split(amp)
-            middle, low = split(amp - high.astype(F32) - rest.astype(F32))
+            middle, _ = split(amp - high.astype(F32) - rest.astype(F32))
             sorted_lanes = mul(high, order) + mul(rest, order) + mul(middle, order)
             for q in range(2):
                 parts_ref[...] = sorted_lanes[:, q * HALF : (q + 1) * HALF]
@@ -109,7 +111,7 @@
         in_specs=[pl.BlockSpec(memory_space=pltpu.SMEM)] + vmem(3),
         out_specs=tuple(vmem(2)),
         scratch_shapes=[pltpu.VMEM((WIN, HALF), F32)],
-        cost_estimate=pl.CostEstimate(flops=400_000_000, bytes_accessed=6_000_000, transcendentals=0),
+        cost_estimate=COST,
         compiler_params=pltpu.CompilerParams(vmem_limit_bytes=VMEM_LIMIT),
         name="prepare",
     )(offsets, probe, amplitudes, order)
@@ -303,9 +305,8 @@
         in_specs=[pl.BlockSpec(memory_space=pltpu.SMEM)] + vmem(4 + len(operands)),
         out_specs=tuple(vmem(len(shapes))),
         scratch_shapes=[pltpu.VMEM((WIN, WIN), BF16)] * 16 + [pltpu.VMEM((WIN, WIN), F32)] * 8,
-        cost_estimate=pl.CostEstimate(flops=1_600_000_000, bytes_accessed=5_000_000, transcendentals=0),
+        cost_estimate=COST,
         compiler_params=pltpu.CompilerParams(vmem_limit_bytes=VMEM_LIMIT),
-        name=f"window_{i}" + ("a" if near else "b"),
     )(*consts, *operands)
 
 
@@ -365,7 +366,7 @@
         in_specs=vmem(len(operands)),
         out_specs=pl.BlockSpec(memory_space=pltpu.VMEM),
         scratch_shapes=[pltpu.VMEM((2, 208, 5 * LANE), F32)],
-        cost_estimate=pl.CostEstimate(flops=200_000_000, bytes_accessed=5_000_000, transcendentals=0),
+        cost_estimate=COST,
         compiler_params=pltpu.CompilerParams(vmem_limit_bytes=VMEM_LIMIT),
         name="variation",
     )(*operands)
@@ -400,7 +401,7 @@
         out_shape=tuple(jax.ShapeDtypeStruct((2, rows, own.shape[2]), F32) for _, rows in outs),
         in_specs=vmem(3 + len(extras)),
         out_specs=tuple(vmem(len(outs))),
-        cost_estimate=pl.CostEstimate(flops=500_000, bytes_accessed=3_000_000, transcendentals=0),
+        cost_estimate=COST,
         compiler_params=pltpu.CompilerParams(vmem_limit_bytes=VMEM_LIMIT),
         name="totals",
     )(own, near, far, *[extra[0] for extra in extras])
@@ -436,7 +437,7 @@
         out_shape=tuple(shape),
         in_specs=vmem(len(operands)),
         out_specs=tuple(vmem(3)),
-        cost_estimate=pl.CostEstimate(flops=1_000_000, bytes_accessed=4_000_000, transcendentals=0),
+        cost_estimate=COST,
         compiler_params=pltpu.CompilerParams(vmem_limit_bytes=VMEM_LIMIT),
         name="update",
     )(*operands)
@@ -457,7 +458,7 @@
         out_shape=jax.ShapeDtypeStruct((2, 3 * LANE, 3 * LANE), F32),
         in_specs=vmem(len(operands)),
         out_specs=pl.BlockSpec(memory_space=pltpu.VMEM),
-        cost_estimate=pl.CostEstimate(flops=1_000_000, bytes_accessed=4_000_000, transcendentals=0),
+        cost_estimate=COST,
         compiler_params=pltpu.CompilerParams(vmem_limit_bytes=VMEM_LIMIT),
         name="finish",
     )(*operands)
@@ -475,13 +476,11 @@
 
 def to_far(block):
     rows, cols = lax.axis_size("row"), lax.axis_size("col")
-    step = 2 if rows % 4 == 0 else 1 if rows % 2 == 0 else 0
     route = []
     for r in range(rows):
         for c in range(cols):
             other = c - 1 if c % 2 == 0 else c + 1
-            inside = 0 <= other < cols
-            route.append((r * cols + c, r * cols + other if inside else (r ^ step) * cols + c))
+            route.append((r * cols + c, r * cols + other % cols))
     return lax.ppermute(block, ("row", "col"), route)
 
 
@@ -538,7 +537,7 @@
     )
     in_b = to_far(hi_b)
     hi_o, hi_a = window(
-        1, True, consts, [(near, MARGIN, last), (bot_a, 0, MARGIN, "below")], own, [(hi_o, 0)], [(mid_a, 0)], whole
+        1, True, consts, [(near, MARGIN, last), (bot_a, 0, MARGIN, "below")], own, [(hi_o, 0)], [(mid_a, 0)], whole,
     )
     in_a = to_near(hi_a)
     tv_bottom = variation(
@@ -585,7 +584,7 @@
     own = [(up, 0, band), (low, 0, band)]
     cut = ((0, MARGIN), (MARGIN, last))
     over_o, over_a, lo_o, lo_a = window(
-        0, True, consts, [(up_a, 0, band), (low_a, 0, band)], own, [(mid_o, band)], [(mid_a, band)], cut
+        0, True, consts, [(up_a, 0, band), (low_a, 0, band)], own, [(mid_o, band)], [(mid_a, band)], cut,
     )
     over_a, in_a = to_near(over_a), to_near(lo_a)
     over_o, over_b, lo_o, lo_b = window(

time: 108 us -> 99.2 us (0.919)
  starting transfers between devices: 37.7 us -> 22.7 us
  waiting for transfers between devices: 37.1 us -> 43.6 us
    ppermute x6, starting transfers between devices: 23.4 us -> 11.3 us  [moved(): lax.ppermute(block, axis, [(n, (n + distance) % count) for n in range(cou...]
    ppermute x10, waiting for transfers between devices: 15 us -> 23.3 us  [to_far(): return lax.ppermute(block, ('row', 'col'), route)]
    ppermute x6, waiting for transfers between devices: 21.8 us -> 19.1 us  [moved(): lax.ppermute(block, axis, [(n, (n + distance) % count) for n in range(cou...]
    ppermute x10, starting transfers between devices: 9.19 us -> 6.6 us  [to_far(): return lax.ppermute(block, ('row', 'col'), route)]
  transfers between devices with their start and end apart: 26 -> 26, of which waited for: 10 -> 14; matrix products, arithmetic and copies ran while one was open for 0% -> 0% of each run, Pallas kernels for 24% -> 27%
where the time goes in v5:
time: 99.2 us; the launch traced here: 99 us
  waiting for transfers between devices  43.6 us (44%)
  Pallas kernels  30.4 us (31%)
  starting transfers between devices  22.7 us (23%)
  local copies, waits for them, and re-layouts  1.93 us (2%)
    ppermute x10, waiting for transfers between devices, to_far(): return lax.ppermute(block, ('row', 'col'), route)  23.3 us
    pallas_call x8, Pallas kernels, window(): pl.pallas_call(kernel, out_shape=tuple(shapes), in_specs=[pl.BlockSpec(me...  21.2 us
    ppermute x6, waiting for transfers between devices, moved(): lax.ppermute(block, axis, [(n, (n + distance) % count) for n in range(cou...  19.1 us
    ppermute x6, starting transfers between devices, moved(): lax.ppermute(block, axis, [(n, (n + distance) % count) for n in range(cou...  11.3 us
    ppermute x10, starting transfers between devices, to_far(): return lax.ppermute(block, ('row', 'col'), route)  6.6 us
    pallas_call x4, Pallas kernels, variation(): pl.pallas_call(functools.partial(variation_kernel, *plan), out_shape=jax....  5.33 us
    ppermute x10, starting transfers between devices, to_near(): lax.ppermute(block, ('row', 'col'), [(r * cols + c, r * cols + (c ^ 1)) f...  4.79 us
  transfers between devices with their start and end apart: 26, of which 14 were waited for; matrix products, arithmetic and copies ran while one was open for 0% of the time, Pallas kernels for 27%

profile of v5, /device:TPU:0, one launch (start us, length us, event | category | flops | bytes accessed | tf_op | source)
XLA Modules:
  0.0 99.0 jit_solution(7365635231244817207)
XLA Ops:
  0.0 1.9 %fusion = (f32[2,96,384]{2,1,0:T(8,128)}, f32[2,96,384]{2,1,0:T(8,128)S(1)}) fusion(f32[2,384,384]{2,1,0:T(8,128)} %refs_0_.13), kind=kLoop, calls=%fused_computation.6 | loop fusion | bytes 1179648 | tf_op jit(solution)/shard_map/slice | solution.py:501
  1.9 3.0 %collective-permute-start = (f32[2,96,384]{2,1,0:T(8,128)}, f32[2,96,384]{2,1,0:T(8,128)S(1)}, u32[]{:S(2)}, u32[]{:S(2)}) collective-permute-start(f32[2,96,384]{2,1,0:T(8,128)} %get-tuple-element.99), channel_id=1, source_target_pairs={{0,4},{4,8},{8,12},{12,16},{16,20},{20,24},{24,28},{28,0},{1,5},{5... | collective-permute-start | bytes 884744 | tf_op jit(solution)/shard_map/ppermute | solution.py:469
  5.0 0.7 collective-permute-start.4
  5.8 1.0 collective-permute-start.2
  6.7 8.5 %collective-permute-done.refs_7_.refs_2_.refs_0_ = f32[2,96,384]{2,1,0:T(8,128)S(1)} collective-permute-done((f32[2,96,384]{2,1,0:T(8,128)}, f32[2,96,384]{2,1,0:T(8,128)S(1)}, u32[]{:S(2)}, u32[]{:S(2)}) %collective-permute-start) | collective-permute-done | bytes 294944 | tf_op jit(solution)/shard_map/ppermute | solution.py:469
  15.2 1.7 %collective-permute-start.7 = (f32[2,96,384]{2,1,0:T(8,128)S(1)}, f32[2,96,384]{2,1,0:T(8,128)S(1)}, u32[]{:S(2)}, u32[]{:S(2)}) collective-permute-start(f32[2,96,384]{2,1,0:T(8,128)S(1)} %get-tuple-element.61), channel_id=1, source_target_pairs={{0,28},{4,0},{8,4},{12,8},{16,12},{20,16},{24,20},{28,24},{1,29},{... | collective-permute-start | bytes 884744 | tf_op jit(solution)/shard_map/ppermute | solution.py:469
  17.0 1.6 %collective-permute-start.1 = (f32[2,96,128]{2,1,0:T(8,128)S(1)}, f32[2,96,128]{2,1,0:T(8,128)S(1)}, u32[]{:S(2)}, u32[]{:S(2)}) collective-permute-start(f32[2,96,128]{2,1,0:T(8,128)S(1)} %get-tuple-element.104), channel_id=1, source_target_pairs={{0,1},{1,0},{2,3},{3,2},{4,5},{5,4},{6,7},{7,6},{8,9},{9,8},{10,11... | collective-permute-start | bytes 294920 | tf_op jit(solution)/shard_map/ppermute | solution.py:474
  18.7 1.8 %prepare.1 = (f32[4,2,256,256]{3,2,1,0:T(8,128)S(1)}, f32[4,512,128]{2,1,0:T(8,128)S(1)}) custom-call(s32[2,2,2]{2,1,0:T(2,128)S(1)} %copy-done.5, f32[2,256,256]{2,1,0:T(8,128)S(1)} %copy-done.4, f32[512,512]{1,0:T(8,128)S(1)} %copy-done.3, bf16[256,256]{1,0:T(8,128)(2,1)S(1)} %copy-done.6), custom_call_target="tpu_custom_call" | custom-call | flops 100000 | bytes 100000 | tf_op jit(solution)/shard_map/prepare/pallas_call | solution.py:105
  20.5 1.6 %collective-permute-done.3.refs_5_.refs_4_ = f32[2,96,128]{2,1,0:T(8,128)S(1)} collective-permute-done((f32[2,96,128]{2,1,0:T(8,128)S(1)}, f32[2,96,128]{2,1,0:T(8,128)S(1)}, u32[]{:S(2)}, u32[]{:S(2)}) %collective-permute-start.3) | collective-permute-done | bytes 98336 | tf_op jit(solution)/shard_map/ppermute | solution.py:484
  22.0 2.6 %shard_map.73 = (f32[2,192,384]{2,1,0:T(8,128)S(1)}, f32[2,192,128]{2,1,0:T(8,128)S(1)}, f32[2,192,384]{2,1,0:T(8,128)S(1)}, f32[2,192,128]{2,1,0:T(8,128)S(1)}) custom-call(s32[2,2,2]{2,1,0:T(2,128)S(1)} %copy-done.5, bf16[4,256,256]{2,1,0:T(8,128)(2,1)S(1)} %copy-done.1, f32[4,128,128]{2,1,0:T(8,128)S(1)} %copy-done.2, ...), custom_call_target="tpu_custom_call" | custom-call | flops 100000 | bytes 100000 | tf_op jit(solution)/shard_map/pallas_call | solution.py:302
  24.8 2.7 %shard_map.74 = (f32[2,192,384]{2,1,0:T(8,128)S(1)}, f32[2,192,128]{2,1,0:T(8,128)S(1)}, f32[2,192,384]{2,1,0:T(8,128)S(1)}, f32[2,192,128]{2,1,0:T(8,128)S(1)}) custom-call(s32[2,2,2]{2,1,0:T(2,128)S(1)} %copy-done.5, bf16[4,256,256]{2,1,0:T(8,128)(2,1)S(1)} %copy-done.1, f32[4,128,128]{2,1,0:T(8,128)S(1)} %copy-done.2, ...), custom_call_target="tpu_custom_call" | custom-call | flops 100000 | bytes 100000 | tf_op jit(solution)/shard_map/pallas_call | solution.py:302
  27.4 0.8 collective-permute-start.5
  28.3 1.2 %collective-permute-start.9 = (f32[2,96,128]{2,1,0:T(8,128)S(1)}, f32[2,96,128]{2,1,0:T(8,128)S(1)}, u32[]{:S(2)}, u32[]{:S(2)}) collective-permute-start(f32[2,96,128]{2,1,0:T(8,128)S(1)} %get-tuple-element.101), channel_id=1, source_target_pairs={{0,3},{1,2},{2,1},{3,0},{4,7},{5,6},{6,5},{7,4},{8,11},{9,10},{10,... | collective-permute-start | bytes 294920 | tf_op jit(solution)/shard_map/ppermute | solution.py:484
  29.5 0.3 collective-permute-start.8
  29.8 1.3 %variation.4.refs_0_ = f32[2,192,384]{2,1,0:T(8,128)S(1)} custom-call(f32[2,96,128]{2,1,0:T(8,128)S(1)} %collective-permute-done.1.refs_5_.refs_0_, f32[2,384,128]{2,1,0:T(8,128)S(1)} %collective-permute-done.2.refs_6_.refs_1_.refs_5_.refs_0_, f32[2,96,384]{2,1,0:T(8,128)S(1)} %collective-permute-done.refs_7_.refs_2_.refs_0_, f32[2,384,384]{2,1,0:T(8,128)S(1)} %copy-done, ...), custom_call_target="tpu_custom_call" | custom-call | flops 100000 | bytes 100000 | tf_op jit(solution)/shard_map/variation/pallas_call | solution.py:363
  31.2 0.4 collective-permute-done.6.far_ref
  31.7 1.5 %collective-permute-start.13 = (f32[2,192,384]{2,1,0:T(8,128)S(1)}, f32[2,192,384]{2,1,0:T(8,128)S(1)}, u32[]{:S(2)}, u32[]{:S(2)}) collective-permute-start(f32[2,192,384]{2,1,0:T(8,128)S(1)} %totals.5.refs_2_), channel_id=1, source_target_pairs={{0,28},{4,0},{8,4},{12,8},{16,12},{20,16},{24,20},{28,24},{1,29},{... | collective-permute-start | bytes 1769480 | tf_op jit(solution)/shard_map/ppermute | solution.py:469
  33.2 0.5 collective-permute-done.9.refs_6_.refs_5_
  33.7 2.6 %shard_map.75 = (f32[2,384,384]{2,1,0:T(8,128)S(1)}, f32[2,384,128]{2,1,0:T(8,128)S(1)}) custom-call(s32[2,2,2]{2,1,0:T(2,128)S(1)} %copy-done.5, bf16[4,256,256]{2,1,0:T(8,128)(2,1)S(1)} %copy-done.1, f32[4,128,128]{2,1,0:T(8,128)S(1)} %copy-done.2, f32[4,2,256,256]{3,2,1,0:T(8,128)S(1)} %get-tuple-element.52.refs_3_, ...), custom_call_target="tpu_custom_call" | custom-call | flops 100000 | bytes 100000 | tf_op jit(solution)/shard_map/pallas_call | solution.py:302
  36.3 2.7 %shard_map.76 = (f32[2,384,384]{2,1,0:T(8,128)S(1)}, f32[2,384,128]{2,1,0:T(8,128)S(1)}) custom-call(s32[2,2,2]{2,1,0:T(2,128)S(1)} %copy-done.5, bf16[4,256,256]{2,1,0:T(8,128)(2,1)S(1)} %copy-done.1, f32[4,128,128]{2,1,0:T(8,128)S(1)} %copy-done.2, f32[4,2,256,256]{3,2,1,0:T(8,128)S(1)} %get-tuple-element.52.refs_3_, ...), custom_call_target="tpu_custom_call" | custom-call | flops 100000 | bytes 100000 | tf_op jit(solution)/shard_map/pallas_call | solution.py:302
  39.0 0.3 collective-permute-start.10
  39.3 0.7 collective-permute-start.11
  40.0 1.3 %variation.5.refs_1_ = f32[2,192,384]{2,1,0:T(8,128)S(1)} custom-call(f32[2,384,128]{2,1,0:T(8,128)S(1)} %collective-permute-done.2.refs_6_.refs_1_.refs_5_.refs_0_, f32[2,96,128]{2,1,0:T(8,128)S(1)} %collective-permute-done.8.refs_6_.refs_1_, f32[2,384,384]{2,1,0:T(8,128)S(1)} %copy-done, f32[2,96,384]{2,1,0:T(8,128)S(1)} %collective-permute-done.7.refs_8_.refs_3_.refs_1_, ...), custom_call_target="tpu_custom_call" | custom-call | flops 100000 | bytes 100000 | tf_op jit(solution)/shard_map/variation/pallas_call | solution.py:363
  41.3 8.9 %collective-permute-done.11.far_ref = f32[2,384,128]{2,1,0:T(8,128)S(1)} collective-permute-done((f32[2,384,128]{2,1,0:T(8,128)S(1)}, f32[2,384,128]{2,1,0:T(8,128)S(1)}, u32[]{:S(2)}, u32[]{:S(2)}) %collective-permute-start.11) | collective-permute-done | bytes 393248 | tf_op jit(solution)/shard_map/ppermute | solution.py:484
  50.4 0.9 collective-permute-start.12
  51.6 0.5 collective-permute-start.15
  52.1 1.2 %collective-permute-done.17.refs_5_.refs_0_.refs_6_.refs_1_ = f32[2,384,128]{2,1,0:T(8,128)S(1)} collective-permute-done((f32[2,384,128]{2,1,0:T(8,128)S(1)}, f32[2,384,128]{2,1,0:T(8,128)S(1)}, u32[]{:S(2)}, u32[]{:S(2)}) %collective-permute-start.17) | collective-permute-done | bytes 393248 | tf_op jit(solution)/shard_map/ppermute | solution.py:474
  53.3 2.6 %shard_map.77 = (f32[2,192,384]{2,1,0:T(8,128)S(1)}, f32[2,192,128]{2,1,0:T(8,128)S(1)}, f32[2,192,384]{2,1,0:T(8,128)S(1)}, f32[2,192,128]{2,1,0:T(8,128)S(1)}) custom-call(s32[2,2,2]{2,1,0:T(2,128)S(1)} %copy-done.5, bf16[4,256,256]{2,1,0:T(8,128)(2,1)S(1)} %copy-done.1, f32[4,128,128]{2,1,0:T(8,128)S(1)} %copy-done.2, ...), custom_call_target="tpu_custom_call" | custom-call | flops 100000 | bytes 100000 | tf_op jit(solution)/shard_map/pallas_call | solution.py:302
  56.1 6.3 %collective-permute-done.15.refs_5_.refs_2_.refs_6_ = f32[2,384,128]{2,1,0:T(8,128)S(1)} collective-permute-done((f32[2,384,128]{2,1,0:T(8,128)S(1)}, f32[2,384,128]{2,1,0:T(8,128)S(1)}, u32[]{:S(2)}, u32[]{:S(2)}) %collective-permute-start.15) | collective-permute-done | bytes 393248 | tf_op jit(solution)/shard_map/ppermute | solution.py:484
  62.5 2.6 %shard_map.78 = (f32[2,192,384]{2,1,0:T(8,128)S(1)}, f32[2,192,128]{2,1,0:T(8,128)S(1)}, f32[2,192,384]{2,1,0:T(8,128)S(1)}, f32[2,192,128]{2,1,0:T(8,128)S(1)}) custom-call(s32[2,2,2]{2,1,0:T(2,128)S(1)} %copy-done.5, bf16[4,256,256]{2,1,0:T(8,128)(2,1)S(1)} %copy-done.1, f32[4,128,128]{2,1,0:T(8,128)S(1)} %copy-done.2, ...), custom_call_target="tpu_custom_call" | custom-call | flops 100000 | bytes 100000 | tf_op jit(solution)/shard_map/pallas_call | solution.py:302
  65.1 0.8 collective-permute-start.19
  65.9 3.0 %collective-permute-done.12.refs_3_ = f32[2,192,384]{2,1,0:T(8,128)S(1)} collective-permute-done((f32[2,192,384]{2,1,0:T(8,128)S(1)}, f32[2,192,384]{2,1,0:T(8,128)S(1)}, u32[]{:S(2)}, u32[]{:S(2)}) %collective-permute-start.12) | collective-permute-done | bytes 589856 | tf_op jit(solution)/shard_map/ppermute | solution.py:469
  69.1 0.8 collective-permute-start.14
  70.0 1.3 %variation.6.refs_0_.refs_1_ = f32[2,192,384]{2,1,0:T(8,128)S(1)} custom-call(f32[2,384,128]{2,1,0:T(8,128)S(1)} %collective-permute-done.17.refs_5_.refs_0_.refs_6_.refs_1_, f32[2,384,384]{2,1,0:T(8,128)S(1)} %get-tuple-element.73.refs_6_.refs_1_.refs_8_.refs_3_.bottom_ref, f32[2,384,128]{2,1,0:T(8,128)S(1)} %collective-permute-done.15.refs_5_.refs_2_.refs_6_), custom_call_target="tpu_custom_call" | custom-call | flops 100000 | bytes 100000 | tf_op jit(solution)/shard_map/variation/pallas_call | solution.py:363
  71.5 2.6 %shard_map.79 = (f32[2,96,384]{2,1,0:T(8,128)S(1)}, f32[2,96,128]{2,1,0:T(8,128)S(1)}, f32[2,288,384]{2,1,0:T(8,128)S(1)}, f32[2,288,128]{2,1,0:T(8,128)S(1)}) custom-call(s32[2,2,2]{2,1,0:T(2,128)S(1)} %copy-done.5, bf16[4,256,256]{2,1,0:T(8,128)(2,1)S(1)} %copy-done.1, f32[4,128,128]{2,1,0:T(8,128)S(1)} %copy-done.2, ...), custom_call_target="tpu_custom_call" | custom-call | flops 100000 | bytes 100000 | tf_op jit(solution)/shard_map/pallas_call | solution.py:302
  74.2 2.0 %collective-permute-done.14.refs_5_.refs_4_ = f32[2,192,128]{2,1,0:T(8,128)S(1)} collective-permute-done((f32[2,192,128]{2,1,0:T(8,128)S(1)}, f32[2,192,128]{2,1,0:T(8,128)S(1)}, u32[]{:S(2)}, u32[]{:S(2)}) %collective-permute-start.14) | collective-permute-done | bytes 196640 | tf_op jit(solution)/shard_map/ppermute | solution.py:484
  76.2 2.7 %shard_map.80 = (f32[2,96,384]{2,1,0:T(8,128)S(1)}, f32[2,96,128]{2,1,0:T(8,128)S(1)}, f32[2,288,384]{2,1,0:T(8,128)S(1)}, f32[2,288,128]{2,1,0:T(8,128)S(1)}) custom-call(s32[2,2,2]{2,1,0:T(2,128)S(1)} %copy-done.5, bf16[4,256,256]{2,1,0:T(8,128)(2,1)S(1)} %copy-done.1, f32[4,128,128]{2,1,0:T(8,128)S(1)} %copy-done.2, ...), custom_call_target="tpu_custom_call" | custom-call | flops 100000 | bytes 100000 | tf_op jit(solution)/shard_map/pallas_call | solution.py:302
  78.9 0.5 collective-permute-start.24
  79.6 1.1 %collective-permute-start.22 = (f32[2,96,384]{2,1,0:T(8,128)S(1)}, f32[2,96,384]{2,1,0:T(8,128)S(1)}, u32[]{:S(2)}, u32[]{:S(2)}) collective-permute-start(f32[2,96,384]{2,1,0:T(8,128)S(1)} %get-tuple-element.84), channel_id=1, source_target_pairs={{0,4},{4,8},{8,12},{12,16},{16,20},{20,24},{24,28},{28,0},{1,5},{5... | collective-permute-start | bytes 884744 | tf_op jit(solution)/shard_map/ppermute | solution.py:469
  80.7 1.1 %collective-permute-start.21 = (f32[2,288,128]{2,1,0:T(8,128)S(1)}, f32[2,288,128]{2,1,0:T(8,128)S(1)}, u32[]{:S(2)}, u32[]{:S(2)}) collective-permute-start(f32[2,288,128]{2,1,0:T(8,128)S(1)} %get-tuple-element.92), channel_id=1, source_target_pairs={{0,3},{1,2},{2,1},{3,0},{4,7},{5,6},{6,5},{7,4},{8,11},{9,10},{10,... | collective-permute-start | bytes 884744 | tf_op jit(solution)/shard_map/ppermute | solution.py:484
  81.9 0.3 collective-permute-start.20
  82.1 1.5 %collective-permute-done.24.far_ref = f32[2,96,128]{2,1,0:T(8,128)S(1)} collective-permute-done((f32[2,96,128]{2,1,0:T(8,128)S(1)}, f32[2,96,128]{2,1,0:T(8,128)S(1)}, u32[]{:S(2)}, u32[]{:S(2)}) %collective-permute-start.24) | collective-permute-done | bytes 98336 | tf_op jit(solution)/shard_map/ppermute | solution.py:484
  83.6 3.1 %collective-permute-start.25 = (f32[2,96,384]{2,1,0:T(8,128)S(1)}, f32[2,96,384]{2,1,0:T(8,128)S(1)}, u32[]{:S(2)}, u32[]{:S(2)}) collective-permute-start(f32[2,96,384]{2,1,0:T(8,128)S(1)} %totals.9), channel_id=1, source_target_pairs={{0,28},{4,0},{8,4},{12,8},{16,12},{20,16},{24,20},{28,24},{1,29},{... | collective-permute-start | bytes 884744 | tf_op jit(solution)/shard_map/ppermute | solution.py:469
  86.7 1.3 %variation.7.refs_0_ = f32[2,192,384]{2,1,0:T(8,128)S(1)} custom-call(f32[2,192,128]{2,1,0:T(8,128)S(1)} %collective-permute-done.16.refs_5_.refs_0_, f32[2,384,128]{2,1,0:T(8,128)S(1)} %collective-permute-done.17.refs_5_.refs_0_.refs_6_.refs_1_, f32[2,192,384]{2,1,0:T(8,128)S(1)} %get-tuple-element.71.refs_7_.refs_2_.top_ref, ...), custom_call_target="tpu_custom_call" | custom-call | flops 100000 | bytes 100000 | tf_op jit(solution)/shard_map/variation/pallas_call | solution.py:363
  88.1 2.0 %collective-permute-done.21.far_ref = f32[2,288,128]{2,1,0:T(8,128)S(1)} collective-permute-done((f32[2,288,128]{2,1,0:T(8,128)S(1)}, f32[2,288,128]{2,1,0:T(8,128)S(1)}, u32[]{:S(2)}, u32[]{:S(2)}) %collective-permute-start.21) | collective-permute-done | bytes 294944 | tf_op jit(solution)/shard_map/ppermute | solution.py:484
  90.2 3.7 %collective-permute-done.22.above_ref = f32[2,96,384]{2,1,0:T(8,128)S(1)} collective-permute-done((f32[2,96,384]{2,1,0:T(8,128)S(1)}, f32[2,96,384]{2,1,0:T(8,128)S(1)}, u32[]{:S(2)}, u32[]{:S(2)}) %collective-permute-start.22) | collective-permute-done | bytes 294944 | tf_op jit(solution)/shard_map/ppermute | solution.py:469
  93.9 3.9 %collective-permute-done.25.below_ref = f32[2,96,384]{2,1,0:T(8,128)S(1)} collective-permute-done((f32[2,96,384]{2,1,0:T(8,128)S(1)}, f32[2,96,384]{2,1,0:T(8,128)S(1)}, u32[]{:S(2)}, u32[]{:S(2)}) %collective-permute-start.25) | collective-permute-done | bytes 294944 | tf_op jit(solution)/shard_map/ppermute | solution.py:469
  97.8 1.2 %finish.1 = f32[2,384,384]{2,1,0:T(8,128)} custom-call(f32[2,192,384]{2,1,0:T(8,128)S(1)} %get-tuple-element.71.refs_7_.refs_2_.top_ref, f32[2,384,384]{2,1,0:T(8,128)S(1)} %get-tuple-element.73.refs_6_.refs_1_.refs_8_.refs_3_.bottom_ref, f32[2,288,384]{2,1,0:T(8,128)S(1)} %totals.8.mid_ref, f32[2,96,384]{2,1,0:T(8,128)S(1)} %get-tuple-element.93.low_ref, ...), custom_call_target="tpu_custom_call" | custom-call | flops 100000 | bytes 100000 | tf_op jit(solution)/shard_map/finish/pallas_call | solution.py:456
  (43 shorter events, 1.9 us)
Async XLA Ops:
  0.0 4.9 %copy-start = (f32[2,384,384]{2,1,0:T(8,128)S(1)}, f32[2,384,384]{2,1,0:T(8,128)}, u32[]{:S(2)}) copy-start(f32[2,384,384]{2,1,0:T(8,128)} %refs_0_.13) | copy-start | bytes 3538948
  1.9 16.8 %copy-start.3 = (f32[512,512]{1,0:T(8,128)S(1)}, f32[512,512]{1,0:T(8,128)}, u32[]{:S(2)}) copy-start(f32[512,512]{1,0:T(8,128)} %amp_ref.1) | copy-start | bytes 3145732
  1.9 16.8 %copy-start.4 = (f32[2,256,256]{2,1,0:T(8,128)S(1)}, f32[2,256,256]{2,1,0:T(8,128)}, u32[]{:S(2)}) copy-start(f32[2,256,256]{2,1,0:T(8,128)} %probe_ref.1) | copy-start | bytes 1572868
  1.9 16.8 %copy-start.5 = (s32[2,2,2]{2,1,0:T(2,128)S(1)}, s32[2,2,2]{2,1,0:T(2,128)}, u32[]{:S(2)}) copy-start(s32[2,2,2]{2,1,0:T(2,128)} %refs_0_.17) | copy-start | bytes 100
  1.9 16.8 %copy-start.6 = (bf16[256,256]{1,0:T(8,128)(2,1)S(1)}, bf16[256,256]{1,0:T(8,128)(2,1)}, u32[]{:S(2)}) copy-start(bf16[256,256]{1,0:T(8,128)(2,1)} %constant.30.clone.order_ref) | copy-start | bytes 393220
  1.9 13.3 %collective-permute-start = (f32[2,96,384]{2,1,0:T(8,128)}, f32[2,96,384]{2,1,0:T(8,128)S(1)}, u32[]{:S(2)}, u32[]{:S(2)}) collective-permute-start(f32[2,96,384]{2,1,0:T(8,128)} %get-tuple-element.99), channel_id=1, source_target_pairs={{0,4},{4,8},{8,12},{12,16},{16,20},{20,24},{24,28},{28,0},{1,5},{5... | collective-permute-start | bytes 884744 | tf_op jit(solution)/shard_map/ppermute | solution.py:469
  5.0 17.0 %copy-start.1 = (bf16[4,256,256]{2,1,0:T(8,128)(2,1)S(1)}, bf16[4,256,256]{2,1,0:T(8,128)(2,1)}, u32[]{:S(2)}) copy-start(bf16[4,256,256]{2,1,0:T(8,128)(2,1)} %constant.28.clone.refs_1_) | copy-start | bytes 1572868
  5.0 17.0 %copy-start.2 = (f32[4,128,128]{2,1,0:T(8,128)S(1)}, f32[4,128,128]{2,1,0:T(8,128)}, u32[]{:S(2)}) copy-start(f32[4,128,128]{2,1,0:T(8,128)} %constant.29.clone.refs_2_) | copy-start | bytes 786436
  5.0 17.0 %collective-permute-start.4 = (f32[2,384,128]{2,1,0:T(8,128)S(1)}, f32[2,384,128]{2,1,0:T(8,128)S(1)}, u32[]{:S(2)}, u32[]{:S(2)}) collective-permute-start(f32[2,384,128]{2,1,0:T(8,128)S(1)} %get-tuple-element.97), channel_id=1, source_target_pairs={{0,3},{1,2},{2,1},{3,0},{4,7},{5,6},{6,5},{7,4},{8,11},{9,10},{10,... | collective-permute-start | bytes 1179656 | tf_op jit(solution)/shard_map/ppermute | solution.py:484
  5.8 19.0 %collective-permute-start.2 = (f32[2,384,128]{2,1,0:T(8,128)S(1)}, f32[2,384,128]{2,1,0:T(8,128)S(1)}, u32[]{:S(2)}, u32[]{:S(2)}) collective-permute-start(f32[2,384,128]{2,1,0:T(8,128)S(1)} %get-tuple-element.98), channel_id=1, source_target_pairs={{0,1},{1,0},{2,3},{3,2},{4,5},{5,4},{6,7},{7,6},{8,9},{9,8},{10,11... | collective-permute-start | bytes 1179656 | tf_op jit(solution)/shard_map/ppermute | solution.py:474
  15.2 13.1 %collective-permute-start.7 = (f32[2,96,384]{2,1,0:T(8,128)S(1)}, f32[2,96,384]{2,1,0:T(8,128)S(1)}, u32[]{:S(2)}, u32[]{:S(2)}) collective-permute-start(f32[2,96,384]{2,1,0:T(8,128)S(1)} %get-tuple-element.61), channel_id=1, source_target_pairs={{0,28},{4,0},{8,4},{12,8},{16,12},{20,16},{24,20},{28,24},{1,29},{... | collective-permute-start | bytes 884744 | tf_op jit(solution)/shard_map/ppermute | solution.py:469
  17.0 5.1 %collective-permute-start.3 = (f32[2,96,128]{2,1,0:T(8,128)S(1)}, f32[2,96,128]{2,1,0:T(8,128)S(1)}, u32[]{:S(2)}, u32[]{:S(2)}) collective-permute-start(f32[2,96,128]{2,1,0:T(8,128)S(1)} %get-tuple-element.103), channel_id=1, source_target_pairs={{0,3},{1,2},{2,1},{3,0},{4,7},{5,6},{6,5},{7,4},{8,11},{9,10},{10,... | collective-permute-start | bytes 294920 | tf_op jit(solution)/shard_map/ppermute | solution.py:484
  17.0 7.7 %collective-permute-start.1 = (f32[2,96,128]{2,1,0:T(8,128)S(1)}, f32[2,96,128]{2,1,0:T(8,128)S(1)}, u32[]{:S(2)}, u32[]{:S(2)}) collective-permute-start(f32[2,96,128]{2,1,0:T(8,128)S(1)} %get-tuple-element.104), channel_id=1, source_target_pairs={{0,1},{1,0},{2,3},{3,2},{4,5},{5,4},{6,7},{7,6},{8,9},{9,8},{10,11... | collective-permute-start | bytes 294920 | tf_op jit(solution)/shard_map/ppermute | solution.py:474
  24.7 6.9 %collective-permute-start.6 = (f32[2,192,128]{2,1,0:T(8,128)S(1)}, f32[2,192,128]{2,1,0:T(8,128)S(1)}, u32[]{:S(2)}, u32[]{:S(2)}) collective-permute-start(f32[2,192,128]{2,1,0:T(8,128)S(1)} %get-tuple-element.59), channel_id=1, source_target_pairs={{0,3},{1,2},{2,1},{3,0},{4,7},{5,6},{6,5},{7,4},{8,11},{9,10},{10,... | collective-permute-start | bytes 589832 | tf_op jit(solution)/shard_map/ppermute | solution.py:484
  27.4 4.1 %collective-permute-start.5 = (f32[2,192,128]{2,1,0:T(8,128)S(1)}, f32[2,192,128]{2,1,0:T(8,128)S(1)}, u32[]{:S(2)}, u32[]{:S(2)}) collective-permute-start(f32[2,192,128]{2,1,0:T(8,128)S(1)} %get-tuple-element.58), channel_id=1, source_target_pairs={{0,1},{1,0},{2,3},{3,2},{4,5},{5,4},{6,7},{7,6},{8,9},{9,8},{10,11... | collective-permute-start | bytes 589832 | tf_op jit(solution)/shard_map/ppermute | solution.py:474
  28.3 5.4 %collective-permute-start.9 = (f32[2,96,128]{2,1,0:T(8,128)S(1)}, f32[2,96,128]{2,1,0:T(8,128)S(1)}, u32[]{:S(2)}, u32[]{:S(2)}) collective-permute-start(f32[2,96,128]{2,1,0:T(8,128)S(1)} %get-tuple-element.101), channel_id=1, source_target_pairs={{0,3},{1,2},{2,1},{3,0},{4,7},{5,6},{6,5},{7,4},{8,11},{9,10},{10,... | collective-permute-start | bytes 294920 | tf_op jit(solution)/shard_map/ppermute | solution.py:484
  29.5 6.8 %collective-permute-start.8 = (f32[2,96,128]{2,1,0:T(8,128)S(1)}, f32[2,96,128]{2,1,0:T(8,128)S(1)}, u32[]{:S(2)}, u32[]{:S(2)}) collective-permute-start(f32[2,96,128]{2,1,0:T(8,128)S(1)} %get-tuple-element.102), channel_id=1, source_target_pairs={{0,1},{1,0},{2,3},{3,2},{4,5},{5,4},{6,7},{7,6},{8,9},{9,8},{10,11... | collective-permute-start | bytes 294920 | tf_op jit(solution)/shard_map/ppermute | solution.py:474
  31.7 19.6 %collective-permute-start.13 = (f32[2,192,384]{2,1,0:T(8,128)S(1)}, f32[2,192,384]{2,1,0:T(8,128)S(1)}, u32[]{:S(2)}, u32[]{:S(2)}) collective-permute-start(f32[2,192,384]{2,1,0:T(8,128)S(1)} %totals.5.refs_2_), channel_id=1, source_target_pairs={{0,28},{4,0},{8,4},{12,8},{16,12},{20,16},{24,20},{28,24},{1,29},{... | collective-permute-start | bytes 1769480 | tf_op jit(solution)/shard_map/ppermute | solution.py:469
  39.0 2.3 %collective-permute-start.10 = (f32[2,384,128]{2,1,0:T(8,128)S(1)}, f32[2,384,128]{2,1,0:T(8,128)S(1)}, u32[]{:S(2)}, u32[]{:S(2)}) collective-permute-start(f32[2,384,128]{2,1,0:T(8,128)S(1)} %get-tuple-element.68), channel_id=1, source_target_pairs={{0,1},{1,0},{2,3},{3,2},{4,5},{5,4},{6,7},{7,6},{8,9},{9,8},{10,11... | collective-permute-start | bytes 1179656 | tf_op jit(solution)/shard_map/ppermute | solution.py:474
  39.3 10.9 %collective-permute-start.11 = (f32[2,384,128]{2,1,0:T(8,128)S(1)}, f32[2,384,128]{2,1,0:T(8,128)S(1)}, u32[]{:S(2)}, u32[]{:S(2)}) collective-permute-start(f32[2,384,128]{2,1,0:T(8,128)S(1)} %get-tuple-element.69), channel_id=1, source_target_pairs={{0,3},{1,2},{2,1},{3,0},{4,7},{5,6},{6,5},{7,4},{8,11},{9,10},{10,... | collective-permute-start | bytes 1179656 | tf_op jit(solution)/shard_map/ppermute | solution.py:484
  50.4 18.5 %collective-permute-start.12 = (f32[2,192,384]{2,1,0:T(8,128)S(1)}, f32[2,192,384]{2,1,0:T(8,128)S(1)}, u32[]{:S(2)}, u32[]{:S(2)}) collective-permute-start(f32[2,192,384]{2,1,0:T(8,128)S(1)} %get-tuple-element.70.refs_3_), channel_id=1, source_target_pairs={{0,4},{4,8},{8,12},{12,16},{16,20},{20,24},{24,28},{28,0},{1,5},{5... | collective-permute-start | bytes 1769480 | tf_op jit(solution)/shard_map/ppermute | solution.py:469
  51.5 1.8 %collective-permute-start.17 = (f32[2,384,128]{2,1,0:T(8,128)S(1)}, f32[2,384,128]{2,1,0:T(8,128)S(1)}, u32[]{:S(2)}, u32[]{:S(2)}) collective-permute-start(f32[2,384,128]{2,1,0:T(8,128)S(1)} %get-tuple-element.77), channel_id=1, source_target_pairs={{0,1},{1,0},{2,3},{3,2},{4,5},{5,4},{6,7},{7,6},{8,9},{9,8},{10,11... | collective-permute-start | bytes 1179656 | tf_op jit(solution)/shard_map/ppermute | solution.py:474
  51.6 10.9 %collective-permute-start.15 = (f32[2,384,128]{2,1,0:T(8,128)S(1)}, f32[2,384,128]{2,1,0:T(8,128)S(1)}, u32[]{:S(2)}, u32[]{:S(2)}) collective-permute-start(f32[2,384,128]{2,1,0:T(8,128)S(1)} %get-tuple-element.75), channel_id=1, source_target_pairs={{0,3},{1,2},{2,1},{3,0},{4,7},{5,6},{6,5},{7,4},{8,11},{9,10},{10,... | collective-permute-start | bytes 1179656 | tf_op jit(solution)/shard_map/ppermute | solution.py:484
  55.9 15.4 %collective-permute-start.18 = (f32[2,192,128]{2,1,0:T(8,128)S(1)}, f32[2,192,128]{2,1,0:T(8,128)S(1)}, u32[]{:S(2)}, u32[]{:S(2)}) collective-permute-start(f32[2,192,128]{2,1,0:T(8,128)S(1)} %get-tuple-element.82), channel_id=1, source_target_pairs={{0,1},{1,0},{2,3},{3,2},{4,5},{5,4},{6,7},{7,6},{8,9},{9,8},{10,11... | collective-permute-start | bytes 589832 | tf_op jit(solution)/shard_map/ppermute | solution.py:474
  65.1 6.3 %collective-permute-start.19 = (f32[2,192,128]{2,1,0:T(8,128)S(1)}, f32[2,192,128]{2,1,0:T(8,128)S(1)}, u32[]{:S(2)}, u32[]{:S(2)}) collective-permute-start(f32[2,192,128]{2,1,0:T(8,128)S(1)} %get-tuple-element.83), channel_id=1, source_target_pairs={{0,3},{1,2},{2,1},{3,0},{4,7},{5,6},{6,5},{7,4},{8,11},{9,10},{10,... | collective-permute-start | bytes 589832 | tf_op jit(solution)/shard_map/ppermute | solution.py:484
  69.0 2.5 %collective-permute-start.16 = (f32[2,192,128]{2,1,0:T(8,128)S(1)}, f32[2,192,128]{2,1,0:T(8,128)S(1)}, u32[]{:S(2)}, u32[]{:S(2)}) collective-permute-start(f32[2,192,128]{2,1,0:T(8,128)S(1)} %get-tuple-element.76), channel_id=1, source_target_pairs={{0,1},{1,0},{2,3},{3,2},{4,5},{5,4},{6,7},{7,6},{8,9},{9,8},{10,11... | collective-permute-start | bytes 589832 | tf_op jit(solution)/shard_map/ppermute | solution.py:474
  69.1 7.1 %collective-permute-start.14 = (f32[2,192,128]{2,1,0:T(8,128)S(1)}, f32[2,192,128]{2,1,0:T(8,128)S(1)}, u32[]{:S(2)}, u32[]{:S(2)}) collective-permute-start(f32[2,192,128]{2,1,0:T(8,128)S(1)} %get-tuple-element.74), channel_id=1, source_target_pairs={{0,3},{1,2},{2,1},{3,0},{4,7},{5,6},{6,5},{7,4},{8,11},{9,10},{10,... | collective-permute-start | bytes 589832 | tf_op jit(solution)/shard_map/ppermute | solution.py:484
  78.9 4.7 %collective-permute-start.24 = (f32[2,96,128]{2,1,0:T(8,128)S(1)}, f32[2,96,128]{2,1,0:T(8,128)S(1)}, u32[]{:S(2)}, u32[]{:S(2)}) collective-permute-start(f32[2,96,128]{2,1,0:T(8,128)S(1)} %get-tuple-element.96), channel_id=1, source_target_pairs={{0,3},{1,2},{2,1},{3,0},{4,7},{5,6},{6,5},{7,4},{8,11},{9,10},{10,... | collective-permute-start | bytes 294920 | tf_op jit(solution)/shard_map/ppermute | solution.py:484
  79.4 4.2 %collective-permute-start.23 = (f32[2,96,128]{2,1,0:T(8,128)S(1)}, f32[2,96,128]{2,1,0:T(8,128)S(1)}, u32[]{:S(2)}, u32[]{:S(2)}) collective-permute-start(f32[2,96,128]{2,1,0:T(8,128)S(1)} %get-tuple-element.95), channel_id=1, source_target_pairs={{0,1},{1,0},{2,3},{3,2},{4,5},{5,4},{6,7},{7,6},{8,9},{9,8},{10,11... | collective-permute-start | bytes 294920 | tf_op jit(solution)/shard_map/ppermute | solution.py:474
  79.6 14.3 %collective-permute-start.22 = (f32[2,96,384]{2,1,0:T(8,128)S(1)}, f32[2,96,384]{2,1,0:T(8,128)S(1)}, u32[]{:S(2)}, u32[]{:S(2)}) collective-permute-start(f32[2,96,384]{2,1,0:T(8,128)S(1)} %get-tuple-element.84), channel_id=1, source_target_pairs={{0,4},{4,8},{8,12},{12,16},{16,20},{20,24},{24,28},{28,0},{1,5},{5... | collective-permute-start | bytes 884744 | tf_op jit(solution)/shard_map/ppermute | solution.py:469
  80.7 9.3 %collective-permute-start.21 = (f32[2,288,128]{2,1,0:T(8,128)S(1)}, f32[2,288,128]{2,1,0:T(8,128)S(1)}, u32[]{:S(2)}, u32[]{:S(2)}) collective-permute-start(f32[2,288,128]{2,1,0:T(8,128)S(1)} %get-tuple-element.92), channel_id=1, source_target_pairs={{0,3},{1,2},{2,1},{3,0},{4,7},{5,6},{6,5},{7,4},{8,11},{9,10},{10,... | collective-permute-start | bytes 884744 | tf_op jit(solution)/shard_map/ppermute | solution.py:484
  81.9 8.2 %collective-permute-start.20 = (f32[2,288,128]{2,1,0:T(8,128)S(1)}, f32[2,288,128]{2,1,0:T(8,128)S(1)}, u32[]{:S(2)}, u32[]{:S(2)}) collective-permute-start(f32[2,288,128]{2,1,0:T(8,128)S(1)} %get-tuple-element.91), channel_id=1, source_target_pairs={{0,1},{1,0},{2,3},{3,2},{4,5},{5,4},{6,7},{7,6},{8,9},{9,8},{10,11... | collective-permute-start | bytes 884744 | tf_op jit(solution)/shard_map/ppermute | solution.py:474
  83.6 14.2 %collective-permute-start.25 = (f32[2,96,384]{2,1,0:T(8,128)S(1)}, f32[2,96,384]{2,1,0:T(8,128)S(1)}, u32[]{:S(2)}, u32[]{:S(2)}) collective-permute-start(f32[2,96,384]{2,1,0:T(8,128)S(1)} %totals.9), channel_id=1, source_target_pairs={{0,28},{4,0},{8,4},{12,8},{16,12},{20,16},{24,20},{28,24},{1,29},{... | collective-permute-start | bytes 884744 | tf_op jit(solution)/shard_map/ppermute | solution.py:469

commit v6 on v5

--- a/solution.py
+++ b/solution.py
@@ -474,13 +474,14 @@
     return lax.ppermute(block, ("row", "col"), [(r * cols + c, r * cols + (c ^ 1)) for r in range(rows) for c in range(cols)])
 
 
-def to_far(block):
+def to_far(block, ends=True):
     rows, cols = lax.axis_size("row"), lax.axis_size("col")
     route = []
     for r in range(rows):
         for c in range(cols):
             other = c - 1 if c % 2 == 0 else c + 1
-            route.append((r * cols + c, r * cols + other % cols))
+            if ends or 0 <= other < cols:
+                route.append((r * cols + c, r * cols + other % cols))
     return lax.ppermute(block, ("row", "col"), route)
 
 
@@ -510,15 +511,15 @@
     top_b, top_a = to_far(far_strip), to_near(near_strip)
     own = [(top, 0, MARGIN, "above"), (obj, 0, last)]
     halves = ((0, band), (band, band))
+    lo_o, lo_a, mid_o, mid_a = window(
+        0, True, consts, [(top_a, 0, MARGIN, "above"), (near, 0, last)], own, [], [], halves
+    )
+    in_a = to_near(lo_a)
     lo_o, lo_b, mid_o, mid_b = window(
-        0, False, consts, [(top_b, 0, MARGIN, "above"), (far, 0, last)], own, [], [], halves
+        0, False, consts, [(top_b, 0, MARGIN, "above"), (far, 0, last)], own, [(lo_o, 0), (mid_o, band)], [], halves
     )
     in_b = to_far(lo_b)
-    lo_o, lo_a, mid_o, mid_a = window(
-        0, True, consts, [(top_a, 0, MARGIN, "above"), (near, 0, last)], own, [(lo_o, 0), (mid_o, band)], [], halves
-    )
-    in_a = to_near(lo_a)
-    bottom, lo_a = after((bottom, lo_a))
+    bottom, lo_b = after((bottom, lo_b))
     near_strip, far_strip = edges(bottom)
     bot_b, bot_a = to_far(far_strip), to_near(near_strip)
     tv_top = variation(
@@ -535,7 +536,7 @@
     hi_o, hi_b = window(
         1, False, consts, [(far, MARGIN, last), (bot_b, 0, MARGIN, "below")], own, [(mid_o, 0)], [(mid_b, 0)], whole
     )
-    in_b = to_far(hi_b)
+    in_b = to_far(hi_b, ends=False)
     hi_o, hi_a = window(
         1, True, consts, [(near, MARGIN, last), (bot_a, 0, MARGIN, "below")], own, [(hi_o, 0)], [(mid_a, 0)], whole,
     )
@@ -559,18 +560,15 @@
         ),
         "below",
     )
-    low_b, low_a = to_far(far_strip), to_near(near_strip)
+    low_a, low_b = to_near(near_strip), to_far(far_strip, ends=False)
     own = [(low, 0, tile)]
     mid_o, mid_a, hi_o, hi_a = window(1, True, consts, [(low_a, 0, tile)], own, [], [], halves)
     in_a = to_near(hi_a)
     mid_o, mid_b, hi_o, hi_b = window(
         1, False, consts, [(low_b, 0, tile)], own, [(mid_o, 0), (hi_o, band)], [], halves
     )
-    in_b = to_far(hi_b)
+    hi_in_a, hi_in_b = in_a, to_far(hi_b)
     tv_bottom = variation([(low_a, 88, 208)], [(low, 88, 208)], [(low_b, 88, 208)])
-    low_sum, over = totals(hi_o, in_a, in_b, ((0, MARGIN), (MARGIN, MARGIN)), [(tv_bottom, MARGIN, 0, MARGIN)])
-    last_above = moved(over, "row", 1)
-
     up, near_strip, far_strip = update(
         (top, obj, top_sum, from_above),
         (
@@ -580,15 +578,20 @@
         "above",
     )
     up_b, up_a = to_far(far_strip), to_near(near_strip)
-    mid_o, over = after((mid_o, over))
     own = [(up, 0, band), (low, 0, band)]
     cut = ((0, MARGIN), (MARGIN, last))
     over_o, over_a, lo_o, lo_a = window(
-        0, True, consts, [(up_a, 0, band), (low_a, 0, band)], own, [(mid_o, band)], [(mid_a, band)], cut,
+        0, True, consts, [(up_a, 0, band), (low_a, 0, band)], own, [(mid_o, band)], [(mid_a, band)], cut
     )
     over_a, in_a = to_near(over_a), to_near(lo_a)
+    lo_o, hi_o = after((lo_o, hi_o))
+    low_sum, over = totals(
+        hi_o, hi_in_a, hi_in_b, ((0, MARGIN), (MARGIN, MARGIN)), [(tv_bottom, MARGIN, 0, MARGIN)]
+    )
+    lo_o, over = after((lo_o, over))
+    last_above = moved(over, "row", 1)
     over_o, over_b, lo_o, lo_b = window(
-        0, False, consts, [(up_b, 0, band), (low_b, 0, band)], own, [(over_o, 0), (lo_o, MARGIN)], [(mid_b, band)], cut
+        0, False, consts, [(up_b, 0, band), (low_b, 0, band)], own, [(over_o, 0), (lo_o, MARGIN)], [(mid_b, band)], cut,
     )
     over_b = to_far(over_b)
     (over,) = totals(over_o, over_a, over_b, ((0, MARGIN),), [])

time: 99.2 us -> 114 us (1.15)
  waiting for transfers between devices: 43.6 us -> 51.5 us
  starting transfers between devices: 22.7 us -> 29.6 us
    ppermute x6, waiting for transfers between devices: 19.1 us -> 41.5 us  [moved(): lax.ppermute(block, axis, [(n, (n + distance) % count) for n in range(cou...]
    ppermute x10, waiting for transfers between devices: 23.3 us -> 9.94 us  [to_far(): return lax.ppermute(block, ('row', 'col'), route)]
    ppermute x10, starting transfers between devices: 6.6 us -> 13 us  [to_far(): return lax.ppermute(block, ('row', 'col'), route)]
    ppermute x10, starting transfers between devices: 4.79 us -> 6.28 us  [to_near(): lax.ppermute(block, ('row', 'col'), [(r * cols + c, r * cols + (c ^ 1)) f...]
    ppermute x10, waiting for transfers between devices: 1.22 us -> 0.03 us  [to_near(): lax.ppermute(block, ('row', 'col'), [(r * cols + c, r * cols + (c ^ 1)) f...]
  transfers between devices with their start and end apart: 26 -> 26, of which waited for: 14 -> 9; matrix products, arithmetic and copies ran while one was open for 0% -> 0% of each run, Pallas kernels for 27% -> 21%
where the time goes in v6:
time: 114 us
  waiting for transfers between devices  51.5 us (45%)
  Pallas kernels  30.3 us (27%)
  starting transfers between devices  29.6 us (26%)
  local copies, waits for them, and re-layouts  1.93 us (2%)
    ppermute x6, waiting for transfers between devices, moved(): lax.ppermute(block, axis, [(n, (n + distance) % count) for n in range(cou...  41.5 us
    pallas_call x8, Pallas kernels, window(): pl.pallas_call(kernel, out_shape=tuple(shapes), in_specs=[pl.BlockSpec(me...  21.2 us
    ppermute x10, starting transfers between devices, to_far(): return lax.ppermute(block, ('row', 'col'), route)  13 us
    ppermute x6, starting transfers between devices, moved(): lax.ppermute(block, axis, [(n, (n + distance) % count) for n in range(cou...  10.3 us
    ppermute x10, waiting for transfers between devices, to_far(): return lax.ppermute(block, ('row', 'col'), route)  9.94 us
    ppermute x10, starting transfers between devices, to_near(): lax.ppermute(block, ('row', 'col'), [(r * cols + c, r * cols + (c ^ 1)) f...  6.28 us
    pallas_call x4, Pallas kernels, variation(): pl.pallas_call(functools.partial(variation_kernel, *plan), out_shape=jax....  5.33 us
  transfers between devices with their start and end apart: 26, of which 9 were waited for; matrix products, arithmetic and copies ran while one was open for 0% of the time, Pallas kernels for 21%

profile of v6, /device:TPU:0, one launch (start us, length us, event | category | flops | bytes accessed | tf_op | source)
XLA Modules:
  0.0 113.8 jit_solution(9459761526736213413)
XLA Ops:
  0.0 1.9 %fusion = (f32[2,96,384]{2,1,0:T(8,128)}, f32[2,96,384]{2,1,0:T(8,128)S(1)}) fusion(f32[2,384,384]{2,1,0:T(8,128)} %refs_0_.13), kind=kLoop, calls=%fused_computation.6 | loop fusion | bytes 1179648 | tf_op jit(solution)/shard_map/slice | solution.py:502
  1.9 3.0 %collective-permute-start = (f32[2,96,384]{2,1,0:T(8,128)}, f32[2,96,384]{2,1,0:T(8,128)S(1)}, u32[]{:S(2)}, u32[]{:S(2)}) collective-permute-start(f32[2,96,384]{2,1,0:T(8,128)} %get-tuple-element.105), channel_id=1, source_target_pairs={{0,4},{4,8},{8,12},{12,16},{16,20},{20,24},{24,28},{28,0},{1,5},{5... | collective-permute-start | bytes 884744 | tf_op jit(solution)/shard_map/ppermute | solution.py:469
  5.1 1.6 %collective-permute-start.2 = (f32[2,384,128]{2,1,0:T(8,128)S(1)}, f32[2,384,128]{2,1,0:T(8,128)S(1)}, u32[]{:S(2)}, u32[]{:S(2)}) collective-permute-start(f32[2,384,128]{2,1,0:T(8,128)S(1)} %get-tuple-element.104), channel_id=1, source_target_pairs={{0,3},{1,2},{2,1},{3,0},{4,7},{5,6},{6,5},{7,4},{8,11},{9,10},{10,... | collective-permute-start | bytes 1179656 | tf_op jit(solution)/shard_map/ppermute | solution.py:485
  6.7 8.5 %collective-permute-done.refs_7_.refs_2_.refs_0_ = f32[2,96,384]{2,1,0:T(8,128)S(1)} collective-permute-done((f32[2,96,384]{2,1,0:T(8,128)}, f32[2,96,384]{2,1,0:T(8,128)S(1)}, u32[]{:S(2)}, u32[]{:S(2)}) %collective-permute-start) | collective-permute-done | bytes 294944 | tf_op jit(solution)/shard_map/ppermute | solution.py:469
  15.2 1.7 %collective-permute-start.7 = (f32[2,96,384]{2,1,0:T(8,128)S(1)}, f32[2,96,384]{2,1,0:T(8,128)S(1)}, u32[]{:S(2)}, u32[]{:S(2)}) collective-permute-start(f32[2,96,384]{2,1,0:T(8,128)S(1)} %get-tuple-element.64), channel_id=1, source_target_pairs={{0,28},{4,0},{8,4},{12,8},{16,12},{20,16},{24,20},{28,24},{1,29},{... | collective-permute-start | bytes 884744 | tf_op jit(solution)/shard_map/ppermute | solution.py:469
  17.0 1.6 %collective-permute-start.1 = (f32[2,96,128]{2,1,0:T(8,128)S(1)}, f32[2,96,128]{2,1,0:T(8,128)S(1)}, u32[]{:S(2)}, u32[]{:S(2)}) collective-permute-start(f32[2,96,128]{2,1,0:T(8,128)S(1)} %get-tuple-element.110), channel_id=1, source_target_pairs={{0,3},{1,2},{2,1},{3,0},{4,7},{5,6},{6,5},{7,4},{8,11},{9,10},{10,... | collective-permute-start | bytes 294920 | tf_op jit(solution)/shard_map/ppermute | solution.py:485
  18.7 1.8 %prepare.1 = (f32[4,2,256,256]{3,2,1,0:T(8,128)S(1)}, f32[4,512,128]{2,1,0:T(8,128)S(1)}) custom-call(s32[2,2,2]{2,1,0:T(2,128)S(1)} %copy-done.5, f32[2,256,256]{2,1,0:T(8,128)S(1)} %copy-done.4, f32[512,512]{1,0:T(8,128)S(1)} %copy-done.3, bf16[256,256]{1,0:T(8,128)(2,1)S(1)} %copy-done.6), custom_call_target="tpu_custom_call" | custom-call | flops 100000 | bytes 100000 | tf_op jit(solution)/shard_map/prepare/pallas_call | solution.py:105
  20.5 2.6 %shard_map.73 = (f32[2,192,384]{2,1,0:T(8,128)S(1)}, f32[2,192,128]{2,1,0:T(8,128)S(1)}, f32[2,192,384]{2,1,0:T(8,128)S(1)}, f32[2,192,128]{2,1,0:T(8,128)S(1)}) custom-call(s32[2,2,2]{2,1,0:T(2,128)S(1)} %copy-done.5, bf16[4,256,256]{2,1,0:T(8,128)(2,1)S(1)} %copy-done.1, f32[4,128,128]{2,1,0:T(8,128)S(1)} %copy-done.2, ...), custom_call_target="tpu_custom_call" | custom-call | flops 100000 | bytes 100000 | tf_op jit(solution)/shard_map/pallas_call | solution.py:302
  23.1 2.7 %shard_map.74 = (f32[2,192,384]{2,1,0:T(8,128)S(1)}, f32[2,192,128]{2,1,0:T(8,128)S(1)}, f32[2,192,384]{2,1,0:T(8,128)S(1)}, f32[2,192,128]{2,1,0:T(8,128)S(1)}) custom-call(s32[2,2,2]{2,1,0:T(2,128)S(1)} %copy-done.5, bf16[4,256,256]{2,1,0:T(8,128)(2,1)S(1)} %copy-done.1, f32[4,128,128]{2,1,0:T(8,128)S(1)} %copy-done.2, ...), custom_call_target="tpu_custom_call" | custom-call | flops 100000 | bytes 100000 | tf_op jit(solution)/shard_map/pallas_call | solution.py:302
  25.8 0.4 collective-permute-start.6
  26.2 0.3 collective-permute-start.5
  26.5 1.3 %collective-permute-start.9 = (f32[2,96,128]{2,1,0:T(8,128)S(1)}, f32[2,96,128]{2,1,0:T(8,128)S(1)}, u32[]{:S(2)}, u32[]{:S(2)}) collective-permute-start(f32[2,96,128]{2,1,0:T(8,128)S(1)} %get-tuple-element.107), channel_id=1, source_target_pairs={{0,3},{1,2},{2,1},{3,0},{4,7},{5,6},{6,5},{7,4},{8,11},{9,10},{10,... | collective-permute-start | bytes 294920 | tf_op jit(solution)/shard_map/ppermute | solution.py:485
  27.8 0.4 collective-permute-start.8
  28.2 1.3 %variation.4.refs_0_ = f32[2,192,384]{2,1,0:T(8,128)S(1)} custom-call(f32[2,96,128]{2,1,0:T(8,128)S(1)} %collective-permute-done.3.refs_5_.refs_0_, f32[2,384,128]{2,1,0:T(8,128)S(1)} %collective-permute-done.4.refs_6_.refs_1_.refs_5_.refs_0_, f32[2,96,384]{2,1,0:T(8,128)S(1)} %collective-permute-done.refs_7_.refs_2_.refs_0_, f32[2,384,384]{2,1,0:T(8,128)S(1)} %copy-done, ...), custom_call_target="tpu_custom_call" | custom-call | flops 100000 | bytes 100000 | tf_op jit(solution)/shard_map/variation/pallas_call | solution.py:363
  29.6 3.2 %collective-permute-done.6.far_ref = f32[2,192,128]{2,1,0:T(8,128)S(1)} collective-permute-done((f32[2,192,128]{2,1,0:T(8,128)S(1)}, f32[2,192,128]{2,1,0:T(8,128)S(1)}, u32[]{:S(2)}, u32[]{:S(2)}) %collective-permute-start.6) | collective-permute-done | bytes 196640 | tf_op jit(solution)/shard_map/ppermute | solution.py:485
  32.9 2.0 %collective-permute-done.9.refs_6_.refs_5_ = f32[2,96,128]{2,1,0:T(8,128)S(1)} collective-permute-done((f32[2,96,128]{2,1,0:T(8,128)S(1)}, f32[2,96,128]{2,1,0:T(8,128)S(1)}, u32[]{:S(2)}, u32[]{:S(2)}) %collective-permute-start.9) | collective-permute-done | bytes 98336 | tf_op jit(solution)/shard_map/ppermute | solution.py:485
  34.9 2.6 %shard_map.75 = (f32[2,384,384]{2,1,0:T(8,128)S(1)}, f32[2,384,128]{2,1,0:T(8,128)S(1)}) custom-call(s32[2,2,2]{2,1,0:T(2,128)S(1)} %copy-done.5, bf16[4,256,256]{2,1,0:T(8,128)(2,1)S(1)} %copy-done.1, f32[4,128,128]{2,1,0:T(8,128)S(1)} %copy-done.2, f32[4,2,256,256]{3,2,1,0:T(8,128)S(1)} %get-tuple-element.55.refs_3_, ...), custom_call_target="tpu_custom_call" | custom-call | flops 100000 | bytes 100000 | tf_op jit(solution)/shard_map/pallas_call | solution.py:302
  37.6 2.7 %shard_map.76 = (f32[2,384,384]{2,1,0:T(8,128)S(1)}, f32[2,384,128]{2,1,0:T(8,128)S(1)}) custom-call(s32[2,2,2]{2,1,0:T(2,128)S(1)} %copy-done.5, bf16[4,256,256]{2,1,0:T(8,128)(2,1)S(1)} %copy-done.1, f32[4,128,128]{2,1,0:T(8,128)S(1)} %copy-done.2, f32[4,2,256,256]{3,2,1,0:T(8,128)S(1)} %get-tuple-element.55.refs_3_, ...), custom_call_target="tpu_custom_call" | custom-call | flops 100000 | bytes 100000 | tf_op jit(solution)/shard_map/pallas_call | solution.py:302
  40.3 0.2 collective-permute-start.10
  40.5 0.7 collective-permute-start.11
  41.1 1.5 %collective-permute-start.13 = (f32[2,192,384]{2,1,0:T(8,128)S(1)}, f32[2,192,384]{2,1,0:T(8,128)S(1)}, u32[]{:S(2)}, u32[]{:S(2)}) collective-permute-start(f32[2,192,384]{2,1,0:T(8,128)S(1)} %totals.5.refs_2_), channel_id=1, source_target_pairs={{0,28},{4,0},{8,4},{12,8},{16,12},{20,16},{24,20},{28,24},{1,29},{... | collective-permute-start | bytes 1769480 | tf_op jit(solution)/shard_map/ppermute | solution.py:469
  42.6 1.3 %variation.5.refs_1_ = f32[2,192,384]{2,1,0:T(8,128)S(1)} custom-call(f32[2,384,128]{2,1,0:T(8,128)S(1)} %collective-permute-done.4.refs_6_.refs_1_.refs_5_.refs_0_, f32[2,96,128]{2,1,0:T(8,128)S(1)} %collective-permute-done.8.refs_6_.refs_1_, f32[2,384,384]{2,1,0:T(8,128)S(1)} %copy-done, f32[2,96,384]{2,1,0:T(8,128)S(1)} %collective-permute-done.7.refs_8_.refs_3_.refs_1_, ...), custom_call_target="tpu_custom_call" | custom-call | flops 100000 | bytes 100000 | tf_op jit(solution)/shard_map/variation/pallas_call | solution.py:363
  44.0 0.2 totals.6
  44.2 0.7 collective-permute-start.12
  44.8 24.4 %collective-permute-done.13.refs_4_ = f32[2,192,384]{2,1,0:T(8,128)S(1)} collective-permute-done((f32[2,192,384]{2,1,0:T(8,128)S(1)}, f32[2,192,384]{2,1,0:T(8,128)S(1)}, u32[]{:S(2)}, u32[]{:S(2)}) %collective-permute-start.13) | collective-permute-done | bytes 589856 | tf_op jit(solution)/shard_map/ppermute | solution.py:469
  69.2 0.2 update.3
  69.4 0.7 collective-permute-start.17
  70.1 0.9 collective-permute-start.15
  71.2 1.4 %collective-permute-start.16 = (f32[2,192,128]{2,1,0:T(8,128)S(1)}, f32[2,192,128]{2,1,0:T(8,128)S(1)}, u32[]{:S(2)}, u32[]{:S(2)}) collective-permute-start(f32[2,192,128]{2,1,0:T(8,128)S(1)} %get-tuple-element.79), channel_id=1, source_target_pairs={{0,1},{1,0},{2,3},{3,2},{4,5},{5,4},{6,7},{7,6},{8,9},{9,8},{10,11... | collective-permute-start | bytes 589832 | tf_op jit(solution)/shard_map/ppermute | solution.py:474
  72.6 2.6 %shard_map.77 = (f32[2,192,384]{2,1,0:T(8,128)S(1)}, f32[2,192,128]{2,1,0:T(8,128)S(1)}, f32[2,192,384]{2,1,0:T(8,128)S(1)}, f32[2,192,128]{2,1,0:T(8,128)S(1)}) custom-call(s32[2,2,2]{2,1,0:T(2,128)S(1)} %copy-done.5, bf16[4,256,256]{2,1,0:T(8,128)(2,1)S(1)} %copy-done.1, f32[4,128,128]{2,1,0:T(8,128)S(1)} %copy-done.2, ...), custom_call_target="tpu_custom_call" | custom-call | flops 100000 | bytes 100000 | tf_op jit(solution)/shard_map/pallas_call | solution.py:302
  75.2 2.6 %shard_map.78 = (f32[2,192,384]{2,1,0:T(8,128)S(1)}, f32[2,192,128]{2,1,0:T(8,128)S(1)}, f32[2,192,384]{2,1,0:T(8,128)S(1)}, f32[2,192,128]{2,1,0:T(8,128)S(1)}) custom-call(s32[2,2,2]{2,1,0:T(2,128)S(1)} %copy-done.5, bf16[4,256,256]{2,1,0:T(8,128)(2,1)S(1)} %copy-done.1, f32[4,128,128]{2,1,0:T(8,128)S(1)} %copy-done.2, ...), custom_call_target="tpu_custom_call" | custom-call | flops 100000 | bytes 100000 | tf_op jit(solution)/shard_map/pallas_call | solution.py:302
  77.9 1.7 %collective-permute-start.19 = (f32[2,192,128]{2,1,0:T(8,128)S(1)}, f32[2,192,128]{2,1,0:T(8,128)S(1)}, u32[]{:S(2)}, u32[]{:S(2)}) collective-permute-start(f32[2,192,128]{2,1,0:T(8,128)S(1)} %get-tuple-element.91), channel_id=1, source_target_pairs={{0,3},{1,2},{2,1},{3,0},{4,7},{5,6},{6,5},{7,4},{8,11},{9,10},{10,... | collective-permute-start | bytes 589832 | tf_op jit(solution)/shard_map/ppermute | solution.py:485
  79.6 2.6 %collective-permute-start.18 = (f32[2,192,128]{2,1,0:T(8,128)S(1)}, f32[2,192,128]{2,1,0:T(8,128)S(1)}, u32[]{:S(2)}, u32[]{:S(2)}) collective-permute-start(f32[2,192,128]{2,1,0:T(8,128)S(1)} %get-tuple-element.90), channel_id=1, source_target_pairs={{0,1},{1,0},{2,3},{3,2},{4,5},{5,4},{6,7},{7,6},{8,9},{9,8},{10,11... | collective-permute-start | bytes 589832 | tf_op jit(solution)/shard_map/ppermute | solution.py:474
  82.1 1.6 %collective-permute-start.14 = (f32[2,192,128]{2,1,0:T(8,128)S(1)}, f32[2,192,128]{2,1,0:T(8,128)S(1)}, u32[]{:S(2)}, u32[]{:S(2)}) collective-permute-start(f32[2,192,128]{2,1,0:T(8,128)S(1)} %get-tuple-element.77), channel_id=1, source_target_pairs={{0,3},{1,2},{2,1},{3,0},{4,7},{5,6},{6,5},{7,4},{8,11},{9,10},{10,... | collective-permute-start | bytes 589832 | tf_op jit(solution)/shard_map/ppermute | solution.py:485
  83.7 1.3 %variation.6.refs_0_.refs_1_ = f32[2,192,384]{2,1,0:T(8,128)S(1)} custom-call(f32[2,384,128]{2,1,0:T(8,128)S(1)} %collective-permute-done.17.refs_5_.refs_6_.refs_0_.refs_1_, f32[2,384,384]{2,1,0:T(8,128)S(1)} %get-tuple-element.76.refs_6_.refs_8_.refs_1_.refs_3_.bottom_ref, f32[2,384,128]{2,1,0:T(8,128)S(1)} %collective-permute-done.15.refs_5_.refs_2_.refs_6_), custom_call_target="tpu_custom_call" | custom-call | flops 100000 | bytes 100000 | tf_op jit(solution)/shard_map/variation/pallas_call | solution.py:363
  85.1 2.6 %shard_map.79 = (f32[2,96,384]{2,1,0:T(8,128)S(1)}, f32[2,96,128]{2,1,0:T(8,128)S(1)}, f32[2,288,384]{2,1,0:T(8,128)S(1)}, f32[2,288,128]{2,1,0:T(8,128)S(1)}) custom-call(s32[2,2,2]{2,1,0:T(2,128)S(1)} %copy-done.5, bf16[4,256,256]{2,1,0:T(8,128)(2,1)S(1)} %copy-done.1, f32[4,128,128]{2,1,0:T(8,128)S(1)} %copy-done.2, ...), custom_call_target="tpu_custom_call" | custom-call | flops 100000 | bytes 100000 | tf_op jit(solution)/shard_map/pallas_call | solution.py:302
  87.8 1.4 %collective-permute-done.14.refs_5_.refs_4_ = f32[2,192,128]{2,1,0:T(8,128)S(1)} collective-permute-done((f32[2,192,128]{2,1,0:T(8,128)S(1)}, f32[2,192,128]{2,1,0:T(8,128)S(1)}, u32[]{:S(2)}, u32[]{:S(2)}) %collective-permute-start.14) | collective-permute-done | bytes 196640 | tf_op jit(solution)/shard_map/ppermute | solution.py:485
  89.3 2.6 %shard_map.80 = (f32[2,96,384]{2,1,0:T(8,128)S(1)}, f32[2,96,128]{2,1,0:T(8,128)S(1)}, f32[2,288,384]{2,1,0:T(8,128)S(1)}, f32[2,288,128]{2,1,0:T(8,128)S(1)}) custom-call(s32[2,2,2]{2,1,0:T(2,128)S(1)} %copy-done.5, bf16[4,256,256]{2,1,0:T(8,128)(2,1)S(1)} %copy-done.1, f32[4,128,128]{2,1,0:T(8,128)S(1)} %copy-done.2, ...), custom_call_target="tpu_custom_call" | custom-call | flops 100000 | bytes 100000 | tf_op jit(solution)/shard_map/pallas_call | solution.py:302
  91.9 2.0 %collective-permute-start.24 = (f32[2,96,128]{2,1,0:T(8,128)S(1)}, f32[2,96,128]{2,1,0:T(8,128)S(1)}, u32[]{:S(2)}, u32[]{:S(2)}) collective-permute-start(f32[2,96,128]{2,1,0:T(8,128)S(1)} %get-tuple-element.102), channel_id=1, source_target_pairs={{0,3},{1,2},{2,1},{3,0},{4,7},{5,6},{6,5},{7,4},{8,11},{9,10},{10,... | collective-permute-start | bytes 294920 | tf_op jit(solution)/shard_map/ppermute | solution.py:485
  93.9 0.5 collective-permute-start.23
  94.4 1.3 %collective-permute-start.21 = (f32[2,288,128]{2,1,0:T(8,128)S(1)}, f32[2,288,128]{2,1,0:T(8,128)S(1)}, u32[]{:S(2)}, u32[]{:S(2)}) collective-permute-start(f32[2,288,128]{2,1,0:T(8,128)S(1)} %get-tuple-element.97), channel_id=1, source_target_pairs={{0,3},{1,2},{2,1},{3,0},{4,7},{5,6},{6,5},{7,4},{8,11},{9,10},{10,... | collective-permute-start | bytes 884744 | tf_op jit(solution)/shard_map/ppermute | solution.py:485
  95.7 1.4 %collective-permute-done.24.far_ref = f32[2,96,128]{2,1,0:T(8,128)S(1)} collective-permute-done((f32[2,96,128]{2,1,0:T(8,128)S(1)}, f32[2,96,128]{2,1,0:T(8,128)S(1)}, u32[]{:S(2)}, u32[]{:S(2)}) %collective-permute-start.24) | collective-permute-done | bytes 98336 | tf_op jit(solution)/shard_map/ppermute | solution.py:485
  97.2 3.4 %collective-permute-start.25 = (f32[2,96,384]{2,1,0:T(8,128)S(1)}, f32[2,96,384]{2,1,0:T(8,128)S(1)}, u32[]{:S(2)}, u32[]{:S(2)}) collective-permute-start(f32[2,96,384]{2,1,0:T(8,128)S(1)} %totals.9), channel_id=1, source_target_pairs={{0,28},{4,0},{8,4},{12,8},{16,12},{20,16},{24,20},{28,24},{1,29},{... | collective-permute-start | bytes 884744 | tf_op jit(solution)/shard_map/ppermute | solution.py:469
  100.5 1.3 %variation.7.refs_0_ = f32[2,192,384]{2,1,0:T(8,128)S(1)} custom-call(f32[2,192,128]{2,1,0:T(8,128)S(1)} %collective-permute-done.16.refs_5_.refs_0_, f32[2,384,128]{2,1,0:T(8,128)S(1)} %collective-permute-done.17.refs_5_.refs_6_.refs_0_.refs_1_, f32[2,192,384]{2,1,0:T(8,128)S(1)} %get-tuple-element.74.refs_7_.refs_2_.top_ref, ...), custom_call_target="tpu_custom_call" | custom-call | flops 100000 | bytes 100000 | tf_op jit(solution)/shard_map/variation/pallas_call | solution.py:363
  101.9 1.8 %collective-permute-done.21.far_ref = f32[2,288,128]{2,1,0:T(8,128)S(1)} collective-permute-done((f32[2,288,128]{2,1,0:T(8,128)S(1)}, f32[2,288,128]{2,1,0:T(8,128)S(1)}, u32[]{:S(2)}, u32[]{:S(2)}) %collective-permute-start.21) | collective-permute-done | bytes 294944 | tf_op jit(solution)/shard_map/ppermute | solution.py:485
  103.9 5.4 %collective-permute-done.22.above_ref = f32[2,96,384]{2,1,0:T(8,128)S(1)} collective-permute-done((f32[2,96,384]{2,1,0:T(8,128)S(1)}, f32[2,96,384]{2,1,0:T(8,128)S(1)}, u32[]{:S(2)}, u32[]{:S(2)}) %collective-permute-start.22) | collective-permute-done | bytes 294944 | tf_op jit(solution)/shard_map/ppermute | solution.py:469
  109.3 3.3 %collective-permute-done.25.below_ref = f32[2,96,384]{2,1,0:T(8,128)S(1)} collective-permute-done((f32[2,96,384]{2,1,0:T(8,128)S(1)}, f32[2,96,384]{2,1,0:T(8,128)S(1)}, u32[]{:S(2)}, u32[]{:S(2)}) %collective-permute-start.25) | collective-permute-done | bytes 294944 | tf_op jit(solution)/shard_map/ppermute | solution.py:469
  112.6 1.2 %finish.1 = f32[2,384,384]{2,1,0:T(8,128)} custom-call(f32[2,192,384]{2,1,0:T(8,128)S(1)} %get-tuple-element.74.refs_7_.refs_2_.top_ref, f32[2,384,384]{2,1,0:T(8,128)S(1)} %get-tuple-element.76.refs_6_.refs_8_.refs_1_.refs_3_.bottom_ref, f32[2,288,384]{2,1,0:T(8,128)S(1)} %totals.8.mid_ref, f32[2,96,384]{2,1,0:T(8,128)S(1)} %get-tuple-element.98.low_ref, ...), custom_call_target="tpu_custom_call" | custom-call | flops 100000 | bytes 100000 | tf_op jit(solution)/shard_map/finish/pallas_call | solution.py:456
  (43 shorter events, 0.8 us)
Async XLA Ops:
  0.0 4.9 %copy-start = (f32[2,384,384]{2,1,0:T(8,128)S(1)}, f32[2,384,384]{2,1,0:T(8,128)}, u32[]{:S(2)}) copy-start(f32[2,384,384]{2,1,0:T(8,128)} %refs_0_.13) | copy-start | bytes 3538948
  1.9 16.8 %copy-start.3 = (f32[512,512]{1,0:T(8,128)S(1)}, f32[512,512]{1,0:T(8,128)}, u32[]{:S(2)}) copy-start(f32[512,512]{1,0:T(8,128)} %amp_ref.1) | copy-start | bytes 3145732
  1.9 16.8 %copy-start.4 = (f32[2,256,256]{2,1,0:T(8,128)S(1)}, f32[2,256,256]{2,1,0:T(8,128)}, u32[]{:S(2)}) copy-start(f32[2,256,256]{2,1,0:T(8,128)} %probe_ref.1) | copy-start | bytes 1572868
  1.9 16.8 %copy-start.5 = (s32[2,2,2]{2,1,0:T(2,128)S(1)}, s32[2,2,2]{2,1,0:T(2,128)}, u32[]{:S(2)}) copy-start(s32[2,2,2]{2,1,0:T(2,128)} %refs_0_.17) | copy-start | bytes 100
  1.9 16.8 %copy-start.6 = (bf16[256,256]{1,0:T(8,128)(2,1)S(1)}, bf16[256,256]{1,0:T(8,128)(2,1)}, u32[]{:S(2)}) copy-start(bf16[256,256]{1,0:T(8,128)(2,1)} %constant.30.clone.order_ref) | copy-start | bytes 393220
  1.9 13.3 %collective-permute-start = (f32[2,96,384]{2,1,0:T(8,128)}, f32[2,96,384]{2,1,0:T(8,128)S(1)}, u32[]{:S(2)}, u32[]{:S(2)}) collective-permute-start(f32[2,96,384]{2,1,0:T(8,128)} %get-tuple-element.105), channel_id=1, source_target_pairs={{0,4},{4,8},{8,12},{12,16},{16,20},{20,24},{24,28},{28,0},{1,5},{5... | collective-permute-start | bytes 884744 | tf_op jit(solution)/shard_map/ppermute | solution.py:469
  5.0 15.5 %copy-start.1 = (bf16[4,256,256]{2,1,0:T(8,128)(2,1)S(1)}, bf16[4,256,256]{2,1,0:T(8,128)(2,1)}, u32[]{:S(2)}) copy-start(bf16[4,256,256]{2,1,0:T(8,128)(2,1)} %constant.28.clone.refs_1_) | copy-start | bytes 1572868
  5.0 15.5 %copy-start.2 = (f32[4,128,128]{2,1,0:T(8,128)S(1)}, f32[4,128,128]{2,1,0:T(8,128)}, u32[]{:S(2)}) copy-start(f32[4,128,128]{2,1,0:T(8,128)} %constant.29.clone.refs_2_) | copy-start | bytes 786436
  5.0 15.4 %collective-permute-start.4 = (f32[2,384,128]{2,1,0:T(8,128)S(1)}, f32[2,384,128]{2,1,0:T(8,128)S(1)}, u32[]{:S(2)}, u32[]{:S(2)}) collective-permute-start(f32[2,384,128]{2,1,0:T(8,128)S(1)} %get-tuple-element.103), channel_id=1, source_target_pairs={{0,1},{1,0},{2,3},{3,2},{4,5},{5,4},{6,7},{7,6},{8,9},{9,8},{10,11... | collective-permute-start | bytes 1179656 | tf_op jit(solution)/shard_map/ppermute | solution.py:474
  5.1 18.0 %collective-permute-start.2 = (f32[2,384,128]{2,1,0:T(8,128)S(1)}, f32[2,384,128]{2,1,0:T(8,128)S(1)}, u32[]{:S(2)}, u32[]{:S(2)}) collective-permute-start(f32[2,384,128]{2,1,0:T(8,128)S(1)} %get-tuple-element.104), channel_id=1, source_target_pairs={{0,3},{1,2},{2,1},{3,0},{4,7},{5,6},{6,5},{7,4},{8,11},{9,10},{10,... | collective-permute-start | bytes 1179656 | tf_op jit(solution)/shard_map/ppermute | solution.py:485
  15.2 11.3 %collective-permute-start.7 = (f32[2,96,384]{2,1,0:T(8,128)S(1)}, f32[2,96,384]{2,1,0:T(8,128)S(1)}, u32[]{:S(2)}, u32[]{:S(2)}) collective-permute-start(f32[2,96,384]{2,1,0:T(8,128)S(1)} %get-tuple-element.64), channel_id=1, source_target_pairs={{0,28},{4,0},{8,4},{12,8},{16,12},{20,16},{24,20},{28,24},{1,29},{... | collective-permute-start | bytes 884744 | tf_op jit(solution)/shard_map/ppermute | solution.py:469
  17.0 3.5 %collective-permute-start.3 = (f32[2,96,128]{2,1,0:T(8,128)S(1)}, f32[2,96,128]{2,1,0:T(8,128)S(1)}, u32[]{:S(2)}, u32[]{:S(2)}) collective-permute-start(f32[2,96,128]{2,1,0:T(8,128)S(1)} %get-tuple-element.109), channel_id=1, source_target_pairs={{0,1},{1,0},{2,3},{3,2},{4,5},{5,4},{6,7},{7,6},{8,9},{9,8},{10,11... | collective-permute-start | bytes 294920 | tf_op jit(solution)/shard_map/ppermute | solution.py:474
  17.0 6.1 %collective-permute-start.1 = (f32[2,96,128]{2,1,0:T(8,128)S(1)}, f32[2,96,128]{2,1,0:T(8,128)S(1)}, u32[]{:S(2)}, u32[]{:S(2)}) collective-permute-start(f32[2,96,128]{2,1,0:T(8,128)S(1)} %get-tuple-element.110), channel_id=1, source_target_pairs={{0,3},{1,2},{2,1},{3,0},{4,7},{5,6},{6,5},{7,4},{8,11},{9,10},{10,... | collective-permute-start | bytes 294920 | tf_op jit(solution)/shard_map/ppermute | solution.py:485
  25.8 7.0 %collective-permute-start.6 = (f32[2,192,128]{2,1,0:T(8,128)S(1)}, f32[2,192,128]{2,1,0:T(8,128)S(1)}, u32[]{:S(2)}, u32[]{:S(2)}) collective-permute-start(f32[2,192,128]{2,1,0:T(8,128)S(1)} %get-tuple-element.62), channel_id=1, source_target_pairs={{0,3},{1,2},{2,1},{3,0},{4,7},{5,6},{6,5},{7,4},{8,11},{9,10},{10,... | collective-permute-start | bytes 589832 | tf_op jit(solution)/shard_map/ppermute | solution.py:485
  26.2 6.6 %collective-permute-start.5 = (f32[2,192,128]{2,1,0:T(8,128)S(1)}, f32[2,192,128]{2,1,0:T(8,128)S(1)}, u32[]{:S(2)}, u32[]{:S(2)}) collective-permute-start(f32[2,192,128]{2,1,0:T(8,128)S(1)} %get-tuple-element.61), channel_id=1, source_target_pairs={{0,1},{1,0},{2,3},{3,2},{4,5},{5,4},{6,7},{7,6},{8,9},{9,8},{10,11... | collective-permute-start | bytes 589832 | tf_op jit(solution)/shard_map/ppermute | solution.py:474
  26.5 8.4 %collective-permute-start.9 = (f32[2,96,128]{2,1,0:T(8,128)S(1)}, f32[2,96,128]{2,1,0:T(8,128)S(1)}, u32[]{:S(2)}, u32[]{:S(2)}) collective-permute-start(f32[2,96,128]{2,1,0:T(8,128)S(1)} %get-tuple-element.107), channel_id=1, source_target_pairs={{0,3},{1,2},{2,1},{3,0},{4,7},{5,6},{6,5},{7,4},{8,11},{9,10},{10,... | collective-permute-start | bytes 294920 | tf_op jit(solution)/shard_map/ppermute | solution.py:485
  27.8 9.8 %collective-permute-start.8 = (f32[2,96,128]{2,1,0:T(8,128)S(1)}, f32[2,96,128]{2,1,0:T(8,128)S(1)}, u32[]{:S(2)}, u32[]{:S(2)}) collective-permute-start(f32[2,96,128]{2,1,0:T(8,128)S(1)} %get-tuple-element.108), channel_id=1, source_target_pairs={{0,1},{1,0},{2,3},{3,2},{4,5},{5,4},{6,7},{7,6},{8,9},{9,8},{10,11... | collective-permute-start | bytes 294920 | tf_op jit(solution)/shard_map/ppermute | solution.py:474
  40.3 3.7 %collective-permute-start.10 = (f32[2,384,128]{2,1,0:T(8,128)S(1)}, f32[2,384,128]{2,1,0:T(8,128)S(1)}, u32[]{:S(2)}, u32[]{:S(2)}) collective-permute-start(f32[2,384,128]{2,1,0:T(8,128)S(1)} %get-tuple-element.71), channel_id=1, source_target_pairs={{0,1},{1,0},{2,3},{3,2},{4,5},{5,4},{6,7},{7,6},{8,9},{9,8},{10,11... | collective-permute-start | bytes 1179656 | tf_op jit(solution)/shard_map/ppermute | solution.py:474
  40.5 3.5 %collective-permute-start.11 = (f32[2,384,128]{2,1,0:T(8,128)S(1)}, f32[2,384,128]{2,1,0:T(8,128)S(1)}, u32[]{:S(2)}, u32[]{:S(2)}) collective-permute-start(f32[2,384,128]{2,1,0:T(8,128)S(1)} %get-tuple-element.72), channel_id=1, source_target_pairs={{1,2},{2,1},{5,6},{6,5},{9,10},{10,9},{13,14},{14,13},{17,18},{18,... | collective-permute-start | bytes 1179656 | tf_op jit(solution)/shard_map/ppermute | solution.py:485
  41.1 28.1 %collective-permute-start.13 = (f32[2,192,384]{2,1,0:T(8,128)S(1)}, f32[2,192,384]{2,1,0:T(8,128)S(1)}, u32[]{:S(2)}, u32[]{:S(2)}) collective-permute-start(f32[2,192,384]{2,1,0:T(8,128)S(1)} %totals.5.refs_2_), channel_id=1, source_target_pairs={{0,28},{4,0},{8,4},{12,8},{16,12},{20,16},{24,20},{28,24},{1,29},{... | collective-permute-start | bytes 1769480 | tf_op jit(solution)/shard_map/ppermute | solution.py:469
  44.2 26.8 %collective-permute-start.12 = (f32[2,192,384]{2,1,0:T(8,128)S(1)}, f32[2,192,384]{2,1,0:T(8,128)S(1)}, u32[]{:S(2)}, u32[]{:S(2)}) collective-permute-start(f32[2,192,384]{2,1,0:T(8,128)S(1)} %get-tuple-element.73.refs_3_), channel_id=1, source_target_pairs={{0,4},{4,8},{8,12},{12,16},{16,20},{20,24},{24,28},{28,0},{1,5},{5... | collective-permute-start | bytes 1769480 | tf_op jit(solution)/shard_map/ppermute | solution.py:469
  69.4 3.2 %collective-permute-start.17 = (f32[2,384,128]{2,1,0:T(8,128)S(1)}, f32[2,384,128]{2,1,0:T(8,128)S(1)}, u32[]{:S(2)}, u32[]{:S(2)}) collective-permute-start(f32[2,384,128]{2,1,0:T(8,128)S(1)} %get-tuple-element.80), channel_id=1, source_target_pairs={{0,1},{1,0},{2,3},{3,2},{4,5},{5,4},{6,7},{7,6},{8,9},{9,8},{10,11... | collective-permute-start | bytes 1179656 | tf_op jit(solution)/shard_map/ppermute | solution.py:474
  70.1 5.1 %collective-permute-start.15 = (f32[2,384,128]{2,1,0:T(8,128)S(1)}, f32[2,384,128]{2,1,0:T(8,128)S(1)}, u32[]{:S(2)}, u32[]{:S(2)}) collective-permute-start(f32[2,384,128]{2,1,0:T(8,128)S(1)} %get-tuple-element.78), channel_id=1, source_target_pairs={{1,2},{2,1},{5,6},{6,5},{9,10},{10,9},{13,14},{14,13},{17,18},{18,... | collective-permute-start | bytes 1179656 | tf_op jit(solution)/shard_map/ppermute | solution.py:485
  71.2 13.9 %collective-permute-start.16 = (f32[2,192,128]{2,1,0:T(8,128)S(1)}, f32[2,192,128]{2,1,0:T(8,128)S(1)}, u32[]{:S(2)}, u32[]{:S(2)}) collective-permute-start(f32[2,192,128]{2,1,0:T(8,128)S(1)} %get-tuple-element.79), channel_id=1, source_target_pairs={{0,1},{1,0},{2,3},{3,2},{4,5},{5,4},{6,7},{7,6},{8,9},{9,8},{10,11... | collective-permute-start | bytes 589832 | tf_op jit(solution)/shard_map/ppermute | solution.py:474
  77.9 9.8 %collective-permute-start.19 = (f32[2,192,128]{2,1,0:T(8,128)S(1)}, f32[2,192,128]{2,1,0:T(8,128)S(1)}, u32[]{:S(2)}, u32[]{:S(2)}) collective-permute-start(f32[2,192,128]{2,1,0:T(8,128)S(1)} %get-tuple-element.91), channel_id=1, source_target_pairs={{0,3},{1,2},{2,1},{3,0},{4,7},{5,6},{6,5},{7,4},{8,11},{9,10},{10,... | collective-permute-start | bytes 589832 | tf_op jit(solution)/shard_map/ppermute | solution.py:485
  79.6 8.2 %collective-permute-start.18 = (f32[2,192,128]{2,1,0:T(8,128)S(1)}, f32[2,192,128]{2,1,0:T(8,128)S(1)}, u32[]{:S(2)}, u32[]{:S(2)}) collective-permute-start(f32[2,192,128]{2,1,0:T(8,128)S(1)} %get-tuple-element.90), channel_id=1, source_target_pairs={{0,1},{1,0},{2,3},{3,2},{4,5},{5,4},{6,7},{7,6},{8,9},{9,8},{10,11... | collective-permute-start | bytes 589832 | tf_op jit(solution)/shard_map/ppermute | solution.py:474
  82.1 7.2 %collective-permute-start.14 = (f32[2,192,128]{2,1,0:T(8,128)S(1)}, f32[2,192,128]{2,1,0:T(8,128)S(1)}, u32[]{:S(2)}, u32[]{:S(2)}) collective-permute-start(f32[2,192,128]{2,1,0:T(8,128)S(1)} %get-tuple-element.77), channel_id=1, source_target_pairs={{0,3},{1,2},{2,1},{3,0},{4,7},{5,6},{6,5},{7,4},{8,11},{9,10},{10,... | collective-permute-start | bytes 589832 | tf_op jit(solution)/shard_map/ppermute | solution.py:485
  91.9 5.2 %collective-permute-start.24 = (f32[2,96,128]{2,1,0:T(8,128)S(1)}, f32[2,96,128]{2,1,0:T(8,128)S(1)}, u32[]{:S(2)}, u32[]{:S(2)}) collective-permute-start(f32[2,96,128]{2,1,0:T(8,128)S(1)} %get-tuple-element.102), channel_id=1, source_target_pairs={{0,3},{1,2},{2,1},{3,0},{4,7},{5,6},{6,5},{7,4},{8,11},{9,10},{10,... | collective-permute-start | bytes 294920 | tf_op jit(solution)/shard_map/ppermute | solution.py:485
  93.9 3.2 %collective-permute-start.23 = (f32[2,96,128]{2,1,0:T(8,128)S(1)}, f32[2,96,128]{2,1,0:T(8,128)S(1)}, u32[]{:S(2)}, u32[]{:S(2)}) collective-permute-start(f32[2,96,128]{2,1,0:T(8,128)S(1)} %get-tuple-element.101), channel_id=1, source_target_pairs={{0,1},{1,0},{2,3},{3,2},{4,5},{5,4},{6,7},{7,6},{8,9},{9,8},{10,11... | collective-permute-start | bytes 294920 | tf_op jit(solution)/shard_map/ppermute | solution.py:474
  94.4 9.3 %collective-permute-start.21 = (f32[2,288,128]{2,1,0:T(8,128)S(1)}, f32[2,288,128]{2,1,0:T(8,128)S(1)}, u32[]{:S(2)}, u32[]{:S(2)}) collective-permute-start(f32[2,288,128]{2,1,0:T(8,128)S(1)} %get-tuple-element.97), channel_id=1, source_target_pairs={{0,3},{1,2},{2,1},{3,0},{4,7},{5,6},{6,5},{7,4},{8,11},{9,10},{10,... | collective-permute-start | bytes 884744 | tf_op jit(solution)/shard_map/ppermute | solution.py:485
  95.7 8.0 %collective-permute-start.20 = (f32[2,288,128]{2,1,0:T(8,128)S(1)}, f32[2,288,128]{2,1,0:T(8,128)S(1)}, u32[]{:S(2)}, u32[]{:S(2)}) collective-permute-start(f32[2,288,128]{2,1,0:T(8,128)S(1)} %get-tuple-element.96), channel_id=1, source_target_pairs={{0,1},{1,0},{2,3},{3,2},{4,5},{5,4},{6,7},{7,6},{8,9},{9,8},{10,11... | collective-permute-start | bytes 884744 | tf_op jit(solution)/shard_map/ppermute | solution.py:474
  95.7 13.5 %collective-permute-start.22 = (f32[2,96,384]{2,1,0:T(8,128)S(1)}, f32[2,96,384]{2,1,0:T(8,128)S(1)}, u32[]{:S(2)}, u32[]{:S(2)}) collective-permute-start(f32[2,96,384]{2,1,0:T(8,128)S(1)} %get-tuple-element.99), channel_id=1, source_target_pairs={{0,4},{4,8},{8,12},{12,16},{16,20},{20,24},{24,28},{28,0},{1,5},{5... | collective-permute-start | bytes 884744 | tf_op jit(solution)/shard_map/ppermute | solution.py:469
  97.2 15.4 %collective-permute-start.25 = (f32[2,96,384]{2,1,0:T(8,128)S(1)}, f32[2,96,384]{2,1,0:T(8,128)S(1)}, u32[]{:S(2)}, u32[]{:S(2)}) collective-permute-start(f32[2,96,384]{2,1,0:T(8,128)S(1)} %totals.9), channel_id=1, source_target_pairs={{0,28},{4,0},{8,4},{12,8},{16,12},{20,16},{24,20},{28,24},{1,29},{... | collective-permute-start | bytes 884744 | tf_op jit(solution)/shard_map/ppermute | solution.py:469

commit v7 on v6

--- a/solution.py
+++ b/solution.py
@@ -534,7 +534,7 @@
     own = [(obj, MARGIN, last), (bottom, 0, MARGIN, "below")]
     whole = ((0, tile),)
     hi_o, hi_b = window(
-        1, False, consts, [(far, MARGIN, last), (bot_b, 0, MARGIN, "below")], own, [(mid_o, 0)], [(mid_b, 0)], whole
+        1, False, consts, [(far, MARGIN, last), (bot_b, 0, MARGIN, "below")], own, [(mid_o, 0)], [(mid_b, 0)], whole,
     )
     in_b = to_far(hi_b, ends=False)
     hi_o, hi_a = window(
@@ -567,8 +567,10 @@
     mid_o, mid_b, hi_o, hi_b = window(
         1, False, consts, [(low_b, 0, tile)], own, [(mid_o, 0), (hi_o, band)], [], halves
     )
-    hi_in_a, hi_in_b = in_a, to_far(hi_b)
+    hi_in_b = to_far(hi_b)
+    hi_in_a = in_a
     tv_bottom = variation([(low_a, 88, 208)], [(low, 88, 208)], [(low_b, 88, 208)])
+    top, hi_b = after((top, hi_b))
     up, near_strip, far_strip = update(
         (top, obj, top_sum, from_above),
         (

time: 114 us -> 104 us (0.912); the launches traced: 114 us -> 102 us
  waiting for transfers between devices: 51.5 us -> 33.4 us
  starting transfers between devices: 29.6 us -> 36.2 us
    ppermute x6, waiting for transfers between devices: 41.5 us -> 21.4 us  [moved(): lax.ppermute(block, axis, [(n, (n + distance) % count) for n in range(cou...]
    ppermute x10, starting transfers between devices: 6.28 us -> 12.2 us  [to_near(): lax.ppermute(block, ('row', 'col'), [(r * cols + c, r * cols + (c ^ 1)) f...]
    ppermute x6, starting transfers between devices: 10.3 us -> 13.9 us  [moved(): lax.ppermute(block, axis, [(n, (n + distance) % count) for n in range(cou...]
    ppermute x10, starting transfers between devices: 13 us -> 10.1 us  [to_far(): return lax.ppermute(block, ('row', 'col'), route)]
    ppermute x10, waiting for transfers between devices: 9.94 us -> 11.5 us  [to_far(): return lax.ppermute(block, ('row', 'col'), route)]
  transfers between devices with their start and end apart: 26 -> 26, of which waited for: 9 -> 10; matrix products, arithmetic and copies ran while one was open for 0% -> 0% of each run, Pallas kernels for 21% -> 26%
where the time goes in v7:
time: 104 us; the launch traced here: 102 us
  starting transfers between devices  36.2 us (35%)
  waiting for transfers between devices  33.4 us (32%)
  Pallas kernels  30.4 us (29%)
  local copies, waits for them, and re-layouts  1.93 us (2%)
    ppermute x6, waiting for transfers between devices, moved(): lax.ppermute(block, axis, [(n, (n + distance) % count) for n in range(cou...  21.4 us
    pallas_call x8, Pallas kernels, window(): pl.pallas_call(kernel, out_shape=tuple(shapes), in_specs=[pl.BlockSpec(me...  21.2 us
    ppermute x6, starting transfers between devices, moved(): lax.ppermute(block, axis, [(n, (n + distance) % count) for n in range(cou...  13.9 us
    ppermute x10, starting transfers between devices, to_near(): lax.ppermute(block, ('row', 'col'), [(r * cols + c, r * cols + (c ^ 1)) f...  12.2 us
    ppermute x10, waiting for transfers between devices, to_far(): return lax.ppermute(block, ('row', 'col'), route)  11.5 us
    ppermute x10, starting transfers between devices, to_far(): return lax.ppermute(block, ('row', 'col'), route)  10.1 us
    pallas_call x4, Pallas kernels, variation(): pl.pallas_call(functools.partial(variation_kernel, *plan), out_shape=jax....  5.33 us
  transfers between devices with their start and end apart: 26, of which 10 were waited for; matrix products, arithmetic and copies ran while one was open for 0% of the time, Pallas kernels for 26%

profile of v7, /device:TPU:0, one launch (start us, length us, event | category | flops | bytes accessed | tf_op | source)
XLA Modules:
  0.0 102.3 jit_solution(16426764399350786396)
XLA Ops:
  0.0 1.9 %fusion = (f32[2,96,384]{2,1,0:T(8,128)}, f32[2,96,384]{2,1,0:T(8,128)S(1)}) fusion(f32[2,384,384]{2,1,0:T(8,128)} %refs_1_.9), kind=kLoop, calls=%fused_computation.6 | loop fusion | bytes 1179648 | tf_op jit(solution)/shard_map/slice | solution.py:502
  1.9 3.0 %collective-permute-start = (f32[2,96,384]{2,1,0:T(8,128)}, f32[2,96,384]{2,1,0:T(8,128)S(1)}, u32[]{:S(2)}, u32[]{:S(2)}) collective-permute-start(f32[2,96,384]{2,1,0:T(8,128)} %get-tuple-element.107), channel_id=1, source_target_pairs={{0,4},{4,8},{8,12},{12,16},{16,20},{20,24},{24,28},{28,0},{1,5},{5... | collective-permute-start | bytes 884744 | tf_op jit(solution)/shard_map/ppermute | solution.py:469
  5.1 1.6 %collective-permute-start.3 = (f32[2,384,128]{2,1,0:T(8,128)S(1)}, f32[2,384,128]{2,1,0:T(8,128)S(1)}, u32[]{:S(2)}, u32[]{:S(2)}) collective-permute-start(f32[2,384,128]{2,1,0:T(8,128)S(1)} %get-tuple-element.106), channel_id=1, source_target_pairs={{0,3},{1,2},{2,1},{3,0},{4,7},{5,6},{6,5},{7,4},{8,11},{9,10},{10,... | collective-permute-start | bytes 1179656 | tf_op jit(solution)/shard_map/ppermute | solution.py:485
  6.7 8.5 %collective-permute-done.refs_7_.refs_2_.refs_0_ = f32[2,96,384]{2,1,0:T(8,128)S(1)} collective-permute-done((f32[2,96,384]{2,1,0:T(8,128)}, f32[2,96,384]{2,1,0:T(8,128)S(1)}, u32[]{:S(2)}, u32[]{:S(2)}) %collective-permute-start) | collective-permute-done | bytes 294944 | tf_op jit(solution)/shard_map/ppermute | solution.py:469
  15.2 1.7 %collective-permute-start.1 = (f32[2,96,384]{2,1,0:T(8,128)S(1)}, f32[2,96,384]{2,1,0:T(8,128)S(1)}, u32[]{:S(2)}, u32[]{:S(2)}) collective-permute-start(f32[2,96,384]{2,1,0:T(8,128)S(1)} %get-tuple-element.58), channel_id=1, source_target_pairs={{0,28},{4,0},{8,4},{12,8},{16,12},{20,16},{24,20},{28,24},{1,29},{... | collective-permute-start | bytes 884744 | tf_op jit(solution)/shard_map/ppermute | solution.py:469
  17.0 1.6 %collective-permute-start.2 = (f32[2,96,128]{2,1,0:T(8,128)S(1)}, f32[2,96,128]{2,1,0:T(8,128)S(1)}, u32[]{:S(2)}, u32[]{:S(2)}) collective-permute-start(f32[2,96,128]{2,1,0:T(8,128)S(1)} %get-tuple-element.112), channel_id=1, source_target_pairs={{0,3},{1,2},{2,1},{3,0},{4,7},{5,6},{6,5},{7,4},{8,11},{9,10},{10,... | collective-permute-start | bytes 294920 | tf_op jit(solution)/shard_map/ppermute | solution.py:485
  18.7 1.8 %prepare.1 = (f32[4,2,256,256]{3,2,1,0:T(8,128)S(1)}, f32[4,512,128]{2,1,0:T(8,128)S(1)}) custom-call(s32[2,2,2]{2,1,0:T(2,128)S(1)} %copy-done.5, f32[2,256,256]{2,1,0:T(8,128)S(1)} %copy-done.4, f32[512,512]{1,0:T(8,128)S(1)} %copy-done.3, bf16[256,256]{1,0:T(8,128)(2,1)S(1)} %copy-done.6), custom_call_target="tpu_custom_call" | custom-call | flops 100000 | bytes 100000 | tf_op jit(solution)/shard_map/prepare/pallas_call | solution.py:105
  20.5 2.6 %shard_map.73 = (f32[2,192,384]{2,1,0:T(8,128)S(1)}, f32[2,192,128]{2,1,0:T(8,128)S(1)}, f32[2,192,384]{2,1,0:T(8,128)S(1)}, f32[2,192,128]{2,1,0:T(8,128)S(1)}) custom-call(s32[2,2,2]{2,1,0:T(2,128)S(1)} %copy-done.5, bf16[4,256,256]{2,1,0:T(8,128)(2,1)S(1)} %copy-done.1, f32[4,128,128]{2,1,0:T(8,128)S(1)} %copy-done.2, ...), custom_call_target="tpu_custom_call" | custom-call | flops 100000 | bytes 100000 | tf_op jit(solution)/shard_map/pallas_call | solution.py:302
  23.1 2.7 %shard_map.74 = (f32[2,192,384]{2,1,0:T(8,128)S(1)}, f32[2,192,128]{2,1,0:T(8,128)S(1)}, f32[2,192,384]{2,1,0:T(8,128)S(1)}, f32[2,192,128]{2,1,0:T(8,128)S(1)}) custom-call(s32[2,2,2]{2,1,0:T(2,128)S(1)} %copy-done.5, bf16[4,256,256]{2,1,0:T(8,128)(2,1)S(1)} %copy-done.1, f32[4,128,128]{2,1,0:T(8,128)S(1)} %copy-done.2, ...), custom_call_target="tpu_custom_call" | custom-call | flops 100000 | bytes 100000 | tf_op jit(solution)/shard_map/pallas_call | solution.py:302
  25.8 0.4 collective-permute-start.9
  26.2 0.3 collective-permute-start.8
  26.5 1.3 %collective-permute-start.7 = (f32[2,96,128]{2,1,0:T(8,128)S(1)}, f32[2,96,128]{2,1,0:T(8,128)S(1)}, u32[]{:S(2)}, u32[]{:S(2)}) collective-permute-start(f32[2,96,128]{2,1,0:T(8,128)S(1)} %get-tuple-element.109), channel_id=1, source_target_pairs={{0,3},{1,2},{2,1},{3,0},{4,7},{5,6},{6,5},{7,4},{8,11},{9,10},{10,... | collective-permute-start | bytes 294920 | tf_op jit(solution)/shard_map/ppermute | solution.py:485
  27.8 0.4 collective-permute-start.6
  28.2 1.3 %variation.4.refs_0_ = f32[2,192,384]{2,1,0:T(8,128)S(1)} custom-call(f32[2,96,128]{2,1,0:T(8,128)S(1)} %collective-permute-done.4.refs_5_.refs_0_, f32[2,384,128]{2,1,0:T(8,128)S(1)} %collective-permute-done.5.refs_6_.refs_1_.refs_5_.refs_0_, f32[2,96,384]{2,1,0:T(8,128)S(1)} %collective-permute-done.refs_7_.refs_2_.refs_0_, f32[2,384,384]{2,1,0:T(8,128)S(1)} %copy-done, ...), custom_call_target="tpu_custom_call" | custom-call | flops 100000 | bytes 100000 | tf_op jit(solution)/shard_map/variation/pallas_call | solution.py:363
  29.6 3.2 %collective-permute-done.9.far_ref = f32[2,192,128]{2,1,0:T(8,128)S(1)} collective-permute-done((f32[2,192,128]{2,1,0:T(8,128)S(1)}, f32[2,192,128]{2,1,0:T(8,128)S(1)}, u32[]{:S(2)}, u32[]{:S(2)}) %collective-permute-start.9) | collective-permute-done | bytes 196640 | tf_op jit(solution)/shard_map/ppermute | solution.py:485
  32.9 1.5 %collective-permute-start.12 = (f32[2,192,384]{2,1,0:T(8,128)S(1)}, f32[2,192,384]{2,1,0:T(8,128)S(1)}, u32[]{:S(2)}, u32[]{:S(2)}) collective-permute-start(f32[2,192,384]{2,1,0:T(8,128)S(1)} %totals.5.refs_2_), channel_id=1, source_target_pairs={{0,28},{4,0},{8,4},{12,8},{16,12},{20,16},{24,20},{28,24},{1,29},{... | collective-permute-start | bytes 1769480 | tf_op jit(solution)/shard_map/ppermute | solution.py:469
  34.4 0.6 collective-permute-done.7.refs_6_.refs_5_
  34.9 2.6 %shard_map.75 = (f32[2,384,384]{2,1,0:T(8,128)S(1)}, f32[2,384,128]{2,1,0:T(8,128)S(1)}) custom-call(s32[2,2,2]{2,1,0:T(2,128)S(1)} %copy-done.5, bf16[4,256,256]{2,1,0:T(8,128)(2,1)S(1)} %copy-done.1, f32[4,128,128]{2,1,0:T(8,128)S(1)} %copy-done.2, f32[4,2,256,256]{3,2,1,0:T(8,128)S(1)} %get-tuple-element.56.refs_3_, ...), custom_call_target="tpu_custom_call" | custom-call | flops 100000 | bytes 100000 | tf_op jit(solution)/shard_map/pallas_call | solution.py:302
  37.6 2.7 %shard_map.76 = (f32[2,384,384]{2,1,0:T(8,128)S(1)}, f32[2,384,128]{2,1,0:T(8,128)S(1)}) custom-call(s32[2,2,2]{2,1,0:T(2,128)S(1)} %copy-done.5, bf16[4,256,256]{2,1,0:T(8,128)(2,1)S(1)} %copy-done.1, f32[4,128,128]{2,1,0:T(8,128)S(1)} %copy-done.2, f32[4,2,256,256]{3,2,1,0:T(8,128)S(1)} %get-tuple-element.56.refs_3_, ...), custom_call_target="tpu_custom_call" | custom-call | flops 100000 | bytes 100000 | tf_op jit(solution)/shard_map/pallas_call | solution.py:302
  40.3 0.2 collective-permute-start.10
  40.4 0.7 collective-permute-start.11
  41.1 1.3 %variation.5.refs_1_ = f32[2,192,384]{2,1,0:T(8,128)S(1)} custom-call(f32[2,384,128]{2,1,0:T(8,128)S(1)} %collective-permute-done.5.refs_6_.refs_1_.refs_5_.refs_0_, f32[2,96,128]{2,1,0:T(8,128)S(1)} %collective-permute-done.6.refs_6_.refs_1_, f32[2,384,384]{2,1,0:T(8,128)S(1)} %copy-done, f32[2,96,384]{2,1,0:T(8,128)S(1)} %collective-permute-done.1.refs_8_.refs_3_.refs_1_, ...), custom_call_target="tpu_custom_call" | custom-call | flops 100000 | bytes 100000 | tf_op jit(solution)/shard_map/variation/pallas_call | solution.py:363
  42.5 0.2 totals.6
  42.7 0.4 collective-permute-start.15
  43.0 5.8 %collective-permute-done.12.refs_4_ = f32[2,192,384]{2,1,0:T(8,128)S(1)} collective-permute-done((f32[2,192,384]{2,1,0:T(8,128)S(1)}, f32[2,192,384]{2,1,0:T(8,128)S(1)}, u32[]{:S(2)}, u32[]{:S(2)}) %collective-permute-start.12) | collective-permute-done | bytes 589856 | tf_op jit(solution)/shard_map/ppermute | solution.py:469
  48.8 0.2 update.2
  49.0 1.7 %collective-permute-start.14 = (f32[2,384,128]{2,1,0:T(8,128)S(1)}, f32[2,384,128]{2,1,0:T(8,128)S(1)}, u32[]{:S(2)}, u32[]{:S(2)}) collective-permute-start(f32[2,384,128]{2,1,0:T(8,128)S(1)} %get-tuple-element.77), channel_id=1, source_target_pairs={{0,1},{1,0},{2,3},{3,2},{4,5},{5,4},{6,7},{7,6},{8,9},{9,8},{10,11... | collective-permute-start | bytes 1179656 | tf_op jit(solution)/shard_map/ppermute | solution.py:474
  50.8 0.9 collective-permute-start.13
  51.6 0.5 collective-permute-done.14.refs_5_.refs_6_.refs_0_.refs_1_
  52.1 2.6 %shard_map.77 = (f32[2,192,384]{2,1,0:T(8,128)S(1)}, f32[2,192,128]{2,1,0:T(8,128)S(1)}, f32[2,192,384]{2,1,0:T(8,128)S(1)}, f32[2,192,128]{2,1,0:T(8,128)S(1)}) custom-call(s32[2,2,2]{2,1,0:T(2,128)S(1)} %copy-done.5, bf16[4,256,256]{2,1,0:T(8,128)(2,1)S(1)} %copy-done.1, f32[4,128,128]{2,1,0:T(8,128)S(1)} %copy-done.2, ...), custom_call_target="tpu_custom_call" | custom-call | flops 100000 | bytes 100000 | tf_op jit(solution)/shard_map/pallas_call | solution.py:302
  54.7 2.7 %shard_map.78 = (f32[2,192,384]{2,1,0:T(8,128)S(1)}, f32[2,192,128]{2,1,0:T(8,128)S(1)}, f32[2,192,384]{2,1,0:T(8,128)S(1)}, f32[2,192,128]{2,1,0:T(8,128)S(1)}) custom-call(s32[2,2,2]{2,1,0:T(2,128)S(1)} %copy-done.5, bf16[4,256,256]{2,1,0:T(8,128)(2,1)S(1)} %copy-done.1, f32[4,128,128]{2,1,0:T(8,128)S(1)} %copy-done.2, ...), custom_call_target="tpu_custom_call" | custom-call | flops 100000 | bytes 100000 | tf_op jit(solution)/shard_map/pallas_call | solution.py:302
  57.6 8.9 %collective-permute-start.17 = (f32[2,192,128]{2,1,0:T(8,128)S(1)}, f32[2,192,128]{2,1,0:T(8,128)S(1)}, u32[]{:S(2)}, u32[]{:S(2)}) collective-permute-start(f32[2,192,128]{2,1,0:T(8,128)S(1)} %get-tuple-element.85), channel_id=1, source_target_pairs={{0,1},{1,0},{2,3},{3,2},{4,5},{5,4},{6,7},{7,6},{8,9},{9,8},{10,11... | collective-permute-start | bytes 589832 | tf_op jit(solution)/shard_map/ppermute | solution.py:474
  66.4 1.7 %collective-permute-start.19 = (f32[2,192,128]{2,1,0:T(8,128)S(1)}, f32[2,192,128]{2,1,0:T(8,128)S(1)}, u32[]{:S(2)}, u32[]{:S(2)}) collective-permute-start(f32[2,192,128]{2,1,0:T(8,128)S(1)} %get-tuple-element.80), channel_id=1, source_target_pairs={{0,3},{1,2},{2,1},{3,0},{4,7},{5,6},{6,5},{7,4},{8,11},{9,10},{10,... | collective-permute-start | bytes 589832 | tf_op jit(solution)/shard_map/ppermute | solution.py:485
  68.3 1.3 %variation.6.refs_0_.refs_1_ = f32[2,192,384]{2,1,0:T(8,128)S(1)} custom-call(f32[2,384,128]{2,1,0:T(8,128)S(1)} %collective-permute-done.14.refs_5_.refs_6_.refs_0_.refs_1_, f32[2,384,384]{2,1,0:T(8,128)S(1)} %get-tuple-element.76.refs_6_.refs_8_.refs_1_.refs_3_.bottom_ref, f32[2,384,128]{2,1,0:T(8,128)S(1)} %collective-permute-done.13.refs_5_.refs_2_.refs_6_), custom_call_target="tpu_custom_call" | custom-call | flops 100000 | bytes 100000 | tf_op jit(solution)/shard_map/variation/pallas_call | solution.py:363
  69.7 2.6 %shard_map.79 = (f32[2,96,384]{2,1,0:T(8,128)S(1)}, f32[2,96,128]{2,1,0:T(8,128)S(1)}, f32[2,288,384]{2,1,0:T(8,128)S(1)}, f32[2,288,128]{2,1,0:T(8,128)S(1)}) custom-call(s32[2,2,2]{2,1,0:T(2,128)S(1)} %copy-done.5, bf16[4,256,256]{2,1,0:T(8,128)(2,1)S(1)} %copy-done.1, f32[4,128,128]{2,1,0:T(8,128)S(1)} %copy-done.2, ...), custom_call_target="tpu_custom_call" | custom-call | flops 100000 | bytes 100000 | tf_op jit(solution)/shard_map/pallas_call | solution.py:302
  72.3 1.1 %collective-permute-done.19.far_ref = f32[2,192,128]{2,1,0:T(8,128)S(1)} collective-permute-done((f32[2,192,128]{2,1,0:T(8,128)S(1)}, f32[2,192,128]{2,1,0:T(8,128)S(1)}, u32[]{:S(2)}, u32[]{:S(2)}) %collective-permute-start.19) | collective-permute-done | bytes 196640 | tf_op jit(solution)/shard_map/ppermute | solution.py:485
  73.5 4.0 %collective-permute-done.16.refs_5_.refs_4_ = f32[2,192,128]{2,1,0:T(8,128)S(1)} collective-permute-done((f32[2,192,128]{2,1,0:T(8,128)S(1)}, f32[2,192,128]{2,1,0:T(8,128)S(1)}, u32[]{:S(2)}, u32[]{:S(2)}) %collective-permute-start.16) | collective-permute-done | bytes 196640 | tf_op jit(solution)/shard_map/ppermute | solution.py:485
  77.6 2.6 %shard_map.80 = (f32[2,96,384]{2,1,0:T(8,128)S(1)}, f32[2,96,128]{2,1,0:T(8,128)S(1)}, f32[2,288,384]{2,1,0:T(8,128)S(1)}, f32[2,288,128]{2,1,0:T(8,128)S(1)}) custom-call(s32[2,2,2]{2,1,0:T(2,128)S(1)} %copy-done.5, bf16[4,256,256]{2,1,0:T(8,128)(2,1)S(1)} %copy-done.1, f32[4,128,128]{2,1,0:T(8,128)S(1)} %copy-done.2, ...), custom_call_target="tpu_custom_call" | custom-call | flops 100000 | bytes 100000 | tf_op jit(solution)/shard_map/pallas_call | solution.py:302
  80.2 1.4 %collective-permute-start.24 = (f32[2,96,128]{2,1,0:T(8,128)S(1)}, f32[2,96,128]{2,1,0:T(8,128)S(1)}, u32[]{:S(2)}, u32[]{:S(2)}) collective-permute-start(f32[2,96,128]{2,1,0:T(8,128)S(1)} %get-tuple-element.104), channel_id=1, source_target_pairs={{0,3},{1,2},{2,1},{3,0},{4,7},{5,6},{6,5},{7,4},{8,11},{9,10},{10,... | collective-permute-start | bytes 294920 | tf_op jit(solution)/shard_map/ppermute | solution.py:485
  81.8 0.4 collective-permute-start.21
  82.2 0.4 collective-permute-start.20
  82.5 2.5 %collective-permute-done.24.far_ref = f32[2,96,128]{2,1,0:T(8,128)S(1)} collective-permute-done((f32[2,96,128]{2,1,0:T(8,128)S(1)}, f32[2,96,128]{2,1,0:T(8,128)S(1)}, u32[]{:S(2)}, u32[]{:S(2)}) %collective-permute-start.24) | collective-permute-done | bytes 98336 | tf_op jit(solution)/shard_map/ppermute | solution.py:485
  85.1 7.3 %collective-permute-start.25 = (f32[2,96,384]{2,1,0:T(8,128)S(1)}, f32[2,96,384]{2,1,0:T(8,128)S(1)}, u32[]{:S(2)}, u32[]{:S(2)}) collective-permute-start(f32[2,96,384]{2,1,0:T(8,128)S(1)} %totals.9), channel_id=1, source_target_pairs={{0,28},{4,0},{8,4},{12,8},{16,12},{20,16},{24,20},{28,24},{1,29},{... | collective-permute-start | bytes 884744 | tf_op jit(solution)/shard_map/ppermute | solution.py:469
  92.4 1.3 %variation.7.refs_0_ = f32[2,192,384]{2,1,0:T(8,128)S(1)} custom-call(f32[2,192,128]{2,1,0:T(8,128)S(1)} %collective-permute-done.17.refs_5_.refs_0_, f32[2,384,128]{2,1,0:T(8,128)S(1)} %collective-permute-done.14.refs_5_.refs_6_.refs_0_.refs_1_, f32[2,192,384]{2,1,0:T(8,128)S(1)} %get-tuple-element.83.refs_7_.refs_2_.top_ref, ...), custom_call_target="tpu_custom_call" | custom-call | flops 100000 | bytes 100000 | tf_op jit(solution)/shard_map/variation/pallas_call | solution.py:363
  93.8 0.2 totals.8.mid_ref
  94.0 3.2 %collective-permute-done.22.above_ref = f32[2,96,384]{2,1,0:T(8,128)S(1)} collective-permute-done((f32[2,96,384]{2,1,0:T(8,128)S(1)}, f32[2,96,384]{2,1,0:T(8,128)S(1)}, u32[]{:S(2)}, u32[]{:S(2)}) %collective-permute-start.22) | collective-permute-done | bytes 294944 | tf_op jit(solution)/shard_map/ppermute | solution.py:469
  97.2 3.9 %collective-permute-done.25.below_ref = f32[2,96,384]{2,1,0:T(8,128)S(1)} collective-permute-done((f32[2,96,384]{2,1,0:T(8,128)S(1)}, f32[2,96,384]{2,1,0:T(8,128)S(1)}, u32[]{:S(2)}, u32[]{:S(2)}) %collective-permute-start.25) | collective-permute-done | bytes 294944 | tf_op jit(solution)/shard_map/ppermute | solution.py:469
  101.1 1.2 %finish.1 = f32[2,384,384]{2,1,0:T(8,128)} custom-call(f32[2,192,384]{2,1,0:T(8,128)S(1)} %get-tuple-element.83.refs_7_.refs_2_.top_ref, f32[2,384,384]{2,1,0:T(8,128)S(1)} %get-tuple-element.76.refs_6_.refs_8_.refs_1_.refs_3_.bottom_ref, f32[2,288,384]{2,1,0:T(8,128)S(1)} %totals.8.mid_ref, f32[2,96,384]{2,1,0:T(8,128)S(1)} %get-tuple-element.100.low_ref, ...), custom_call_target="tpu_custom_call" | custom-call | flops 100000 | bytes 100000 | tf_op jit(solution)/shard_map/finish/pallas_call | solution.py:456
  (43 shorter events, 0.9 us)
Async XLA Ops:
  0.0 4.9 %copy-start = (f32[2,384,384]{2,1,0:T(8,128)S(1)}, f32[2,384,384]{2,1,0:T(8,128)}, u32[]{:S(2)}) copy-start(f32[2,384,384]{2,1,0:T(8,128)} %refs_1_.9) | copy-start | bytes 3538948
  1.9 16.8 %copy-start.3 = (f32[512,512]{1,0:T(8,128)S(1)}, f32[512,512]{1,0:T(8,128)}, u32[]{:S(2)}) copy-start(f32[512,512]{1,0:T(8,128)} %amp_ref.1) | copy-start | bytes 3145732
  1.9 16.8 %copy-start.4 = (f32[2,256,256]{2,1,0:T(8,128)S(1)}, f32[2,256,256]{2,1,0:T(8,128)}, u32[]{:S(2)}) copy-start(f32[2,256,256]{2,1,0:T(8,128)} %probe_ref.1) | copy-start | bytes 1572868
  1.9 16.8 %copy-start.5 = (s32[2,2,2]{2,1,0:T(2,128)S(1)}, s32[2,2,2]{2,1,0:T(2,128)}, u32[]{:S(2)}) copy-start(s32[2,2,2]{2,1,0:T(2,128)} %refs_0_.17) | copy-start | bytes 100
  1.9 16.8 %copy-start.6 = (bf16[256,256]{1,0:T(8,128)(2,1)S(1)}, bf16[256,256]{1,0:T(8,128)(2,1)}, u32[]{:S(2)}) copy-start(bf16[256,256]{1,0:T(8,128)(2,1)} %constant.30.clone.order_ref) | copy-start | bytes 393220
  1.9 13.3 %collective-permute-start = (f32[2,96,384]{2,1,0:T(8,128)}, f32[2,96,384]{2,1,0:T(8,128)S(1)}, u32[]{:S(2)}, u32[]{:S(2)}) collective-permute-start(f32[2,96,384]{2,1,0:T(8,128)} %get-tuple-element.107), channel_id=1, source_target_pairs={{0,4},{4,8},{8,12},{12,16},{16,20},{20,24},{24,28},{28,0},{1,5},{5... | collective-permute-start | bytes 884744 | tf_op jit(solution)/shard_map/ppermute | solution.py:469
  5.0 15.5 %copy-start.1 = (bf16[4,256,256]{2,1,0:T(8,128)(2,1)S(1)}, bf16[4,256,256]{2,1,0:T(8,128)(2,1)}, u32[]{:S(2)}) copy-start(bf16[4,256,256]{2,1,0:T(8,128)(2,1)} %constant.28.clone.refs_1_) | copy-start | bytes 1572868
  5.0 15.5 %copy-start.2 = (f32[4,128,128]{2,1,0:T(8,128)S(1)}, f32[4,128,128]{2,1,0:T(8,128)}, u32[]{:S(2)}) copy-start(f32[4,128,128]{2,1,0:T(8,128)} %constant.29.clone.refs_2_) | copy-start | bytes 786436
  5.0 15.4 %collective-permute-start.5 = (f32[2,384,128]{2,1,0:T(8,128)S(1)}, f32[2,384,128]{2,1,0:T(8,128)S(1)}, u32[]{:S(2)}, u32[]{:S(2)}) collective-permute-start(f32[2,384,128]{2,1,0:T(8,128)S(1)} %get-tuple-element.105), channel_id=1, source_target_pairs={{0,1},{1,0},{2,3},{3,2},{4,5},{5,4},{6,7},{7,6},{8,9},{9,8},{10,11... | collective-permute-start | bytes 1179656 | tf_op jit(solution)/shard_map/ppermute | solution.py:474
  5.1 18.0 %collective-permute-start.3 = (f32[2,384,128]{2,1,0:T(8,128)S(1)}, f32[2,384,128]{2,1,0:T(8,128)S(1)}, u32[]{:S(2)}, u32[]{:S(2)}) collective-permute-start(f32[2,384,128]{2,1,0:T(8,128)S(1)} %get-tuple-element.106), channel_id=1, source_target_pairs={{0,3},{1,2},{2,1},{3,0},{4,7},{5,6},{6,5},{7,4},{8,11},{9,10},{10,... | collective-permute-start | bytes 1179656 | tf_op jit(solution)/shard_map/ppermute | solution.py:485
  15.2 11.3 %collective-permute-start.1 = (f32[2,96,384]{2,1,0:T(8,128)S(1)}, f32[2,96,384]{2,1,0:T(8,128)S(1)}, u32[]{:S(2)}, u32[]{:S(2)}) collective-permute-start(f32[2,96,384]{2,1,0:T(8,128)S(1)} %get-tuple-element.58), channel_id=1, source_target_pairs={{0,28},{4,0},{8,4},{12,8},{16,12},{20,16},{24,20},{28,24},{1,29},{... | collective-permute-start | bytes 884744 | tf_op jit(solution)/shard_map/ppermute | solution.py:469
  17.0 3.5 %collective-permute-start.4 = (f32[2,96,128]{2,1,0:T(8,128)S(1)}, f32[2,96,128]{2,1,0:T(8,128)S(1)}, u32[]{:S(2)}, u32[]{:S(2)}) collective-permute-start(f32[2,96,128]{2,1,0:T(8,128)S(1)} %get-tuple-element.111), channel_id=1, source_target_pairs={{0,1},{1,0},{2,3},{3,2},{4,5},{5,4},{6,7},{7,6},{8,9},{9,8},{10,11... | collective-permute-start | bytes 294920 | tf_op jit(solution)/shard_map/ppermute | solution.py:474
  17.0 6.1 %collective-permute-start.2 = (f32[2,96,128]{2,1,0:T(8,128)S(1)}, f32[2,96,128]{2,1,0:T(8,128)S(1)}, u32[]{:S(2)}, u32[]{:S(2)}) collective-permute-start(f32[2,96,128]{2,1,0:T(8,128)S(1)} %get-tuple-element.112), channel_id=1, source_target_pairs={{0,3},{1,2},{2,1},{3,0},{4,7},{5,6},{6,5},{7,4},{8,11},{9,10},{10,... | collective-permute-start | bytes 294920 | tf_op jit(solution)/shard_map/ppermute | solution.py:485
  25.8 7.0 %collective-permute-start.9 = (f32[2,192,128]{2,1,0:T(8,128)S(1)}, f32[2,192,128]{2,1,0:T(8,128)S(1)}, u32[]{:S(2)}, u32[]{:S(2)}) collective-permute-start(f32[2,192,128]{2,1,0:T(8,128)S(1)} %get-tuple-element.61), channel_id=1, source_target_pairs={{0,3},{1,2},{2,1},{3,0},{4,7},{5,6},{6,5},{7,4},{8,11},{9,10},{10,... | collective-permute-start | bytes 589832 | tf_op jit(solution)/shard_map/ppermute | solution.py:485
  26.2 6.6 %collective-permute-start.8 = (f32[2,192,128]{2,1,0:T(8,128)S(1)}, f32[2,192,128]{2,1,0:T(8,128)S(1)}, u32[]{:S(2)}, u32[]{:S(2)}) collective-permute-start(f32[2,192,128]{2,1,0:T(8,128)S(1)} %get-tuple-element.65), channel_id=1, source_target_pairs={{0,1},{1,0},{2,3},{3,2},{4,5},{5,4},{6,7},{7,6},{8,9},{9,8},{10,11... | collective-permute-start | bytes 589832 | tf_op jit(solution)/shard_map/ppermute | solution.py:474
  26.5 8.4 %collective-permute-start.7 = (f32[2,96,128]{2,1,0:T(8,128)S(1)}, f32[2,96,128]{2,1,0:T(8,128)S(1)}, u32[]{:S(2)}, u32[]{:S(2)}) collective-permute-start(f32[2,96,128]{2,1,0:T(8,128)S(1)} %get-tuple-element.109), channel_id=1, source_target_pairs={{0,3},{1,2},{2,1},{3,0},{4,7},{5,6},{6,5},{7,4},{8,11},{9,10},{10,... | collective-permute-start | bytes 294920 | tf_op jit(solution)/shard_map/ppermute | solution.py:485
  27.8 9.8 %collective-permute-start.6 = (f32[2,96,128]{2,1,0:T(8,128)S(1)}, f32[2,96,128]{2,1,0:T(8,128)S(1)}, u32[]{:S(2)}, u32[]{:S(2)}) collective-permute-start(f32[2,96,128]{2,1,0:T(8,128)S(1)} %get-tuple-element.110), channel_id=1, source_target_pairs={{0,1},{1,0},{2,3},{3,2},{4,5},{5,4},{6,7},{7,6},{8,9},{9,8},{10,11... | collective-permute-start | bytes 294920 | tf_op jit(solution)/shard_map/ppermute | solution.py:474
  32.9 15.9 %collective-permute-start.12 = (f32[2,192,384]{2,1,0:T(8,128)S(1)}, f32[2,192,384]{2,1,0:T(8,128)S(1)}, u32[]{:S(2)}, u32[]{:S(2)}) collective-permute-start(f32[2,192,384]{2,1,0:T(8,128)S(1)} %totals.5.refs_2_), channel_id=1, source_target_pairs={{0,28},{4,0},{8,4},{12,8},{16,12},{20,16},{24,20},{28,24},{1,29},{... | collective-permute-start | bytes 1769480 | tf_op jit(solution)/shard_map/ppermute | solution.py:469
  40.3 2.2 %collective-permute-start.10 = (f32[2,384,128]{2,1,0:T(8,128)S(1)}, f32[2,384,128]{2,1,0:T(8,128)S(1)}, u32[]{:S(2)}, u32[]{:S(2)}) collective-permute-start(f32[2,384,128]{2,1,0:T(8,128)S(1)} %get-tuple-element.71), channel_id=1, source_target_pairs={{0,1},{1,0},{2,3},{3,2},{4,5},{5,4},{6,7},{7,6},{8,9},{9,8},{10,11... | collective-permute-start | bytes 1179656 | tf_op jit(solution)/shard_map/ppermute | solution.py:474
  40.4 2.0 %collective-permute-start.11 = (f32[2,384,128]{2,1,0:T(8,128)S(1)}, f32[2,384,128]{2,1,0:T(8,128)S(1)}, u32[]{:S(2)}, u32[]{:S(2)}) collective-permute-start(f32[2,384,128]{2,1,0:T(8,128)S(1)} %get-tuple-element.72), channel_id=1, source_target_pairs={{1,2},{2,1},{5,6},{6,5},{9,10},{10,9},{13,14},{14,13},{17,18},{18,... | collective-permute-start | bytes 1179656 | tf_op jit(solution)/shard_map/ppermute | solution.py:485
  42.7 14.7 %collective-permute-start.15 = (f32[2,192,384]{2,1,0:T(8,128)S(1)}, f32[2,192,384]{2,1,0:T(8,128)S(1)}, u32[]{:S(2)}, u32[]{:S(2)}) collective-permute-start(f32[2,192,384]{2,1,0:T(8,128)S(1)} %get-tuple-element.74.refs_3_), channel_id=1, source_target_pairs={{0,4},{4,8},{8,12},{12,16},{16,20},{20,24},{24,28},{28,0},{1,5},{5... | collective-permute-start | bytes 1769480 | tf_op jit(solution)/shard_map/ppermute | solution.py:469
  49.0 3.1 %collective-permute-start.14 = (f32[2,384,128]{2,1,0:T(8,128)S(1)}, f32[2,384,128]{2,1,0:T(8,128)S(1)}, u32[]{:S(2)}, u32[]{:S(2)}) collective-permute-start(f32[2,384,128]{2,1,0:T(8,128)S(1)} %get-tuple-element.77), channel_id=1, source_target_pairs={{0,1},{1,0},{2,3},{3,2},{4,5},{5,4},{6,7},{7,6},{8,9},{9,8},{10,11... | collective-permute-start | bytes 1179656 | tf_op jit(solution)/shard_map/ppermute | solution.py:474
  50.8 4.0 %collective-permute-start.13 = (f32[2,384,128]{2,1,0:T(8,128)S(1)}, f32[2,384,128]{2,1,0:T(8,128)S(1)}, u32[]{:S(2)}, u32[]{:S(2)}) collective-permute-start(f32[2,384,128]{2,1,0:T(8,128)S(1)} %get-tuple-element.75), channel_id=1, source_target_pairs={{1,2},{2,1},{5,6},{6,5},{9,10},{10,9},{13,14},{14,13},{17,18},{18,... | collective-permute-start | bytes 1179656 | tf_op jit(solution)/shard_map/ppermute | solution.py:485
  57.6 12.1 %collective-permute-start.17 = (f32[2,192,128]{2,1,0:T(8,128)S(1)}, f32[2,192,128]{2,1,0:T(8,128)S(1)}, u32[]{:S(2)}, u32[]{:S(2)}) collective-permute-start(f32[2,192,128]{2,1,0:T(8,128)S(1)} %get-tuple-element.85), channel_id=1, source_target_pairs={{0,1},{1,0},{2,3},{3,2},{4,5},{5,4},{6,7},{7,6},{8,9},{9,8},{10,11... | collective-permute-start | bytes 589832 | tf_op jit(solution)/shard_map/ppermute | solution.py:474
  66.4 7.0 %collective-permute-start.19 = (f32[2,192,128]{2,1,0:T(8,128)S(1)}, f32[2,192,128]{2,1,0:T(8,128)S(1)}, u32[]{:S(2)}, u32[]{:S(2)}) collective-permute-start(f32[2,192,128]{2,1,0:T(8,128)S(1)} %get-tuple-element.80), channel_id=1, source_target_pairs={{0,3},{1,2},{2,1},{3,0},{4,7},{5,6},{6,5},{7,4},{8,11},{9,10},{10,... | collective-permute-start | bytes 589832 | tf_op jit(solution)/shard_map/ppermute | solution.py:485
  68.1 5.3 %collective-permute-start.18 = (f32[2,192,128]{2,1,0:T(8,128)S(1)}, f32[2,192,128]{2,1,0:T(8,128)S(1)}, u32[]{:S(2)}, u32[]{:S(2)}) collective-permute-start(f32[2,192,128]{2,1,0:T(8,128)S(1)} %get-tuple-element.93), channel_id=1, source_target_pairs={{0,1},{1,0},{2,3},{3,2},{4,5},{5,4},{6,7},{7,6},{8,9},{9,8},{10,11... | collective-permute-start | bytes 589832 | tf_op jit(solution)/shard_map/ppermute | solution.py:474
  68.2 9.3 %collective-permute-start.16 = (f32[2,192,128]{2,1,0:T(8,128)S(1)}, f32[2,192,128]{2,1,0:T(8,128)S(1)}, u32[]{:S(2)}, u32[]{:S(2)}) collective-permute-start(f32[2,192,128]{2,1,0:T(8,128)S(1)} %get-tuple-element.84), channel_id=1, source_target_pairs={{0,3},{1,2},{2,1},{3,0},{4,7},{5,6},{6,5},{7,4},{8,11},{9,10},{10,... | collective-permute-start | bytes 589832 | tf_op jit(solution)/shard_map/ppermute | solution.py:485
  80.2 4.9 %collective-permute-start.24 = (f32[2,96,128]{2,1,0:T(8,128)S(1)}, f32[2,96,128]{2,1,0:T(8,128)S(1)}, u32[]{:S(2)}, u32[]{:S(2)}) collective-permute-start(f32[2,96,128]{2,1,0:T(8,128)S(1)} %get-tuple-element.104), channel_id=1, source_target_pairs={{0,3},{1,2},{2,1},{3,0},{4,7},{5,6},{6,5},{7,4},{8,11},{9,10},{10,... | collective-permute-start | bytes 294920 | tf_op jit(solution)/shard_map/ppermute | solution.py:485
  81.7 3.4 %collective-permute-start.23 = (f32[2,96,128]{2,1,0:T(8,128)S(1)}, f32[2,96,128]{2,1,0:T(8,128)S(1)}, u32[]{:S(2)}, u32[]{:S(2)}) collective-permute-start(f32[2,96,128]{2,1,0:T(8,128)S(1)} %get-tuple-element.103), channel_id=1, source_target_pairs={{0,1},{1,0},{2,3},{3,2},{4,5},{5,4},{6,7},{7,6},{8,9},{9,8},{10,11... | collective-permute-start | bytes 294920 | tf_op jit(solution)/shard_map/ppermute | solution.py:474
  81.8 12.0 %collective-permute-start.21 = (f32[2,288,128]{2,1,0:T(8,128)S(1)}, f32[2,288,128]{2,1,0:T(8,128)S(1)}, u32[]{:S(2)}, u32[]{:S(2)}) collective-permute-start(f32[2,288,128]{2,1,0:T(8,128)S(1)} %get-tuple-element.99), channel_id=1, source_target_pairs={{0,3},{1,2},{2,1},{3,0},{4,7},{5,6},{6,5},{7,4},{8,11},{9,10},{10,... | collective-permute-start | bytes 884744 | tf_op jit(solution)/shard_map/ppermute | solution.py:485
  82.2 11.6 %collective-permute-start.20 = (f32[2,288,128]{2,1,0:T(8,128)S(1)}, f32[2,288,128]{2,1,0:T(8,128)S(1)}, u32[]{:S(2)}, u32[]{:S(2)}) collective-permute-start(f32[2,288,128]{2,1,0:T(8,128)S(1)} %get-tuple-element.98), channel_id=1, source_target_pairs={{0,1},{1,0},{2,3},{3,2},{4,5},{5,4},{6,7},{7,6},{8,9},{9,8},{10,11... | collective-permute-start | bytes 884744 | tf_op jit(solution)/shard_map/ppermute | solution.py:474
  82.5 14.7 %collective-permute-start.22 = (f32[2,96,384]{2,1,0:T(8,128)S(1)}, f32[2,96,384]{2,1,0:T(8,128)S(1)}, u32[]{:S(2)}, u32[]{:S(2)}) collective-permute-start(f32[2,96,384]{2,1,0:T(8,128)S(1)} %get-tuple-element.101), channel_id=1, source_target_pairs={{0,4},{4,8},{8,12},{12,16},{16,20},{20,24},{24,28},{28,0},{1,5},{5... | collective-permute-start | bytes 884744 | tf_op jit(solution)/shard_map/ppermute | solution.py:469
  85.1 16.0 %collective-permute-start.25 = (f32[2,96,384]{2,1,0:T(8,128)S(1)}, f32[2,96,384]{2,1,0:T(8,128)S(1)}, u32[]{:S(2)}, u32[]{:S(2)}) collective-permute-start(f32[2,96,384]{2,1,0:T(8,128)S(1)} %totals.9), channel_id=1, source_target_pairs={{0,28},{4,0},{8,4},{12,8},{16,12},{20,16},{24,20},{28,24},{1,29},{... | collective-permute-start | bytes 884744 | tf_op jit(solution)/shard_map/ppermute | solution.py:469

commit v8 on v7

--- a/solution.py
+++ b/solution.py
@@ -443,13 +443,40 @@
     )(*operands)
 
 
-def finish_kernel(top_ref, bottom_ref, mid_ref, low_ref, above_ref, below_ref, out_ref):
+def near_kernel(own_ref, near_ref, out_ref):
+    even = even_column()
+    for channel in range(2):
+        strip = near_ref[channel]
+        out_ref[channel, :, :LANE] = own_ref[channel, :, :LANE] + jnp.where(even, 0.0, strip)
+        out_ref[channel, :, LANE : 2 * LANE] = own_ref[channel, :, LANE : 2 * LANE]
+        out_ref[channel, :, 2 * LANE :] = own_ref[channel, :, 2 * LANE :] + jnp.where(even, strip, 0.0)
+
+
+def sums_near(own, near):
+    return (
+        pl.pallas_call(
+            near_kernel,
+            out_shape=jax.ShapeDtypeStruct(own.shape, F32),
+            in_specs=vmem(2),
+            out_specs=pl.BlockSpec(memory_space=pltpu.VMEM),
+            cost_estimate=COST,
+            compiler_params=pltpu.CompilerParams(vmem_limit_bytes=VMEM_LIMIT),
+            name="sums_near",
+        )(own, near),
+    )
+
+
+def finish_kernel(top_ref, bottom_ref, mid_ref, low_ref, above_ref, below_ref, corner_ref, out_ref):
     for channel in range(2):
         above = mid_ref[channel, :MARGIN, :] + kept(above_ref[channel], "above")
         out_ref[channel, :MARGIN, :] = top_ref[channel, MARGIN:, :] - step_size * above
         out_ref[channel, MARGIN:288, :] = bottom_ref[channel, :192, :] - step_size * mid_ref[channel, MARGIN:, :]
-        below = low_ref[channel] + kept(below_ref[channel], "below")
-        out_ref[channel, 288:, :] = bottom_ref[channel, 192:288, :] - step_size * below
+        base = bottom_ref[channel, 192:288, :] - step_size * (low_ref[channel] + kept(below_ref[channel], "below"))
+        corner = step_size * kept(corner_ref[channel], "below", "beside")
+        even = even_column()
+        out_ref[channel, 288:, :LANE] = base[:, :LANE] - jnp.where(even, corner, 0.0)
+        out_ref[channel, 288:, LANE : 2 * LANE] = base[:, LANE : 2 * LANE]
+        out_ref[channel, 288:, 2 * LANE :] = base[:, 2 * LANE :] - jnp.where(even, 0.0, corner)
 
 
 def finish(*operands):
@@ -485,6 +512,16 @@
     return lax.ppermute(block, ("row", "col"), route)
 
 
+def to_far_above(block):
+    rows, cols = lax.axis_size("row"), lax.axis_size("col")
+    route = []
+    for r in range(rows):
+        for c in range(cols):
+            other = c - 1 if c % 2 == 0 else c + 1
+            route.append((r * cols + c, (r - 1) % rows * cols + other % cols))
+    return lax.ppermute(block, ("row", "col"), route)
+
+
 def edges(block):
     width = block.shape[2]
     low, high = block[:, :, :LANE], block[:, :, width - LANE :]
@@ -527,20 +564,19 @@
         [(top, 88, 8, "above"), (obj, 0, 200)],
         [(top_b, 88, 8, "above"), (far, 0, 200)],
     )
+    own = [(obj, MARGIN, last), (bottom, 0, MARGIN, "below")]
+    whole = ((0, tile),)
+    hi_o, hi_a = window(
+        1, True, consts, [(near, MARGIN, last), (bot_a, 0, MARGIN, "below")], own, [(mid_o, 0)], [(mid_a, 0)], whole
+    )
+    lo_o, hi_o = after((lo_o, hi_o))
     (top_sum,) = totals(lo_o, in_a, in_b, ((0, band),), [(tv_top, 0, MARGIN, MARGIN)])
     from_below = moved(top_sum, "row", -1)
-
-    mid_o, top_sum = after((mid_o, top_sum))
-    own = [(obj, MARGIN, last), (bottom, 0, MARGIN, "below")]
-    whole = ((0, tile),)
+    in_a = to_near(hi_a)
     hi_o, hi_b = window(
-        1, False, consts, [(far, MARGIN, last), (bot_b, 0, MARGIN, "below")], own, [(mid_o, 0)], [(mid_b, 0)], whole,
+        1, False, consts, [(far, MARGIN, last), (bot_b, 0, MARGIN, "below")], own, [(hi_o, 0)], [(mid_b, 0)], whole,
     )
     in_b = to_far(hi_b, ends=False)
-    hi_o, hi_a = window(
-        1, True, consts, [(near, MARGIN, last), (bot_a, 0, MARGIN, "below")], own, [(hi_o, 0)], [(mid_a, 0)], whole,
-    )
-    in_a = to_near(hi_a)
     tv_bottom = variation(
         [(near, 184, 200), (bot_a, 0, 8, "below")],
         [(obj, 184, 200), (bottom, 0, 8, "below")],
@@ -549,8 +585,8 @@
     mid_sum, bot_sum = totals(
         hi_o, in_a, in_b, halves, [(tv_top, MARGIN, 0, MARGIN), (tv_bottom, 0, MARGIN, band)]
     )
-    from_above = moved(bot_sum, "row", 1)
-
+
+    bot_sum, from_below = after((bot_sum, from_below))
     low, near_strip, far_strip = update(
         (obj, bottom, mid_sum, bot_sum, from_below),
         (
@@ -560,7 +596,9 @@
         ),
         "below",
     )
-    low_a, low_b = to_near(near_strip), to_far(far_strip, ends=False)
+    low_a = to_near(near_strip)
+    low_b = to_far(far_strip, ends=False)
+    from_above = moved(bot_sum, "row", 1)
     own = [(low, 0, tile)]
     mid_o, mid_a, hi_o, hi_a = window(1, True, consts, [(low_a, 0, tile)], own, [], [], halves)
     in_a = to_near(hi_a)
@@ -595,15 +633,15 @@
     over_o, over_b, lo_o, lo_b = window(
         0, False, consts, [(up_b, 0, band), (low_b, 0, band)], own, [(over_o, 0), (lo_o, MARGIN)], [(mid_b, band)], cut,
     )
-    over_b = to_far(over_b)
-    (over,) = totals(over_o, over_a, over_b, ((0, MARGIN),), [])
+    (over,) = sums_near(over_o, over_a)
     last_below = moved(over, "row", -1)
+    corner = to_far_above(over_b)
     in_b = to_far(lo_b)
     tv_top = variation(
         [(up_a, 88, 104), (low_a, 0, 104)], [(up, 88, 104), (low, 0, 104)], [(up_b, 88, 104), (low_b, 0, 104)]
     )
     (mid_sum,) = totals(lo_o, in_a, in_b, ((0, last),), [(tv_top, 0, 0, band), (tv_bottom, 0, band, MARGIN)])
-    return finish(up, low, mid_sum, low_sum, last_above, last_below)
+    return finish(up, low, mid_sum, low_sum, last_above, last_below, corner)
 
 
 def solution(mesh):

time: 104 us -> 101 us (0.971); the launches traced: 102 us -> 101 us
  starting transfers between devices: 36.2 us -> 28 us
  waiting for transfers between devices: 33.4 us -> 39.9 us
    ppermute x0 -> x1, waiting for transfers between devices: none -> 9.11 us  [to_far_above(): return lax.ppermute(block, ('row', 'col'), route)]
    ppermute x6, waiting for transfers between devices: 21.4 us -> 16.7 us  [moved(): lax.ppermute(block, axis, [(n, (n + distance) % count) for n in range(cou...]
    ppermute x10, starting transfers between devices: 12.2 us -> 8.05 us  [to_near(): lax.ppermute(block, ('row', 'col'), [(r * cols + c, r * cols + (c ^ 1)) f...]
    ppermute x10 -> x9, starting transfers between devices: 10.1 us -> 6.89 us  [to_far(): return lax.ppermute(block, ('row', 'col'), route)]
    ppermute x10 -> x9, waiting for transfers between devices: 11.5 us -> 13.6 us  [to_far(): return lax.ppermute(block, ('row', 'col'), route)]
    ppermute x6, starting transfers between devices: 13.9 us -> 12.2 us  [moved(): lax.ppermute(block, axis, [(n, (n + distance) % count) for n in range(cou...]
  transfers between devices with their start and end apart: 26 -> 26, of which waited for: 10 -> 10; matrix products, arithmetic and copies ran while one was open for 0% -> 0% of each run, Pallas kernels for 26% -> 29%
where the time goes in v8:
time: 101 us
  waiting for transfers between devices  39.9 us (40%)
  Pallas kernels  30.4 us (30%)
  starting transfers between devices  28 us (28%)
  local copies, waits for them, and re-layouts  1.93 us (2%)
    pallas_call x8, Pallas kernels, window(): pl.pallas_call(kernel, out_shape=tuple(shapes), in_specs=[pl.BlockSpec(me...  21.2 us
    ppermute x6, waiting for transfers between devices, moved(): lax.ppermute(block, axis, [(n, (n + distance) % count) for n in range(cou...  16.7 us
    ppermute x9, waiting for transfers between devices, to_far(): return lax.ppermute(block, ('row', 'col'), route)  13.6 us
    ppermute x6, starting transfers between devices, moved(): lax.ppermute(block, axis, [(n, (n + distance) % count) for n in range(cou...  12.2 us
    ppermute x1, waiting for transfers between devices, to_far_above(): return lax.ppermute(block, ('row', 'col'), route)  9.11 us
    ppermute x10, starting transfers between devices, to_near(): lax.ppermute(block, ('row', 'col'), [(r * cols + c, r * cols + (c ^ 1)) f...  8.05 us
    ppermute x9, starting transfers between devices, to_far(): return lax.ppermute(block, ('row', 'col'), route)  6.89 us
    pallas_call x4, Pallas kernels, variation(): pl.pallas_call(functools.partial(variation_kernel, *plan), out_shape=jax....  5.33 us
  transfers between devices with their start and end apart: 26, of which 10 were waited for; matrix products, arithmetic and copies ran while one was open for 0% of the time, Pallas kernels for 29%

profile of v8, /device:TPU:0, one launch (start us, length us, event | category | flops | bytes accessed | tf_op | source)
XLA Modules:
  0.0 100.6 jit_solution(4046619726160401718)
XLA Ops:
  0.0 1.9 %fusion = (f32[2,96,384]{2,1,0:T(8,128)}, f32[2,96,384]{2,1,0:T(8,128)S(1)}) fusion(f32[2,384,384]{2,1,0:T(8,128)} %refs_1_.9), kind=kLoop, calls=%fused_computation.6 | loop fusion | bytes 1179648 | tf_op jit(solution)/shard_map/slice | solution.py:539
  1.9 3.0 %collective-permute-start = (f32[2,96,384]{2,1,0:T(8,128)}, f32[2,96,384]{2,1,0:T(8,128)S(1)}, u32[]{:S(2)}, u32[]{:S(2)}) collective-permute-start(f32[2,96,384]{2,1,0:T(8,128)} %get-tuple-element.111), channel_id=1, source_target_pairs={{0,4},{4,8},{8,12},{12,16},{16,20},{20,24},{24,28},{28,0},{1,5},{5... | collective-permute-start | bytes 884744 | tf_op jit(solution)/shard_map/ppermute | solution.py:496
  5.1 1.6 %collective-permute-start.3 = (f32[2,384,128]{2,1,0:T(8,128)S(1)}, f32[2,384,128]{2,1,0:T(8,128)S(1)}, u32[]{:S(2)}, u32[]{:S(2)}) collective-permute-start(f32[2,384,128]{2,1,0:T(8,128)S(1)} %get-tuple-element.110), channel_id=1, source_target_pairs={{0,3},{1,2},{2,1},{3,0},{4,7},{5,6},{6,5},{7,4},{8,11},{9,10},{10,... | collective-permute-start | bytes 1179656 | tf_op jit(solution)/shard_map/ppermute | solution.py:512
  6.7 8.5 %collective-permute-done.refs_7_.refs_2_.refs_0_ = f32[2,96,384]{2,1,0:T(8,128)S(1)} collective-permute-done((f32[2,96,384]{2,1,0:T(8,128)}, f32[2,96,384]{2,1,0:T(8,128)S(1)}, u32[]{:S(2)}, u32[]{:S(2)}) %collective-permute-start) | collective-permute-done | bytes 294944 | tf_op jit(solution)/shard_map/ppermute | solution.py:496
  15.2 1.7 %collective-permute-start.1 = (f32[2,96,384]{2,1,0:T(8,128)S(1)}, f32[2,96,384]{2,1,0:T(8,128)S(1)}, u32[]{:S(2)}, u32[]{:S(2)}) collective-permute-start(f32[2,96,384]{2,1,0:T(8,128)S(1)} %get-tuple-element.60), channel_id=1, source_target_pairs={{0,28},{4,0},{8,4},{12,8},{16,12},{20,16},{24,20},{28,24},{1,29},{... | collective-permute-start | bytes 884744 | tf_op jit(solution)/shard_map/ppermute | solution.py:496
  17.0 1.6 %collective-permute-start.2 = (f32[2,96,128]{2,1,0:T(8,128)S(1)}, f32[2,96,128]{2,1,0:T(8,128)S(1)}, u32[]{:S(2)}, u32[]{:S(2)}) collective-permute-start(f32[2,96,128]{2,1,0:T(8,128)S(1)} %get-tuple-element.116), channel_id=1, source_target_pairs={{0,3},{1,2},{2,1},{3,0},{4,7},{5,6},{6,5},{7,4},{8,11},{9,10},{10,... | collective-permute-start | bytes 294920 | tf_op jit(solution)/shard_map/ppermute | solution.py:512
  18.7 1.8 %prepare.1 = (f32[4,2,256,256]{3,2,1,0:T(8,128)S(1)}, f32[4,512,128]{2,1,0:T(8,128)S(1)}) custom-call(s32[2,2,2]{2,1,0:T(2,128)S(1)} %copy-done.5, f32[2,256,256]{2,1,0:T(8,128)S(1)} %copy-done.4, f32[512,512]{1,0:T(8,128)S(1)} %copy-done.3, bf16[256,256]{1,0:T(8,128)(2,1)S(1)} %copy-done.6), custom_call_target="tpu_custom_call" | custom-call | flops 100000 | bytes 100000 | tf_op jit(solution)/shard_map/prepare/pallas_call | solution.py:105
  20.5 2.6 %shard_map.73 = (f32[2,192,384]{2,1,0:T(8,128)S(1)}, f32[2,192,128]{2,1,0:T(8,128)S(1)}, f32[2,192,384]{2,1,0:T(8,128)S(1)}, f32[2,192,128]{2,1,0:T(8,128)S(1)}) custom-call(s32[2,2,2]{2,1,0:T(2,128)S(1)} %copy-done.5, bf16[4,256,256]{2,1,0:T(8,128)(2,1)S(1)} %copy-done.1, f32[4,128,128]{2,1,0:T(8,128)S(1)} %copy-done.2, ...), custom_call_target="tpu_custom_call" | custom-call | flops 100000 | bytes 100000 | tf_op jit(solution)/shard_map/pallas_call | solution.py:302
  23.1 2.7 %shard_map.74 = (f32[2,192,384]{2,1,0:T(8,128)S(1)}, f32[2,192,128]{2,1,0:T(8,128)S(1)}, f32[2,192,384]{2,1,0:T(8,128)S(1)}, f32[2,192,128]{2,1,0:T(8,128)S(1)}) custom-call(s32[2,2,2]{2,1,0:T(2,128)S(1)} %copy-done.5, bf16[4,256,256]{2,1,0:T(8,128)(2,1)S(1)} %copy-done.1, f32[4,128,128]{2,1,0:T(8,128)S(1)} %copy-done.2, ...), custom_call_target="tpu_custom_call" | custom-call | flops 100000 | bytes 100000 | tf_op jit(solution)/shard_map/pallas_call | solution.py:302
  25.8 0.4 collective-permute-start.11
  26.2 0.3 collective-permute-start.10
  26.5 0.2 collective-permute-start.7
  26.8 1.3 %variation.4.refs_0_ = f32[2,192,384]{2,1,0:T(8,128)S(1)} custom-call(f32[2,96,128]{2,1,0:T(8,128)S(1)} %collective-permute-done.4.refs_5_.refs_0_, f32[2,384,128]{2,1,0:T(8,128)S(1)} %collective-permute-done.5.refs_6_.refs_5_.refs_1_.refs_0_, f32[2,96,384]{2,1,0:T(8,128)S(1)} %collective-permute-done.refs_7_.refs_2_.refs_0_, f32[2,384,384]{2,1,0:T(8,128)S(1)} %copy-done, ...), custom_call_target="tpu_custom_call" | custom-call | flops 100000 | bytes 100000 | tf_op jit(solution)/shard_map/variation/pallas_call | solution.py:363
  28.1 2.7 %shard_map.75 = (f32[2,384,384]{2,1,0:T(8,128)S(1)}, f32[2,384,128]{2,1,0:T(8,128)S(1)}) custom-call(s32[2,2,2]{2,1,0:T(2,128)S(1)} %copy-done.5, bf16[4,256,256]{2,1,0:T(8,128)(2,1)S(1)} %copy-done.1, f32[4,128,128]{2,1,0:T(8,128)S(1)} %copy-done.2, f32[4,2,256,256]{3,2,1,0:T(8,128)S(1)} %get-tuple-element.58.refs_3_, ...), custom_call_target="tpu_custom_call" | custom-call | flops 100000 | bytes 100000 | tf_op jit(solution)/shard_map/pallas_call | solution.py:302
  30.8 2.0 %collective-permute-done.11.far_ref = f32[2,192,128]{2,1,0:T(8,128)S(1)} collective-permute-done((f32[2,192,128]{2,1,0:T(8,128)S(1)}, f32[2,192,128]{2,1,0:T(8,128)S(1)}, u32[]{:S(2)}, u32[]{:S(2)}) %collective-permute-start.11) | collective-permute-done | bytes 196640 | tf_op jit(solution)/shard_map/ppermute | solution.py:512
  32.9 1.5 %collective-permute-start.12 = (f32[2,192,384]{2,1,0:T(8,128)S(1)}, f32[2,192,384]{2,1,0:T(8,128)S(1)}, u32[]{:S(2)}, u32[]{:S(2)}) collective-permute-start(f32[2,192,384]{2,1,0:T(8,128)S(1)} %totals.5.refs_2_), channel_id=1, source_target_pairs={{0,28},{4,0},{8,4},{12,8},{16,12},{20,16},{24,20},{28,24},{1,29},{... | collective-permute-start | bytes 1769480 | tf_op jit(solution)/shard_map/ppermute | solution.py:496
  34.4 5.1 %collective-permute-done.6.refs_6_.refs_5_ = f32[2,96,128]{2,1,0:T(8,128)S(1)} collective-permute-done((f32[2,96,128]{2,1,0:T(8,128)S(1)}, f32[2,96,128]{2,1,0:T(8,128)S(1)}, u32[]{:S(2)}, u32[]{:S(2)}) %collective-permute-start.6) | collective-permute-done | bytes 98336 | tf_op jit(solution)/shard_map/ppermute | solution.py:512
  39.5 2.7 %shard_map.76 = (f32[2,384,384]{2,1,0:T(8,128)S(1)}, f32[2,384,128]{2,1,0:T(8,128)S(1)}) custom-call(s32[2,2,2]{2,1,0:T(2,128)S(1)} %copy-done.5, bf16[4,256,256]{2,1,0:T(8,128)(2,1)S(1)} %copy-done.1, f32[4,128,128]{2,1,0:T(8,128)S(1)} %copy-done.2, f32[4,2,256,256]{3,2,1,0:T(8,128)S(1)} %get-tuple-element.58.refs_3_, ...), custom_call_target="tpu_custom_call" | custom-call | flops 100000 | bytes 100000 | tf_op jit(solution)/shard_map/pallas_call | solution.py:302
  42.1 0.7 collective-permute-start.9
  42.8 1.8 %collective-permute-start.8 = (f32[2,384,128]{2,1,0:T(8,128)S(1)}, f32[2,384,128]{2,1,0:T(8,128)S(1)}, u32[]{:S(2)}, u32[]{:S(2)}) collective-permute-start(f32[2,384,128]{2,1,0:T(8,128)S(1)} %get-tuple-element.72), channel_id=1, source_target_pairs={{0,1},{1,0},{2,3},{3,2},{4,5},{5,4},{6,7},{7,6},{8,9},{9,8},{10,11... | collective-permute-start | bytes 1179656 | tf_op jit(solution)/shard_map/ppermute | solution.py:501
  44.6 1.3 %variation.5.refs_1_ = f32[2,192,384]{2,1,0:T(8,128)S(1)} custom-call(f32[2,384,128]{2,1,0:T(8,128)S(1)} %collective-permute-done.5.refs_6_.refs_5_.refs_1_.refs_0_, f32[2,96,128]{2,1,0:T(8,128)S(1)} %collective-permute-done.7.refs_6_.refs_1_, f32[2,384,384]{2,1,0:T(8,128)S(1)} %copy-done, f32[2,96,384]{2,1,0:T(8,128)S(1)} %collective-permute-done.1.refs_8_.refs_3_.refs_1_, ...), custom_call_target="tpu_custom_call" | custom-call | flops 100000 | bytes 100000 | tf_op jit(solution)/shard_map/variation/pallas_call | solution.py:363
  45.9 0.2 totals.4
  46.1 2.2 %collective-permute-done.12.refs_4_ = f32[2,192,384]{2,1,0:T(8,128)S(1)} collective-permute-done((f32[2,192,384]{2,1,0:T(8,128)S(1)}, f32[2,192,384]{2,1,0:T(8,128)S(1)}, u32[]{:S(2)}, u32[]{:S(2)}) %collective-permute-start.12) | collective-permute-done | bytes 589856 | tf_op jit(solution)/shard_map/ppermute | solution.py:496
  48.3 1.2 %collective-permute-start.15 = (f32[2,192,384]{2,1,0:T(8,128)S(1)}, f32[2,192,384]{2,1,0:T(8,128)S(1)}, u32[]{:S(2)}, u32[]{:S(2)}) collective-permute-start(f32[2,192,384]{2,1,0:T(8,128)S(1)} %get-tuple-element.78.refs_3_), channel_id=1, source_target_pairs={{0,4},{4,8},{8,12},{12,16},{16,20},{20,24},{24,28},{28,0},{1,5},{5... | collective-permute-start | bytes 1769480 | tf_op jit(solution)/shard_map/ppermute | solution.py:496
  49.5 0.2 update.2
  49.7 2.5 %collective-permute-start.14 = (f32[2,384,128]{2,1,0:T(8,128)S(1)}, f32[2,384,128]{2,1,0:T(8,128)S(1)}, u32[]{:S(2)}, u32[]{:S(2)}) collective-permute-start(f32[2,384,128]{2,1,0:T(8,128)S(1)} %get-tuple-element.82), channel_id=1, source_target_pairs={{0,1},{1,0},{2,3},{3,2},{4,5},{5,4},{6,7},{7,6},{8,9},{9,8},{10,11... | collective-permute-start | bytes 1179656 | tf_op jit(solution)/shard_map/ppermute | solution.py:501
  52.2 0.9 collective-permute-start.13
  53.1 0.5 collective-permute-done.14.refs_5_.refs_6_.refs_0_.refs_1_
  53.6 2.6 %shard_map.77 = (f32[2,192,384]{2,1,0:T(8,128)S(1)}, f32[2,192,128]{2,1,0:T(8,128)S(1)}, f32[2,192,384]{2,1,0:T(8,128)S(1)}, f32[2,192,128]{2,1,0:T(8,128)S(1)}) custom-call(s32[2,2,2]{2,1,0:T(2,128)S(1)} %copy-done.5, bf16[4,256,256]{2,1,0:T(8,128)(2,1)S(1)} %copy-done.1, f32[4,128,128]{2,1,0:T(8,128)S(1)} %copy-done.2, ...), custom_call_target="tpu_custom_call" | custom-call | flops 100000 | bytes 100000 | tf_op jit(solution)/shard_map/pallas_call | solution.py:302
  56.2 2.6 %shard_map.78 = (f32[2,192,384]{2,1,0:T(8,128)S(1)}, f32[2,192,128]{2,1,0:T(8,128)S(1)}, f32[2,192,384]{2,1,0:T(8,128)S(1)}, f32[2,192,128]{2,1,0:T(8,128)S(1)}) custom-call(s32[2,2,2]{2,1,0:T(2,128)S(1)} %copy-done.5, bf16[4,256,256]{2,1,0:T(8,128)(2,1)S(1)} %copy-done.1, f32[4,128,128]{2,1,0:T(8,128)S(1)} %copy-done.2, ...), custom_call_target="tpu_custom_call" | custom-call | flops 100000 | bytes 100000 | tf_op jit(solution)/shard_map/pallas_call | solution.py:302
  58.9 6.0 %collective-permute-done.15.refs_3_ = f32[2,192,384]{2,1,0:T(8,128)S(1)} collective-permute-done((f32[2,192,384]{2,1,0:T(8,128)S(1)}, f32[2,192,384]{2,1,0:T(8,128)S(1)}, u32[]{:S(2)}, u32[]{:S(2)}) %collective-permute-start.15) | collective-permute-done | bytes 589856 | tf_op jit(solution)/shard_map/ppermute | solution.py:496
  65.0 2.2 %collective-permute-start.17 = (f32[2,192,128]{2,1,0:T(8,128)S(1)}, f32[2,192,128]{2,1,0:T(8,128)S(1)}, u32[]{:S(2)}, u32[]{:S(2)}) collective-permute-start(f32[2,192,128]{2,1,0:T(8,128)S(1)} %get-tuple-element.89), channel_id=1, source_target_pairs={{0,1},{1,0},{2,3},{3,2},{4,5},{5,4},{6,7},{7,6},{8,9},{9,8},{10,11... | collective-permute-start | bytes 589832 | tf_op jit(solution)/shard_map/ppermute | solution.py:501
  67.2 0.2 collective-permute-start.18
  67.4 1.7 %collective-permute-start.16 = (f32[2,192,128]{2,1,0:T(8,128)S(1)}, f32[2,192,128]{2,1,0:T(8,128)S(1)}, u32[]{:S(2)}, u32[]{:S(2)}) collective-permute-start(f32[2,192,128]{2,1,0:T(8,128)S(1)} %get-tuple-element.88), channel_id=1, source_target_pairs={{0,3},{1,2},{2,1},{3,0},{4,7},{5,6},{6,5},{7,4},{8,11},{9,10},{10,... | collective-permute-start | bytes 589832 | tf_op jit(solution)/shard_map/ppermute | solution.py:512
  69.1 2.6 %shard_map.79 = (f32[2,96,384]{2,1,0:T(8,128)S(1)}, f32[2,96,128]{2,1,0:T(8,128)S(1)}, f32[2,288,384]{2,1,0:T(8,128)S(1)}, f32[2,288,128]{2,1,0:T(8,128)S(1)}) custom-call(s32[2,2,2]{2,1,0:T(2,128)S(1)} %copy-done.5, bf16[4,256,256]{2,1,0:T(8,128)(2,1)S(1)} %copy-done.1, f32[4,128,128]{2,1,0:T(8,128)S(1)} %copy-done.2, ...), custom_call_target="tpu_custom_call" | custom-call | flops 100000 | bytes 100000 | tf_op jit(solution)/shard_map/pallas_call | solution.py:302
  71.7 0.5 collective-permute-start.23
  72.2 1.3 %variation.6.refs_0_.refs_1_ = f32[2,192,384]{2,1,0:T(8,128)S(1)} custom-call(f32[2,384,128]{2,1,0:T(8,128)S(1)} %collective-permute-done.14.refs_5_.refs_6_.refs_0_.refs_1_, f32[2,384,384]{2,1,0:T(8,128)S(1)} %get-tuple-element.81.refs_6_.refs_8_.refs_1_.refs_3_.bottom_ref, f32[2,384,128]{2,1,0:T(8,128)S(1)} %collective-permute-done.13.refs_5_.refs_2_.refs_6_), custom_call_target="tpu_custom_call" | custom-call | flops 100000 | bytes 100000 | tf_op jit(solution)/shard_map/variation/pallas_call | solution.py:363
  73.5 0.6 collective-permute-done.19.far_ref
  74.3 4.1 %collective-permute-done.16.refs_5_.refs_4_ = f32[2,192,128]{2,1,0:T(8,128)S(1)} collective-permute-done((f32[2,192,128]{2,1,0:T(8,128)S(1)}, f32[2,192,128]{2,1,0:T(8,128)S(1)}, u32[]{:S(2)}, u32[]{:S(2)}) %collective-permute-start.16) | collective-permute-done | bytes 196640 | tf_op jit(solution)/shard_map/ppermute | solution.py:512
  78.4 2.7 %shard_map.80 = (f32[2,96,384]{2,1,0:T(8,128)S(1)}, f32[2,96,128]{2,1,0:T(8,128)S(1)}, f32[2,288,384]{2,1,0:T(8,128)S(1)}, f32[2,288,128]{2,1,0:T(8,128)S(1)}) custom-call(s32[2,2,2]{2,1,0:T(2,128)S(1)} %copy-done.5, bf16[4,256,256]{2,1,0:T(8,128)(2,1)S(1)} %copy-done.1, f32[4,128,128]{2,1,0:T(8,128)S(1)} %copy-done.2, ...), custom_call_target="tpu_custom_call" | custom-call | flops 100000 | bytes 100000 | tf_op jit(solution)/shard_map/pallas_call | solution.py:302
  81.1 0.2 collective-permute-start.20
  81.4 4.8 %collective-permute-start.24 = (f32[2,96,384]{2,1,0:T(8,128)S(1)}, f32[2,96,384]{2,1,0:T(8,128)S(1)}, u32[]{:S(2)}, u32[]{:S(2)}) collective-permute-start(f32[2,96,384]{2,1,0:T(8,128)S(1)} %sums_near.1), channel_id=1, source_target_pairs={{0,28},{4,0},{8,4},{12,8},{16,12},{20,16},{24,20},{28,24},{1,29},{... | collective-permute-start | bytes 884744 | tf_op jit(solution)/shard_map/ppermute | solution.py:496
  86.1 0.9 collective-permute-start.25
  87.0 1.3 %variation.7.refs_0_ = f32[2,192,384]{2,1,0:T(8,128)S(1)} custom-call(f32[2,192,128]{2,1,0:T(8,128)S(1)} %collective-permute-done.17.refs_5_.refs_0_, f32[2,384,128]{2,1,0:T(8,128)S(1)} %collective-permute-done.14.refs_5_.refs_6_.refs_0_.refs_1_, f32[2,192,384]{2,1,0:T(8,128)S(1)} %get-tuple-element.87.refs_7_.refs_2_.top_ref, ...), custom_call_target="tpu_custom_call" | custom-call | flops 100000 | bytes 100000 | tf_op jit(solution)/shard_map/variation/pallas_call | solution.py:363
  88.4 1.8 %collective-permute-done.21.far_ref = f32[2,288,128]{2,1,0:T(8,128)S(1)} collective-permute-done((f32[2,288,128]{2,1,0:T(8,128)S(1)}, f32[2,288,128]{2,1,0:T(8,128)S(1)}, u32[]{:S(2)}, u32[]{:S(2)}) %collective-permute-start.21) | collective-permute-done | bytes 294944 | tf_op jit(solution)/shard_map/ppermute | solution.py:512
  90.1 0.2 totals.7.mid_ref
  90.3 9.1 %collective-permute-done.25.corner_ref = f32[2,96,128]{2,1,0:T(8,128)S(1)} collective-permute-done((f32[2,96,128]{2,1,0:T(8,128)S(1)}, f32[2,96,128]{2,1,0:T(8,128)S(1)}, u32[]{:S(2)}, u32[]{:S(2)}) %collective-permute-start.25) | collective-permute-done | bytes 98336 | tf_op jit(solution)/shard_map/ppermute | solution.py:522
  99.4 1.2 %finish.1 = f32[2,384,384]{2,1,0:T(8,128)} custom-call(f32[2,192,384]{2,1,0:T(8,128)S(1)} %get-tuple-element.87.refs_7_.refs_2_.top_ref, f32[2,384,384]{2,1,0:T(8,128)S(1)} %get-tuple-element.81.refs_6_.refs_8_.refs_1_.refs_3_.bottom_ref, f32[2,288,384]{2,1,0:T(8,128)S(1)} %totals.7.mid_ref, f32[2,96,384]{2,1,0:T(8,128)S(1)} %get-tuple-element.104.low_ref, ...), custom_call_target="tpu_custom_call" | custom-call | flops 100000 | bytes 100000 | tf_op jit(solution)/shard_map/finish/pallas_call | solution.py:483
  (43 shorter events, 0.7 us)
Async XLA Ops:
  0.0 4.9 %copy-start = (f32[2,384,384]{2,1,0:T(8,128)S(1)}, f32[2,384,384]{2,1,0:T(8,128)}, u32[]{:S(2)}) copy-start(f32[2,384,384]{2,1,0:T(8,128)} %refs_1_.9) | copy-start | bytes 3538948
  1.9 16.8 %copy-start.3 = (f32[512,512]{1,0:T(8,128)S(1)}, f32[512,512]{1,0:T(8,128)}, u32[]{:S(2)}) copy-start(f32[512,512]{1,0:T(8,128)} %amp_ref.1) | copy-start | bytes 3145732
  1.9 16.8 %copy-start.4 = (f32[2,256,256]{2,1,0:T(8,128)S(1)}, f32[2,256,256]{2,1,0:T(8,128)}, u32[]{:S(2)}) copy-start(f32[2,256,256]{2,1,0:T(8,128)} %probe_ref.1) | copy-start | bytes 1572868
  1.9 16.8 %copy-start.5 = (s32[2,2,2]{2,1,0:T(2,128)S(1)}, s32[2,2,2]{2,1,0:T(2,128)}, u32[]{:S(2)}) copy-start(s32[2,2,2]{2,1,0:T(2,128)} %refs_0_.17) | copy-start | bytes 100
  1.9 16.8 %copy-start.6 = (bf16[256,256]{1,0:T(8,128)(2,1)S(1)}, bf16[256,256]{1,0:T(8,128)(2,1)}, u32[]{:S(2)}) copy-start(bf16[256,256]{1,0:T(8,128)(2,1)} %constant.30.clone.order_ref) | copy-start | bytes 393220
  1.9 13.3 %collective-permute-start = (f32[2,96,384]{2,1,0:T(8,128)}, f32[2,96,384]{2,1,0:T(8,128)S(1)}, u32[]{:S(2)}, u32[]{:S(2)}) collective-permute-start(f32[2,96,384]{2,1,0:T(8,128)} %get-tuple-element.111), channel_id=1, source_target_pairs={{0,4},{4,8},{8,12},{12,16},{16,20},{20,24},{24,28},{28,0},{1,5},{5... | collective-permute-start | bytes 884744 | tf_op jit(solution)/shard_map/ppermute | solution.py:496
  5.0 15.5 %copy-start.1 = (bf16[4,256,256]{2,1,0:T(8,128)(2,1)S(1)}, bf16[4,256,256]{2,1,0:T(8,128)(2,1)}, u32[]{:S(2)}) copy-start(bf16[4,256,256]{2,1,0:T(8,128)(2,1)} %constant.28.clone.refs_1_) | copy-start | bytes 1572868
  5.0 15.5 %copy-start.2 = (f32[4,128,128]{2,1,0:T(8,128)S(1)}, f32[4,128,128]{2,1,0:T(8,128)}, u32[]{:S(2)}) copy-start(f32[4,128,128]{2,1,0:T(8,128)} %constant.29.clone.refs_2_) | copy-start | bytes 786436
  5.0 15.4 %collective-permute-start.5 = (f32[2,384,128]{2,1,0:T(8,128)S(1)}, f32[2,384,128]{2,1,0:T(8,128)S(1)}, u32[]{:S(2)}, u32[]{:S(2)}) collective-permute-start(f32[2,384,128]{2,1,0:T(8,128)S(1)} %get-tuple-element.109), channel_id=1, source_target_pairs={{0,1},{1,0},{2,3},{3,2},{4,5},{5,4},{6,7},{7,6},{8,9},{9,8},{10,11... | collective-permute-start | bytes 1179656 | tf_op jit(solution)/shard_map/ppermute | solution.py:501
  5.1 18.0 %collective-permute-start.3 = (f32[2,384,128]{2,1,0:T(8,128)S(1)}, f32[2,384,128]{2,1,0:T(8,128)S(1)}, u32[]{:S(2)}, u32[]{:S(2)}) collective-permute-start(f32[2,384,128]{2,1,0:T(8,128)S(1)} %get-tuple-element.110), channel_id=1, source_target_pairs={{0,3},{1,2},{2,1},{3,0},{4,7},{5,6},{6,5},{7,4},{8,11},{9,10},{10,... | collective-permute-start | bytes 1179656 | tf_op jit(solution)/shard_map/ppermute | solution.py:512
  15.2 11.3 %collective-permute-start.1 = (f32[2,96,384]{2,1,0:T(8,128)S(1)}, f32[2,96,384]{2,1,0:T(8,128)S(1)}, u32[]{:S(2)}, u32[]{:S(2)}) collective-permute-start(f32[2,96,384]{2,1,0:T(8,128)S(1)} %get-tuple-element.60), channel_id=1, source_target_pairs={{0,28},{4,0},{8,4},{12,8},{16,12},{20,16},{24,20},{28,24},{1,29},{... | collective-permute-start | bytes 884744 | tf_op jit(solution)/shard_map/ppermute | solution.py:496
  17.0 3.5 %collective-permute-start.4 = (f32[2,96,128]{2,1,0:T(8,128)S(1)}, f32[2,96,128]{2,1,0:T(8,128)S(1)}, u32[]{:S(2)}, u32[]{:S(2)}) collective-permute-start(f32[2,96,128]{2,1,0:T(8,128)S(1)} %get-tuple-element.115), channel_id=1, source_target_pairs={{0,1},{1,0},{2,3},{3,2},{4,5},{5,4},{6,7},{7,6},{8,9},{9,8},{10,11... | collective-permute-start | bytes 294920 | tf_op jit(solution)/shard_map/ppermute | solution.py:501
  17.0 6.1 %collective-permute-start.2 = (f32[2,96,128]{2,1,0:T(8,128)S(1)}, f32[2,96,128]{2,1,0:T(8,128)S(1)}, u32[]{:S(2)}, u32[]{:S(2)}) collective-permute-start(f32[2,96,128]{2,1,0:T(8,128)S(1)} %get-tuple-element.116), channel_id=1, source_target_pairs={{0,3},{1,2},{2,1},{3,0},{4,7},{5,6},{6,5},{7,4},{8,11},{9,10},{10,... | collective-permute-start | bytes 294920 | tf_op jit(solution)/shard_map/ppermute | solution.py:512
  25.8 7.0 %collective-permute-start.11 = (f32[2,192,128]{2,1,0:T(8,128)S(1)}, f32[2,192,128]{2,1,0:T(8,128)S(1)}, u32[]{:S(2)}, u32[]{:S(2)}) collective-permute-start(f32[2,192,128]{2,1,0:T(8,128)S(1)} %get-tuple-element.63), channel_id=1, source_target_pairs={{0,3},{1,2},{2,1},{3,0},{4,7},{5,6},{6,5},{7,4},{8,11},{9,10},{10,... | collective-permute-start | bytes 589832 | tf_op jit(solution)/shard_map/ppermute | solution.py:512
  26.2 6.6 %collective-permute-start.10 = (f32[2,192,128]{2,1,0:T(8,128)S(1)}, f32[2,192,128]{2,1,0:T(8,128)S(1)}, u32[]{:S(2)}, u32[]{:S(2)}) collective-permute-start(f32[2,192,128]{2,1,0:T(8,128)S(1)} %get-tuple-element.77), channel_id=1, source_target_pairs={{0,1},{1,0},{2,3},{3,2},{4,5},{5,4},{6,7},{7,6},{8,9},{9,8},{10,11... | collective-permute-start | bytes 589832 | tf_op jit(solution)/shard_map/ppermute | solution.py:501
  26.5 1.6 %collective-permute-start.7 = (f32[2,96,128]{2,1,0:T(8,128)S(1)}, f32[2,96,128]{2,1,0:T(8,128)S(1)}, u32[]{:S(2)}, u32[]{:S(2)}) collective-permute-start(f32[2,96,128]{2,1,0:T(8,128)S(1)} %get-tuple-element.113), channel_id=1, source_target_pairs={{0,1},{1,0},{2,3},{3,2},{4,5},{5,4},{6,7},{7,6},{8,9},{9,8},{10,11... | collective-permute-start | bytes 294920 | tf_op jit(solution)/shard_map/ppermute | solution.py:501
  32.9 15.4 %collective-permute-start.12 = (f32[2,192,384]{2,1,0:T(8,128)S(1)}, f32[2,192,384]{2,1,0:T(8,128)S(1)}, u32[]{:S(2)}, u32[]{:S(2)}) collective-permute-start(f32[2,192,384]{2,1,0:T(8,128)S(1)} %totals.5.refs_2_), channel_id=1, source_target_pairs={{0,28},{4,0},{8,4},{12,8},{16,12},{20,16},{24,20},{28,24},{1,29},{... | collective-permute-start | bytes 1769480 | tf_op jit(solution)/shard_map/ppermute | solution.py:496
  34.4 5.1 %collective-permute-start.6 = (f32[2,96,128]{2,1,0:T(8,128)S(1)}, f32[2,96,128]{2,1,0:T(8,128)S(1)}, u32[]{:S(2)}, u32[]{:S(2)}) collective-permute-start(f32[2,96,128]{2,1,0:T(8,128)S(1)} %get-tuple-element.114), channel_id=1, source_target_pairs={{0,3},{1,2},{2,1},{3,0},{4,7},{5,6},{6,5},{7,4},{8,11},{9,10},{10,... | collective-permute-start | bytes 294920 | tf_op jit(solution)/shard_map/ppermute | solution.py:512
  42.1 3.8 %collective-permute-start.9 = (f32[2,384,128]{2,1,0:T(8,128)S(1)}, f32[2,384,128]{2,1,0:T(8,128)S(1)}, u32[]{:S(2)}, u32[]{:S(2)}) collective-permute-start(f32[2,384,128]{2,1,0:T(8,128)S(1)} %get-tuple-element.73), channel_id=1, source_target_pairs={{1,2},{2,1},{5,6},{6,5},{9,10},{10,9},{13,14},{14,13},{17,18},{18,... | collective-permute-start | bytes 1179656 | tf_op jit(solution)/shard_map/ppermute | solution.py:512
  42.8 3.1 %collective-permute-start.8 = (f32[2,384,128]{2,1,0:T(8,128)S(1)}, f32[2,384,128]{2,1,0:T(8,128)S(1)}, u32[]{:S(2)}, u32[]{:S(2)}) collective-permute-start(f32[2,384,128]{2,1,0:T(8,128)S(1)} %get-tuple-element.72), channel_id=1, source_target_pairs={{0,1},{1,0},{2,3},{3,2},{4,5},{5,4},{6,7},{7,6},{8,9},{9,8},{10,11... | collective-permute-start | bytes 1179656 | tf_op jit(solution)/shard_map/ppermute | solution.py:501
  48.3 16.6 %collective-permute-start.15 = (f32[2,192,384]{2,1,0:T(8,128)S(1)}, f32[2,192,384]{2,1,0:T(8,128)S(1)}, u32[]{:S(2)}, u32[]{:S(2)}) collective-permute-start(f32[2,192,384]{2,1,0:T(8,128)S(1)} %get-tuple-element.78.refs_3_), channel_id=1, source_target_pairs={{0,4},{4,8},{8,12},{12,16},{16,20},{20,24},{24,28},{28,0},{1,5},{5... | collective-permute-start | bytes 1769480 | tf_op jit(solution)/shard_map/ppermute | solution.py:496
  49.7 3.9 %collective-permute-start.14 = (f32[2,384,128]{2,1,0:T(8,128)S(1)}, f32[2,384,128]{2,1,0:T(8,128)S(1)}, u32[]{:S(2)}, u32[]{:S(2)}) collective-permute-start(f32[2,384,128]{2,1,0:T(8,128)S(1)} %get-tuple-element.82), channel_id=1, source_target_pairs={{0,1},{1,0},{2,3},{3,2},{4,5},{5,4},{6,7},{7,6},{8,9},{9,8},{10,11... | collective-permute-start | bytes 1179656 | tf_op jit(solution)/shard_map/ppermute | solution.py:501
  52.2 4.0 %collective-permute-start.13 = (f32[2,384,128]{2,1,0:T(8,128)S(1)}, f32[2,384,128]{2,1,0:T(8,128)S(1)}, u32[]{:S(2)}, u32[]{:S(2)}) collective-permute-start(f32[2,384,128]{2,1,0:T(8,128)S(1)} %get-tuple-element.80), channel_id=1, source_target_pairs={{1,2},{2,1},{5,6},{6,5},{9,10},{10,9},{13,14},{14,13},{17,18},{18,... | collective-permute-start | bytes 1179656 | tf_op jit(solution)/shard_map/ppermute | solution.py:512
  65.0 4.1 %collective-permute-start.17 = (f32[2,192,128]{2,1,0:T(8,128)S(1)}, f32[2,192,128]{2,1,0:T(8,128)S(1)}, u32[]{:S(2)}, u32[]{:S(2)}) collective-permute-start(f32[2,192,128]{2,1,0:T(8,128)S(1)} %get-tuple-element.89), channel_id=1, source_target_pairs={{0,1},{1,0},{2,3},{3,2},{4,5},{5,4},{6,7},{7,6},{8,9},{9,8},{10,11... | collective-permute-start | bytes 589832 | tf_op jit(solution)/shard_map/ppermute | solution.py:501
  67.2 6.9 %collective-permute-start.19 = (f32[2,192,128]{2,1,0:T(8,128)S(1)}, f32[2,192,128]{2,1,0:T(8,128)S(1)}, u32[]{:S(2)}, u32[]{:S(2)}) collective-permute-start(f32[2,192,128]{2,1,0:T(8,128)S(1)} %get-tuple-element.85), channel_id=1, source_target_pairs={{0,3},{1,2},{2,1},{3,0},{4,7},{5,6},{6,5},{7,4},{8,11},{9,10},{10,... | collective-permute-start | bytes 589832 | tf_op jit(solution)/shard_map/ppermute | solution.py:512
  67.2 6.9 %collective-permute-start.18 = (f32[2,192,128]{2,1,0:T(8,128)S(1)}, f32[2,192,128]{2,1,0:T(8,128)S(1)}, u32[]{:S(2)}, u32[]{:S(2)}) collective-permute-start(f32[2,192,128]{2,1,0:T(8,128)S(1)} %get-tuple-element.97), channel_id=1, source_target_pairs={{0,1},{1,0},{2,3},{3,2},{4,5},{5,4},{6,7},{7,6},{8,9},{9,8},{10,11... | collective-permute-start | bytes 589832 | tf_op jit(solution)/shard_map/ppermute | solution.py:501
  67.4 11.0 %collective-permute-start.16 = (f32[2,192,128]{2,1,0:T(8,128)S(1)}, f32[2,192,128]{2,1,0:T(8,128)S(1)}, u32[]{:S(2)}, u32[]{:S(2)}) collective-permute-start(f32[2,192,128]{2,1,0:T(8,128)S(1)} %get-tuple-element.88), channel_id=1, source_target_pairs={{0,3},{1,2},{2,1},{3,0},{4,7},{5,6},{6,5},{7,4},{8,11},{9,10},{10,... | collective-permute-start | bytes 589832 | tf_op jit(solution)/shard_map/ppermute | solution.py:512
  71.7 9.6 %collective-permute-start.23 = (f32[2,96,128]{2,1,0:T(8,128)S(1)}, f32[2,96,128]{2,1,0:T(8,128)S(1)}, u32[]{:S(2)}, u32[]{:S(2)}) collective-permute-start(f32[2,96,128]{2,1,0:T(8,128)S(1)} %get-tuple-element.107), channel_id=1, source_target_pairs={{0,1},{1,0},{2,3},{3,2},{4,5},{5,4},{6,7},{7,6},{8,9},{9,8},{10,11... | collective-permute-start | bytes 294920 | tf_op jit(solution)/shard_map/ppermute | solution.py:501
  81.0 9.1 %collective-permute-start.21 = (f32[2,288,128]{2,1,0:T(8,128)S(1)}, f32[2,288,128]{2,1,0:T(8,128)S(1)}, u32[]{:S(2)}, u32[]{:S(2)}) collective-permute-start(f32[2,288,128]{2,1,0:T(8,128)S(1)} %get-tuple-element.103), channel_id=1, source_target_pairs={{0,3},{1,2},{2,1},{3,0},{4,7},{5,6},{6,5},{7,4},{8,11},{9,10},{10,... | collective-permute-start | bytes 884744 | tf_op jit(solution)/shard_map/ppermute | solution.py:512
  81.1 9.0 %collective-permute-start.20 = (f32[2,288,128]{2,1,0:T(8,128)S(1)}, f32[2,288,128]{2,1,0:T(8,128)S(1)}, u32[]{:S(2)}, u32[]{:S(2)}) collective-permute-start(f32[2,288,128]{2,1,0:T(8,128)S(1)} %get-tuple-element.102), channel_id=1, source_target_pairs={{0,1},{1,0},{2,3},{3,2},{4,5},{5,4},{6,7},{7,6},{8,9},{9,8},{10,11... | collective-permute-start | bytes 884744 | tf_op jit(solution)/shard_map/ppermute | solution.py:501
  81.3 18.1 %collective-permute-start.22 = (f32[2,96,384]{2,1,0:T(8,128)S(1)}, f32[2,96,384]{2,1,0:T(8,128)S(1)}, u32[]{:S(2)}, u32[]{:S(2)}) collective-permute-start(f32[2,96,384]{2,1,0:T(8,128)S(1)} %get-tuple-element.105), channel_id=1, source_target_pairs={{0,4},{4,8},{8,12},{12,16},{16,20},{20,24},{24,28},{28,0},{1,5},{5... | collective-permute-start | bytes 884744 | tf_op jit(solution)/shard_map/ppermute | solution.py:496
  81.4 18.0 %collective-permute-start.24 = (f32[2,96,384]{2,1,0:T(8,128)S(1)}, f32[2,96,384]{2,1,0:T(8,128)S(1)}, u32[]{:S(2)}, u32[]{:S(2)}) collective-permute-start(f32[2,96,384]{2,1,0:T(8,128)S(1)} %sums_near.1), channel_id=1, source_target_pairs={{0,28},{4,0},{8,4},{12,8},{16,12},{20,16},{24,20},{28,24},{1,29},{... | collective-permute-start | bytes 884744 | tf_op jit(solution)/shard_map/ppermute | solution.py:496
  86.1 13.3 %collective-permute-start.25 = (f32[2,96,128]{2,1,0:T(8,128)S(1)}, f32[2,96,128]{2,1,0:T(8,128)S(1)}, u32[]{:S(2)}, u32[]{:S(2)}) collective-permute-start(f32[2,96,128]{2,1,0:T(8,128)S(1)} %get-tuple-element.108), channel_id=1, source_target_pairs={{0,31},{1,30},{2,29},{3,28},{4,3},{5,2},{6,1},{7,0},{8,7},{9,6},{1... | collective-permute-start | bytes 294920 | tf_op jit(solution)/shard_map/ppermute | solution.py:522

commit v9 on v8

--- a/solution.py
+++ b/solution.py
@@ -558,7 +558,8 @@
     in_b = to_far(lo_b)
     bottom, lo_b = after((bottom, lo_b))
     near_strip, far_strip = edges(bottom)
-    bot_b, bot_a = to_far(far_strip), to_near(near_strip)
+    bot_b = to_far(far_strip)
+    bot_a = to_near(near_strip)
     tv_top = variation(
         [(top_a, 88, 8, "above"), (near, 0, 200)],
         [(top, 88, 8, "above"), (obj, 0, 200)],
@@ -567,7 +568,7 @@
     own = [(obj, MARGIN, last), (bottom, 0, MARGIN, "below")]
     whole = ((0, tile),)
     hi_o, hi_a = window(
-        1, True, consts, [(near, MARGIN, last), (bot_a, 0, MARGIN, "below")], own, [(mid_o, 0)], [(mid_a, 0)], whole
+        1, True, consts, [(near, MARGIN, last), (bot_a, 0, MARGIN, "below")], own, [(mid_o, 0)], [(mid_a, 0)], whole,
     )
     lo_o, hi_o = after((lo_o, hi_o))
     (top_sum,) = totals(lo_o, in_a, in_b, ((0, band),), [(tv_top, 0, MARGIN, MARGIN)])

time: 101 us -> 101 us (level)
  no operation moved by 1% of the time
where the time goes in v9:
time: 101 us
  waiting for transfers between devices  39.9 us (40%)
  Pallas kernels  30.4 us (30%)
  starting transfers between devices  28 us (28%)
  local copies, waits for them, and re-layouts  1.93 us (2%)
    pallas_call x8, Pallas kernels, window(): pl.pallas_call(kernel, out_shape=tuple(shapes), in_specs=[pl.BlockSpec(me...  21.2 us
    ppermute x6, waiting for transfers between devices, moved(): lax.ppermute(block, axis, [(n, (n + distance) % count) for n in range(cou...  16.7 us
    ppermute x9, waiting for transfers between devices, to_far(): return lax.ppermute(block, ('row', 'col'), route)  13.6 us
    ppermute x6, starting transfers between devices, moved(): lax.ppermute(block, axis, [(n, (n + distance) % count) for n in range(cou...  12.2 us
    ppermute x1, waiting for transfers between devices, to_far_above(): return lax.ppermute(block, ('row', 'col'), route)  9.11 us
    ppermute x10, starting transfers between devices, to_near(): lax.ppermute(block, ('row', 'col'), [(r * cols + c, r * cols + (c ^ 1)) f...  8.05 us
    ppermute x9, starting transfers between devices, to_far(): return lax.ppermute(block, ('row', 'col'), route)  6.89 us
    pallas_call x4, Pallas kernels, variation(): pl.pallas_call(functools.partial(variation_kernel, *plan), out_shape=jax....  5.33 us
  transfers between devices with their start and end apart: 26, of which 10 were waited for; matrix products, arithmetic and copies ran while one was open for 0% of the time, Pallas kernels for 29%

profile of v9, /device:TPU:0, one launch (start us, length us, event | category | flops | bytes accessed | tf_op | source)
XLA Modules:
  0.0 100.6 jit_solution(4046619726160401718)
XLA Ops:
  0.0 1.9 %fusion = (f32[2,96,384]{2,1,0:T(8,128)}, f32[2,96,384]{2,1,0:T(8,128)S(1)}) fusion(f32[2,384,384]{2,1,0:T(8,128)} %refs_1_.9), kind=kLoop, calls=%fused_computation.6 | loop fusion | bytes 1179648 | tf_op jit(solution)/shard_map/slice | solution.py:539
  1.9 3.0 %collective-permute-start = (f32[2,96,384]{2,1,0:T(8,128)}, f32[2,96,384]{2,1,0:T(8,128)S(1)}, u32[]{:S(2)}, u32[]{:S(2)}) collective-permute-start(f32[2,96,384]{2,1,0:T(8,128)} %get-tuple-element.111), channel_id=1, source_target_pairs={{0,4},{4,8},{8,12},{12,16},{16,20},{20,24},{24,28},{28,0},{1,5},{5... | collective-permute-start | bytes 884744 | tf_op jit(solution)/shard_map/ppermute | solution.py:496
  5.1 1.6 %collective-permute-start.3 = (f32[2,384,128]{2,1,0:T(8,128)S(1)}, f32[2,384,128]{2,1,0:T(8,128)S(1)}, u32[]{:S(2)}, u32[]{:S(2)}) collective-permute-start(f32[2,384,128]{2,1,0:T(8,128)S(1)} %get-tuple-element.110), channel_id=1, source_target_pairs={{0,3},{1,2},{2,1},{3,0},{4,7},{5,6},{6,5},{7,4},{8,11},{9,10},{10,... | collective-permute-start | bytes 1179656 | tf_op jit(solution)/shard_map/ppermute | solution.py:512
  6.7 8.5 %collective-permute-done.refs_7_.refs_2_.refs_0_ = f32[2,96,384]{2,1,0:T(8,128)S(1)} collective-permute-done((f32[2,96,384]{2,1,0:T(8,128)}, f32[2,96,384]{2,1,0:T(8,128)S(1)}, u32[]{:S(2)}, u32[]{:S(2)}) %collective-permute-start) | collective-permute-done | bytes 294944 | tf_op jit(solution)/shard_map/ppermute | solution.py:496
  15.2 1.7 %collective-permute-start.1 = (f32[2,96,384]{2,1,0:T(8,128)S(1)}, f32[2,96,384]{2,1,0:T(8,128)S(1)}, u32[]{:S(2)}, u32[]{:S(2)}) collective-permute-start(f32[2,96,384]{2,1,0:T(8,128)S(1)} %get-tuple-element.60), channel_id=1, source_target_pairs={{0,28},{4,0},{8,4},{12,8},{16,12},{20,16},{24,20},{28,24},{1,29},{... | collective-permute-start | bytes 884744 | tf_op jit(solution)/shard_map/ppermute | solution.py:496
  17.0 1.6 %collective-permute-start.2 = (f32[2,96,128]{2,1,0:T(8,128)S(1)}, f32[2,96,128]{2,1,0:T(8,128)S(1)}, u32[]{:S(2)}, u32[]{:S(2)}) collective-permute-start(f32[2,96,128]{2,1,0:T(8,128)S(1)} %get-tuple-element.116), channel_id=1, source_target_pairs={{0,3},{1,2},{2,1},{3,0},{4,7},{5,6},{6,5},{7,4},{8,11},{9,10},{10,... | collective-permute-start | bytes 294920 | tf_op jit(solution)/shard_map/ppermute | solution.py:512
  18.7 1.8 %prepare.1 = (f32[4,2,256,256]{3,2,1,0:T(8,128)S(1)}, f32[4,512,128]{2,1,0:T(8,128)S(1)}) custom-call(s32[2,2,2]{2,1,0:T(2,128)S(1)} %copy-done.5, f32[2,256,256]{2,1,0:T(8,128)S(1)} %copy-done.4, f32[512,512]{1,0:T(8,128)S(1)} %copy-done.3, bf16[256,256]{1,0:T(8,128)(2,1)S(1)} %copy-done.6), custom_call_target="tpu_custom_call" | custom-call | flops 100000 | bytes 100000 | tf_op jit(solution)/shard_map/prepare/pallas_call | solution.py:105
  20.5 2.6 %shard_map.73 = (f32[2,192,384]{2,1,0:T(8,128)S(1)}, f32[2,192,128]{2,1,0:T(8,128)S(1)}, f32[2,192,384]{2,1,0:T(8,128)S(1)}, f32[2,192,128]{2,1,0:T(8,128)S(1)}) custom-call(s32[2,2,2]{2,1,0:T(2,128)S(1)} %copy-done.5, bf16[4,256,256]{2,1,0:T(8,128)(2,1)S(1)} %copy-done.1, f32[4,128,128]{2,1,0:T(8,128)S(1)} %copy-done.2, ...), custom_call_target="tpu_custom_call" | custom-call | flops 100000 | bytes 100000 | tf_op jit(solution)/shard_map/pallas_call | solution.py:302
  23.1 2.7 %shard_map.74 = (f32[2,192,384]{2,1,0:T(8,128)S(1)}, f32[2,192,128]{2,1,0:T(8,128)S(1)}, f32[2,192,384]{2,1,0:T(8,128)S(1)}, f32[2,192,128]{2,1,0:T(8,128)S(1)}) custom-call(s32[2,2,2]{2,1,0:T(2,128)S(1)} %copy-done.5, bf16[4,256,256]{2,1,0:T(8,128)(2,1)S(1)} %copy-done.1, f32[4,128,128]{2,1,0:T(8,128)S(1)} %copy-done.2, ...), custom_call_target="tpu_custom_call" | custom-call | flops 100000 | bytes 100000 | tf_op jit(solution)/shard_map/pallas_call | solution.py:302
  25.8 0.4 collective-permute-start.11
  26.2 0.3 collective-permute-start.10
  26.5 0.2 collective-permute-start.7
  26.8 1.3 %variation.4.refs_0_ = f32[2,192,384]{2,1,0:T(8,128)S(1)} custom-call(f32[2,96,128]{2,1,0:T(8,128)S(1)} %collective-permute-done.4.refs_5_.refs_0_, f32[2,384,128]{2,1,0:T(8,128)S(1)} %collective-permute-done.5.refs_6_.refs_5_.refs_1_.refs_0_, f32[2,96,384]{2,1,0:T(8,128)S(1)} %collective-permute-done.refs_7_.refs_2_.refs_0_, f32[2,384,384]{2,1,0:T(8,128)S(1)} %copy-done, ...), custom_call_target="tpu_custom_call" | custom-call | flops 100000 | bytes 100000 | tf_op jit(solution)/shard_map/variation/pallas_call | solution.py:363
  28.1 2.7 %shard_map.75 = (f32[2,384,384]{2,1,0:T(8,128)S(1)}, f32[2,384,128]{2,1,0:T(8,128)S(1)}) custom-call(s32[2,2,2]{2,1,0:T(2,128)S(1)} %copy-done.5, bf16[4,256,256]{2,1,0:T(8,128)(2,1)S(1)} %copy-done.1, f32[4,128,128]{2,1,0:T(8,128)S(1)} %copy-done.2, f32[4,2,256,256]{3,2,1,0:T(8,128)S(1)} %get-tuple-element.58.refs_3_, ...), custom_call_target="tpu_custom_call" | custom-call | flops 100000 | bytes 100000 | tf_op jit(solution)/shard_map/pallas_call | solution.py:302
  30.8 2.0 %collective-permute-done.11.far_ref = f32[2,192,128]{2,1,0:T(8,128)S(1)} collective-permute-done((f32[2,192,128]{2,1,0:T(8,128)S(1)}, f32[2,192,128]{2,1,0:T(8,128)S(1)}, u32[]{:S(2)}, u32[]{:S(2)}) %collective-permute-start.11) | collective-permute-done | bytes 196640 | tf_op jit(solution)/shard_map/ppermute | solution.py:512
  32.9 1.5 %collective-permute-start.12 = (f32[2,192,384]{2,1,0:T(8,128)S(1)}, f32[2,192,384]{2,1,0:T(8,128)S(1)}, u32[]{:S(2)}, u32[]{:S(2)}) collective-permute-start(f32[2,192,384]{2,1,0:T(8,128)S(1)} %totals.5.refs_2_), channel_id=1, source_target_pairs={{0,28},{4,0},{8,4},{12,8},{16,12},{20,16},{24,20},{28,24},{1,29},{... | collective-permute-start | bytes 1769480 | tf_op jit(solution)/shard_map/ppermute | solution.py:496
  34.4 5.1 %collective-permute-done.6.refs_6_.refs_5_ = f32[2,96,128]{2,1,0:T(8,128)S(1)} collective-permute-done((f32[2,96,128]{2,1,0:T(8,128)S(1)}, f32[2,96,128]{2,1,0:T(8,128)S(1)}, u32[]{:S(2)}, u32[]{:S(2)}) %collective-permute-start.6) | collective-permute-done | bytes 98336 | tf_op jit(solution)/shard_map/ppermute | solution.py:512
  39.5 2.7 %shard_map.76 = (f32[2,384,384]{2,1,0:T(8,128)S(1)}, f32[2,384,128]{2,1,0:T(8,128)S(1)}) custom-call(s32[2,2,2]{2,1,0:T(2,128)S(1)} %copy-done.5, bf16[4,256,256]{2,1,0:T(8,128)(2,1)S(1)} %copy-done.1, f32[4,128,128]{2,1,0:T(8,128)S(1)} %copy-done.2, f32[4,2,256,256]{3,2,1,0:T(8,128)S(1)} %get-tuple-element.58.refs_3_, ...), custom_call_target="tpu_custom_call" | custom-call | flops 100000 | bytes 100000 | tf_op jit(solution)/shard_map/pallas_call | solution.py:302
  42.1 0.7 collective-permute-start.9
  42.8 1.8 %collective-permute-start.8 = (f32[2,384,128]{2,1,0:T(8,128)S(1)}, f32[2,384,128]{2,1,0:T(8,128)S(1)}, u32[]{:S(2)}, u32[]{:S(2)}) collective-permute-start(f32[2,384,128]{2,1,0:T(8,128)S(1)} %get-tuple-element.72), channel_id=1, source_target_pairs={{0,1},{1,0},{2,3},{3,2},{4,5},{5,4},{6,7},{7,6},{8,9},{9,8},{10,11... | collective-permute-start | bytes 1179656 | tf_op jit(solution)/shard_map/ppermute | solution.py:501
  44.6 1.3 %variation.5.refs_1_ = f32[2,192,384]{2,1,0:T(8,128)S(1)} custom-call(f32[2,384,128]{2,1,0:T(8,128)S(1)} %collective-permute-done.5.refs_6_.refs_5_.refs_1_.refs_0_, f32[2,96,128]{2,1,0:T(8,128)S(1)} %collective-permute-done.7.refs_6_.refs_1_, f32[2,384,384]{2,1,0:T(8,128)S(1)} %copy-done, f32[2,96,384]{2,1,0:T(8,128)S(1)} %collective-permute-done.1.refs_8_.refs_3_.refs_1_, ...), custom_call_target="tpu_custom_call" | custom-call | flops 100000 | bytes 100000 | tf_op jit(solution)/shard_map/variation/pallas_call | solution.py:363
  45.9 0.2 totals.4
  46.1 2.2 %collective-permute-done.12.refs_4_ = f32[2,192,384]{2,1,0:T(8,128)S(1)} collective-permute-done((f32[2,192,384]{2,1,0:T(8,128)S(1)}, f32[2,192,384]{2,1,0:T(8,128)S(1)}, u32[]{:S(2)}, u32[]{:S(2)}) %collective-permute-start.12) | collective-permute-done | bytes 589856 | tf_op jit(solution)/shard_map/ppermute | solution.py:496
  48.3 1.2 %collective-permute-start.15 = (f32[2,192,384]{2,1,0:T(8,128)S(1)}, f32[2,192,384]{2,1,0:T(8,128)S(1)}, u32[]{:S(2)}, u32[]{:S(2)}) collective-permute-start(f32[2,192,384]{2,1,0:T(8,128)S(1)} %get-tuple-element.78.refs_3_), channel_id=1, source_target_pairs={{0,4},{4,8},{8,12},{12,16},{16,20},{20,24},{24,28},{28,0},{1,5},{5... | collective-permute-start | bytes 1769480 | tf_op jit(solution)/shard_map/ppermute | solution.py:496
  49.5 0.2 update.2
  49.7 2.5 %collective-permute-start.14 = (f32[2,384,128]{2,1,0:T(8,128)S(1)}, f32[2,384,128]{2,1,0:T(8,128)S(1)}, u32[]{:S(2)}, u32[]{:S(2)}) collective-permute-start(f32[2,384,128]{2,1,0:T(8,128)S(1)} %get-tuple-element.82), channel_id=1, source_target_pairs={{0,1},{1,0},{2,3},{3,2},{4,5},{5,4},{6,7},{7,6},{8,9},{9,8},{10,11... | collective-permute-start | bytes 1179656 | tf_op jit(solution)/shard_map/ppermute | solution.py:501
  52.2 0.9 collective-permute-start.13
  53.1 0.5 collective-permute-done.14.refs_5_.refs_6_.refs_0_.refs_1_
  53.6 2.6 %shard_map.77 = (f32[2,192,384]{2,1,0:T(8,128)S(1)}, f32[2,192,128]{2,1,0:T(8,128)S(1)}, f32[2,192,384]{2,1,0:T(8,128)S(1)}, f32[2,192,128]{2,1,0:T(8,128)S(1)}) custom-call(s32[2,2,2]{2,1,0:T(2,128)S(1)} %copy-done.5, bf16[4,256,256]{2,1,0:T(8,128)(2,1)S(1)} %copy-done.1, f32[4,128,128]{2,1,0:T(8,128)S(1)} %copy-done.2, ...), custom_call_target="tpu_custom_call" | custom-call | flops 100000 | bytes 100000 | tf_op jit(solution)/shard_map/pallas_call | solution.py:302
  56.2 2.6 %shard_map.78 = (f32[2,192,384]{2,1,0:T(8,128)S(1)}, f32[2,192,128]{2,1,0:T(8,128)S(1)}, f32[2,192,384]{2,1,0:T(8,128)S(1)}, f32[2,192,128]{2,1,0:T(8,128)S(1)}) custom-call(s32[2,2,2]{2,1,0:T(2,128)S(1)} %copy-done.5, bf16[4,256,256]{2,1,0:T(8,128)(2,1)S(1)} %copy-done.1, f32[4,128,128]{2,1,0:T(8,128)S(1)} %copy-done.2, ...), custom_call_target="tpu_custom_call" | custom-call | flops 100000 | bytes 100000 | tf_op jit(solution)/shard_map/pallas_call | solution.py:302
  58.9 6.0 %collective-permute-done.15.refs_3_ = f32[2,192,384]{2,1,0:T(8,128)S(1)} collective-permute-done((f32[2,192,384]{2,1,0:T(8,128)S(1)}, f32[2,192,384]{2,1,0:T(8,128)S(1)}, u32[]{:S(2)}, u32[]{:S(2)}) %collective-permute-start.15) | collective-permute-done | bytes 589856 | tf_op jit(solution)/shard_map/ppermute | solution.py:496
  65.0 2.2 %collective-permute-start.17 = (f32[2,192,128]{2,1,0:T(8,128)S(1)}, f32[2,192,128]{2,1,0:T(8,128)S(1)}, u32[]{:S(2)}, u32[]{:S(2)}) collective-permute-start(f32[2,192,128]{2,1,0:T(8,128)S(1)} %get-tuple-element.89), channel_id=1, source_target_pairs={{0,1},{1,0},{2,3},{3,2},{4,5},{5,4},{6,7},{7,6},{8,9},{9,8},{10,11... | collective-permute-start | bytes 589832 | tf_op jit(solution)/shard_map/ppermute | solution.py:501
  67.2 0.2 collective-permute-start.18
  67.4 1.7 %collective-permute-start.16 = (f32[2,192,128]{2,1,0:T(8,128)S(1)}, f32[2,192,128]{2,1,0:T(8,128)S(1)}, u32[]{:S(2)}, u32[]{:S(2)}) collective-permute-start(f32[2,192,128]{2,1,0:T(8,128)S(1)} %get-tuple-element.88), channel_id=1, source_target_pairs={{0,3},{1,2},{2,1},{3,0},{4,7},{5,6},{6,5},{7,4},{8,11},{9,10},{10,... | collective-permute-start | bytes 589832 | tf_op jit(solution)/shard_map/ppermute | solution.py:512
  69.1 2.6 %shard_map.79 = (f32[2,96,384]{2,1,0:T(8,128)S(1)}, f32[2,96,128]{2,1,0:T(8,128)S(1)}, f32[2,288,384]{2,1,0:T(8,128)S(1)}, f32[2,288,128]{2,1,0:T(8,128)S(1)}) custom-call(s32[2,2,2]{2,1,0:T(2,128)S(1)} %copy-done.5, bf16[4,256,256]{2,1,0:T(8,128)(2,1)S(1)} %copy-done.1, f32[4,128,128]{2,1,0:T(8,128)S(1)} %copy-done.2, ...), custom_call_target="tpu_custom_call" | custom-call | flops 100000 | bytes 100000 | tf_op jit(solution)/shard_map/pallas_call | solution.py:302
  71.7 0.5 collective-permute-start.23
  72.2 1.3 %variation.6.refs_0_.refs_1_ = f32[2,192,384]{2,1,0:T(8,128)S(1)} custom-call(f32[2,384,128]{2,1,0:T(8,128)S(1)} %collective-permute-done.14.refs_5_.refs_6_.refs_0_.refs_1_, f32[2,384,384]{2,1,0:T(8,128)S(1)} %get-tuple-element.81.refs_6_.refs_8_.refs_1_.refs_3_.bottom_ref, f32[2,384,128]{2,1,0:T(8,128)S(1)} %collective-permute-done.13.refs_5_.refs_2_.refs_6_), custom_call_target="tpu_custom_call" | custom-call | flops 100000 | bytes 100000 | tf_op jit(solution)/shard_map/variation/pallas_call | solution.py:363
  73.5 0.6 collective-permute-done.19.far_ref
  74.3 4.1 %collective-permute-done.16.refs_5_.refs_4_ = f32[2,192,128]{2,1,0:T(8,128)S(1)} collective-permute-done((f32[2,192,128]{2,1,0:T(8,128)S(1)}, f32[2,192,128]{2,1,0:T(8,128)S(1)}, u32[]{:S(2)}, u32[]{:S(2)}) %collective-permute-start.16) | collective-permute-done | bytes 196640 | tf_op jit(solution)/shard_map/ppermute | solution.py:512
  78.4 2.7 %shard_map.80 = (f32[2,96,384]{2,1,0:T(8,128)S(1)}, f32[2,96,128]{2,1,0:T(8,128)S(1)}, f32[2,288,384]{2,1,0:T(8,128)S(1)}, f32[2,288,128]{2,1,0:T(8,128)S(1)}) custom-call(s32[2,2,2]{2,1,0:T(2,128)S(1)} %copy-done.5, bf16[4,256,256]{2,1,0:T(8,128)(2,1)S(1)} %copy-done.1, f32[4,128,128]{2,1,0:T(8,128)S(1)} %copy-done.2, ...), custom_call_target="tpu_custom_call" | custom-call | flops 100000 | bytes 100000 | tf_op jit(solution)/shard_map/pallas_call | solution.py:302
  81.1 0.2 collective-permute-start.20
  81.4 4.8 %collective-permute-start.24 = (f32[2,96,384]{2,1,0:T(8,128)S(1)}, f32[2,96,384]{2,1,0:T(8,128)S(1)}, u32[]{:S(2)}, u32[]{:S(2)}) collective-permute-start(f32[2,96,384]{2,1,0:T(8,128)S(1)} %sums_near.1), channel_id=1, source_target_pairs={{0,28},{4,0},{8,4},{12,8},{16,12},{20,16},{24,20},{28,24},{1,29},{... | collective-permute-start | bytes 884744 | tf_op jit(solution)/shard_map/ppermute | solution.py:496
  86.1 0.9 collective-permute-start.25
  87.0 1.3 %variation.7.refs_0_ = f32[2,192,384]{2,1,0:T(8,128)S(1)} custom-call(f32[2,192,128]{2,1,0:T(8,128)S(1)} %collective-permute-done.17.refs_5_.refs_0_, f32[2,384,128]{2,1,0:T(8,128)S(1)} %collective-permute-done.14.refs_5_.refs_6_.refs_0_.refs_1_, f32[2,192,384]{2,1,0:T(8,128)S(1)} %get-tuple-element.87.refs_7_.refs_2_.top_ref, ...), custom_call_target="tpu_custom_call" | custom-call | flops 100000 | bytes 100000 | tf_op jit(solution)/shard_map/variation/pallas_call | solution.py:363
  88.4 1.8 %collective-permute-done.21.far_ref = f32[2,288,128]{2,1,0:T(8,128)S(1)} collective-permute-done((f32[2,288,128]{2,1,0:T(8,128)S(1)}, f32[2,288,128]{2,1,0:T(8,128)S(1)}, u32[]{:S(2)}, u32[]{:S(2)}) %collective-permute-start.21) | collective-permute-done | bytes 294944 | tf_op jit(solution)/shard_map/ppermute | solution.py:512
  90.1 0.2 totals.7.mid_ref
  90.3 9.1 %collective-permute-done.25.corner_ref = f32[2,96,128]{2,1,0:T(8,128)S(1)} collective-permute-done((f32[2,96,128]{2,1,0:T(8,128)S(1)}, f32[2,96,128]{2,1,0:T(8,128)S(1)}, u32[]{:S(2)}, u32[]{:S(2)}) %collective-permute-start.25) | collective-permute-done | bytes 98336 | tf_op jit(solution)/shard_map/ppermute | solution.py:522
  99.4 1.2 %finish.1 = f32[2,384,384]{2,1,0:T(8,128)} custom-call(f32[2,192,384]{2,1,0:T(8,128)S(1)} %get-tuple-element.87.refs_7_.refs_2_.top_ref, f32[2,384,384]{2,1,0:T(8,128)S(1)} %get-tuple-element.81.refs_6_.refs_8_.refs_1_.refs_3_.bottom_ref, f32[2,288,384]{2,1,0:T(8,128)S(1)} %totals.7.mid_ref, f32[2,96,384]{2,1,0:T(8,128)S(1)} %get-tuple-element.104.low_ref, ...), custom_call_target="tpu_custom_call" | custom-call | flops 100000 | bytes 100000 | tf_op jit(solution)/shard_map/finish/pallas_call | solution.py:483
  (43 shorter events, 0.7 us)
Async XLA Ops:
  0.0 4.9 %copy-start = (f32[2,384,384]{2,1,0:T(8,128)S(1)}, f32[2,384,384]{2,1,0:T(8,128)}, u32[]{:S(2)}) copy-start(f32[2,384,384]{2,1,0:T(8,128)} %refs_1_.9) | copy-start | bytes 3538948
  1.9 16.8 %copy-start.3 = (f32[512,512]{1,0:T(8,128)S(1)}, f32[512,512]{1,0:T(8,128)}, u32[]{:S(2)}) copy-start(f32[512,512]{1,0:T(8,128)} %amp_ref.1) | copy-start | bytes 3145732
  1.9 16.8 %copy-start.4 = (f32[2,256,256]{2,1,0:T(8,128)S(1)}, f32[2,256,256]{2,1,0:T(8,128)}, u32[]{:S(2)}) copy-start(f32[2,256,256]{2,1,0:T(8,128)} %probe_ref.1) | copy-start | bytes 1572868
  1.9 16.8 %copy-start.5 = (s32[2,2,2]{2,1,0:T(2,128)S(1)}, s32[2,2,2]{2,1,0:T(2,128)}, u32[]{:S(2)}) copy-start(s32[2,2,2]{2,1,0:T(2,128)} %refs_0_.17) | copy-start | bytes 100
  1.9 16.8 %copy-start.6 = (bf16[256,256]{1,0:T(8,128)(2,1)S(1)}, bf16[256,256]{1,0:T(8,128)(2,1)}, u32[]{:S(2)}) copy-start(bf16[256,256]{1,0:T(8,128)(2,1)} %constant.30.clone.order_ref) | copy-start | bytes 393220
  1.9 13.3 %collective-permute-start = (f32[2,96,384]{2,1,0:T(8,128)}, f32[2,96,384]{2,1,0:T(8,128)S(1)}, u32[]{:S(2)}, u32[]{:S(2)}) collective-permute-start(f32[2,96,384]{2,1,0:T(8,128)} %get-tuple-element.111), channel_id=1, source_target_pairs={{0,4},{4,8},{8,12},{12,16},{16,20},{20,24},{24,28},{28,0},{1,5},{5... | collective-permute-start | bytes 884744 | tf_op jit(solution)/shard_map/ppermute | solution.py:496
  5.0 15.5 %copy-start.1 = (bf16[4,256,256]{2,1,0:T(8,128)(2,1)S(1)}, bf16[4,256,256]{2,1,0:T(8,128)(2,1)}, u32[]{:S(2)}) copy-start(bf16[4,256,256]{2,1,0:T(8,128)(2,1)} %constant.28.clone.refs_1_) | copy-start | bytes 1572868
  5.0 15.5 %copy-start.2 = (f32[4,128,128]{2,1,0:T(8,128)S(1)}, f32[4,128,128]{2,1,0:T(8,128)}, u32[]{:S(2)}) copy-start(f32[4,128,128]{2,1,0:T(8,128)} %constant.29.clone.refs_2_) | copy-start | bytes 786436
  5.0 15.4 %collective-permute-start.5 = (f32[2,384,128]{2,1,0:T(8,128)S(1)}, f32[2,384,128]{2,1,0:T(8,128)S(1)}, u32[]{:S(2)}, u32[]{:S(2)}) collective-permute-start(f32[2,384,128]{2,1,0:T(8,128)S(1)} %get-tuple-element.109), channel_id=1, source_target_pairs={{0,1},{1,0},{2,3},{3,2},{4,5},{5,4},{6,7},{7,6},{8,9},{9,8},{10,11... | collective-permute-start | bytes 1179656 | tf_op jit(solution)/shard_map/ppermute | solution.py:501
  5.1 18.0 %collective-permute-start.3 = (f32[2,384,128]{2,1,0:T(8,128)S(1)}, f32[2,384,128]{2,1,0:T(8,128)S(1)}, u32[]{:S(2)}, u32[]{:S(2)}) collective-permute-start(f32[2,384,128]{2,1,0:T(8,128)S(1)} %get-tuple-element.110), channel_id=1, source_target_pairs={{0,3},{1,2},{2,1},{3,0},{4,7},{5,6},{6,5},{7,4},{8,11},{9,10},{10,... | collective-permute-start | bytes 1179656 | tf_op jit(solution)/shard_map/ppermute | solution.py:512
  15.2 11.3 %collective-permute-start.1 = (f32[2,96,384]{2,1,0:T(8,128)S(1)}, f32[2,96,384]{2,1,0:T(8,128)S(1)}, u32[]{:S(2)}, u32[]{:S(2)}) collective-permute-start(f32[2,96,384]{2,1,0:T(8,128)S(1)} %get-tuple-element.60), channel_id=1, source_target_pairs={{0,28},{4,0},{8,4},{12,8},{16,12},{20,16},{24,20},{28,24},{1,29},{... | collective-permute-start | bytes 884744 | tf_op jit(solution)/shard_map/ppermute | solution.py:496
  17.0 3.5 %collective-permute-start.4 = (f32[2,96,128]{2,1,0:T(8,128)S(1)}, f32[2,96,128]{2,1,0:T(8,128)S(1)}, u32[]{:S(2)}, u32[]{:S(2)}) collective-permute-start(f32[2,96,128]{2,1,0:T(8,128)S(1)} %get-tuple-element.115), channel_id=1, source_target_pairs={{0,1},{1,0},{2,3},{3,2},{4,5},{5,4},{6,7},{7,6},{8,9},{9,8},{10,11... | collective-permute-start | bytes 294920 | tf_op jit(solution)/shard_map/ppermute | solution.py:501
  17.0 6.1 %collective-permute-start.2 = (f32[2,96,128]{2,1,0:T(8,128)S(1)}, f32[2,96,128]{2,1,0:T(8,128)S(1)}, u32[]{:S(2)}, u32[]{:S(2)}) collective-permute-start(f32[2,96,128]{2,1,0:T(8,128)S(1)} %get-tuple-element.116), channel_id=1, source_target_pairs={{0,3},{1,2},{2,1},{3,0},{4,7},{5,6},{6,5},{7,4},{8,11},{9,10},{10,... | collective-permute-start | bytes 294920 | tf_op jit(solution)/shard_map/ppermute | solution.py:512
  25.8 7.0 %collective-permute-start.11 = (f32[2,192,128]{2,1,0:T(8,128)S(1)}, f32[2,192,128]{2,1,0:T(8,128)S(1)}, u32[]{:S(2)}, u32[]{:S(2)}) collective-permute-start(f32[2,192,128]{2,1,0:T(8,128)S(1)} %get-tuple-element.63), channel_id=1, source_target_pairs={{0,3},{1,2},{2,1},{3,0},{4,7},{5,6},{6,5},{7,4},{8,11},{9,10},{10,... | collective-permute-start | bytes 589832 | tf_op jit(solution)/shard_map/ppermute | solution.py:512
  26.2 6.6 %collective-permute-start.10 = (f32[2,192,128]{2,1,0:T(8,128)S(1)}, f32[2,192,128]{2,1,0:T(8,128)S(1)}, u32[]{:S(2)}, u32[]{:S(2)}) collective-permute-start(f32[2,192,128]{2,1,0:T(8,128)S(1)} %get-tuple-element.77), channel_id=1, source_target_pairs={{0,1},{1,0},{2,3},{3,2},{4,5},{5,4},{6,7},{7,6},{8,9},{9,8},{10,11... | collective-permute-start | bytes 589832 | tf_op jit(solution)/shard_map/ppermute | solution.py:501
  26.5 1.6 %collective-permute-start.7 = (f32[2,96,128]{2,1,0:T(8,128)S(1)}, f32[2,96,128]{2,1,0:T(8,128)S(1)}, u32[]{:S(2)}, u32[]{:S(2)}) collective-permute-start(f32[2,96,128]{2,1,0:T(8,128)S(1)} %get-tuple-element.113), channel_id=1, source_target_pairs={{0,1},{1,0},{2,3},{3,2},{4,5},{5,4},{6,7},{7,6},{8,9},{9,8},{10,11... | collective-permute-start | bytes 294920 | tf_op jit(solution)/shard_map/ppermute | solution.py:501
  32.9 15.4 %collective-permute-start.12 = (f32[2,192,384]{2,1,0:T(8,128)S(1)}, f32[2,192,384]{2,1,0:T(8,128)S(1)}, u32[]{:S(2)}, u32[]{:S(2)}) collective-permute-start(f32[2,192,384]{2,1,0:T(8,128)S(1)} %totals.5.refs_2_), channel_id=1, source_target_pairs={{0,28},{4,0},{8,4},{12,8},{16,12},{20,16},{24,20},{28,24},{1,29},{... | collective-permute-start | bytes 1769480 | tf_op jit(solution)/shard_map/ppermute | solution.py:496
  34.4 5.1 %collective-permute-start.6 = (f32[2,96,128]{2,1,0:T(8,128)S(1)}, f32[2,96,128]{2,1,0:T(8,128)S(1)}, u32[]{:S(2)}, u32[]{:S(2)}) collective-permute-start(f32[2,96,128]{2,1,0:T(8,128)S(1)} %get-tuple-element.114), channel_id=1, source_target_pairs={{0,3},{1,2},{2,1},{3,0},{4,7},{5,6},{6,5},{7,4},{8,11},{9,10},{10,... | collective-permute-start | bytes 294920 | tf_op jit(solution)/shard_map/ppermute | solution.py:512
  42.1 3.8 %collective-permute-start.9 = (f32[2,384,128]{2,1,0:T(8,128)S(1)}, f32[2,384,128]{2,1,0:T(8,128)S(1)}, u32[]{:S(2)}, u32[]{:S(2)}) collective-permute-start(f32[2,384,128]{2,1,0:T(8,128)S(1)} %get-tuple-element.73), channel_id=1, source_target_pairs={{1,2},{2,1},{5,6},{6,5},{9,10},{10,9},{13,14},{14,13},{17,18},{18,... | collective-permute-start | bytes 1179656 | tf_op jit(solution)/shard_map/ppermute | solution.py:512
  42.8 3.1 %collective-permute-start.8 = (f32[2,384,128]{2,1,0:T(8,128)S(1)}, f32[2,384,128]{2,1,0:T(8,128)S(1)}, u32[]{:S(2)}, u32[]{:S(2)}) collective-permute-start(f32[2,384,128]{2,1,0:T(8,128)S(1)} %get-tuple-element.72), channel_id=1, source_target_pairs={{0,1},{1,0},{2,3},{3,2},{4,5},{5,4},{6,7},{7,6},{8,9},{9,8},{10,11... | collective-permute-start | bytes 1179656 | tf_op jit(solution)/shard_map/ppermute | solution.py:501
  48.3 16.6 %collective-permute-start.15 = (f32[2,192,384]{2,1,0:T(8,128)S(1)}, f32[2,192,384]{2,1,0:T(8,128)S(1)}, u32[]{:S(2)}, u32[]{:S(2)}) collective-permute-start(f32[2,192,384]{2,1,0:T(8,128)S(1)} %get-tuple-element.78.refs_3_), channel_id=1, source_target_pairs={{0,4},{4,8},{8,12},{12,16},{16,20},{20,24},{24,28},{28,0},{1,5},{5... | collective-permute-start | bytes 1769480 | tf_op jit(solution)/shard_map/ppermute | solution.py:496
  49.7 3.9 %collective-permute-start.14 = (f32[2,384,128]{2,1,0:T(8,128)S(1)}, f32[2,384,128]{2,1,0:T(8,128)S(1)}, u32[]{:S(2)}, u32[]{:S(2)}) collective-permute-start(f32[2,384,128]{2,1,0:T(8,128)S(1)} %get-tuple-element.82), channel_id=1, source_target_pairs={{0,1},{1,0},{2,3},{3,2},{4,5},{5,4},{6,7},{7,6},{8,9},{9,8},{10,11... | collective-permute-start | bytes 1179656 | tf_op jit(solution)/shard_map/ppermute | solution.py:501
  52.2 4.0 %collective-permute-start.13 = (f32[2,384,128]{2,1,0:T(8,128)S(1)}, f32[2,384,128]{2,1,0:T(8,128)S(1)}, u32[]{:S(2)}, u32[]{:S(2)}) collective-permute-start(f32[2,384,128]{2,1,0:T(8,128)S(1)} %get-tuple-element.80), channel_id=1, source_target_pairs={{1,2},{2,1},{5,6},{6,5},{9,10},{10,9},{13,14},{14,13},{17,18},{18,... | collective-permute-start | bytes 1179656 | tf_op jit(solution)/shard_map/ppermute | solution.py:512
  65.0 4.1 %collective-permute-start.17 = (f32[2,192,128]{2,1,0:T(8,128)S(1)}, f32[2,192,128]{2,1,0:T(8,128)S(1)}, u32[]{:S(2)}, u32[]{:S(2)}) collective-permute-start(f32[2,192,128]{2,1,0:T(8,128)S(1)} %get-tuple-element.89), channel_id=1, source_target_pairs={{0,1},{1,0},{2,3},{3,2},{4,5},{5,4},{6,7},{7,6},{8,9},{9,8},{10,11... | collective-permute-start | bytes 589832 | tf_op jit(solution)/shard_map/ppermute | solution.py:501
  67.2 6.9 %collective-permute-start.19 = (f32[2,192,128]{2,1,0:T(8,128)S(1)}, f32[2,192,128]{2,1,0:T(8,128)S(1)}, u32[]{:S(2)}, u32[]{:S(2)}) collective-permute-start(f32[2,192,128]{2,1,0:T(8,128)S(1)} %get-tuple-element.85), channel_id=1, source_target_pairs={{0,3},{1,2},{2,1},{3,0},{4,7},{5,6},{6,5},{7,4},{8,11},{9,10},{10,... | collective-permute-start | bytes 589832 | tf_op jit(solution)/shard_map/ppermute | solution.py:512
  67.2 6.9 %collective-permute-start.18 = (f32[2,192,128]{2,1,0:T(8,128)S(1)}, f32[2,192,128]{2,1,0:T(8,128)S(1)}, u32[]{:S(2)}, u32[]{:S(2)}) collective-permute-start(f32[2,192,128]{2,1,0:T(8,128)S(1)} %get-tuple-element.97), channel_id=1, source_target_pairs={{0,1},{1,0},{2,3},{3,2},{4,5},{5,4},{6,7},{7,6},{8,9},{9,8},{10,11... | collective-permute-start | bytes 589832 | tf_op jit(solution)/shard_map/ppermute | solution.py:501
  67.4 11.0 %collective-permute-start.16 = (f32[2,192,128]{2,1,0:T(8,128)S(1)}, f32[2,192,128]{2,1,0:T(8,128)S(1)}, u32[]{:S(2)}, u32[]{:S(2)}) collective-permute-start(f32[2,192,128]{2,1,0:T(8,128)S(1)} %get-tuple-element.88), channel_id=1, source_target_pairs={{0,3},{1,2},{2,1},{3,0},{4,7},{5,6},{6,5},{7,4},{8,11},{9,10},{10,... | collective-permute-start | bytes 589832 | tf_op jit(solution)/shard_map/ppermute | solution.py:512
  71.7 9.6 %collective-permute-start.23 = (f32[2,96,128]{2,1,0:T(8,128)S(1)}, f32[2,96,128]{2,1,0:T(8,128)S(1)}, u32[]{:S(2)}, u32[]{:S(2)}) collective-permute-start(f32[2,96,128]{2,1,0:T(8,128)S(1)} %get-tuple-element.107), channel_id=1, source_target_pairs={{0,1},{1,0},{2,3},{3,2},{4,5},{5,4},{6,7},{7,6},{8,9},{9,8},{10,11... | collective-permute-start | bytes 294920 | tf_op jit(solution)/shard_map/ppermute | solution.py:501
  81.0 9.1 %collective-permute-start.21 = (f32[2,288,128]{2,1,0:T(8,128)S(1)}, f32[2,288,128]{2,1,0:T(8,128)S(1)}, u32[]{:S(2)}, u32[]{:S(2)}) collective-permute-start(f32[2,288,128]{2,1,0:T(8,128)S(1)} %get-tuple-element.103), channel_id=1, source_target_pairs={{0,3},{1,2},{2,1},{3,0},{4,7},{5,6},{6,5},{7,4},{8,11},{9,10},{10,... | collective-permute-start | bytes 884744 | tf_op jit(solution)/shard_map/ppermute | solution.py:512
  81.1 9.0 %collective-permute-start.20 = (f32[2,288,128]{2,1,0:T(8,128)S(1)}, f32[2,288,128]{2,1,0:T(8,128)S(1)}, u32[]{:S(2)}, u32[]{:S(2)}) collective-permute-start(f32[2,288,128]{2,1,0:T(8,128)S(1)} %get-tuple-element.102), channel_id=1, source_target_pairs={{0,1},{1,0},{2,3},{3,2},{4,5},{5,4},{6,7},{7,6},{8,9},{9,8},{10,11... | collective-permute-start | bytes 884744 | tf_op jit(solution)/shard_map/ppermute | solution.py:501
  81.3 18.1 %collective-permute-start.22 = (f32[2,96,384]{2,1,0:T(8,128)S(1)}, f32[2,96,384]{2,1,0:T(8,128)S(1)}, u32[]{:S(2)}, u32[]{:S(2)}) collective-permute-start(f32[2,96,384]{2,1,0:T(8,128)S(1)} %get-tuple-element.105), channel_id=1, source_target_pairs={{0,4},{4,8},{8,12},{12,16},{16,20},{20,24},{24,28},{28,0},{1,5},{5... | collective-permute-start | bytes 884744 | tf_op jit(solution)/shard_map/ppermute | solution.py:496
  81.4 18.0 %collective-permute-start.24 = (f32[2,96,384]{2,1,0:T(8,128)S(1)}, f32[2,96,384]{2,1,0:T(8,128)S(1)}, u32[]{:S(2)}, u32[]{:S(2)}) collective-permute-start(f32[2,96,384]{2,1,0:T(8,128)S(1)} %sums_near.1), channel_id=1, source_target_pairs={{0,28},{4,0},{8,4},{12,8},{16,12},{20,16},{24,20},{28,24},{1,29},{... | collective-permute-start | bytes 884744 | tf_op jit(solution)/shard_map/ppermute | solution.py:496
  86.1 13.3 %collective-permute-start.25 = (f32[2,96,128]{2,1,0:T(8,128)S(1)}, f32[2,96,128]{2,1,0:T(8,128)S(1)}, u32[]{:S(2)}, u32[]{:S(2)}) collective-permute-start(f32[2,96,128]{2,1,0:T(8,128)S(1)} %get-tuple-element.108), channel_id=1, source_target_pairs={{0,31},{1,30},{2,29},{3,28},{4,3},{5,2},{6,1},{7,0},{8,7},{9,6},{1... | collective-permute-start | bytes 294920 | tf_op jit(solution)/shard_map/ppermute | solution.py:522

commit v10 on v7

--- a/solution.py
+++ b/solution.py
@@ -464,9 +464,10 @@
     )(*operands)
 
 
-def moved(block, axis, distance):
+def moved(block, axis, distance, ring=True):
     count = lax.axis_size(axis)
-    return lax.ppermute(block, axis, [(n, (n + distance) % count) for n in range(count)])
+    route = [(n, (n + distance) % count) for n in range(count) if ring or 0 <= n + distance < count]
+    return lax.ppermute(block, axis, route)
 
 
 def to_near(block):
@@ -499,7 +500,7 @@
     obj = object_field
     after = lax.optimization_barrier
 
-    top = moved(obj[:, last:, :], "row", 1)
+    top = moved(obj[:, last:, :], "row", 1, ring=False)
     near_strip, far_strip = edges(obj)
     far, near = to_far(far_strip), to_near(near_strip)
     up_rows, top = after((obj[:, :MARGIN, :], top))

time: 104 us -> 107 us (1.029); the launches traced: 102 us -> 107 us
  starting transfers between devices: 36.2 us -> 41.8 us
  waiting for transfers between devices: 33.4 us -> 32 us
    ppermute x6, starting transfers between devices: 13.9 us -> 19.7 us  [moved(): return lax.ppermute(block, axis, route)]
    ppermute x6, waiting for transfers between devices: 21.4 us -> 20 us  [moved(): return lax.ppermute(block, axis, route)]
  transfers between devices with their start and end apart: 26 -> 26, of which waited for: 10 -> 10; matrix products, arithmetic and copies ran while one was open for 0% -> 0% of each run, Pallas kernels for 26% -> 25%
where the time goes in v10:
time: 107 us
  starting transfers between devices  41.8 us (39%)
  waiting for transfers between devices  32 us (30%)
  Pallas kernels  30.4 us (28%)
  local copies, waits for them, and re-layouts  1.93 us (2%)
    pallas_call x8, Pallas kernels, window(): pl.pallas_call(kernel, out_shape=tuple(shapes), in_specs=[pl.BlockSpec(me...  21.2 us
    ppermute x6, waiting for transfers between devices, moved(): return lax.ppermute(block, axis, route)  20 us
    ppermute x6, starting transfers between devices, moved(): return lax.ppermute(block, axis, route)  19.7 us
    ppermute x10, starting transfers between devices, to_near(): lax.ppermute(block, ('row', 'col'), [(r * cols + c, r * cols + (c ^ 1)) f...  12.2 us
    ppermute x10, waiting for transfers between devices, to_far(): return lax.ppermute(block, ('row', 'col'), route)  11.5 us
    ppermute x10, starting transfers between devices, to_far(): return lax.ppermute(block, ('row', 'col'), route)  9.96 us
    pallas_call x4, Pallas kernels, variation(): pl.pallas_call(functools.partial(variation_kernel, *plan), out_shape=jax....  5.33 us
  transfers between devices with their start and end apart: 26, of which 10 were waited for; matrix products, arithmetic and copies ran while one was open for 0% of the time, Pallas kernels for 25%

profile of v10, /device:TPU:0, one launch (start us, length us, event | category | flops | bytes accessed | tf_op | source)
XLA Modules:
  0.0 106.6 jit_solution(877646301226553502)
XLA Ops:
  0.0 1.9 %fusion = (f32[2,96,384]{2,1,0:T(8,128)}, f32[2,96,384]{2,1,0:T(8,128)S(1)}) fusion(f32[2,384,384]{2,1,0:T(8,128)} %refs_1_.9), kind=kLoop, calls=%fused_computation.6 | loop fusion | bytes 1179648 | tf_op jit(solution)/shard_map/slice | solution.py:503
  1.9 5.0 %collective-permute-start = (f32[2,96,384]{2,1,0:T(8,128)}, f32[2,96,384]{2,1,0:T(8,128)S(1)}, u32[]{:S(2)}, u32[]{:S(2)}) collective-permute-start(f32[2,96,384]{2,1,0:T(8,128)} %get-tuple-element.107), channel_id=1, source_target_pairs={{0,4},{4,8},{8,12},{12,16},{16,20},{20,24},{24,28},{1,5},{5,9},{9,... | collective-permute-start | bytes 884744 | tf_op jit(solution)/shard_map/ppermute | solution.py:470
  7.1 1.6 %collective-permute-start.3 = (f32[2,384,128]{2,1,0:T(8,128)S(1)}, f32[2,384,128]{2,1,0:T(8,128)S(1)}, u32[]{:S(2)}, u32[]{:S(2)}) collective-permute-start(f32[2,384,128]{2,1,0:T(8,128)S(1)} %get-tuple-element.106), channel_id=1, source_target_pairs={{0,3},{1,2},{2,1},{3,0},{4,7},{5,6},{6,5},{7,4},{8,11},{9,10},{10,... | collective-permute-start | bytes 1179656 | tf_op jit(solution)/shard_map/ppermute | solution.py:486
  8.8 4.7 %collective-permute-done.refs_7_.refs_2_.refs_0_ = f32[2,96,384]{2,1,0:T(8,128)S(1)} collective-permute-done((f32[2,96,384]{2,1,0:T(8,128)}, f32[2,96,384]{2,1,0:T(8,128)S(1)}, u32[]{:S(2)}, u32[]{:S(2)}) %collective-permute-start) | collective-permute-done | bytes 294944 | tf_op jit(solution)/shard_map/ppermute | solution.py:470
  13.5 5.4 %collective-permute-start.1 = (f32[2,96,384]{2,1,0:T(8,128)S(1)}, f32[2,96,384]{2,1,0:T(8,128)S(1)}, u32[]{:S(2)}, u32[]{:S(2)}) collective-permute-start(f32[2,96,384]{2,1,0:T(8,128)S(1)} %get-tuple-element.58), channel_id=1, source_target_pairs={{0,28},{4,0},{8,4},{12,8},{16,12},{20,16},{24,20},{28,24},{1,29},{... | collective-permute-start | bytes 884744 | tf_op jit(solution)/shard_map/ppermute | solution.py:470
  19.0 1.6 %collective-permute-start.2 = (f32[2,96,128]{2,1,0:T(8,128)S(1)}, f32[2,96,128]{2,1,0:T(8,128)S(1)}, u32[]{:S(2)}, u32[]{:S(2)}) collective-permute-start(f32[2,96,128]{2,1,0:T(8,128)S(1)} %get-tuple-element.112), channel_id=1, source_target_pairs={{0,3},{1,2},{2,1},{3,0},{4,7},{5,6},{6,5},{7,4},{8,11},{9,10},{10,... | collective-permute-start | bytes 294920 | tf_op jit(solution)/shard_map/ppermute | solution.py:486
  20.6 1.8 %prepare.1 = (f32[4,2,256,256]{3,2,1,0:T(8,128)S(1)}, f32[4,512,128]{2,1,0:T(8,128)S(1)}) custom-call(s32[2,2,2]{2,1,0:T(2,128)S(1)} %copy-done.5, f32[2,256,256]{2,1,0:T(8,128)S(1)} %copy-done.4, f32[512,512]{1,0:T(8,128)S(1)} %copy-done.3, bf16[256,256]{1,0:T(8,128)(2,1)S(1)} %copy-done.6), custom_call_target="tpu_custom_call" | custom-call | flops 100000 | bytes 100000 | tf_op jit(solution)/shard_map/prepare/pallas_call | solution.py:105
  22.5 2.6 %shard_map.73 = (f32[2,192,384]{2,1,0:T(8,128)S(1)}, f32[2,192,128]{2,1,0:T(8,128)S(1)}, f32[2,192,384]{2,1,0:T(8,128)S(1)}, f32[2,192,128]{2,1,0:T(8,128)S(1)}) custom-call(s32[2,2,2]{2,1,0:T(2,128)S(1)} %copy-done.5, bf16[4,256,256]{2,1,0:T(8,128)(2,1)S(1)} %copy-done.1, f32[4,128,128]{2,1,0:T(8,128)S(1)} %copy-done.2, ...), custom_call_target="tpu_custom_call" | custom-call | flops 100000 | bytes 100000 | tf_op jit(solution)/shard_map/pallas_call | solution.py:302
  25.1 2.7 %shard_map.74 = (f32[2,192,384]{2,1,0:T(8,128)S(1)}, f32[2,192,128]{2,1,0:T(8,128)S(1)}, f32[2,192,384]{2,1,0:T(8,128)S(1)}, f32[2,192,128]{2,1,0:T(8,128)S(1)}) custom-call(s32[2,2,2]{2,1,0:T(2,128)S(1)} %copy-done.5, bf16[4,256,256]{2,1,0:T(8,128)(2,1)S(1)} %copy-done.1, f32[4,128,128]{2,1,0:T(8,128)S(1)} %copy-done.2, ...), custom_call_target="tpu_custom_call" | custom-call | flops 100000 | bytes 100000 | tf_op jit(solution)/shard_map/pallas_call | solution.py:302
  27.8 0.2 collective-permute-start.9
  28.0 0.4 collective-permute-start.8
  28.5 1.3 %collective-permute-start.7 = (f32[2,96,128]{2,1,0:T(8,128)S(1)}, f32[2,96,128]{2,1,0:T(8,128)S(1)}, u32[]{:S(2)}, u32[]{:S(2)}) collective-permute-start(f32[2,96,128]{2,1,0:T(8,128)S(1)} %get-tuple-element.109), channel_id=1, source_target_pairs={{0,3},{1,2},{2,1},{3,0},{4,7},{5,6},{6,5},{7,4},{8,11},{9,10},{10,... | collective-permute-start | bytes 294920 | tf_op jit(solution)/shard_map/ppermute | solution.py:486
  29.8 0.4 collective-permute-start.6
  30.2 1.3 %variation.4.refs_0_ = f32[2,192,384]{2,1,0:T(8,128)S(1)} custom-call(f32[2,96,128]{2,1,0:T(8,128)S(1)} %collective-permute-done.4.refs_5_.refs_0_, f32[2,384,128]{2,1,0:T(8,128)S(1)} %collective-permute-done.5.refs_6_.refs_1_.refs_5_.refs_0_, f32[2,96,384]{2,1,0:T(8,128)S(1)} %collective-permute-done.refs_7_.refs_2_.refs_0_, f32[2,384,384]{2,1,0:T(8,128)S(1)} %copy-done, ...), custom_call_target="tpu_custom_call" | custom-call | flops 100000 | bytes 100000 | tf_op jit(solution)/shard_map/variation/pallas_call | solution.py:363
  31.5 3.2 %collective-permute-done.9.far_ref = f32[2,192,128]{2,1,0:T(8,128)S(1)} collective-permute-done((f32[2,192,128]{2,1,0:T(8,128)S(1)}, f32[2,192,128]{2,1,0:T(8,128)S(1)}, u32[]{:S(2)}, u32[]{:S(2)}) %collective-permute-start.9) | collective-permute-done | bytes 196640 | tf_op jit(solution)/shard_map/ppermute | solution.py:486
  34.9 1.5 %collective-permute-start.12 = (f32[2,192,384]{2,1,0:T(8,128)S(1)}, f32[2,192,384]{2,1,0:T(8,128)S(1)}, u32[]{:S(2)}, u32[]{:S(2)}) collective-permute-start(f32[2,192,384]{2,1,0:T(8,128)S(1)} %totals.5.refs_2_), channel_id=1, source_target_pairs={{0,28},{4,0},{8,4},{12,8},{16,12},{20,16},{24,20},{28,24},{1,29},{... | collective-permute-start | bytes 1769480 | tf_op jit(solution)/shard_map/ppermute | solution.py:470
  36.4 0.5 collective-permute-done.7.refs_6_.refs_5_
  36.9 2.6 %shard_map.75 = (f32[2,384,384]{2,1,0:T(8,128)S(1)}, f32[2,384,128]{2,1,0:T(8,128)S(1)}) custom-call(s32[2,2,2]{2,1,0:T(2,128)S(1)} %copy-done.5, bf16[4,256,256]{2,1,0:T(8,128)(2,1)S(1)} %copy-done.1, f32[4,128,128]{2,1,0:T(8,128)S(1)} %copy-done.2, f32[4,2,256,256]{3,2,1,0:T(8,128)S(1)} %get-tuple-element.56.refs_3_, ...), custom_call_target="tpu_custom_call" | custom-call | flops 100000 | bytes 100000 | tf_op jit(solution)/shard_map/pallas_call | solution.py:302
  39.6 2.7 %shard_map.76 = (f32[2,384,384]{2,1,0:T(8,128)S(1)}, f32[2,384,128]{2,1,0:T(8,128)S(1)}) custom-call(s32[2,2,2]{2,1,0:T(2,128)S(1)} %copy-done.5, bf16[4,256,256]{2,1,0:T(8,128)(2,1)S(1)} %copy-done.1, f32[4,128,128]{2,1,0:T(8,128)S(1)} %copy-done.2, f32[4,2,256,256]{3,2,1,0:T(8,128)S(1)} %get-tuple-element.56.refs_3_, ...), custom_call_target="tpu_custom_call" | custom-call | flops 100000 | bytes 100000 | tf_op jit(solution)/shard_map/pallas_call | solution.py:302
  42.2 0.2 collective-permute-start.10
  42.4 0.7 collective-permute-start.11
  43.1 1.3 %variation.5.refs_1_ = f32[2,192,384]{2,1,0:T(8,128)S(1)} custom-call(f32[2,384,128]{2,1,0:T(8,128)S(1)} %collective-permute-done.5.refs_6_.refs_1_.refs_5_.refs_0_, f32[2,96,128]{2,1,0:T(8,128)S(1)} %collective-permute-done.6.refs_6_.refs_1_, f32[2,384,384]{2,1,0:T(8,128)S(1)} %copy-done, f32[2,96,384]{2,1,0:T(8,128)S(1)} %collective-permute-done.1.refs_8_.refs_3_.refs_1_, ...), custom_call_target="tpu_custom_call" | custom-call | flops 100000 | bytes 100000 | tf_op jit(solution)/shard_map/variation/pallas_call | solution.py:363
  44.5 0.2 totals.6
  44.7 0.3 collective-permute-start.15
  45.0 5.8 %collective-permute-done.12.refs_4_ = f32[2,192,384]{2,1,0:T(8,128)S(1)} collective-permute-done((f32[2,192,384]{2,1,0:T(8,128)S(1)}, f32[2,192,384]{2,1,0:T(8,128)S(1)}, u32[]{:S(2)}, u32[]{:S(2)}) %collective-permute-start.12) | collective-permute-done | bytes 589856 | tf_op jit(solution)/shard_map/ppermute | solution.py:470
  50.8 0.2 update.2
  51.0 1.7 %collective-permute-start.14 = (f32[2,384,128]{2,1,0:T(8,128)S(1)}, f32[2,384,128]{2,1,0:T(8,128)S(1)}, u32[]{:S(2)}, u32[]{:S(2)}) collective-permute-start(f32[2,384,128]{2,1,0:T(8,128)S(1)} %get-tuple-element.77), channel_id=1, source_target_pairs={{0,1},{1,0},{2,3},{3,2},{4,5},{5,4},{6,7},{7,6},{8,9},{9,8},{10,11... | collective-permute-start | bytes 1179656 | tf_op jit(solution)/shard_map/ppermute | solution.py:475
  52.7 0.9 collective-permute-start.13
  53.6 0.5 collective-permute-done.14.refs_5_.refs_6_.refs_0_.refs_1_
  54.1 2.6 %shard_map.77 = (f32[2,192,384]{2,1,0:T(8,128)S(1)}, f32[2,192,128]{2,1,0:T(8,128)S(1)}, f32[2,192,384]{2,1,0:T(8,128)S(1)}, f32[2,192,128]{2,1,0:T(8,128)S(1)}) custom-call(s32[2,2,2]{2,1,0:T(2,128)S(1)} %copy-done.5, bf16[4,256,256]{2,1,0:T(8,128)(2,1)S(1)} %copy-done.1, f32[4,128,128]{2,1,0:T(8,128)S(1)} %copy-done.2, ...), custom_call_target="tpu_custom_call" | custom-call | flops 100000 | bytes 100000 | tf_op jit(solution)/shard_map/pallas_call | solution.py:302
  56.7 2.7 %shard_map.78 = (f32[2,192,384]{2,1,0:T(8,128)S(1)}, f32[2,192,128]{2,1,0:T(8,128)S(1)}, f32[2,192,384]{2,1,0:T(8,128)S(1)}, f32[2,192,128]{2,1,0:T(8,128)S(1)}) custom-call(s32[2,2,2]{2,1,0:T(2,128)S(1)} %copy-done.5, bf16[4,256,256]{2,1,0:T(8,128)(2,1)S(1)} %copy-done.1, f32[4,128,128]{2,1,0:T(8,128)S(1)} %copy-done.2, ...), custom_call_target="tpu_custom_call" | custom-call | flops 100000 | bytes 100000 | tf_op jit(solution)/shard_map/pallas_call | solution.py:302
  59.5 8.7 %collective-permute-start.17 = (f32[2,192,128]{2,1,0:T(8,128)S(1)}, f32[2,192,128]{2,1,0:T(8,128)S(1)}, u32[]{:S(2)}, u32[]{:S(2)}) collective-permute-start(f32[2,192,128]{2,1,0:T(8,128)S(1)} %get-tuple-element.85), channel_id=1, source_target_pairs={{0,1},{1,0},{2,3},{3,2},{4,5},{5,4},{6,7},{7,6},{8,9},{9,8},{10,11... | collective-permute-start | bytes 589832 | tf_op jit(solution)/shard_map/ppermute | solution.py:475
  68.3 1.7 %collective-permute-start.19 = (f32[2,192,128]{2,1,0:T(8,128)S(1)}, f32[2,192,128]{2,1,0:T(8,128)S(1)}, u32[]{:S(2)}, u32[]{:S(2)}) collective-permute-start(f32[2,192,128]{2,1,0:T(8,128)S(1)} %get-tuple-element.80), channel_id=1, source_target_pairs={{0,3},{1,2},{2,1},{3,0},{4,7},{5,6},{6,5},{7,4},{8,11},{9,10},{10,... | collective-permute-start | bytes 589832 | tf_op jit(solution)/shard_map/ppermute | solution.py:486
  70.2 1.3 %variation.6.refs_0_.refs_1_ = f32[2,192,384]{2,1,0:T(8,128)S(1)} custom-call(f32[2,384,128]{2,1,0:T(8,128)S(1)} %collective-permute-done.14.refs_5_.refs_6_.refs_0_.refs_1_, f32[2,384,384]{2,1,0:T(8,128)S(1)} %get-tuple-element.76.refs_6_.refs_8_.refs_1_.refs_3_.bottom_ref, f32[2,384,128]{2,1,0:T(8,128)S(1)} %collective-permute-done.13.refs_5_.refs_2_.refs_6_), custom_call_target="tpu_custom_call" | custom-call | flops 100000 | bytes 100000 | tf_op jit(solution)/shard_map/variation/pallas_call | solution.py:363
  71.5 2.6 %shard_map.79 = (f32[2,96,384]{2,1,0:T(8,128)S(1)}, f32[2,96,128]{2,1,0:T(8,128)S(1)}, f32[2,288,384]{2,1,0:T(8,128)S(1)}, f32[2,288,128]{2,1,0:T(8,128)S(1)}) custom-call(s32[2,2,2]{2,1,0:T(2,128)S(1)} %copy-done.5, bf16[4,256,256]{2,1,0:T(8,128)(2,1)S(1)} %copy-done.1, f32[4,128,128]{2,1,0:T(8,128)S(1)} %copy-done.2, ...), custom_call_target="tpu_custom_call" | custom-call | flops 100000 | bytes 100000 | tf_op jit(solution)/shard_map/pallas_call | solution.py:302
  74.2 1.1 %collective-permute-done.19.far_ref = f32[2,192,128]{2,1,0:T(8,128)S(1)} collective-permute-done((f32[2,192,128]{2,1,0:T(8,128)S(1)}, f32[2,192,128]{2,1,0:T(8,128)S(1)}, u32[]{:S(2)}, u32[]{:S(2)}) %collective-permute-start.19) | collective-permute-done | bytes 196640 | tf_op jit(solution)/shard_map/ppermute | solution.py:486
  75.4 4.0 %collective-permute-done.16.refs_5_.refs_4_ = f32[2,192,128]{2,1,0:T(8,128)S(1)} collective-permute-done((f32[2,192,128]{2,1,0:T(8,128)S(1)}, f32[2,192,128]{2,1,0:T(8,128)S(1)}, u32[]{:S(2)}, u32[]{:S(2)}) %collective-permute-start.16) | collective-permute-done | bytes 196640 | tf_op jit(solution)/shard_map/ppermute | solution.py:486
  79.4 2.6 %shard_map.80 = (f32[2,96,384]{2,1,0:T(8,128)S(1)}, f32[2,96,128]{2,1,0:T(8,128)S(1)}, f32[2,288,384]{2,1,0:T(8,128)S(1)}, f32[2,288,128]{2,1,0:T(8,128)S(1)}) custom-call(s32[2,2,2]{2,1,0:T(2,128)S(1)} %copy-done.5, bf16[4,256,256]{2,1,0:T(8,128)(2,1)S(1)} %copy-done.1, f32[4,128,128]{2,1,0:T(8,128)S(1)} %copy-done.2, ...), custom_call_target="tpu_custom_call" | custom-call | flops 100000 | bytes 100000 | tf_op jit(solution)/shard_map/pallas_call | solution.py:302
  82.1 1.5 %collective-permute-start.24 = (f32[2,96,128]{2,1,0:T(8,128)S(1)}, f32[2,96,128]{2,1,0:T(8,128)S(1)}, u32[]{:S(2)}, u32[]{:S(2)}) collective-permute-start(f32[2,96,128]{2,1,0:T(8,128)S(1)} %get-tuple-element.104), channel_id=1, source_target_pairs={{0,3},{1,2},{2,1},{3,0},{4,7},{5,6},{6,5},{7,4},{8,11},{9,10},{10,... | collective-permute-start | bytes 294920 | tf_op jit(solution)/shard_map/ppermute | solution.py:486
  83.6 0.4 collective-permute-start.21
  84.0 0.4 collective-permute-start.20
  84.4 2.5 %collective-permute-done.24.far_ref = f32[2,96,128]{2,1,0:T(8,128)S(1)} collective-permute-done((f32[2,96,128]{2,1,0:T(8,128)S(1)}, f32[2,96,128]{2,1,0:T(8,128)S(1)}, u32[]{:S(2)}, u32[]{:S(2)}) %collective-permute-start.24) | collective-permute-done | bytes 98336 | tf_op jit(solution)/shard_map/ppermute | solution.py:486
  87.0 7.4 %collective-permute-start.25 = (f32[2,96,384]{2,1,0:T(8,128)S(1)}, f32[2,96,384]{2,1,0:T(8,128)S(1)}, u32[]{:S(2)}, u32[]{:S(2)}) collective-permute-start(f32[2,96,384]{2,1,0:T(8,128)S(1)} %totals.9), channel_id=1, source_target_pairs={{0,28},{4,0},{8,4},{12,8},{16,12},{20,16},{24,20},{28,24},{1,29},{... | collective-permute-start | bytes 884744 | tf_op jit(solution)/shard_map/ppermute | solution.py:470
  94.4 1.3 %variation.7.refs_0_ = f32[2,192,384]{2,1,0:T(8,128)S(1)} custom-call(f32[2,192,128]{2,1,0:T(8,128)S(1)} %collective-permute-done.17.refs_5_.refs_0_, f32[2,384,128]{2,1,0:T(8,128)S(1)} %collective-permute-done.14.refs_5_.refs_6_.refs_0_.refs_1_, f32[2,192,384]{2,1,0:T(8,128)S(1)} %get-tuple-element.83.refs_7_.refs_2_.top_ref, ...), custom_call_target="tpu_custom_call" | custom-call | flops 100000 | bytes 100000 | tf_op jit(solution)/shard_map/variation/pallas_call | solution.py:363
  95.7 0.2 totals.8.mid_ref
  95.9 3.2 %collective-permute-done.22.above_ref = f32[2,96,384]{2,1,0:T(8,128)S(1)} collective-permute-done((f32[2,96,384]{2,1,0:T(8,128)S(1)}, f32[2,96,384]{2,1,0:T(8,128)S(1)}, u32[]{:S(2)}, u32[]{:S(2)}) %collective-permute-start.22) | collective-permute-done | bytes 294944 | tf_op jit(solution)/shard_map/ppermute | solution.py:470
  99.2 6.2 %collective-permute-done.25.below_ref = f32[2,96,384]{2,1,0:T(8,128)S(1)} collective-permute-done((f32[2,96,384]{2,1,0:T(8,128)S(1)}, f32[2,96,384]{2,1,0:T(8,128)S(1)}, u32[]{:S(2)}, u32[]{:S(2)}) %collective-permute-start.25) | collective-permute-done | bytes 294944 | tf_op jit(solution)/shard_map/ppermute | solution.py:470
  105.4 1.2 %finish.1 = f32[2,384,384]{2,1,0:T(8,128)} custom-call(f32[2,192,384]{2,1,0:T(8,128)S(1)} %get-tuple-element.83.refs_7_.refs_2_.top_ref, f32[2,384,384]{2,1,0:T(8,128)S(1)} %get-tuple-element.76.refs_6_.refs_8_.refs_1_.refs_3_.bottom_ref, f32[2,288,384]{2,1,0:T(8,128)S(1)} %totals.8.mid_ref, f32[2,96,384]{2,1,0:T(8,128)S(1)} %get-tuple-element.100.low_ref, ...), custom_call_target="tpu_custom_call" | custom-call | flops 100000 | bytes 100000 | tf_op jit(solution)/shard_map/finish/pallas_call | solution.py:456
  (43 shorter events, 0.9 us)
Async XLA Ops:
  0.0 7.0 %copy-start = (f32[2,384,384]{2,1,0:T(8,128)S(1)}, f32[2,384,384]{2,1,0:T(8,128)}, u32[]{:S(2)}) copy-start(f32[2,384,384]{2,1,0:T(8,128)} %refs_1_.9) | copy-start | bytes 3538948
  1.9 18.7 %copy-start.3 = (f32[512,512]{1,0:T(8,128)S(1)}, f32[512,512]{1,0:T(8,128)}, u32[]{:S(2)}) copy-start(f32[512,512]{1,0:T(8,128)} %amp_ref.1) | copy-start | bytes 3145732
  1.9 18.7 %copy-start.4 = (f32[2,256,256]{2,1,0:T(8,128)S(1)}, f32[2,256,256]{2,1,0:T(8,128)}, u32[]{:S(2)}) copy-start(f32[2,256,256]{2,1,0:T(8,128)} %probe_ref.1) | copy-start | bytes 1572868
  1.9 18.7 %copy-start.5 = (s32[2,2,2]{2,1,0:T(2,128)S(1)}, s32[2,2,2]{2,1,0:T(2,128)}, u32[]{:S(2)}) copy-start(s32[2,2,2]{2,1,0:T(2,128)} %refs_0_.17) | copy-start | bytes 100
  1.9 18.7 %copy-start.6 = (bf16[256,256]{1,0:T(8,128)(2,1)S(1)}, bf16[256,256]{1,0:T(8,128)(2,1)}, u32[]{:S(2)}) copy-start(bf16[256,256]{1,0:T(8,128)(2,1)} %constant.30.clone.order_ref) | copy-start | bytes 393220
  1.9 11.6 %collective-permute-start = (f32[2,96,384]{2,1,0:T(8,128)}, f32[2,96,384]{2,1,0:T(8,128)S(1)}, u32[]{:S(2)}, u32[]{:S(2)}) collective-permute-start(f32[2,96,384]{2,1,0:T(8,128)} %get-tuple-element.107), channel_id=1, source_target_pairs={{0,4},{4,8},{8,12},{12,16},{16,20},{20,24},{24,28},{1,5},{5,9},{9,... | collective-permute-start | bytes 884744 | tf_op jit(solution)/shard_map/ppermute | solution.py:470
  7.0 15.4 %copy-start.1 = (bf16[4,256,256]{2,1,0:T(8,128)(2,1)S(1)}, bf16[4,256,256]{2,1,0:T(8,128)(2,1)}, u32[]{:S(2)}) copy-start(bf16[4,256,256]{2,1,0:T(8,128)(2,1)} %constant.28.clone.refs_1_) | copy-start | bytes 1572868
  7.0 15.4 %copy-start.2 = (f32[4,128,128]{2,1,0:T(8,128)S(1)}, f32[4,128,128]{2,1,0:T(8,128)}, u32[]{:S(2)}) copy-start(f32[4,128,128]{2,1,0:T(8,128)} %constant.29.clone.refs_2_) | copy-start | bytes 786436
  7.1 15.4 %collective-permute-start.5 = (f32[2,384,128]{2,1,0:T(8,128)S(1)}, f32[2,384,128]{2,1,0:T(8,128)S(1)}, u32[]{:S(2)}, u32[]{:S(2)}) collective-permute-start(f32[2,384,128]{2,1,0:T(8,128)S(1)} %get-tuple-element.105), channel_id=1, source_target_pairs={{0,1},{1,0},{2,3},{3,2},{4,5},{5,4},{6,7},{7,6},{8,9},{9,8},{10,11... | collective-permute-start | bytes 1179656 | tf_op jit(solution)/shard_map/ppermute | solution.py:475
  7.1 18.0 %collective-permute-start.3 = (f32[2,384,128]{2,1,0:T(8,128)S(1)}, f32[2,384,128]{2,1,0:T(8,128)S(1)}, u32[]{:S(2)}, u32[]{:S(2)}) collective-permute-start(f32[2,384,128]{2,1,0:T(8,128)S(1)} %get-tuple-element.106), channel_id=1, source_target_pairs={{0,3},{1,2},{2,1},{3,0},{4,7},{5,6},{6,5},{7,4},{8,11},{9,10},{10,... | collective-permute-start | bytes 1179656 | tf_op jit(solution)/shard_map/ppermute | solution.py:486
  13.5 15.0 %collective-permute-start.1 = (f32[2,96,384]{2,1,0:T(8,128)S(1)}, f32[2,96,384]{2,1,0:T(8,128)S(1)}, u32[]{:S(2)}, u32[]{:S(2)}) collective-permute-start(f32[2,96,384]{2,1,0:T(8,128)S(1)} %get-tuple-element.58), channel_id=1, source_target_pairs={{0,28},{4,0},{8,4},{12,8},{16,12},{20,16},{24,20},{28,24},{1,29},{... | collective-permute-start | bytes 884744 | tf_op jit(solution)/shard_map/ppermute | solution.py:470
  18.9 3.5 %collective-permute-start.4 = (f32[2,96,128]{2,1,0:T(8,128)S(1)}, f32[2,96,128]{2,1,0:T(8,128)S(1)}, u32[]{:S(2)}, u32[]{:S(2)}) collective-permute-start(f32[2,96,128]{2,1,0:T(8,128)S(1)} %get-tuple-element.111), channel_id=1, source_target_pairs={{0,1},{1,0},{2,3},{3,2},{4,5},{5,4},{6,7},{7,6},{8,9},{9,8},{10,11... | collective-permute-start | bytes 294920 | tf_op jit(solution)/shard_map/ppermute | solution.py:475
  19.0 6.1 %collective-permute-start.2 = (f32[2,96,128]{2,1,0:T(8,128)S(1)}, f32[2,96,128]{2,1,0:T(8,128)S(1)}, u32[]{:S(2)}, u32[]{:S(2)}) collective-permute-start(f32[2,96,128]{2,1,0:T(8,128)S(1)} %get-tuple-element.112), channel_id=1, source_target_pairs={{0,3},{1,2},{2,1},{3,0},{4,7},{5,6},{6,5},{7,4},{8,11},{9,10},{10,... | collective-permute-start | bytes 294920 | tf_op jit(solution)/shard_map/ppermute | solution.py:486
  27.8 7.0 %collective-permute-start.9 = (f32[2,192,128]{2,1,0:T(8,128)S(1)}, f32[2,192,128]{2,1,0:T(8,128)S(1)}, u32[]{:S(2)}, u32[]{:S(2)}) collective-permute-start(f32[2,192,128]{2,1,0:T(8,128)S(1)} %get-tuple-element.61), channel_id=1, source_target_pairs={{0,3},{1,2},{2,1},{3,0},{4,7},{5,6},{6,5},{7,4},{8,11},{9,10},{10,... | collective-permute-start | bytes 589832 | tf_op jit(solution)/shard_map/ppermute | solution.py:486
  28.0 6.8 %collective-permute-start.8 = (f32[2,192,128]{2,1,0:T(8,128)S(1)}, f32[2,192,128]{2,1,0:T(8,128)S(1)}, u32[]{:S(2)}, u32[]{:S(2)}) collective-permute-start(f32[2,192,128]{2,1,0:T(8,128)S(1)} %get-tuple-element.65), channel_id=1, source_target_pairs={{0,1},{1,0},{2,3},{3,2},{4,5},{5,4},{6,7},{7,6},{8,9},{9,8},{10,11... | collective-permute-start | bytes 589832 | tf_op jit(solution)/shard_map/ppermute | solution.py:475
  28.5 8.4 %collective-permute-start.7 = (f32[2,96,128]{2,1,0:T(8,128)S(1)}, f32[2,96,128]{2,1,0:T(8,128)S(1)}, u32[]{:S(2)}, u32[]{:S(2)}) collective-permute-start(f32[2,96,128]{2,1,0:T(8,128)S(1)} %get-tuple-element.109), channel_id=1, source_target_pairs={{0,3},{1,2},{2,1},{3,0},{4,7},{5,6},{6,5},{7,4},{8,11},{9,10},{10,... | collective-permute-start | bytes 294920 | tf_op jit(solution)/shard_map/ppermute | solution.py:486
  29.8 9.8 %collective-permute-start.6 = (f32[2,96,128]{2,1,0:T(8,128)S(1)}, f32[2,96,128]{2,1,0:T(8,128)S(1)}, u32[]{:S(2)}, u32[]{:S(2)}) collective-permute-start(f32[2,96,128]{2,1,0:T(8,128)S(1)} %get-tuple-element.110), channel_id=1, source_target_pairs={{0,1},{1,0},{2,3},{3,2},{4,5},{5,4},{6,7},{7,6},{8,9},{9,8},{10,11... | collective-permute-start | bytes 294920 | tf_op jit(solution)/shard_map/ppermute | solution.py:475
  34.9 15.9 %collective-permute-start.12 = (f32[2,192,384]{2,1,0:T(8,128)S(1)}, f32[2,192,384]{2,1,0:T(8,128)S(1)}, u32[]{:S(2)}, u32[]{:S(2)}) collective-permute-start(f32[2,192,384]{2,1,0:T(8,128)S(1)} %totals.5.refs_2_), channel_id=1, source_target_pairs={{0,28},{4,0},{8,4},{12,8},{16,12},{20,16},{24,20},{28,24},{1,29},{... | collective-permute-start | bytes 1769480 | tf_op jit(solution)/shard_map/ppermute | solution.py:470
  42.2 2.2 %collective-permute-start.10 = (f32[2,384,128]{2,1,0:T(8,128)S(1)}, f32[2,384,128]{2,1,0:T(8,128)S(1)}, u32[]{:S(2)}, u32[]{:S(2)}) collective-permute-start(f32[2,384,128]{2,1,0:T(8,128)S(1)} %get-tuple-element.71), channel_id=1, source_target_pairs={{0,1},{1,0},{2,3},{3,2},{4,5},{5,4},{6,7},{7,6},{8,9},{9,8},{10,11... | collective-permute-start | bytes 1179656 | tf_op jit(solution)/shard_map/ppermute | solution.py:475
  42.4 2.0 %collective-permute-start.11 = (f32[2,384,128]{2,1,0:T(8,128)S(1)}, f32[2,384,128]{2,1,0:T(8,128)S(1)}, u32[]{:S(2)}, u32[]{:S(2)}) collective-permute-start(f32[2,384,128]{2,1,0:T(8,128)S(1)} %get-tuple-element.72), channel_id=1, source_target_pairs={{1,2},{2,1},{5,6},{6,5},{9,10},{10,9},{13,14},{14,13},{17,18},{18,... | collective-permute-start | bytes 1179656 | tf_op jit(solution)/shard_map/ppermute | solution.py:486
  44.7 14.7 %collective-permute-start.15 = (f32[2,192,384]{2,1,0:T(8,128)S(1)}, f32[2,192,384]{2,1,0:T(8,128)S(1)}, u32[]{:S(2)}, u32[]{:S(2)}) collective-permute-start(f32[2,192,384]{2,1,0:T(8,128)S(1)} %get-tuple-element.74.refs_3_), channel_id=1, source_target_pairs={{0,4},{4,8},{8,12},{12,16},{16,20},{20,24},{24,28},{28,0},{1,5},{5... | collective-permute-start | bytes 1769480 | tf_op jit(solution)/shard_map/ppermute | solution.py:470
  51.0 3.1 %collective-permute-start.14 = (f32[2,384,128]{2,1,0:T(8,128)S(1)}, f32[2,384,128]{2,1,0:T(8,128)S(1)}, u32[]{:S(2)}, u32[]{:S(2)}) collective-permute-start(f32[2,384,128]{2,1,0:T(8,128)S(1)} %get-tuple-element.77), channel_id=1, source_target_pairs={{0,1},{1,0},{2,3},{3,2},{4,5},{5,4},{6,7},{7,6},{8,9},{9,8},{10,11... | collective-permute-start | bytes 1179656 | tf_op jit(solution)/shard_map/ppermute | solution.py:475
  52.7 4.0 %collective-permute-start.13 = (f32[2,384,128]{2,1,0:T(8,128)S(1)}, f32[2,384,128]{2,1,0:T(8,128)S(1)}, u32[]{:S(2)}, u32[]{:S(2)}) collective-permute-start(f32[2,384,128]{2,1,0:T(8,128)S(1)} %get-tuple-element.75), channel_id=1, source_target_pairs={{1,2},{2,1},{5,6},{6,5},{9,10},{10,9},{13,14},{14,13},{17,18},{18,... | collective-permute-start | bytes 1179656 | tf_op jit(solution)/shard_map/ppermute | solution.py:486
  59.5 12.0 %collective-permute-start.17 = (f32[2,192,128]{2,1,0:T(8,128)S(1)}, f32[2,192,128]{2,1,0:T(8,128)S(1)}, u32[]{:S(2)}, u32[]{:S(2)}) collective-permute-start(f32[2,192,128]{2,1,0:T(8,128)S(1)} %get-tuple-element.85), channel_id=1, source_target_pairs={{0,1},{1,0},{2,3},{3,2},{4,5},{5,4},{6,7},{7,6},{8,9},{9,8},{10,11... | collective-permute-start | bytes 589832 | tf_op jit(solution)/shard_map/ppermute | solution.py:475
  68.3 7.0 %collective-permute-start.19 = (f32[2,192,128]{2,1,0:T(8,128)S(1)}, f32[2,192,128]{2,1,0:T(8,128)S(1)}, u32[]{:S(2)}, u32[]{:S(2)}) collective-permute-start(f32[2,192,128]{2,1,0:T(8,128)S(1)} %get-tuple-element.80), channel_id=1, source_target_pairs={{0,3},{1,2},{2,1},{3,0},{4,7},{5,6},{6,5},{7,4},{8,11},{9,10},{10,... | collective-permute-start | bytes 589832 | tf_op jit(solution)/shard_map/ppermute | solution.py:486
  70.0 5.3 %collective-permute-start.18 = (f32[2,192,128]{2,1,0:T(8,128)S(1)}, f32[2,192,128]{2,1,0:T(8,128)S(1)}, u32[]{:S(2)}, u32[]{:S(2)}) collective-permute-start(f32[2,192,128]{2,1,0:T(8,128)S(1)} %get-tuple-element.93), channel_id=1, source_target_pairs={{0,1},{1,0},{2,3},{3,2},{4,5},{5,4},{6,7},{7,6},{8,9},{9,8},{10,11... | collective-permute-start | bytes 589832 | tf_op jit(solution)/shard_map/ppermute | solution.py:475
  70.1 9.3 %collective-permute-start.16 = (f32[2,192,128]{2,1,0:T(8,128)S(1)}, f32[2,192,128]{2,1,0:T(8,128)S(1)}, u32[]{:S(2)}, u32[]{:S(2)}) collective-permute-start(f32[2,192,128]{2,1,0:T(8,128)S(1)} %get-tuple-element.84), channel_id=1, source_target_pairs={{0,3},{1,2},{2,1},{3,0},{4,7},{5,6},{6,5},{7,4},{8,11},{9,10},{10,... | collective-permute-start | bytes 589832 | tf_op jit(solution)/shard_map/ppermute | solution.py:486
  82.1 4.8 %collective-permute-start.24 = (f32[2,96,128]{2,1,0:T(8,128)S(1)}, f32[2,96,128]{2,1,0:T(8,128)S(1)}, u32[]{:S(2)}, u32[]{:S(2)}) collective-permute-start(f32[2,96,128]{2,1,0:T(8,128)S(1)} %get-tuple-element.104), channel_id=1, source_target_pairs={{0,3},{1,2},{2,1},{3,0},{4,7},{5,6},{6,5},{7,4},{8,11},{9,10},{10,... | collective-permute-start | bytes 294920 | tf_op jit(solution)/shard_map/ppermute | solution.py:486
  83.5 3.4 %collective-permute-start.23 = (f32[2,96,128]{2,1,0:T(8,128)S(1)}, f32[2,96,128]{2,1,0:T(8,128)S(1)}, u32[]{:S(2)}, u32[]{:S(2)}) collective-permute-start(f32[2,96,128]{2,1,0:T(8,128)S(1)} %get-tuple-element.103), channel_id=1, source_target_pairs={{0,1},{1,0},{2,3},{3,2},{4,5},{5,4},{6,7},{7,6},{8,9},{9,8},{10,11... | collective-permute-start | bytes 294920 | tf_op jit(solution)/shard_map/ppermute | solution.py:475
  83.6 12.1 %collective-permute-start.21 = (f32[2,288,128]{2,1,0:T(8,128)S(1)}, f32[2,288,128]{2,1,0:T(8,128)S(1)}, u32[]{:S(2)}, u32[]{:S(2)}) collective-permute-start(f32[2,288,128]{2,1,0:T(8,128)S(1)} %get-tuple-element.99), channel_id=1, source_target_pairs={{0,3},{1,2},{2,1},{3,0},{4,7},{5,6},{6,5},{7,4},{8,11},{9,10},{10,... | collective-permute-start | bytes 884744 | tf_op jit(solution)/shard_map/ppermute | solution.py:486
  84.0 11.7 %collective-permute-start.20 = (f32[2,288,128]{2,1,0:T(8,128)S(1)}, f32[2,288,128]{2,1,0:T(8,128)S(1)}, u32[]{:S(2)}, u32[]{:S(2)}) collective-permute-start(f32[2,288,128]{2,1,0:T(8,128)S(1)} %get-tuple-element.98), channel_id=1, source_target_pairs={{0,1},{1,0},{2,3},{3,2},{4,5},{5,4},{6,7},{7,6},{8,9},{9,8},{10,11... | collective-permute-start | bytes 884744 | tf_op jit(solution)/shard_map/ppermute | solution.py:475
  84.4 14.7 %collective-permute-start.22 = (f32[2,96,384]{2,1,0:T(8,128)S(1)}, f32[2,96,384]{2,1,0:T(8,128)S(1)}, u32[]{:S(2)}, u32[]{:S(2)}) collective-permute-start(f32[2,96,384]{2,1,0:T(8,128)S(1)} %get-tuple-element.101), channel_id=1, source_target_pairs={{0,4},{4,8},{8,12},{12,16},{16,20},{20,24},{24,28},{28,0},{1,5},{5... | collective-permute-start | bytes 884744 | tf_op jit(solution)/shard_map/ppermute | solution.py:470
  87.0 18.4 %collective-permute-start.25 = (f32[2,96,384]{2,1,0:T(8,128)S(1)}, f32[2,96,384]{2,1,0:T(8,128)S(1)}, u32[]{:S(2)}, u32[]{:S(2)}) collective-permute-start(f32[2,96,384]{2,1,0:T(8,128)S(1)} %totals.9), channel_id=1, source_target_pairs={{0,28},{4,0},{8,4},{12,8},{16,12},{20,16},{24,20},{28,24},{1,29},{... | collective-permute-start | bytes 884744 | tf_op jit(solution)/shard_map/ppermute | solution.py:470

commit v11 on v9

--- a/solution.py
+++ b/solution.py
@@ -539,8 +539,8 @@
     top = moved(obj[:, last:, :], "row", 1)
     near_strip, far_strip = edges(obj)
     far, near = to_far(far_strip), to_near(near_strip)
-    up_rows, top = after((obj[:, :MARGIN, :], top))
-    bottom = moved(up_rows, "row", -1)
+    held, top = after((obj, top))
+    bottom = moved(held[:, :MARGIN, :], "row", -1)
     probes, amps = prepare(offsets, probe, amplitudes, order)
     consts = (offsets, table, twiddle, probes, amps)
 
@@ -565,19 +565,20 @@
         [(top, 88, 8, "above"), (obj, 0, 200)],
         [(top_b, 88, 8, "above"), (far, 0, 200)],
     )
+    (top_sum,) = totals(lo_o, in_a, in_b, ((0, band),), [(tv_top, 0, MARGIN, MARGIN)])
+    from_below = moved(top_sum, "row", -1)
+
+    mid_o, top_sum = after((mid_o, top_sum))
     own = [(obj, MARGIN, last), (bottom, 0, MARGIN, "below")]
     whole = ((0, tile),)
+    hi_o, hi_b = window(
+        1, False, consts, [(far, MARGIN, last), (bot_b, 0, MARGIN, "below")], own, [(mid_o, 0)], [(mid_b, 0)], whole,
+    )
+    in_b = to_far(hi_b, ends=False)
     hi_o, hi_a = window(
-        1, True, consts, [(near, MARGIN, last), (bot_a, 0, MARGIN, "below")], own, [(mid_o, 0)], [(mid_a, 0)], whole,
-    )
-    lo_o, hi_o = after((lo_o, hi_o))
-    (top_sum,) = totals(lo_o, in_a, in_b, ((0, band),), [(tv_top, 0, MARGIN, MARGIN)])
-    from_below = moved(top_sum, "row", -1)
+        1, True, consts, [(near, MARGIN, last), (bot_a, 0, MARGIN, "below")], own, [(hi_o, 0)], [(mid_a, 0)], whole,
+    )
     in_a = to_near(hi_a)
-    hi_o, hi_b = window(
-        1, False, consts, [(far, MARGIN, last), (bot_b, 0, MARGIN, "below")], own, [(hi_o, 0)], [(mid_b, 0)], whole,
-    )
-    in_b = to_far(hi_b, ends=False)
     tv_bottom = variation(
         [(near, 184, 200), (bot_a, 0, 8, "below")],
         [(obj, 184, 200), (bottom, 0, 8, "below")],
@@ -586,8 +587,8 @@
     mid_sum, bot_sum = totals(
         hi_o, in_a, in_b, halves, [(tv_top, MARGIN, 0, MARGIN), (tv_bottom, 0, MARGIN, band)]
     )
-
-    bot_sum, from_below = after((bot_sum, from_below))
+    from_above = moved(bot_sum, "row", 1)
+
     low, near_strip, far_strip = update(
         (obj, bottom, mid_sum, bot_sum, from_below),
         (
@@ -597,9 +598,7 @@
         ),
         "below",
     )
-    low_a = to_near(near_strip)
-    low_b = to_far(far_strip, ends=False)
-    from_above = moved(bot_sum, "row", 1)
+    low_a, low_b = to_near(near_strip), to_far(far_strip, ends=False)
     own = [(low, 0, tile)]
     mid_o, mid_a, hi_o, hi_a = window(1, True, consts, [(low_a, 0, tile)], own, [], [], halves)
     in_a = to_near(hi_a)
@@ -634,10 +633,10 @@
     over_o, over_b, lo_o, lo_b = window(
         0, False, consts, [(up_b, 0, band), (low_b, 0, band)], own, [(over_o, 0), (lo_o, MARGIN)], [(mid_b, band)], cut,
     )
+    corner = to_far_above(over_b)
     (over,) = sums_near(over_o, over_a)
     last_below = moved(over, "row", -1)
-    corner = to_far_above(over_b)
-    in_b = to_far(lo_b)
+    in_b = to_far(lo_b, ends=False)
     tv_top = variation(
         [(up_a, 88, 104), (low_a, 0, 104)], [(up, 88, 104), (low, 0, 104)], [(up_b, 88, 104), (low_b, 0, 104)]
     )

time: 101 us -> 106 us (1.050)
  the two profiles are of different devices: /device:TPU:0 before, /device:TPU:17 now
where the time goes in v11:
time: 106 us
  waiting for transfers between devices  46.1 us (43%)
  Pallas kernels  30.5 us (29%)
  starting transfers between devices  26.6 us (25%)
  other arithmetic  1.33 us (1%)
  local copies, waits for them, and re-layouts  1.13 us (1%)
    pallas_call x8, Pallas kernels, window(): pl.pallas_call(kernel, out_shape=tuple(shapes), in_specs=[pl.BlockSpec(me...  21.2 us
    ppermute x9, waiting for transfers between devices, to_far(): return lax.ppermute(block, ('row', 'col'), route)  18.9 us
    ppermute x6, waiting for transfers between devices, moved(): lax.ppermute(block, axis, [(n, (n + distance) % count) for n in range(cou...  13.8 us
    ppermute x1, waiting for transfers between devices, to_far_above(): return lax.ppermute(block, ('row', 'col'), route)  13.3 us
    ppermute x9, starting transfers between devices, to_far(): return lax.ppermute(block, ('row', 'col'), route)  12.8 us
    ppermute x6, starting transfers between devices, moved(): lax.ppermute(block, axis, [(n, (n + distance) % count) for n in range(cou...  6.49 us
    ppermute x10, starting transfers between devices, to_near(): lax.ppermute(block, ('row', 'col'), [(r * cols + c, r * cols + (c ^ 1)) f...  5.59 us
    pallas_call x4, Pallas kernels, variation(): pl.pallas_call(functools.partial(variation_kernel, *plan), out_shape=jax....  5.34 us
  transfers between devices with their start and end apart: 26, of which 11 were waited for; matrix products, arithmetic and copies ran while one was open for 1% of the time, Pallas kernels for 27%

profile of v11, /device:TPU:17, one launch (start us, length us, event | category | flops | bytes accessed | tf_op | source)
XLA Modules:
  0.0 105.9 jit_solution(3731682654442142941)
XLA Ops:
  0.0 1.1 %slice.24 = f32[2,96,384]{2,1,0:T(8,128)S(1)} slice(f32[2,384,384]{2,1,0:T(8,128)} %refs_1_.9), slice={[0:2], [288:384], [0:384]} | slice | bytes 589824 | tf_op jit(solution)/shard_map/slice | solution.py:539
  1.1 1.3 %collective-permute-start = (f32[2,96,384]{2,1,0:T(8,128)S(1)}, f32[2,96,384]{2,1,0:T(8,128)S(1)}, u32[]{:S(2)}, u32[]{:S(2)}) collective-permute-start(f32[2,96,384]{2,1,0:T(8,128)S(1)} %slice.24), channel_id=1, source_target_pairs={{0,4},{4,8},{8,12},{12,16},{16,20},{20,24},{24,28},{28,0},{1,5},{5... | collective-permute-start | bytes 884744 | tf_op jit(solution)/shard_map/ppermute | solution.py:496
  2.4 1.3 %slice_select_fusion = (f32[2,384,128]{2,1,0:T(8,128)S(1)}, f32[2,384,128]{2,1,0:T(8,128)S(1)}) fusion(f32[2,384,384]{2,1,0:T(8,128)} %refs_1_.9, pred[]{:T(512)S(6)} %eq.9), kind=kLoop, calls=%fused_computation | loop fusion | flops 196608 | bytes 1572865 | tf_op jit(solution)/shard_map/jit(_where)/select_n | solution.py:529
  3.7 1.0 collective-permute-start.5
  4.7 1.2 %collective-permute-start.3 = (f32[2,384,128]{2,1,0:T(8,128)S(1)}, f32[2,384,128]{2,1,0:T(8,128)S(1)}, u32[]{:S(2)}, u32[]{:S(2)}) collective-permute-start(f32[2,384,128]{2,1,0:T(8,128)S(1)} %get-tuple-element.106), channel_id=1, source_target_pairs={{0,3},{1,2},{2,1},{3,0},{4,7},{5,6},{6,5},{7,4},{8,11},{9,10},{10,... | collective-permute-start | bytes 1179656 | tf_op jit(solution)/shard_map/ppermute | solution.py:512
  5.9 4.0 %collective-permute-done.refs_7_.refs_2_.refs_0_ = f32[2,96,384]{2,1,0:T(8,128)S(1)} collective-permute-done((f32[2,96,384]{2,1,0:T(8,128)S(1)}, f32[2,96,384]{2,1,0:T(8,128)S(1)}, u32[]{:S(2)}, u32[]{:S(2)}) %collective-permute-start) | collective-permute-done | bytes 294944 | tf_op jit(solution)/shard_map/ppermute | solution.py:496
  10.0 0.3 collective-permute-start.1
  10.3 1.9 %collective-permute-start.4 = (f32[2,96,128]{2,1,0:T(8,128)S(1)}, f32[2,96,128]{2,1,0:T(8,128)S(1)}, u32[]{:S(2)}, u32[]{:S(2)}) collective-permute-start(f32[2,96,128]{2,1,0:T(8,128)S(1)} %get-tuple-element.109), channel_id=1, source_target_pairs={{0,1},{1,0},{2,3},{3,2},{4,5},{5,4},{6,7},{7,6},{8,9},{9,8},{10,11... | collective-permute-start | bytes 294920 | tf_op jit(solution)/shard_map/ppermute | solution.py:501
  12.1 1.2 %collective-permute-start.2 = (f32[2,96,128]{2,1,0:T(8,128)S(1)}, f32[2,96,128]{2,1,0:T(8,128)S(1)}, u32[]{:S(2)}, u32[]{:S(2)}) collective-permute-start(f32[2,96,128]{2,1,0:T(8,128)S(1)} %get-tuple-element.110), channel_id=1, source_target_pairs={{0,3},{1,2},{2,1},{3,0},{4,7},{5,6},{6,5},{7,4},{8,11},{9,10},{10,... | collective-permute-start | bytes 294920 | tf_op jit(solution)/shard_map/ppermute | solution.py:512
  13.3 1.8 %prepare.1 = (f32[4,2,256,256]{3,2,1,0:T(8,128)S(1)}, f32[4,512,128]{2,1,0:T(8,128)S(1)}) custom-call(s32[2,2,2]{2,1,0:T(2,128)S(1)} %copy-done.5, f32[2,256,256]{2,1,0:T(8,128)S(1)} %copy-done.4, f32[512,512]{1,0:T(8,128)S(1)} %copy-done.3, bf16[256,256]{1,0:T(8,128)(2,1)S(1)} %copy-done.6), custom_call_target="tpu_custom_call" | custom-call | flops 100000 | bytes 100000 | tf_op jit(solution)/shard_map/prepare/pallas_call | solution.py:105
  15.2 2.6 %shard_map.73 = (f32[2,192,384]{2,1,0:T(8,128)S(1)}, f32[2,192,128]{2,1,0:T(8,128)S(1)}, f32[2,192,384]{2,1,0:T(8,128)S(1)}, f32[2,192,128]{2,1,0:T(8,128)S(1)}) custom-call(s32[2,2,2]{2,1,0:T(2,128)S(1)} %copy-done.5, bf16[4,256,256]{2,1,0:T(8,128)(2,1)S(1)} %copy-done.1, f32[4,128,128]{2,1,0:T(8,128)S(1)} %copy-done.2, ...), custom_call_target="tpu_custom_call" | custom-call | flops 100000 | bytes 100000 | tf_op jit(solution)/shard_map/pallas_call | solution.py:302
  17.9 2.7 %shard_map.74 = (f32[2,192,384]{2,1,0:T(8,128)S(1)}, f32[2,192,128]{2,1,0:T(8,128)S(1)}, f32[2,192,384]{2,1,0:T(8,128)S(1)}, f32[2,192,128]{2,1,0:T(8,128)S(1)}) custom-call(s32[2,2,2]{2,1,0:T(2,128)S(1)} %copy-done.5, bf16[4,256,256]{2,1,0:T(8,128)(2,1)S(1)} %copy-done.1, f32[4,128,128]{2,1,0:T(8,128)S(1)} %copy-done.2, ...), custom_call_target="tpu_custom_call" | custom-call | flops 100000 | bytes 100000 | tf_op jit(solution)/shard_map/pallas_call | solution.py:302
  20.6 1.0 collective-permute-start.9
  21.6 0.7 collective-permute-start.8
  22.3 0.6 collective-permute-start.7
  23.0 1.3 %variation.4.refs_0_ = f32[2,192,384]{2,1,0:T(8,128)S(1)} custom-call(f32[2,96,128]{2,1,0:T(8,128)S(1)} %collective-permute-done.4.refs_5_.refs_0_, f32[2,384,128]{2,1,0:T(8,128)S(1)} %collective-permute-done.5.refs_6_.refs_1_.refs_5_.refs_0_, f32[2,96,384]{2,1,0:T(8,128)S(1)} %collective-permute-done.refs_7_.refs_2_.refs_0_, f32[2,384,384]{2,1,0:T(8,128)S(1)} %copy-done, ...), custom_call_target="tpu_custom_call" | custom-call | flops 100000 | bytes 100000 | tf_op jit(solution)/shard_map/variation/pallas_call | solution.py:363
  24.3 3.8 %collective-permute-done.9.far_ref = f32[2,192,128]{2,1,0:T(8,128)S(1)} collective-permute-done((f32[2,192,128]{2,1,0:T(8,128)S(1)}, f32[2,192,128]{2,1,0:T(8,128)S(1)}, u32[]{:S(2)}, u32[]{:S(2)}) %collective-permute-start.9) | collective-permute-done | bytes 196640 | tf_op jit(solution)/shard_map/ppermute | solution.py:512
  28.2 1.2 %collective-permute-start.12 = (f32[2,192,384]{2,1,0:T(8,128)S(1)}, f32[2,192,384]{2,1,0:T(8,128)S(1)}, u32[]{:S(2)}, u32[]{:S(2)}) collective-permute-start(f32[2,192,384]{2,1,0:T(8,128)S(1)} %totals.4.refs_2_), channel_id=1, source_target_pairs={{0,28},{4,0},{8,4},{12,8},{16,12},{20,16},{24,20},{28,24},{1,29},{... | collective-permute-start | bytes 1769480 | tf_op jit(solution)/shard_map/ppermute | solution.py:496
  29.4 0.2 collective-permute-done.7.refs_6_.refs_5_
  29.7 2.6 %shard_map.75 = (f32[2,384,384]{2,1,0:T(8,128)S(1)}, f32[2,384,128]{2,1,0:T(8,128)S(1)}) custom-call(s32[2,2,2]{2,1,0:T(2,128)S(1)} %copy-done.5, bf16[4,256,256]{2,1,0:T(8,128)(2,1)S(1)} %copy-done.1, f32[4,128,128]{2,1,0:T(8,128)S(1)} %copy-done.2, f32[4,2,256,256]{3,2,1,0:T(8,128)S(1)} %get-tuple-element.56.refs_3_, ...), custom_call_target="tpu_custom_call" | custom-call | flops 100000 | bytes 100000 | tf_op jit(solution)/shard_map/pallas_call | solution.py:302
  32.3 2.7 %shard_map.76 = (f32[2,384,384]{2,1,0:T(8,128)S(1)}, f32[2,384,128]{2,1,0:T(8,128)S(1)}) custom-call(s32[2,2,2]{2,1,0:T(2,128)S(1)} %copy-done.5, bf16[4,256,256]{2,1,0:T(8,128)(2,1)S(1)} %copy-done.1, f32[4,128,128]{2,1,0:T(8,128)S(1)} %copy-done.2, f32[4,2,256,256]{3,2,1,0:T(8,128)S(1)} %get-tuple-element.56.refs_3_, ...), custom_call_target="tpu_custom_call" | custom-call | flops 100000 | bytes 100000 | tf_op jit(solution)/shard_map/pallas_call | solution.py:302
  35.0 0.4 collective-permute-start.10
  35.4 2.9 %collective-permute-start.11 = (f32[2,384,128]{2,1,0:T(8,128)S(1)}, f32[2,384,128]{2,1,0:T(8,128)S(1)}, u32[]{:S(2)}, u32[]{:S(2)}) collective-permute-start(f32[2,384,128]{2,1,0:T(8,128)S(1)} %get-tuple-element.72), channel_id=1, source_target_pairs={{1,2},{2,1},{5,6},{6,5},{9,10},{10,9},{13,14},{14,13},{17,18},{18,... | collective-permute-start | bytes 1179656 | tf_op jit(solution)/shard_map/ppermute | solution.py:512
  38.4 1.3 %variation.5.refs_1_ = f32[2,192,384]{2,1,0:T(8,128)S(1)} custom-call(f32[2,384,128]{2,1,0:T(8,128)S(1)} %collective-permute-done.5.refs_6_.refs_1_.refs_5_.refs_0_, f32[2,96,128]{2,1,0:T(8,128)S(1)} %collective-permute-done.6.refs_6_.refs_1_, f32[2,384,384]{2,1,0:T(8,128)S(1)} %copy-done, f32[2,96,384]{2,1,0:T(8,128)S(1)} %collective-permute-done.1.refs_8_.refs_3_.refs_1_, ...), custom_call_target="tpu_custom_call" | custom-call | flops 100000 | bytes 100000 | tf_op jit(solution)/shard_map/variation/pallas_call | solution.py:363
  39.7 5.1 %collective-permute-done.11.far_ref = f32[2,384,128]{2,1,0:T(8,128)S(1)} collective-permute-done((f32[2,384,128]{2,1,0:T(8,128)S(1)}, f32[2,384,128]{2,1,0:T(8,128)S(1)}, u32[]{:S(2)}, u32[]{:S(2)}) %collective-permute-start.11) | collective-permute-done | bytes 393248 | tf_op jit(solution)/shard_map/ppermute | solution.py:512
  44.8 0.2 totals.5
  45.0 1.3 %collective-permute-start.15 = (f32[2,192,384]{2,1,0:T(8,128)S(1)}, f32[2,192,384]{2,1,0:T(8,128)S(1)}, u32[]{:S(2)}, u32[]{:S(2)}) collective-permute-start(f32[2,192,384]{2,1,0:T(8,128)S(1)} %get-tuple-element.74.refs_3_), channel_id=1, source_target_pairs={{0,4},{4,8},{8,12},{12,16},{16,20},{20,24},{24,28},{28,0},{1,5},{5... | collective-permute-start | bytes 1769480 | tf_op jit(solution)/shard_map/ppermute | solution.py:496
  46.3 9.7 %collective-permute-done.12.refs_4_ = f32[2,192,384]{2,1,0:T(8,128)S(1)} collective-permute-done((f32[2,192,384]{2,1,0:T(8,128)S(1)}, f32[2,192,384]{2,1,0:T(8,128)S(1)}, u32[]{:S(2)}, u32[]{:S(2)}) %collective-permute-start.12) | collective-permute-done | bytes 589856 | tf_op jit(solution)/shard_map/ppermute | solution.py:496
  56.0 0.2 update.2
  56.3 0.7 collective-permute-start.14
  56.9 2.1 %collective-permute-start.13 = (f32[2,384,128]{2,1,0:T(8,128)S(1)}, f32[2,384,128]{2,1,0:T(8,128)S(1)}, u32[]{:S(2)}, u32[]{:S(2)}) collective-permute-start(f32[2,384,128]{2,1,0:T(8,128)S(1)} %get-tuple-element.75), channel_id=1, source_target_pairs={{1,2},{2,1},{5,6},{6,5},{9,10},{10,9},{13,14},{14,13},{17,18},{18,... | collective-permute-start | bytes 1179656 | tf_op jit(solution)/shard_map/ppermute | solution.py:512
  59.1 2.6 %shard_map.77 = (f32[2,192,384]{2,1,0:T(8,128)S(1)}, f32[2,192,128]{2,1,0:T(8,128)S(1)}, f32[2,192,384]{2,1,0:T(8,128)S(1)}, f32[2,192,128]{2,1,0:T(8,128)S(1)}) custom-call(s32[2,2,2]{2,1,0:T(2,128)S(1)} %copy-done.5, bf16[4,256,256]{2,1,0:T(8,128)(2,1)S(1)} %copy-done.1, f32[4,128,128]{2,1,0:T(8,128)S(1)} %copy-done.2, ...), custom_call_target="tpu_custom_call" | custom-call | flops 100000 | bytes 100000 | tf_op jit(solution)/shard_map/pallas_call | solution.py:302
  61.7 4.3 %collective-permute-done.13.refs_5_.refs_2_.refs_6_ = f32[2,384,128]{2,1,0:T(8,128)S(1)} collective-permute-done((f32[2,384,128]{2,1,0:T(8,128)S(1)}, f32[2,384,128]{2,1,0:T(8,128)S(1)}, u32[]{:S(2)}, u32[]{:S(2)}) %collective-permute-start.13) | collective-permute-done | bytes 393248 | tf_op jit(solution)/shard_map/ppermute | solution.py:512
  66.0 2.7 %shard_map.78 = (f32[2,192,384]{2,1,0:T(8,128)S(1)}, f32[2,192,128]{2,1,0:T(8,128)S(1)}, f32[2,192,384]{2,1,0:T(8,128)S(1)}, f32[2,192,128]{2,1,0:T(8,128)S(1)}) custom-call(s32[2,2,2]{2,1,0:T(2,128)S(1)} %copy-done.5, bf16[4,256,256]{2,1,0:T(8,128)(2,1)S(1)} %copy-done.1, f32[4,128,128]{2,1,0:T(8,128)S(1)} %copy-done.2, ...), custom_call_target="tpu_custom_call" | custom-call | flops 100000 | bytes 100000 | tf_op jit(solution)/shard_map/pallas_call | solution.py:302
  69.1 0.4 collective-permute-start.18
  69.5 1.7 %collective-permute-start.16 = (f32[2,192,128]{2,1,0:T(8,128)S(1)}, f32[2,192,128]{2,1,0:T(8,128)S(1)}, u32[]{:S(2)}, u32[]{:S(2)}) collective-permute-start(f32[2,192,128]{2,1,0:T(8,128)S(1)} %get-tuple-element.84), channel_id=1, source_target_pairs={{0,3},{1,2},{2,1},{3,0},{4,7},{5,6},{6,5},{7,4},{8,11},{9,10},{10,... | collective-permute-start | bytes 589832 | tf_op jit(solution)/shard_map/ppermute | solution.py:512
  71.2 2.6 %shard_map.79 = (f32[2,96,384]{2,1,0:T(8,128)S(1)}, f32[2,96,128]{2,1,0:T(8,128)S(1)}, f32[2,288,384]{2,1,0:T(8,128)S(1)}, f32[2,288,128]{2,1,0:T(8,128)S(1)}) custom-call(s32[2,2,2]{2,1,0:T(2,128)S(1)} %copy-done.5, bf16[4,256,256]{2,1,0:T(8,128)(2,1)S(1)} %copy-done.1, f32[4,128,128]{2,1,0:T(8,128)S(1)} %copy-done.2, ...), custom_call_target="tpu_custom_call" | custom-call | flops 100000 | bytes 100000 | tf_op jit(solution)/shard_map/pallas_call | solution.py:302
  74.0 1.3 %variation.6.refs_0_.refs_1_ = f32[2,192,384]{2,1,0:T(8,128)S(1)} custom-call(f32[2,384,128]{2,1,0:T(8,128)S(1)} %collective-permute-done.14.refs_5_.refs_6_.refs_0_.refs_1_, f32[2,384,384]{2,1,0:T(8,128)S(1)} %get-tuple-element.76.refs_6_.refs_8_.refs_1_.refs_3_.bottom_ref, f32[2,384,128]{2,1,0:T(8,128)S(1)} %collective-permute-done.13.refs_5_.refs_2_.refs_6_), custom_call_target="tpu_custom_call" | custom-call | flops 100000 | bytes 100000 | tf_op jit(solution)/shard_map/variation/pallas_call | solution.py:363
  75.3 1.2 %collective-permute-done.19.far_ref = f32[2,192,128]{2,1,0:T(8,128)S(1)} collective-permute-done((f32[2,192,128]{2,1,0:T(8,128)S(1)}, f32[2,192,128]{2,1,0:T(8,128)S(1)}, u32[]{:S(2)}, u32[]{:S(2)}) %collective-permute-start.19) | collective-permute-done | bytes 196640 | tf_op jit(solution)/shard_map/ppermute | solution.py:512
  76.6 3.6 %collective-permute-done.16.refs_5_.refs_4_ = f32[2,192,128]{2,1,0:T(8,128)S(1)} collective-permute-done((f32[2,192,128]{2,1,0:T(8,128)S(1)}, f32[2,192,128]{2,1,0:T(8,128)S(1)}, u32[]{:S(2)}, u32[]{:S(2)}) %collective-permute-start.16) | collective-permute-done | bytes 196640 | tf_op jit(solution)/shard_map/ppermute | solution.py:512
  80.2 2.7 %shard_map.80 = (f32[2,96,384]{2,1,0:T(8,128)S(1)}, f32[2,96,128]{2,1,0:T(8,128)S(1)}, f32[2,288,384]{2,1,0:T(8,128)S(1)}, f32[2,288,128]{2,1,0:T(8,128)S(1)}) custom-call(s32[2,2,2]{2,1,0:T(2,128)S(1)} %copy-done.5, bf16[4,256,256]{2,1,0:T(8,128)(2,1)S(1)} %copy-done.1, f32[4,128,128]{2,1,0:T(8,128)S(1)} %copy-done.2, ...), custom_call_target="tpu_custom_call" | custom-call | flops 100000 | bytes 100000 | tf_op jit(solution)/shard_map/pallas_call | solution.py:302
  82.8 1.9 %collective-permute-start.21 = (f32[2,288,128]{2,1,0:T(8,128)S(1)}, f32[2,288,128]{2,1,0:T(8,128)S(1)}, u32[]{:S(2)}, u32[]{:S(2)}) collective-permute-start(f32[2,288,128]{2,1,0:T(8,128)S(1)} %get-tuple-element.99), channel_id=1, source_target_pairs={{1,2},{2,1},{5,6},{6,5},{9,10},{10,9},{13,14},{14,13},{17,18},{18,... | collective-permute-start | bytes 884744 | tf_op jit(solution)/shard_map/ppermute | solution.py:512
  85.0 2.4 %collective-permute-start.24 = (f32[2,96,384]{2,1,0:T(8,128)S(1)}, f32[2,96,384]{2,1,0:T(8,128)S(1)}, u32[]{:S(2)}, u32[]{:S(2)}) collective-permute-start(f32[2,96,384]{2,1,0:T(8,128)S(1)} %sums_near.1), channel_id=1, source_target_pairs={{0,28},{4,0},{8,4},{12,8},{16,12},{20,16},{24,20},{28,24},{1,29},{... | collective-permute-start | bytes 884744 | tf_op jit(solution)/shard_map/ppermute | solution.py:496
  87.4 1.8 %collective-permute-start.25 = (f32[2,96,128]{2,1,0:T(8,128)S(1)}, f32[2,96,128]{2,1,0:T(8,128)S(1)}, u32[]{:S(2)}, u32[]{:S(2)}) collective-permute-start(f32[2,96,128]{2,1,0:T(8,128)S(1)} %get-tuple-element.104), channel_id=1, source_target_pairs={{0,31},{1,30},{2,29},{3,28},{4,3},{5,2},{6,1},{7,0},{8,7},{9,6},{1... | collective-permute-start | bytes 294920 | tf_op jit(solution)/shard_map/ppermute | solution.py:522
  89.2 1.3 %variation.7.refs_0_ = f32[2,192,384]{2,1,0:T(8,128)S(1)} custom-call(f32[2,192,128]{2,1,0:T(8,128)S(1)} %collective-permute-done.17.refs_5_.refs_0_, f32[2,384,128]{2,1,0:T(8,128)S(1)} %collective-permute-done.14.refs_5_.refs_6_.refs_0_.refs_1_, f32[2,192,384]{2,1,0:T(8,128)S(1)} %get-tuple-element.83.refs_7_.refs_2_.top_ref, ...), custom_call_target="tpu_custom_call" | custom-call | flops 100000 | bytes 100000 | tf_op jit(solution)/shard_map/variation/pallas_call | solution.py:363
  90.5 0.7 collective-permute-done.21.far_ref
  91.4 13.3 %collective-permute-done.25.corner_ref = f32[2,96,128]{2,1,0:T(8,128)S(1)} collective-permute-done((f32[2,96,128]{2,1,0:T(8,128)S(1)}, f32[2,96,128]{2,1,0:T(8,128)S(1)}, u32[]{:S(2)}, u32[]{:S(2)}) %collective-permute-start.25) | collective-permute-done | bytes 98336 | tf_op jit(solution)/shard_map/ppermute | solution.py:522
  104.7 1.2 %finish.1 = f32[2,384,384]{2,1,0:T(8,128)} custom-call(f32[2,192,384]{2,1,0:T(8,128)S(1)} %get-tuple-element.83.refs_7_.refs_2_.top_ref, f32[2,384,384]{2,1,0:T(8,128)S(1)} %get-tuple-element.76.refs_6_.refs_8_.refs_1_.refs_3_.bottom_ref, f32[2,288,384]{2,1,0:T(8,128)S(1)} %totals.7.mid_ref, f32[2,96,384]{2,1,0:T(8,128)S(1)} %get-tuple-element.100.low_ref, ...), custom_call_target="tpu_custom_call" | custom-call | flops 100000 | bytes 100000 | tf_op jit(solution)/shard_map/finish/pallas_call | solution.py:483
  (44 shorter events, 1.3 us)
Async XLA Ops:
  0.0 9.9 %copy-start = (f32[2,384,384]{2,1,0:T(8,128)S(1)}, f32[2,384,384]{2,1,0:T(8,128)}, u32[]{:S(2)}) copy-start(f32[2,384,384]{2,1,0:T(8,128)} %refs_1_.9) | copy-start | bytes 3538948
  1.1 8.8 %collective-permute-start = (f32[2,96,384]{2,1,0:T(8,128)S(1)}, f32[2,96,384]{2,1,0:T(8,128)S(1)}, u32[]{:S(2)}, u32[]{:S(2)}) collective-permute-start(f32[2,96,384]{2,1,0:T(8,128)S(1)} %slice.24), channel_id=1, source_target_pairs={{0,4},{4,8},{8,12},{12,16},{16,20},{20,24},{24,28},{28,0},{1,5},{5... | collective-permute-start | bytes 884744 | tf_op jit(solution)/shard_map/ppermute | solution.py:496
  2.3 11.0 %copy-start.3 = (f32[512,512]{1,0:T(8,128)S(1)}, f32[512,512]{1,0:T(8,128)}, u32[]{:S(2)}) copy-start(f32[512,512]{1,0:T(8,128)} %amp_ref.1) | copy-start | bytes 3145732
  2.4 11.0 %copy-start.4 = (f32[2,256,256]{2,1,0:T(8,128)S(1)}, f32[2,256,256]{2,1,0:T(8,128)}, u32[]{:S(2)}) copy-start(f32[2,256,256]{2,1,0:T(8,128)} %probe_ref.1) | copy-start | bytes 1572868
  2.4 11.0 %copy-start.5 = (s32[2,2,2]{2,1,0:T(2,128)S(1)}, s32[2,2,2]{2,1,0:T(2,128)}, u32[]{:S(2)}) copy-start(s32[2,2,2]{2,1,0:T(2,128)} %refs_0_.17) | copy-start | bytes 100
  2.4 11.0 %copy-start.6 = (bf16[256,256]{1,0:T(8,128)(2,1)S(1)}, bf16[256,256]{1,0:T(8,128)(2,1)}, u32[]{:S(2)}) copy-start(bf16[256,256]{1,0:T(8,128)(2,1)} %constant.30.clone.order_ref) | copy-start | bytes 393220
  3.7 11.5 %collective-permute-start.5 = (f32[2,384,128]{2,1,0:T(8,128)S(1)}, f32[2,384,128]{2,1,0:T(8,128)S(1)}, u32[]{:S(2)}, u32[]{:S(2)}) collective-permute-start(f32[2,384,128]{2,1,0:T(8,128)S(1)} %get-tuple-element.105), channel_id=1, source_target_pairs={{0,1},{1,0},{2,3},{3,2},{4,5},{5,4},{6,7},{7,6},{8,9},{9,8},{10,11... | collective-permute-start | bytes 1179656 | tf_op jit(solution)/shard_map/ppermute | solution.py:501
  4.7 13.2 %collective-permute-start.3 = (f32[2,384,128]{2,1,0:T(8,128)S(1)}, f32[2,384,128]{2,1,0:T(8,128)S(1)}, u32[]{:S(2)}, u32[]{:S(2)}) collective-permute-start(f32[2,384,128]{2,1,0:T(8,128)S(1)} %get-tuple-element.106), channel_id=1, source_target_pairs={{0,3},{1,2},{2,1},{3,0},{4,7},{5,6},{6,5},{7,4},{8,11},{9,10},{10,... | collective-permute-start | bytes 1179656 | tf_op jit(solution)/shard_map/ppermute | solution.py:512
  10.0 5.2 %copy-start.1 = (bf16[4,256,256]{2,1,0:T(8,128)(2,1)S(1)}, bf16[4,256,256]{2,1,0:T(8,128)(2,1)}, u32[]{:S(2)}) copy-start(bf16[4,256,256]{2,1,0:T(8,128)(2,1)} %constant.28.clone.refs_1_) | copy-start | bytes 1572868
  10.0 5.2 %copy-start.2 = (f32[4,128,128]{2,1,0:T(8,128)S(1)}, f32[4,128,128]{2,1,0:T(8,128)}, u32[]{:S(2)}) copy-start(f32[4,128,128]{2,1,0:T(8,128)} %constant.29.clone.refs_2_) | copy-start | bytes 786436
  10.0 12.3 %collective-permute-start.1 = (f32[2,96,384]{2,1,0:T(8,128)S(1)}, f32[2,96,384]{2,1,0:T(8,128)S(1)}, u32[]{:S(2)}, u32[]{:S(2)}) collective-permute-start(f32[2,96,384]{2,1,0:T(8,128)S(1)} %slice.25), channel_id=1, source_target_pairs={{0,28},{4,0},{8,4},{12,8},{16,12},{20,16},{24,20},{28,24},{1,29},{... | collective-permute-start | bytes 884744 | tf_op jit(solution)/shard_map/ppermute | solution.py:496
  10.3 4.9 %collective-permute-start.4 = (f32[2,96,128]{2,1,0:T(8,128)S(1)}, f32[2,96,128]{2,1,0:T(8,128)S(1)}, u32[]{:S(2)}, u32[]{:S(2)}) collective-permute-start(f32[2,96,128]{2,1,0:T(8,128)S(1)} %get-tuple-element.109), channel_id=1, source_target_pairs={{0,1},{1,0},{2,3},{3,2},{4,5},{5,4},{6,7},{7,6},{8,9},{9,8},{10,11... | collective-permute-start | bytes 294920 | tf_op jit(solution)/shard_map/ppermute | solution.py:501
  12.1 5.8 %collective-permute-start.2 = (f32[2,96,128]{2,1,0:T(8,128)S(1)}, f32[2,96,128]{2,1,0:T(8,128)S(1)}, u32[]{:S(2)}, u32[]{:S(2)}) collective-permute-start(f32[2,96,128]{2,1,0:T(8,128)S(1)} %get-tuple-element.110), channel_id=1, source_target_pairs={{0,3},{1,2},{2,1},{3,0},{4,7},{5,6},{6,5},{7,4},{8,11},{9,10},{10,... | collective-permute-start | bytes 294920 | tf_op jit(solution)/shard_map/ppermute | solution.py:512
  20.6 7.6 %collective-permute-start.9 = (f32[2,192,128]{2,1,0:T(8,128)S(1)}, f32[2,192,128]{2,1,0:T(8,128)S(1)}, u32[]{:S(2)}, u32[]{:S(2)}) collective-permute-start(f32[2,192,128]{2,1,0:T(8,128)S(1)} %get-tuple-element.61), channel_id=1, source_target_pairs={{0,3},{1,2},{2,1},{3,0},{4,7},{5,6},{6,5},{7,4},{8,11},{9,10},{10,... | collective-permute-start | bytes 589832 | tf_op jit(solution)/shard_map/ppermute | solution.py:512
  21.6 6.6 %collective-permute-start.8 = (f32[2,192,128]{2,1,0:T(8,128)S(1)}, f32[2,192,128]{2,1,0:T(8,128)S(1)}, u32[]{:S(2)}, u32[]{:S(2)}) collective-permute-start(f32[2,192,128]{2,1,0:T(8,128)S(1)} %get-tuple-element.65), channel_id=1, source_target_pairs={{0,1},{1,0},{2,3},{3,2},{4,5},{5,4},{6,7},{7,6},{8,9},{9,8},{10,11... | collective-permute-start | bytes 589832 | tf_op jit(solution)/shard_map/ppermute | solution.py:501
  22.3 7.3 %collective-permute-start.7 = (f32[2,96,128]{2,1,0:T(8,128)S(1)}, f32[2,96,128]{2,1,0:T(8,128)S(1)}, u32[]{:S(2)}, u32[]{:S(2)}) collective-permute-start(f32[2,96,128]{2,1,0:T(8,128)S(1)} %get-tuple-element.107), channel_id=1, source_target_pairs={{0,3},{1,2},{2,1},{3,0},{4,7},{5,6},{6,5},{7,4},{8,11},{9,10},{10,... | collective-permute-start | bytes 294920 | tf_op jit(solution)/shard_map/ppermute | solution.py:512
  22.9 9.4 %collective-permute-start.6 = (f32[2,96,128]{2,1,0:T(8,128)S(1)}, f32[2,96,128]{2,1,0:T(8,128)S(1)}, u32[]{:S(2)}, u32[]{:S(2)}) collective-permute-start(f32[2,96,128]{2,1,0:T(8,128)S(1)} %get-tuple-element.108), channel_id=1, source_target_pairs={{0,1},{1,0},{2,3},{3,2},{4,5},{5,4},{6,7},{7,6},{8,9},{9,8},{10,11... | collective-permute-start | bytes 294920 | tf_op jit(solution)/shard_map/ppermute | solution.py:501
  28.2 27.8 %collective-permute-start.12 = (f32[2,192,384]{2,1,0:T(8,128)S(1)}, f32[2,192,384]{2,1,0:T(8,128)S(1)}, u32[]{:S(2)}, u32[]{:S(2)}) collective-permute-start(f32[2,192,384]{2,1,0:T(8,128)S(1)} %totals.4.refs_2_), channel_id=1, source_target_pairs={{0,28},{4,0},{8,4},{12,8},{16,12},{20,16},{24,20},{28,24},{1,29},{... | collective-permute-start | bytes 1769480 | tf_op jit(solution)/shard_map/ppermute | solution.py:496
  35.0 4.7 %collective-permute-start.10 = (f32[2,384,128]{2,1,0:T(8,128)S(1)}, f32[2,384,128]{2,1,0:T(8,128)S(1)}, u32[]{:S(2)}, u32[]{:S(2)}) collective-permute-start(f32[2,384,128]{2,1,0:T(8,128)S(1)} %get-tuple-element.71), channel_id=1, source_target_pairs={{0,1},{1,0},{2,3},{3,2},{4,5},{5,4},{6,7},{7,6},{8,9},{9,8},{10,11... | collective-permute-start | bytes 1179656 | tf_op jit(solution)/shard_map/ppermute | solution.py:501
  35.4 9.4 %collective-permute-start.11 = (f32[2,384,128]{2,1,0:T(8,128)S(1)}, f32[2,384,128]{2,1,0:T(8,128)S(1)}, u32[]{:S(2)}, u32[]{:S(2)}) collective-permute-start(f32[2,384,128]{2,1,0:T(8,128)S(1)} %get-tuple-element.72), channel_id=1, source_target_pairs={{1,2},{2,1},{5,6},{6,5},{9,10},{10,9},{13,14},{14,13},{17,18},{18,... | collective-permute-start | bytes 1179656 | tf_op jit(solution)/shard_map/ppermute | solution.py:512
  45.0 23.7 %collective-permute-start.15 = (f32[2,192,384]{2,1,0:T(8,128)S(1)}, f32[2,192,384]{2,1,0:T(8,128)S(1)}, u32[]{:S(2)}, u32[]{:S(2)}) collective-permute-start(f32[2,192,384]{2,1,0:T(8,128)S(1)} %get-tuple-element.74.refs_3_), channel_id=1, source_target_pairs={{0,4},{4,8},{8,12},{12,16},{16,20},{20,24},{24,28},{28,0},{1,5},{5... | collective-permute-start | bytes 1769480 | tf_op jit(solution)/shard_map/ppermute | solution.py:496
  56.3 2.8 %collective-permute-start.14 = (f32[2,384,128]{2,1,0:T(8,128)S(1)}, f32[2,384,128]{2,1,0:T(8,128)S(1)}, u32[]{:S(2)}, u32[]{:S(2)}) collective-permute-start(f32[2,384,128]{2,1,0:T(8,128)S(1)} %get-tuple-element.77), channel_id=1, source_target_pairs={{0,1},{1,0},{2,3},{3,2},{4,5},{5,4},{6,7},{7,6},{8,9},{9,8},{10,11... | collective-permute-start | bytes 1179656 | tf_op jit(solution)/shard_map/ppermute | solution.py:501
  56.9 9.1 %collective-permute-start.13 = (f32[2,384,128]{2,1,0:T(8,128)S(1)}, f32[2,384,128]{2,1,0:T(8,128)S(1)}, u32[]{:S(2)}, u32[]{:S(2)}) collective-permute-start(f32[2,384,128]{2,1,0:T(8,128)S(1)} %get-tuple-element.75), channel_id=1, source_target_pairs={{1,2},{2,1},{5,6},{6,5},{9,10},{10,9},{13,14},{14,13},{17,18},{18,... | collective-permute-start | bytes 1179656 | tf_op jit(solution)/shard_map/ppermute | solution.py:512
  68.9 2.3 %collective-permute-start.17 = (f32[2,192,128]{2,1,0:T(8,128)S(1)}, f32[2,192,128]{2,1,0:T(8,128)S(1)}, u32[]{:S(2)}, u32[]{:S(2)}) collective-permute-start(f32[2,192,128]{2,1,0:T(8,128)S(1)} %get-tuple-element.85), channel_id=1, source_target_pairs={{0,1},{1,0},{2,3},{3,2},{4,5},{5,4},{6,7},{7,6},{8,9},{9,8},{10,11... | collective-permute-start | bytes 589832 | tf_op jit(solution)/shard_map/ppermute | solution.py:501
  68.9 7.6 %collective-permute-start.19 = (f32[2,192,128]{2,1,0:T(8,128)S(1)}, f32[2,192,128]{2,1,0:T(8,128)S(1)}, u32[]{:S(2)}, u32[]{:S(2)}) collective-permute-start(f32[2,192,128]{2,1,0:T(8,128)S(1)} %get-tuple-element.80), channel_id=1, source_target_pairs={{0,3},{1,2},{2,1},{3,0},{4,7},{5,6},{6,5},{7,4},{8,11},{9,10},{10,... | collective-permute-start | bytes 589832 | tf_op jit(solution)/shard_map/ppermute | solution.py:512
  69.1 7.4 %collective-permute-start.18 = (f32[2,192,128]{2,1,0:T(8,128)S(1)}, f32[2,192,128]{2,1,0:T(8,128)S(1)}, u32[]{:S(2)}, u32[]{:S(2)}) collective-permute-start(f32[2,192,128]{2,1,0:T(8,128)S(1)} %get-tuple-element.93), channel_id=1, source_target_pairs={{0,1},{1,0},{2,3},{3,2},{4,5},{5,4},{6,7},{7,6},{8,9},{9,8},{10,11... | collective-permute-start | bytes 589832 | tf_op jit(solution)/shard_map/ppermute | solution.py:501
  69.5 10.7 %collective-permute-start.16 = (f32[2,192,128]{2,1,0:T(8,128)S(1)}, f32[2,192,128]{2,1,0:T(8,128)S(1)}, u32[]{:S(2)}, u32[]{:S(2)}) collective-permute-start(f32[2,192,128]{2,1,0:T(8,128)S(1)} %get-tuple-element.84), channel_id=1, source_target_pairs={{0,3},{1,2},{2,1},{3,0},{4,7},{5,6},{6,5},{7,4},{8,11},{9,10},{10,... | collective-permute-start | bytes 589832 | tf_op jit(solution)/shard_map/ppermute | solution.py:512
  73.8 11.1 %collective-permute-start.23 = (f32[2,96,128]{2,1,0:T(8,128)S(1)}, f32[2,96,128]{2,1,0:T(8,128)S(1)}, u32[]{:S(2)}, u32[]{:S(2)}) collective-permute-start(f32[2,96,128]{2,1,0:T(8,128)S(1)} %get-tuple-element.103), channel_id=1, source_target_pairs={{0,1},{1,0},{2,3},{3,2},{4,5},{5,4},{6,7},{7,6},{8,9},{9,8},{10,11... | collective-permute-start | bytes 294920 | tf_op jit(solution)/shard_map/ppermute | solution.py:501
  82.8 8.3 %collective-permute-start.21 = (f32[2,288,128]{2,1,0:T(8,128)S(1)}, f32[2,288,128]{2,1,0:T(8,128)S(1)}, u32[]{:S(2)}, u32[]{:S(2)}) collective-permute-start(f32[2,288,128]{2,1,0:T(8,128)S(1)} %get-tuple-element.99), channel_id=1, source_target_pairs={{1,2},{2,1},{5,6},{6,5},{9,10},{10,9},{13,14},{14,13},{17,18},{18,... | collective-permute-start | bytes 884744 | tf_op jit(solution)/shard_map/ppermute | solution.py:512
  84.8 6.4 %collective-permute-start.20 = (f32[2,288,128]{2,1,0:T(8,128)S(1)}, f32[2,288,128]{2,1,0:T(8,128)S(1)}, u32[]{:S(2)}, u32[]{:S(2)}) collective-permute-start(f32[2,288,128]{2,1,0:T(8,128)S(1)} %get-tuple-element.98), channel_id=1, source_target_pairs={{0,1},{1,0},{2,3},{3,2},{4,5},{5,4},{6,7},{7,6},{8,9},{9,8},{10,11... | collective-permute-start | bytes 884744 | tf_op jit(solution)/shard_map/ppermute | solution.py:501
  84.9 19.9 %collective-permute-start.22 = (f32[2,96,384]{2,1,0:T(8,128)S(1)}, f32[2,96,384]{2,1,0:T(8,128)S(1)}, u32[]{:S(2)}, u32[]{:S(2)}) collective-permute-start(f32[2,96,384]{2,1,0:T(8,128)S(1)} %get-tuple-element.101), channel_id=1, source_target_pairs={{0,4},{4,8},{8,12},{12,16},{16,20},{20,24},{24,28},{28,0},{1,5},{5... | collective-permute-start | bytes 884744 | tf_op jit(solution)/shard_map/ppermute | solution.py:496
  85.0 19.7 %collective-permute-start.24 = (f32[2,96,384]{2,1,0:T(8,128)S(1)}, f32[2,96,384]{2,1,0:T(8,128)S(1)}, u32[]{:S(2)}, u32[]{:S(2)}) collective-permute-start(f32[2,96,384]{2,1,0:T(8,128)S(1)} %sums_near.1), channel_id=1, source_target_pairs={{0,28},{4,0},{8,4},{12,8},{16,12},{20,16},{24,20},{28,24},{1,29},{... | collective-permute-start | bytes 884744 | tf_op jit(solution)/shard_map/ppermute | solution.py:496
  87.4 17.4 %collective-permute-start.25 = (f32[2,96,128]{2,1,0:T(8,128)S(1)}, f32[2,96,128]{2,1,0:T(8,128)S(1)}, u32[]{:S(2)}, u32[]{:S(2)}) collective-permute-start(f32[2,96,128]{2,1,0:T(8,128)S(1)} %get-tuple-element.104), channel_id=1, source_target_pairs={{0,31},{1,30},{2,29},{3,28},{4,3},{5,2},{6,1},{7,0},{8,7},{9,6},{1... | collective-permute-start | bytes 294920 | tf_op jit(solution)/shard_map/ppermute | solution.py:522

commit v12 on v11

--- a/solution.py
+++ b/solution.py
@@ -539,8 +539,8 @@
     top = moved(obj[:, last:, :], "row", 1)
     near_strip, far_strip = edges(obj)
     far, near = to_far(far_strip), to_near(near_strip)
-    held, top = after((obj, top))
-    bottom = moved(held[:, :MARGIN, :], "row", -1)
+    up_rows, top = after((obj[:, :MARGIN, :], top))
+    bottom = moved(up_rows, "row", -1)
     probes, amps = prepare(offsets, probe, amplitudes, order)
     consts = (offsets, table, twiddle, probes, amps)
 
@@ -558,8 +558,7 @@
     in_b = to_far(lo_b)
     bottom, lo_b = after((bottom, lo_b))
     near_strip, far_strip = edges(bottom)
-    bot_b = to_far(far_strip)
-    bot_a = to_near(near_strip)
+    bot_b, bot_a = to_far(far_strip), to_near(near_strip)
     tv_top = variation(
         [(top_a, 88, 8, "above"), (near, 0, 200)],
         [(top, 88, 8, "above"), (obj, 0, 200)],
@@ -636,7 +635,7 @@
     corner = to_far_above(over_b)
     (over,) = sums_near(over_o, over_a)
     last_below = moved(over, "row", -1)
-    in_b = to_far(lo_b, ends=False)
+    in_b = to_far(lo_b)
     tv_top = variation(
         [(up_a, 88, 104), (low_a, 0, 104)], [(up, 88, 104), (low, 0, 104)], [(up_b, 88, 104), (low_b, 0, 104)]
     )

time: 106 us -> 105 us (level)
  starting transfers between devices: 26.6 us -> 24.5 us
  waiting for transfers between devices: 46.1 us -> 47.6 us
  other arithmetic: 1.33 us -> 0.09 us
    ppermute x9, waiting for transfers between devices: 18.9 us -> 22.2 us  [to_far(): return lax.ppermute(block, ('row', 'col'), route)]
    ppermute x1, waiting for transfers between devices: 13.3 us -> 10.4 us  [to_far_above(): return lax.ppermute(block, ('row', 'col'), route)]
    ppermute x9, starting transfers between devices: 12.8 us -> 10.8 us  [to_far(): return lax.ppermute(block, ('row', 'col'), route)]
    select_n x3, other arithmetic: 1.33 us -> 0.09 us  [edges(): return (jnp.where(even, high, low), jnp.where(even, low, high))]
    ppermute x6, waiting for transfers between devices: 13.8 us -> 15 us  [moved(): lax.ppermute(block, axis, [(n, (n + distance) % count) for n in range(cou...]
  transfers between devices with their start and end apart: 26 -> 26, of which waited for: 11 -> 10; matrix products, arithmetic and copies ran while one was open for 1% -> 0% of each run, Pallas kernels for 27% -> 28%
where the time goes in v12:
time: 105 us
  waiting for transfers between devices  47.6 us (45%)
  Pallas kernels  30.4 us (29%)
  starting transfers between devices  24.5 us (23%)
  local copies, waits for them, and re-layouts  1.93 us (2%)
    ppermute x9, waiting for transfers between devices, to_far(): return lax.ppermute(block, ('row', 'col'), route)  22.2 us
    pallas_call x8, Pallas kernels, window(): pl.pallas_call(kernel, out_shape=tuple(shapes), in_specs=[pl.BlockSpec(me...  21.2 us
    ppermute x6, waiting for transfers between devices, moved(): lax.ppermute(block, axis, [(n, (n + distance) % count) for n in range(cou...  15 us
    ppermute x9, starting transfers between devices, to_far(): return lax.ppermute(block, ('row', 'col'), route)  10.8 us
    ppermute x1, waiting for transfers between devices, to_far_above(): return lax.ppermute(block, ('row', 'col'), route)  10.4 us
    ppermute x6, starting transfers between devices, moved(): lax.ppermute(block, axis, [(n, (n + distance) % count) for n in range(cou...  6.41 us
    ppermute x10, starting transfers between devices, to_near(): lax.ppermute(block, ('row', 'col'), [(r * cols + c, r * cols + (c ^ 1)) f...  5.48 us
    pallas_call x4, Pallas kernels, variation(): pl.pallas_call(functools.partial(variation_kernel, *plan), out_shape=jax....  5.34 us
  transfers between devices with their start and end apart: 26, of which 10 were waited for; matrix products, arithmetic and copies ran while one was open for 0% of the time, Pallas kernels for 28%

profile of v12, /device:TPU:17, one launch (start us, length us, event | category | flops | bytes accessed | tf_op | source)
XLA Modules:
  0.0 104.8 jit_solution(13824571685752191969)
XLA Ops:
  0.0 1.9 %fusion = (f32[2,96,384]{2,1,0:T(8,128)}, f32[2,96,384]{2,1,0:T(8,128)S(1)}) fusion(f32[2,384,384]{2,1,0:T(8,128)} %refs_1_.9), kind=kLoop, calls=%fused_computation.6 | loop fusion | bytes 1179648 | tf_op jit(solution)/shard_map/slice | solution.py:539
  1.9 1.3 %collective-permute-start = (f32[2,96,384]{2,1,0:T(8,128)}, f32[2,96,384]{2,1,0:T(8,128)S(1)}, u32[]{:S(2)}, u32[]{:S(2)}) collective-permute-start(f32[2,96,384]{2,1,0:T(8,128)} %get-tuple-element.107), channel_id=1, source_target_pairs={{0,4},{4,8},{8,12},{12,16},{16,20},{20,24},{24,28},{28,0},{1,5},{5... | collective-permute-start | bytes 884744 | tf_op jit(solution)/shard_map/ppermute | solution.py:496
  3.3 1.0 collective-permute-start.5
  4.3 1.2 %collective-permute-start.3 = (f32[2,384,128]{2,1,0:T(8,128)S(1)}, f32[2,384,128]{2,1,0:T(8,128)S(1)}, u32[]{:S(2)}, u32[]{:S(2)}) collective-permute-start(f32[2,384,128]{2,1,0:T(8,128)S(1)} %get-tuple-element.106), channel_id=1, source_target_pairs={{0,3},{1,2},{2,1},{3,0},{4,7},{5,6},{6,5},{7,4},{8,11},{9,10},{10,... | collective-permute-start | bytes 1179656 | tf_op jit(solution)/shard_map/ppermute | solution.py:512
  5.5 5.5 %collective-permute-done.refs_7_.refs_2_.refs_0_ = f32[2,96,384]{2,1,0:T(8,128)S(1)} collective-permute-done((f32[2,96,384]{2,1,0:T(8,128)}, f32[2,96,384]{2,1,0:T(8,128)S(1)}, u32[]{:S(2)}, u32[]{:S(2)}) %collective-permute-start) | collective-permute-done | bytes 294944 | tf_op jit(solution)/shard_map/ppermute | solution.py:496
  11.0 0.2 collective-permute-start.1
  11.2 1.9 %collective-permute-start.4 = (f32[2,96,128]{2,1,0:T(8,128)S(1)}, f32[2,96,128]{2,1,0:T(8,128)S(1)}, u32[]{:S(2)}, u32[]{:S(2)}) collective-permute-start(f32[2,96,128]{2,1,0:T(8,128)S(1)} %get-tuple-element.111), channel_id=1, source_target_pairs={{0,1},{1,0},{2,3},{3,2},{4,5},{5,4},{6,7},{7,6},{8,9},{9,8},{10,11... | collective-permute-start | bytes 294920 | tf_op jit(solution)/shard_map/ppermute | solution.py:501
  13.1 1.2 %collective-permute-start.2 = (f32[2,96,128]{2,1,0:T(8,128)S(1)}, f32[2,96,128]{2,1,0:T(8,128)S(1)}, u32[]{:S(2)}, u32[]{:S(2)}) collective-permute-start(f32[2,96,128]{2,1,0:T(8,128)S(1)} %get-tuple-element.112), channel_id=1, source_target_pairs={{0,3},{1,2},{2,1},{3,0},{4,7},{5,6},{6,5},{7,4},{8,11},{9,10},{10,... | collective-permute-start | bytes 294920 | tf_op jit(solution)/shard_map/ppermute | solution.py:512
  14.3 1.8 %prepare.1 = (f32[4,2,256,256]{3,2,1,0:T(8,128)S(1)}, f32[4,512,128]{2,1,0:T(8,128)S(1)}) custom-call(s32[2,2,2]{2,1,0:T(2,128)S(1)} %copy-done.5, f32[2,256,256]{2,1,0:T(8,128)S(1)} %copy-done.4, f32[512,512]{1,0:T(8,128)S(1)} %copy-done.3, bf16[256,256]{1,0:T(8,128)(2,1)S(1)} %copy-done.6), custom_call_target="tpu_custom_call" | custom-call | flops 100000 | bytes 100000 | tf_op jit(solution)/shard_map/prepare/pallas_call | solution.py:105
  16.1 2.6 %shard_map.73 = (f32[2,192,384]{2,1,0:T(8,128)S(1)}, f32[2,192,128]{2,1,0:T(8,128)S(1)}, f32[2,192,384]{2,1,0:T(8,128)S(1)}, f32[2,192,128]{2,1,0:T(8,128)S(1)}) custom-call(s32[2,2,2]{2,1,0:T(2,128)S(1)} %copy-done.5, bf16[4,256,256]{2,1,0:T(8,128)(2,1)S(1)} %copy-done.1, f32[4,128,128]{2,1,0:T(8,128)S(1)} %copy-done.2, ...), custom_call_target="tpu_custom_call" | custom-call | flops 100000 | bytes 100000 | tf_op jit(solution)/shard_map/pallas_call | solution.py:302
  18.8 2.7 %shard_map.74 = (f32[2,192,384]{2,1,0:T(8,128)S(1)}, f32[2,192,128]{2,1,0:T(8,128)S(1)}, f32[2,192,384]{2,1,0:T(8,128)S(1)}, f32[2,192,128]{2,1,0:T(8,128)S(1)}) custom-call(s32[2,2,2]{2,1,0:T(2,128)S(1)} %copy-done.5, bf16[4,256,256]{2,1,0:T(8,128)(2,1)S(1)} %copy-done.1, f32[4,128,128]{2,1,0:T(8,128)S(1)} %copy-done.2, ...), custom_call_target="tpu_custom_call" | custom-call | flops 100000 | bytes 100000 | tf_op jit(solution)/shard_map/pallas_call | solution.py:302
  21.4 0.6 collective-permute-start.9
  22.1 0.2 collective-permute-start.8
  22.3 1.5 %collective-permute-start.7 = (f32[2,96,128]{2,1,0:T(8,128)S(1)}, f32[2,96,128]{2,1,0:T(8,128)S(1)}, u32[]{:S(2)}, u32[]{:S(2)}) collective-permute-start(f32[2,96,128]{2,1,0:T(8,128)S(1)} %get-tuple-element.109), channel_id=1, source_target_pairs={{0,3},{1,2},{2,1},{3,0},{4,7},{5,6},{6,5},{7,4},{8,11},{9,10},{10,... | collective-permute-start | bytes 294920 | tf_op jit(solution)/shard_map/ppermute | solution.py:512
  23.9 1.3 %variation.4.refs_0_ = f32[2,192,384]{2,1,0:T(8,128)S(1)} custom-call(f32[2,96,128]{2,1,0:T(8,128)S(1)} %collective-permute-done.4.refs_5_.refs_0_, f32[2,384,128]{2,1,0:T(8,128)S(1)} %collective-permute-done.5.refs_6_.refs_1_.refs_5_.refs_0_, f32[2,96,384]{2,1,0:T(8,128)S(1)} %collective-permute-done.refs_7_.refs_2_.refs_0_, f32[2,384,384]{2,1,0:T(8,128)S(1)} %copy-done, ...), custom_call_target="tpu_custom_call" | custom-call | flops 100000 | bytes 100000 | tf_op jit(solution)/shard_map/variation/pallas_call | solution.py:363
  25.2 3.8 %collective-permute-done.9.far_ref = f32[2,192,128]{2,1,0:T(8,128)S(1)} collective-permute-done((f32[2,192,128]{2,1,0:T(8,128)S(1)}, f32[2,192,128]{2,1,0:T(8,128)S(1)}, u32[]{:S(2)}, u32[]{:S(2)}) %collective-permute-start.9) | collective-permute-done | bytes 196640 | tf_op jit(solution)/shard_map/ppermute | solution.py:512
  29.1 1.2 %collective-permute-start.12 = (f32[2,192,384]{2,1,0:T(8,128)S(1)}, f32[2,192,384]{2,1,0:T(8,128)S(1)}, u32[]{:S(2)}, u32[]{:S(2)}) collective-permute-start(f32[2,192,384]{2,1,0:T(8,128)S(1)} %totals.4.refs_2_), channel_id=1, source_target_pairs={{0,28},{4,0},{8,4},{12,8},{16,12},{20,16},{24,20},{28,24},{1,29},{... | collective-permute-start | bytes 1769480 | tf_op jit(solution)/shard_map/ppermute | solution.py:496
  30.3 0.3 collective-permute-done.7.refs_6_.refs_5_
  30.6 2.6 %shard_map.75 = (f32[2,384,384]{2,1,0:T(8,128)S(1)}, f32[2,384,128]{2,1,0:T(8,128)S(1)}) custom-call(s32[2,2,2]{2,1,0:T(2,128)S(1)} %copy-done.5, bf16[4,256,256]{2,1,0:T(8,128)(2,1)S(1)} %copy-done.1, f32[4,128,128]{2,1,0:T(8,128)S(1)} %copy-done.2, f32[4,2,256,256]{3,2,1,0:T(8,128)S(1)} %get-tuple-element.56.refs_3_, ...), custom_call_target="tpu_custom_call" | custom-call | flops 100000 | bytes 100000 | tf_op jit(solution)/shard_map/pallas_call | solution.py:302
  33.3 2.7 %shard_map.76 = (f32[2,384,384]{2,1,0:T(8,128)S(1)}, f32[2,384,128]{2,1,0:T(8,128)S(1)}) custom-call(s32[2,2,2]{2,1,0:T(2,128)S(1)} %copy-done.5, bf16[4,256,256]{2,1,0:T(8,128)(2,1)S(1)} %copy-done.1, f32[4,128,128]{2,1,0:T(8,128)S(1)} %copy-done.2, f32[4,2,256,256]{3,2,1,0:T(8,128)S(1)} %get-tuple-element.56.refs_3_, ...), custom_call_target="tpu_custom_call" | custom-call | flops 100000 | bytes 100000 | tf_op jit(solution)/shard_map/pallas_call | solution.py:302
  35.9 0.4 collective-permute-start.10
  36.4 2.1 %collective-permute-start.11 = (f32[2,384,128]{2,1,0:T(8,128)S(1)}, f32[2,384,128]{2,1,0:T(8,128)S(1)}, u32[]{:S(2)}, u32[]{:S(2)}) collective-permute-start(f32[2,384,128]{2,1,0:T(8,128)S(1)} %get-tuple-element.72), channel_id=1, source_target_pairs={{1,2},{2,1},{5,6},{6,5},{9,10},{10,9},{13,14},{14,13},{17,18},{18,... | collective-permute-start | bytes 1179656 | tf_op jit(solution)/shard_map/ppermute | solution.py:512
  38.5 1.3 %variation.5.refs_1_ = f32[2,192,384]{2,1,0:T(8,128)S(1)} custom-call(f32[2,384,128]{2,1,0:T(8,128)S(1)} %collective-permute-done.5.refs_6_.refs_1_.refs_5_.refs_0_, f32[2,96,128]{2,1,0:T(8,128)S(1)} %collective-permute-done.6.refs_6_.refs_1_, f32[2,384,384]{2,1,0:T(8,128)S(1)} %copy-done, f32[2,96,384]{2,1,0:T(8,128)S(1)} %collective-permute-done.1.refs_8_.refs_3_.refs_1_, ...), custom_call_target="tpu_custom_call" | custom-call | flops 100000 | bytes 100000 | tf_op jit(solution)/shard_map/variation/pallas_call | solution.py:363
  39.8 5.9 %collective-permute-done.11.far_ref = f32[2,384,128]{2,1,0:T(8,128)S(1)} collective-permute-done((f32[2,384,128]{2,1,0:T(8,128)S(1)}, f32[2,384,128]{2,1,0:T(8,128)S(1)}, u32[]{:S(2)}, u32[]{:S(2)}) %collective-permute-start.11) | collective-permute-done | bytes 393248 | tf_op jit(solution)/shard_map/ppermute | solution.py:512
  45.8 0.2 totals.5
  45.9 1.3 %collective-permute-start.15 = (f32[2,192,384]{2,1,0:T(8,128)S(1)}, f32[2,192,384]{2,1,0:T(8,128)S(1)}, u32[]{:S(2)}, u32[]{:S(2)}) collective-permute-start(f32[2,192,384]{2,1,0:T(8,128)S(1)} %get-tuple-element.74.refs_3_), channel_id=1, source_target_pairs={{0,4},{4,8},{8,12},{12,16},{16,20},{20,24},{24,28},{28,0},{1,5},{5... | collective-permute-start | bytes 1769480 | tf_op jit(solution)/shard_map/ppermute | solution.py:496
  47.3 9.5 %collective-permute-done.12.refs_4_ = f32[2,192,384]{2,1,0:T(8,128)S(1)} collective-permute-done((f32[2,192,384]{2,1,0:T(8,128)S(1)}, f32[2,192,384]{2,1,0:T(8,128)S(1)}, u32[]{:S(2)}, u32[]{:S(2)}) %collective-permute-start.12) | collective-permute-done | bytes 589856 | tf_op jit(solution)/shard_map/ppermute | solution.py:496
  56.8 0.2 update.2
  57.0 0.8 collective-permute-start.14
  57.8 2.3 %collective-permute-start.13 = (f32[2,384,128]{2,1,0:T(8,128)S(1)}, f32[2,384,128]{2,1,0:T(8,128)S(1)}, u32[]{:S(2)}, u32[]{:S(2)}) collective-permute-start(f32[2,384,128]{2,1,0:T(8,128)S(1)} %get-tuple-element.75), channel_id=1, source_target_pairs={{1,2},{2,1},{5,6},{6,5},{9,10},{10,9},{13,14},{14,13},{17,18},{18,... | collective-permute-start | bytes 1179656 | tf_op jit(solution)/shard_map/ppermute | solution.py:512
  60.1 2.6 %shard_map.77 = (f32[2,192,384]{2,1,0:T(8,128)S(1)}, f32[2,192,128]{2,1,0:T(8,128)S(1)}, f32[2,192,384]{2,1,0:T(8,128)S(1)}, f32[2,192,128]{2,1,0:T(8,128)S(1)}) custom-call(s32[2,2,2]{2,1,0:T(2,128)S(1)} %copy-done.5, bf16[4,256,256]{2,1,0:T(8,128)(2,1)S(1)} %copy-done.1, f32[4,128,128]{2,1,0:T(8,128)S(1)} %copy-done.2, ...), custom_call_target="tpu_custom_call" | custom-call | flops 100000 | bytes 100000 | tf_op jit(solution)/shard_map/pallas_call | solution.py:302
  62.8 4.1 %collective-permute-done.13.refs_5_.refs_2_.refs_6_ = f32[2,384,128]{2,1,0:T(8,128)S(1)} collective-permute-done((f32[2,384,128]{2,1,0:T(8,128)S(1)}, f32[2,384,128]{2,1,0:T(8,128)S(1)}, u32[]{:S(2)}, u32[]{:S(2)}) %collective-permute-start.13) | collective-permute-done | bytes 393248 | tf_op jit(solution)/shard_map/ppermute | solution.py:512
  66.9 2.7 %shard_map.78 = (f32[2,192,384]{2,1,0:T(8,128)S(1)}, f32[2,192,128]{2,1,0:T(8,128)S(1)}, f32[2,192,384]{2,1,0:T(8,128)S(1)}, f32[2,192,128]{2,1,0:T(8,128)S(1)}) custom-call(s32[2,2,2]{2,1,0:T(2,128)S(1)} %copy-done.5, bf16[4,256,256]{2,1,0:T(8,128)(2,1)S(1)} %copy-done.1, f32[4,128,128]{2,1,0:T(8,128)S(1)} %copy-done.2, ...), custom_call_target="tpu_custom_call" | custom-call | flops 100000 | bytes 100000 | tf_op jit(solution)/shard_map/pallas_call | solution.py:302
  69.8 0.3 collective-permute-start.19
  70.1 0.4 collective-permute-start.18
  70.5 1.5 %collective-permute-start.16 = (f32[2,192,128]{2,1,0:T(8,128)S(1)}, f32[2,192,128]{2,1,0:T(8,128)S(1)}, u32[]{:S(2)}, u32[]{:S(2)}) collective-permute-start(f32[2,192,128]{2,1,0:T(8,128)S(1)} %get-tuple-element.84), channel_id=1, source_target_pairs={{0,3},{1,2},{2,1},{3,0},{4,7},{5,6},{6,5},{7,4},{8,11},{9,10},{10,... | collective-permute-start | bytes 589832 | tf_op jit(solution)/shard_map/ppermute | solution.py:512
  72.0 2.6 %shard_map.79 = (f32[2,96,384]{2,1,0:T(8,128)S(1)}, f32[2,96,128]{2,1,0:T(8,128)S(1)}, f32[2,288,384]{2,1,0:T(8,128)S(1)}, f32[2,288,128]{2,1,0:T(8,128)S(1)}) custom-call(s32[2,2,2]{2,1,0:T(2,128)S(1)} %copy-done.5, bf16[4,256,256]{2,1,0:T(8,128)(2,1)S(1)} %copy-done.1, f32[4,128,128]{2,1,0:T(8,128)S(1)} %copy-done.2, ...), custom_call_target="tpu_custom_call" | custom-call | flops 100000 | bytes 100000 | tf_op jit(solution)/shard_map/pallas_call | solution.py:302
  74.8 1.3 %variation.6.refs_0_.refs_1_ = f32[2,192,384]{2,1,0:T(8,128)S(1)} custom-call(f32[2,384,128]{2,1,0:T(8,128)S(1)} %collective-permute-done.14.refs_5_.refs_6_.refs_0_.refs_1_, f32[2,384,384]{2,1,0:T(8,128)S(1)} %get-tuple-element.76.refs_6_.refs_8_.refs_1_.refs_3_.bottom_ref, f32[2,384,128]{2,1,0:T(8,128)S(1)} %collective-permute-done.13.refs_5_.refs_2_.refs_6_), custom_call_target="tpu_custom_call" | custom-call | flops 100000 | bytes 100000 | tf_op jit(solution)/shard_map/variation/pallas_call | solution.py:363
  76.2 1.2 %collective-permute-done.19.far_ref = f32[2,192,128]{2,1,0:T(8,128)S(1)} collective-permute-done((f32[2,192,128]{2,1,0:T(8,128)S(1)}, f32[2,192,128]{2,1,0:T(8,128)S(1)}, u32[]{:S(2)}, u32[]{:S(2)}) %collective-permute-start.19) | collective-permute-done | bytes 196640 | tf_op jit(solution)/shard_map/ppermute | solution.py:512
  77.4 3.6 %collective-permute-done.16.refs_5_.refs_4_ = f32[2,192,128]{2,1,0:T(8,128)S(1)} collective-permute-done((f32[2,192,128]{2,1,0:T(8,128)S(1)}, f32[2,192,128]{2,1,0:T(8,128)S(1)}, u32[]{:S(2)}, u32[]{:S(2)}) %collective-permute-start.16) | collective-permute-done | bytes 196640 | tf_op jit(solution)/shard_map/ppermute | solution.py:512
  81.0 2.7 %shard_map.80 = (f32[2,96,384]{2,1,0:T(8,128)S(1)}, f32[2,96,128]{2,1,0:T(8,128)S(1)}, f32[2,288,384]{2,1,0:T(8,128)S(1)}, f32[2,288,128]{2,1,0:T(8,128)S(1)}) custom-call(s32[2,2,2]{2,1,0:T(2,128)S(1)} %copy-done.5, bf16[4,256,256]{2,1,0:T(8,128)(2,1)S(1)} %copy-done.1, f32[4,128,128]{2,1,0:T(8,128)S(1)} %copy-done.2, ...), custom_call_target="tpu_custom_call" | custom-call | flops 100000 | bytes 100000 | tf_op jit(solution)/shard_map/pallas_call | solution.py:302
  83.8 0.5 collective-permute-start.20
  84.3 2.4 %collective-permute-start.24 = (f32[2,96,384]{2,1,0:T(8,128)S(1)}, f32[2,96,384]{2,1,0:T(8,128)S(1)}, u32[]{:S(2)}, u32[]{:S(2)}) collective-permute-start(f32[2,96,384]{2,1,0:T(8,128)S(1)} %sums_near.1), channel_id=1, source_target_pairs={{0,28},{4,0},{8,4},{12,8},{16,12},{20,16},{24,20},{28,24},{1,29},{... | collective-permute-start | bytes 884744 | tf_op jit(solution)/shard_map/ppermute | solution.py:496
  86.7 1.7 %collective-permute-start.25 = (f32[2,96,128]{2,1,0:T(8,128)S(1)}, f32[2,96,128]{2,1,0:T(8,128)S(1)}, u32[]{:S(2)}, u32[]{:S(2)}) collective-permute-start(f32[2,96,128]{2,1,0:T(8,128)S(1)} %get-tuple-element.104), channel_id=1, source_target_pairs={{0,31},{1,30},{2,29},{3,28},{4,3},{5,2},{6,1},{7,0},{8,7},{9,6},{1... | collective-permute-start | bytes 294920 | tf_op jit(solution)/shard_map/ppermute | solution.py:522
  88.4 1.3 %variation.7.refs_0_ = f32[2,192,384]{2,1,0:T(8,128)S(1)} custom-call(f32[2,192,128]{2,1,0:T(8,128)S(1)} %collective-permute-done.17.refs_5_.refs_0_, f32[2,384,128]{2,1,0:T(8,128)S(1)} %collective-permute-done.14.refs_5_.refs_6_.refs_0_.refs_1_, f32[2,192,384]{2,1,0:T(8,128)S(1)} %get-tuple-element.83.refs_7_.refs_2_.top_ref, ...), custom_call_target="tpu_custom_call" | custom-call | flops 100000 | bytes 100000 | tf_op jit(solution)/shard_map/variation/pallas_call | solution.py:363
  89.8 3.3 %collective-permute-done.21.far_ref = f32[2,288,128]{2,1,0:T(8,128)S(1)} collective-permute-done((f32[2,288,128]{2,1,0:T(8,128)S(1)}, f32[2,288,128]{2,1,0:T(8,128)S(1)}, u32[]{:S(2)}, u32[]{:S(2)}) %collective-permute-start.21) | collective-permute-done | bytes 294944 | tf_op jit(solution)/shard_map/ppermute | solution.py:512
  93.3 10.4 %collective-permute-done.25.corner_ref = f32[2,96,128]{2,1,0:T(8,128)S(1)} collective-permute-done((f32[2,96,128]{2,1,0:T(8,128)S(1)}, f32[2,96,128]{2,1,0:T(8,128)S(1)}, u32[]{:S(2)}, u32[]{:S(2)}) %collective-permute-start.25) | collective-permute-done | bytes 98336 | tf_op jit(solution)/shard_map/ppermute | solution.py:522
  103.6 1.2 %finish.1 = f32[2,384,384]{2,1,0:T(8,128)} custom-call(f32[2,192,384]{2,1,0:T(8,128)S(1)} %get-tuple-element.83.refs_7_.refs_2_.top_ref, f32[2,384,384]{2,1,0:T(8,128)S(1)} %get-tuple-element.76.refs_6_.refs_8_.refs_1_.refs_3_.bottom_ref, f32[2,288,384]{2,1,0:T(8,128)S(1)} %totals.7.mid_ref, f32[2,96,384]{2,1,0:T(8,128)S(1)} %get-tuple-element.100.low_ref, ...), custom_call_target="tpu_custom_call" | custom-call | flops 100000 | bytes 100000 | tf_op jit(solution)/shard_map/finish/pallas_call | solution.py:483
  (43 shorter events, 1.0 us)
Async XLA Ops:
  0.0 3.2 %copy-start = (f32[2,384,384]{2,1,0:T(8,128)S(1)}, f32[2,384,384]{2,1,0:T(8,128)}, u32[]{:S(2)}) copy-start(f32[2,384,384]{2,1,0:T(8,128)} %refs_1_.9) | copy-start | bytes 3538948
  1.9 12.4 %copy-start.3 = (f32[512,512]{1,0:T(8,128)S(1)}, f32[512,512]{1,0:T(8,128)}, u32[]{:S(2)}) copy-start(f32[512,512]{1,0:T(8,128)} %amp_ref.1) | copy-start | bytes 3145732
  1.9 12.4 %copy-start.4 = (f32[2,256,256]{2,1,0:T(8,128)S(1)}, f32[2,256,256]{2,1,0:T(8,128)}, u32[]{:S(2)}) copy-start(f32[2,256,256]{2,1,0:T(8,128)} %probe_ref.1) | copy-start | bytes 1572868
  1.9 12.4 %copy-start.5 = (s32[2,2,2]{2,1,0:T(2,128)S(1)}, s32[2,2,2]{2,1,0:T(2,128)}, u32[]{:S(2)}) copy-start(s32[2,2,2]{2,1,0:T(2,128)} %refs_0_.17) | copy-start | bytes 100
  1.9 12.4 %copy-start.6 = (bf16[256,256]{1,0:T(8,128)(2,1)S(1)}, bf16[256,256]{1,0:T(8,128)(2,1)}, u32[]{:S(2)}) copy-start(bf16[256,256]{1,0:T(8,128)(2,1)} %constant.30.clone.order_ref) | copy-start | bytes 393220
  1.9 9.1 %collective-permute-start = (f32[2,96,384]{2,1,0:T(8,128)}, f32[2,96,384]{2,1,0:T(8,128)S(1)}, u32[]{:S(2)}, u32[]{:S(2)}) collective-permute-start(f32[2,96,384]{2,1,0:T(8,128)} %get-tuple-element.107), channel_id=1, source_target_pairs={{0,4},{4,8},{8,12},{12,16},{16,20},{20,24},{24,28},{28,0},{1,5},{5... | collective-permute-start | bytes 884744 | tf_op jit(solution)/shard_map/ppermute | solution.py:496
  3.2 12.9 %copy-start.1 = (bf16[4,256,256]{2,1,0:T(8,128)(2,1)S(1)}, bf16[4,256,256]{2,1,0:T(8,128)(2,1)}, u32[]{:S(2)}) copy-start(bf16[4,256,256]{2,1,0:T(8,128)(2,1)} %constant.28.clone.refs_1_) | copy-start | bytes 1572868
  3.3 12.8 %copy-start.2 = (f32[4,128,128]{2,1,0:T(8,128)S(1)}, f32[4,128,128]{2,1,0:T(8,128)}, u32[]{:S(2)}) copy-start(f32[4,128,128]{2,1,0:T(8,128)} %constant.29.clone.refs_2_) | copy-start | bytes 786436
  3.3 12.8 %collective-permute-start.5 = (f32[2,384,128]{2,1,0:T(8,128)S(1)}, f32[2,384,128]{2,1,0:T(8,128)S(1)}, u32[]{:S(2)}, u32[]{:S(2)}) collective-permute-start(f32[2,384,128]{2,1,0:T(8,128)S(1)} %get-tuple-element.105), channel_id=1, source_target_pairs={{0,1},{1,0},{2,3},{3,2},{4,5},{5,4},{6,7},{7,6},{8,9},{9,8},{10,11... | collective-permute-start | bytes 1179656 | tf_op jit(solution)/shard_map/ppermute | solution.py:501
  4.3 14.5 %collective-permute-start.3 = (f32[2,384,128]{2,1,0:T(8,128)S(1)}, f32[2,384,128]{2,1,0:T(8,128)S(1)}, u32[]{:S(2)}, u32[]{:S(2)}) collective-permute-start(f32[2,384,128]{2,1,0:T(8,128)S(1)} %get-tuple-element.106), channel_id=1, source_target_pairs={{0,3},{1,2},{2,1},{3,0},{4,7},{5,6},{6,5},{7,4},{8,11},{9,10},{10,... | collective-permute-start | bytes 1179656 | tf_op jit(solution)/shard_map/ppermute | solution.py:512
  11.0 11.3 %collective-permute-start.1 = (f32[2,96,384]{2,1,0:T(8,128)S(1)}, f32[2,96,384]{2,1,0:T(8,128)S(1)}, u32[]{:S(2)}, u32[]{:S(2)}) collective-permute-start(f32[2,96,384]{2,1,0:T(8,128)S(1)} %get-tuple-element.58), channel_id=1, source_target_pairs={{0,28},{4,0},{8,4},{12,8},{16,12},{20,16},{24,20},{28,24},{1,29},{... | collective-permute-start | bytes 884744 | tf_op jit(solution)/shard_map/ppermute | solution.py:496
  11.2 4.9 %collective-permute-start.4 = (f32[2,96,128]{2,1,0:T(8,128)S(1)}, f32[2,96,128]{2,1,0:T(8,128)S(1)}, u32[]{:S(2)}, u32[]{:S(2)}) collective-permute-start(f32[2,96,128]{2,1,0:T(8,128)S(1)} %get-tuple-element.111), channel_id=1, source_target_pairs={{0,1},{1,0},{2,3},{3,2},{4,5},{5,4},{6,7},{7,6},{8,9},{9,8},{10,11... | collective-permute-start | bytes 294920 | tf_op jit(solution)/shard_map/ppermute | solution.py:501
  13.1 5.7 %collective-permute-start.2 = (f32[2,96,128]{2,1,0:T(8,128)S(1)}, f32[2,96,128]{2,1,0:T(8,128)S(1)}, u32[]{:S(2)}, u32[]{:S(2)}) collective-permute-start(f32[2,96,128]{2,1,0:T(8,128)S(1)} %get-tuple-element.112), channel_id=1, source_target_pairs={{0,3},{1,2},{2,1},{3,0},{4,7},{5,6},{6,5},{7,4},{8,11},{9,10},{10,... | collective-permute-start | bytes 294920 | tf_op jit(solution)/shard_map/ppermute | solution.py:512
  21.4 7.6 %collective-permute-start.9 = (f32[2,192,128]{2,1,0:T(8,128)S(1)}, f32[2,192,128]{2,1,0:T(8,128)S(1)}, u32[]{:S(2)}, u32[]{:S(2)}) collective-permute-start(f32[2,192,128]{2,1,0:T(8,128)S(1)} %get-tuple-element.61), channel_id=1, source_target_pairs={{0,3},{1,2},{2,1},{3,0},{4,7},{5,6},{6,5},{7,4},{8,11},{9,10},{10,... | collective-permute-start | bytes 589832 | tf_op jit(solution)/shard_map/ppermute | solution.py:512
  22.1 7.0 %collective-permute-start.8 = (f32[2,192,128]{2,1,0:T(8,128)S(1)}, f32[2,192,128]{2,1,0:T(8,128)S(1)}, u32[]{:S(2)}, u32[]{:S(2)}) collective-permute-start(f32[2,192,128]{2,1,0:T(8,128)S(1)} %get-tuple-element.65), channel_id=1, source_target_pairs={{0,1},{1,0},{2,3},{3,2},{4,5},{5,4},{6,7},{7,6},{8,9},{9,8},{10,11... | collective-permute-start | bytes 589832 | tf_op jit(solution)/shard_map/ppermute | solution.py:501
  22.3 8.3 %collective-permute-start.7 = (f32[2,96,128]{2,1,0:T(8,128)S(1)}, f32[2,96,128]{2,1,0:T(8,128)S(1)}, u32[]{:S(2)}, u32[]{:S(2)}) collective-permute-start(f32[2,96,128]{2,1,0:T(8,128)S(1)} %get-tuple-element.109), channel_id=1, source_target_pairs={{0,3},{1,2},{2,1},{3,0},{4,7},{5,6},{6,5},{7,4},{8,11},{9,10},{10,... | collective-permute-start | bytes 294920 | tf_op jit(solution)/shard_map/ppermute | solution.py:512
  23.8 9.5 %collective-permute-start.6 = (f32[2,96,128]{2,1,0:T(8,128)S(1)}, f32[2,96,128]{2,1,0:T(8,128)S(1)}, u32[]{:S(2)}, u32[]{:S(2)}) collective-permute-start(f32[2,96,128]{2,1,0:T(8,128)S(1)} %get-tuple-element.110), channel_id=1, source_target_pairs={{0,1},{1,0},{2,3},{3,2},{4,5},{5,4},{6,7},{7,6},{8,9},{9,8},{10,11... | collective-permute-start | bytes 294920 | tf_op jit(solution)/shard_map/ppermute | solution.py:501
  29.1 27.7 %collective-permute-start.12 = (f32[2,192,384]{2,1,0:T(8,128)S(1)}, f32[2,192,384]{2,1,0:T(8,128)S(1)}, u32[]{:S(2)}, u32[]{:S(2)}) collective-permute-start(f32[2,192,384]{2,1,0:T(8,128)S(1)} %totals.4.refs_2_), channel_id=1, source_target_pairs={{0,28},{4,0},{8,4},{12,8},{16,12},{20,16},{24,20},{28,24},{1,29},{... | collective-permute-start | bytes 1769480 | tf_op jit(solution)/shard_map/ppermute | solution.py:496
  35.9 3.9 %collective-permute-start.10 = (f32[2,384,128]{2,1,0:T(8,128)S(1)}, f32[2,384,128]{2,1,0:T(8,128)S(1)}, u32[]{:S(2)}, u32[]{:S(2)}) collective-permute-start(f32[2,384,128]{2,1,0:T(8,128)S(1)} %get-tuple-element.71), channel_id=1, source_target_pairs={{0,1},{1,0},{2,3},{3,2},{4,5},{5,4},{6,7},{7,6},{8,9},{9,8},{10,11... | collective-permute-start | bytes 1179656 | tf_op jit(solution)/shard_map/ppermute | solution.py:501
  36.4 9.4 %collective-permute-start.11 = (f32[2,384,128]{2,1,0:T(8,128)S(1)}, f32[2,384,128]{2,1,0:T(8,128)S(1)}, u32[]{:S(2)}, u32[]{:S(2)}) collective-permute-start(f32[2,384,128]{2,1,0:T(8,128)S(1)} %get-tuple-element.72), channel_id=1, source_target_pairs={{1,2},{2,1},{5,6},{6,5},{9,10},{10,9},{13,14},{14,13},{17,18},{18,... | collective-permute-start | bytes 1179656 | tf_op jit(solution)/shard_map/ppermute | solution.py:512
  45.9 23.6 %collective-permute-start.15 = (f32[2,192,384]{2,1,0:T(8,128)S(1)}, f32[2,192,384]{2,1,0:T(8,128)S(1)}, u32[]{:S(2)}, u32[]{:S(2)}) collective-permute-start(f32[2,192,384]{2,1,0:T(8,128)S(1)} %get-tuple-element.74.refs_3_), channel_id=1, source_target_pairs={{0,4},{4,8},{8,12},{12,16},{16,20},{20,24},{24,28},{28,0},{1,5},{5... | collective-permute-start | bytes 1769480 | tf_op jit(solution)/shard_map/ppermute | solution.py:496
  57.0 3.1 %collective-permute-start.14 = (f32[2,384,128]{2,1,0:T(8,128)S(1)}, f32[2,384,128]{2,1,0:T(8,128)S(1)}, u32[]{:S(2)}, u32[]{:S(2)}) collective-permute-start(f32[2,384,128]{2,1,0:T(8,128)S(1)} %get-tuple-element.77), channel_id=1, source_target_pairs={{0,1},{1,0},{2,3},{3,2},{4,5},{5,4},{6,7},{7,6},{8,9},{9,8},{10,11... | collective-permute-start | bytes 1179656 | tf_op jit(solution)/shard_map/ppermute | solution.py:501
  57.8 9.1 %collective-permute-start.13 = (f32[2,384,128]{2,1,0:T(8,128)S(1)}, f32[2,384,128]{2,1,0:T(8,128)S(1)}, u32[]{:S(2)}, u32[]{:S(2)}) collective-permute-start(f32[2,384,128]{2,1,0:T(8,128)S(1)} %get-tuple-element.75), channel_id=1, source_target_pairs={{1,2},{2,1},{5,6},{6,5},{9,10},{10,9},{13,14},{14,13},{17,18},{18,... | collective-permute-start | bytes 1179656 | tf_op jit(solution)/shard_map/ppermute | solution.py:512
  69.7 2.3 %collective-permute-start.17 = (f32[2,192,128]{2,1,0:T(8,128)S(1)}, f32[2,192,128]{2,1,0:T(8,128)S(1)}, u32[]{:S(2)}, u32[]{:S(2)}) collective-permute-start(f32[2,192,128]{2,1,0:T(8,128)S(1)} %get-tuple-element.85), channel_id=1, source_target_pairs={{0,1},{1,0},{2,3},{3,2},{4,5},{5,4},{6,7},{7,6},{8,9},{9,8},{10,11... | collective-permute-start | bytes 589832 | tf_op jit(solution)/shard_map/ppermute | solution.py:501
  69.8 7.6 %collective-permute-start.19 = (f32[2,192,128]{2,1,0:T(8,128)S(1)}, f32[2,192,128]{2,1,0:T(8,128)S(1)}, u32[]{:S(2)}, u32[]{:S(2)}) collective-permute-start(f32[2,192,128]{2,1,0:T(8,128)S(1)} %get-tuple-element.80), channel_id=1, source_target_pairs={{0,3},{1,2},{2,1},{3,0},{4,7},{5,6},{6,5},{7,4},{8,11},{9,10},{10,... | collective-permute-start | bytes 589832 | tf_op jit(solution)/shard_map/ppermute | solution.py:512
  70.1 7.3 %collective-permute-start.18 = (f32[2,192,128]{2,1,0:T(8,128)S(1)}, f32[2,192,128]{2,1,0:T(8,128)S(1)}, u32[]{:S(2)}, u32[]{:S(2)}) collective-permute-start(f32[2,192,128]{2,1,0:T(8,128)S(1)} %get-tuple-element.93), channel_id=1, source_target_pairs={{0,1},{1,0},{2,3},{3,2},{4,5},{5,4},{6,7},{7,6},{8,9},{9,8},{10,11... | collective-permute-start | bytes 589832 | tf_op jit(solution)/shard_map/ppermute | solution.py:501
  70.5 10.5 %collective-permute-start.16 = (f32[2,192,128]{2,1,0:T(8,128)S(1)}, f32[2,192,128]{2,1,0:T(8,128)S(1)}, u32[]{:S(2)}, u32[]{:S(2)}) collective-permute-start(f32[2,192,128]{2,1,0:T(8,128)S(1)} %get-tuple-element.84), channel_id=1, source_target_pairs={{0,3},{1,2},{2,1},{3,0},{4,7},{5,6},{6,5},{7,4},{8,11},{9,10},{10,... | collective-permute-start | bytes 589832 | tf_op jit(solution)/shard_map/ppermute | solution.py:512
  74.7 9.6 %collective-permute-start.23 = (f32[2,96,128]{2,1,0:T(8,128)S(1)}, f32[2,96,128]{2,1,0:T(8,128)S(1)}, u32[]{:S(2)}, u32[]{:S(2)}) collective-permute-start(f32[2,96,128]{2,1,0:T(8,128)S(1)} %get-tuple-element.103), channel_id=1, source_target_pairs={{0,1},{1,0},{2,3},{3,2},{4,5},{5,4},{6,7},{7,6},{8,9},{9,8},{10,11... | collective-permute-start | bytes 294920 | tf_op jit(solution)/shard_map/ppermute | solution.py:501
  83.7 9.4 %collective-permute-start.21 = (f32[2,288,128]{2,1,0:T(8,128)S(1)}, f32[2,288,128]{2,1,0:T(8,128)S(1)}, u32[]{:S(2)}, u32[]{:S(2)}) collective-permute-start(f32[2,288,128]{2,1,0:T(8,128)S(1)} %get-tuple-element.99), channel_id=1, source_target_pairs={{0,3},{1,2},{2,1},{3,0},{4,7},{5,6},{6,5},{7,4},{8,11},{9,10},{10,... | collective-permute-start | bytes 884744 | tf_op jit(solution)/shard_map/ppermute | solution.py:512
  83.8 9.3 %collective-permute-start.20 = (f32[2,288,128]{2,1,0:T(8,128)S(1)}, f32[2,288,128]{2,1,0:T(8,128)S(1)}, u32[]{:S(2)}, u32[]{:S(2)}) collective-permute-start(f32[2,288,128]{2,1,0:T(8,128)S(1)} %get-tuple-element.98), channel_id=1, source_target_pairs={{0,1},{1,0},{2,3},{3,2},{4,5},{5,4},{6,7},{7,6},{8,9},{9,8},{10,11... | collective-permute-start | bytes 884744 | tf_op jit(solution)/shard_map/ppermute | solution.py:501
  84.2 19.4 %collective-permute-start.22 = (f32[2,96,384]{2,1,0:T(8,128)S(1)}, f32[2,96,384]{2,1,0:T(8,128)S(1)}, u32[]{:S(2)}, u32[]{:S(2)}) collective-permute-start(f32[2,96,384]{2,1,0:T(8,128)S(1)} %get-tuple-element.101), channel_id=1, source_target_pairs={{0,4},{4,8},{8,12},{12,16},{16,20},{20,24},{24,28},{28,0},{1,5},{5... | collective-permute-start | bytes 884744 | tf_op jit(solution)/shard_map/ppermute | solution.py:496
  84.3 19.3 %collective-permute-start.24 = (f32[2,96,384]{2,1,0:T(8,128)S(1)}, f32[2,96,384]{2,1,0:T(8,128)S(1)}, u32[]{:S(2)}, u32[]{:S(2)}) collective-permute-start(f32[2,96,384]{2,1,0:T(8,128)S(1)} %sums_near.1), channel_id=1, source_target_pairs={{0,28},{4,0},{8,4},{12,8},{16,12},{20,16},{24,20},{28,24},{1,29},{... | collective-permute-start | bytes 884744 | tf_op jit(solution)/shard_map/ppermute | solution.py:496
  86.7 16.9 %collective-permute-start.25 = (f32[2,96,128]{2,1,0:T(8,128)S(1)}, f32[2,96,128]{2,1,0:T(8,128)S(1)}, u32[]{:S(2)}, u32[]{:S(2)}) collective-permute-start(f32[2,96,128]{2,1,0:T(8,128)S(1)} %get-tuple-element.104), channel_id=1, source_target_pairs={{0,31},{1,30},{2,29},{3,28},{4,3},{5,2},{6,1},{7,0},{8,7},{9,6},{1... | collective-permute-start | bytes 294920 | tf_op jit(solution)/shard_map/ppermute | solution.py:522
